TPU v7x, 256 devices: a whole 4x4x8 slice. The times are simulated.
256 devices in a mesh: segment: 4 (over z_lo, core), zero: 64 (over x, y, z_hi).
Axes of the slice: x: 4, y: 4, z: 8 (z_hi: 4, z_lo: 2; z = z_hi * 2 + z_lo), core: 2. Of those that a mesh axis runs over, the one named last changes fastest.
Arguments:
- inputs: bfloat16 [2, 2, 8192, 2048], P(None, None, 'zero'), may hold values from -6 to 6
- cotangent: bfloat16 [2, 2, 8192, 2048], P(None, None, 'zero'), may hold values from -0.078125 to 0.078125
- norm_gain: bfloat16 [4, 2048], P('segment', 'zero'), may hold values from 0.099609375 to 1.8984375
- proj_in: bfloat16 [4, 2048, 256], P('segment', 'zero'), may hold values from -0.125 to 0.125
- proj_out: bfloat16 [4, 256, 2048], P('segment', 'zero'), may hold values from -0.375 to 0.375
Outputs:
- grad_norm_gain: float32 [4, 2048], P('segment', 'zero')
- grad_proj_in: float32 [4, 2048, 256], P('segment', 'zero')
- grad_proj_out: float32 [4, 256, 2048], P('segment', 'zero')
All inputs are finite; a program needn't handle non-finite values.
Results may differ from a plain program's by a relative error of at most 0.012.
Values may be sent and summed in bfloat16 or wider, within the bound.
No kernel may reach another device: no remote copies, remote signals or barrier semaphores. Data moves between devices by JAX's collectives and lax.ppermute only.
A program may use at most 64 MiB of HBM per device.

v0:
```python
import functools
import itertools

import jax
import jax.numpy as jnp
import numpy as np
from jax import lax
from jax.experimental import pallas as pl
from jax.experimental.pallas import tpu as pltpu
from jax.sharding import Mesh
from jax.sharding import PartitionSpec as P


gelu_coeff = 0.7978845608028654
cubic_coeff = 0.044715
norm_eps = 1e-05

AXES = ("zl", "c", "x", "y", "zh")
DIMS = (2, 2, 4, 4, 4)
D = 2048
R = 256
ROWS = 128
CHUNK = 16
F32 = jnp.float32
BF16 = jnp.bfloat16


def flat_perm(move):
    pairs = []
    for src, coords in enumerate(itertools.product(*[range(n) for n in DIMS])):
        dst = [v % n for v, n in zip(move(*coords), DIMS)]
        pairs.append((src, int(np.ravel_multi_index(dst, DIMS))))
    return pairs


def send_first(k):
    return flat_perm(
        lambda zl, c, x, y, zh: (zl, c, x + k, y, zh) if c == 0 else (zl, c, x, y + k, zh)
    )


def send_second(k):
    return flat_perm(
        lambda zl, c, x, y, zh: (zl, c, x, y + k, zh) if c == 0 else (zl, c, x + k, y, zh)
    )


SWAP = flat_perm(lambda zl, c, x, y, zh: (zl, c + 1, x, y, zh))


def shift(value, pairs):
    return lax.ppermute(value, AXES, pairs)


def dot(left, right, left_dim=1, right_dim=0):
    return lax.dot_general(
        left, right, (((left_dim,), (right_dim,)), ((), ())), preferred_element_type=F32
    )


def gelu_parts(v):
    inner = jnp.tanh(gelu_coeff * (v + cubic_coeff * v * v * v))
    return inner, (0.5 * v * (1.0 + inner)).astype(BF16)


def gelu_slope(v, inner):
    return 0.5 * (1.0 + inner) + 0.5 * v * (1.0 - inner * inner) * gelu_coeff * (
        1.0 + 3.0 * cubic_coeff * v * v
    )


def weight_copies(s_ref, pieces, win, wout, sems):
    mx, my, c = s_ref[0], s_ref[1], s_ref[2]
    copies = []
    for o in range(2):
        par = c if o == 0 else 1 - c
        for b in range(4):
            for a in range(4):
                x = (mx + jnp.where(par == 0, a, b)) & 3
                y = (my + jnp.where(par == 0, b, a)) & 3
                xy = x * 4 + y
                src = pieces[o * 4 + b]
                n = (b * 4 + a) * 2
                copies.append(
                    pltpu.make_async_copy(
                        src.at[a, pl.ds(0, 8)], win.at[par, pl.ds(xy * 8, 8)], sems.at[par, n]
                    )
                )
                copies.append(
                    pltpu.make_async_copy(
                        src.at[a, pl.ds(8, 9)], wout.at[par, :, xy], sems.at[par, n + 1]
                    )
                )
    return copies


def wait_layer(pieces, win, wout, sems, par):
    src = pieces[0]
    for n in range(16):
        pltpu.make_async_copy(
            src.at[0, pl.ds(0, 8)], win.at[par, pl.ds(0, 8)], sems.at[par, 2 * n]
        ).wait()
        pltpu.make_async_copy(
            src.at[0, pl.ds(8, 9)], wout.at[par, :, 0], sems.at[par, 2 * n + 1]
        ).wait()


def gain_row(wout, par):
    return jnp.concatenate(
        [wout[par, 8, xy, 0:1, 0:128] for xy in range(16)], axis=1
    ).astype(F32)


def over_rows(step):
    def body(i, carry):
        step(pl.ds(pl.multiple_of(i * CHUNK, CHUNK), CHUNK))
        return carry

    lax.fori_loop(0, ROWS // CHUNK, body, 0, unroll=UNROLL)


def hat_pass(x_at, hat, keep_stat):
    def step(rows):
        xf = x_at(rows).astype(F32)
        mean = jnp.mean(xf, axis=-1, keepdims=True)
        centered = xf - mean
        variance = jnp.mean(centered * centered, axis=-1, keepdims=True)
        recip_std = lax.rsqrt(variance + norm_eps)
        hat[rows, :] = centered * recip_std
        keep_stat(rows, mean, recip_std)

    over_rows(step)


def spread(column):
    return jnp.broadcast_to(column, (CHUNK, 128))


def layer_out(x_at, act, wout, par, out_ref):
    for k in range(8):
        cols = pl.ds(k * 256, 256)
        out_ref[:, cols] = (
            x_at(cols).astype(F32) + dot(act, wout[par, k].reshape(R, 256))
        ).astype(BF16)


def layer_back(up_at, acts, slot, hat, rstd_at, preact, win, wout, par, gain, gnorm, gsum, up_out):
    inner, act = gelu_parts(preact)
    grad_act = jnp.zeros((ROWS, R), F32)
    for k in range(8):
        grad_act += dot(
            up_at(pl.ds(0, ROWS), pl.ds(k * 256, 256)), wout[par, k].reshape(R, 256), 1, 1
        )
    grad_pre = (grad_act * gelu_slope(preact, inner)).astype(BF16)
    acts[slot, 0:ROWS, ACT_AT : ACT_AT + R] = act
    acts[slot, 0:ROWS, PRE_AT : PRE_AT + R] = grad_pre
    for k in range(8):
        gnorm[:, pl.ds(k * 256, 256)] = dot(
            grad_pre, win[par, pl.ds(k * 16, 16)].reshape(256, R), 1, 1
        )
    gsum[...] = jnp.zeros((CHUNK, D), F32)

    def step(rows):
        grad_normed = gnorm[rows, :]
        hatted = hat[rows, :]
        product = grad_normed * hatted
        gsum[...] += product
        up = up_at(rows, pl.ds(0, D))
        acts[slot, rows, UP_AT : UP_AT + D] = up
        if up_out is not None:
            grad_hat = grad_normed * gain
            mean_hat = jnp.mean(grad_hat, axis=-1, keepdims=True)
            mean_both = jnp.mean(product * gain, axis=-1, keepdims=True)
            through = rstd_at(rows) * (grad_hat - mean_hat - hatted * mean_both)
            up_out[rows, :] = (up.astype(F32) + through).astype(BF16)

    over_rows(step)
    acts[slot, ROWS : ROWS + 16, 0:D] = jnp.broadcast_to(
        jnp.sum(gsum[...], axis=0, keepdims=True), (16, D)
    ).astype(BF16)


def start_all(copies):
    for copy in copies:
        copy.start()


def kernel_low_forward(s_ref, xs, *refs):
    pieces, (x1, x2, win, wout, stats, pre, normed, hat, sems) = refs[:8], refs[8:]
    start_all(weight_copies(s_ref, pieces, win, wout, sems))
    c, zl = s_ref[2], s_ref[3]
    for par in range(2):

        def x_at(rows=slice(None), cols=slice(None), par=par):
            return xs[zl, c, rows, cols] if par == 0 else x1[rows, cols]

        def keep_stat(rows, mean, recip_std, par=par):
            stats[par, 0, rows, :] = spread(mean)
            stats[par, 1, rows, :] = spread(recip_std)

        hat_pass(x_at, hat, keep_stat)
        wait_layer(pieces, win, wout, sems, par)
        gain = gain_row(wout, par)

        def step(rows, gain=gain):
            normed[rows, :] = (hat[rows, :] * gain).astype(BF16)

        over_rows(step)
        pre[par] = dot(normed[...], win[par].reshape(D, R))
        act = gelu_parts(pre[par])[1]
        layer_out(lambda cols: x_at(slice(None), cols), act, wout, par, x2 if par else x1)


def kernel_high(s_ref, x2, cots, *refs):
    pieces = refs[:8]
    up2, acts, win, wout, hat0, hat1, rstd, x3, up3, pre0, gnorm, gsum, sems = refs[8:]
    start_all(weight_copies(s_ref, pieces, win, wout, sems))
    c, zl = s_ref[2], s_ref[3]
    gains = []
    for par, (src, hat) in enumerate(((x2, hat0), (x3, hat1))):

        def keep_stat(rows, mean, recip_std, par=par):
            rstd[par, rows, :] = spread(recip_std)

        hat_pass(lambda rows, src=src: src[rows, :], hat, keep_stat)
        wait_layer(pieces, win, wout, sems, par)
        gain = gain_row(wout, par)
        slot = jnp.where(c == par, 0, 1)

        def step(rows, gain=gain, hat=hat, slot=slot):
            acts[slot, rows, 0:D] = (hat[rows, :] * gain).astype(BF16)

        over_rows(step)
        preact = dot(acts[slot, 0:ROWS, 0:D], win[par].reshape(D, R))
        gains.append(gain)
        if par == 0:
            pre0[...] = preact
            layer_out(lambda cols: x2[:, cols], gelu_parts(preact)[1], wout, 0, x3)
    layer_back(
        lambda rows, cols: cots[zl, c, rows, cols],
        acts, jnp.where(c == 1, 0, 1), hat1, lambda rows: rstd[1, rows, 0:1],
        preact, win, wout, 1, gains[1], gnorm, gsum, up3,
    )
    layer_back(
        lambda rows, cols: up3[rows, cols],
        acts, jnp.where(c == 0, 0, 1), hat0, lambda rows: rstd[0, rows, 0:1],
        pre0[...], win, wout, 0, gains[0], gnorm, gsum, up2,
    )


def kernel_low_back(s_ref, xs, x1, up2, win, wout, stats, pre, acts, hat, up1, gnorm, gsum):
    c, zl = s_ref[2], s_ref[3]
    for par, up, up_out in ((1, up2, up1), (0, up1, None)):
        gain = gain_row(wout, par)
        slot = jnp.where(c == par, 0, 1)

        def step(rows, par=par, gain=gain, slot=slot):
            xf = (x1[rows, :] if par else xs[zl, c, rows, :]).astype(F32)
            hatted = (xf - stats[par, 0, rows, 0:1]) * stats[par, 1, rows, 0:1]
            hat[rows, :] = hatted
            acts[slot, rows, 0:D] = (hatted * gain).astype(BF16)

        over_rows(step)
        layer_back(
            lambda rows, cols, up=up: up[rows, cols],
            acts, slot, hat, lambda rows, par=par: stats[par, 1, rows, 0:1],
            pre[par], win, wout, par, gain, gnorm, gsum, up_out,
        )


def kernel_grads(s_ref, acts, got, out):
    mx, my, c = s_ref[0], s_ref[1], s_ref[2]
    places = []
    for xy in range(16):
        xr = (xy // 4 - mx) & 3
        yr = (xy % 4 - my) & 3
        places.append(jnp.where(c == 0, xr * 4 + yr, yr * 4 + xr))

    def both(start, size):
        cols = pl.ds(start, size)
        return jnp.concatenate([acts[0, 0:ROWS, cols], got[0:ROWS, cols]], axis=0)

    grad_pre = both(PRE_AT, R)
    for xy in range(16):
        block = dot(both(xy * 128, 128).T, grad_pre)
        out[places[xy], 0:8] = block.astype(BF16).reshape(8, 16, 256)
    act_t = both(ACT_AT, R).T
    for k in range(8):
        block = dot(act_t, both(UP_AT + k * 256, 256)).astype(BF16).reshape(16, 16, 256)
        for xy in range(16):
            out[places[xy], 8 + k] = block[xy]
    for xy in range(16):
        cols = pl.ds(xy * 128, 128)
        part = acts[0, ROWS : ROWS + 16, cols].astype(F32) + got[ROWS : ROWS + 16, cols].astype(F32)
        out[places[xy], 16] = jnp.concatenate([part, part], axis=1).astype(BF16)


def vmem(*shape, kind=BF16):
    return pltpu.VMEM(shape, kind)


def array(*shape, kind=BF16):
    return jax.ShapeDtypeStruct(shape, kind)


UNROLL = 2
UP_AT, ACT_AT, PRE_AT, WIDE = D, 2 * D, 2 * D + R, 2 * D + 2 * R
ACT = (ROWS, D)
WIN, WOUT = (2, 128, 16, 256), (2, 9, 16, 16, 256)
ACTS = (2, ROWS + 16, WIDE)
HAT = vmem(ROWS, D, kind=F32)
GSUM = vmem(CHUNK, D, kind=F32)
SEMS = pltpu.SemaphoreType.DMA((2, 32))
WHOLE = pl.BlockSpec(memory_space=pltpu.VMEM)


def call(body, scalars, args, out_shape, scratch):
    return pl.pallas_call(
        body,
        in_specs=[pl.BlockSpec(memory_space=pltpu.SMEM)] + [WHOLE] * len(args),
        out_specs=jax.tree.map(lambda s: WHOLE, out_shape),
        scratch_shapes=scratch,
        out_shape=out_shape,
        compiler_params=pltpu.CompilerParams(vmem_limit_bytes=20 * 1024 * 1024),
    )(scalars, *args)


def add_up(first, got):
    return functools.reduce(lambda p, q: p + q.astype(F32), got, first.astype(F32)).astype(BF16)


def scatter_first(grads):
    both = grads.reshape(4, 4, 17, 16, 256)
    got = [shift(both[k], send_first(k)) for k in (2, 1, 3)]
    return both[0], got


def scatter_second(row):
    got = [shift(row[k], send_second(k)) for k in (2, 1, 3)]
    return add_up(row[0], got)


def device_body(inputs, cotangent, norm_gain, proj_in, proj_out):
    where = [lax.axis_index(n).astype(jnp.int32) for n in ("x", "y", "c", "zl")]
    scalars = jnp.stack(where)
    shard = jnp.concatenate(
        [
            proj_in[0],
            proj_out[0].reshape(4, 8, 256).transpose(1, 0, 2).reshape(32, 256),
            jnp.pad(norm_gain, ((0, 7), (0, 224))),
        ],
        axis=0,
    )
    column = lax.all_to_all(
        jnp.broadcast_to(shard[None], (8, 72, 256)), ("zl", "zh"), 0, 0
    ).reshape(2, 4, 72, 256)
    gain = jnp.pad(column[:, :, 64, :32].reshape(2, 1, 1, 128), ((0, 0), (0, 0), (0, 15), (0, 128)))
    block = jnp.concatenate(
        [
            column[:, :, :32].reshape(2, 8, 16, 256),
            column[:, :, 32:64].reshape(2, 4, 8, 4, 256).transpose(0, 2, 1, 3, 4).reshape(2, 8, 16, 256),
            gain,
        ],
        axis=1,
    )
    near = [block] + [shift(block, send_first(-k)) for k in (1, 2, 3)]
    pairs = []
    for p in range(2):
        row = jnp.stack([v[p] for v in near])
        rows = [row] + [shift(row, send_second(-k)) for k in (1, 2, 3)]
        pairs.append(rows + [shift(v, SWAP) for v in rows])
    x1, x2, win, wout, stats, pre = call(
        kernel_low_forward,
        scalars,
        [inputs, *pairs[0]],
        [
            array(*ACT), array(*ACT), array(*WIN), array(*WOUT),
            array(2, 2, ROWS, 128, kind=F32), array(2, ROWS, R, kind=F32),
        ],
        [vmem(*ACT), HAT, SEMS],
    )
    up2, acts1 = call(
        kernel_high,
        scalars,
        [x2, cotangent, *pairs[1]],
        [array(*ACT), array(*ACTS)],
        [
            vmem(*WIN), vmem(*WOUT), HAT, HAT, vmem(2, ROWS, 128, kind=F32),
            vmem(*ACT), vmem(*ACT), vmem(ROWS, R, kind=F32), HAT, GSUM, SEMS,
        ],
    )
    got1 = shift(acts1[1], SWAP)
    acts0 = call(
        kernel_low_back,
        scalars,
        [inputs, x1, up2, win, wout, stats, pre],
        array(*ACTS),
        [HAT, vmem(*ACT), HAT, GSUM],
    )
    got0 = shift(acts0[1], SWAP)
    grad = array(16, 17, 16, 256)
    own1, first1 = scatter_first(call(kernel_grads, scalars, [acts1, got1], grad, []))
    own0, first0 = scatter_first(call(kernel_grads, scalars, [acts0, got0], grad, []))
    high = scatter_second(add_up(own1, first1))
    low = scatter_second(add_up(own0, first0))
    grads = jnp.stack([low, high])
    parts = jnp.concatenate(
        [
            grads[:, :8].reshape(2, 4, 32, 256),
            grads[:, 8:16].reshape(2, 8, 4, 4, 256).transpose(0, 2, 1, 3, 4).reshape(2, 4, 32, 256),
            jnp.pad(grads[:, 16, 0, :128].reshape(2, 4, 1, 32), ((0, 0), (0, 0), (0, 7), (0, 224))),
        ],
        axis=2,
    ).reshape(8, 72, 256)
    total = jnp.sum(lax.all_to_all(parts, ("zl", "zh"), 0, 0).astype(F32), axis=0)
    grad_in = total[:32]
    grad_out = total[32:64].reshape(8, 4, 256).transpose(1, 0, 2).reshape(4, 2048)
    return (total[64:65, :32], grad_in[None], grad_out[None])


def solution(mesh):
    fine = Mesh(mesh.devices.reshape(DIMS), AXES)
    zero = ("x", "y", "zh")
    segment = ("zl", "c")
    return jax.shard_map(
        device_body,
        mesh=fine,
        in_specs=(
            P(None, None, zero, None),
            P(None, None, zero, None),
            P(segment, zero),
            P(segment, zero, None),
            P(segment, zero, None),
        ),
        out_specs=(P(segment, zero), P(segment, zero, None), P(segment, zero, None)),
        check_vma=False,
    )
```

profile of v0, /device:TPU:32, one launch (start us, length us, event | category | flops | bytes accessed | tf_op | source)
XLA Modules:
  0.0 165.5 jit_solution(14698197968594557652)
XLA Ops:
  0.6 0.7 copy.44
  1.4 0.7 fusion.13
  2.1 19.5 %all_to_all.10 = bf16[8,72,256]{2,1,0:T(8,128)(2,1)S(1)} all-to-all(bf16[8,72,256]{2,1,0:T(8,128)(2,1)S(1)} %broadcast_in_dim.4), channel_id=1, replica_groups=mesh['zl'=2,'c'=2,'x'=4,'y'=4,'zh'=4] {'zl','zh'}, dimensions={0} | all-to-all | bytes 589824 | tf_op jit(solution)/shard_map/all_to_all | solution.py:354
  22.0 2.8 %collective-permute-start = (bf16[2,17,16,256]{3,2,1,0:T(8,128)(2,1)S(1)}, bf16[2,17,16,256]{3,2,1,0:T(8,128)(2,1)S(1)}, u32[]{:S(2)}, u32[]{:S(2)}) collective-permute-start(bf16[2,17,16,256]{3,2,1,0:T(8,128)(2,1)S(1)} %fusion.1), channel_id=1, source_target_pairs={{0,48},{1,49},{2,50},{3,51},{4,52},{5,53},{6,54},{7,55},{8,56},{9,... | collective-permute-start | bytes 835592 | tf_op jit(solution)/shard_map/ppermute | solution.py:52
  24.8 0.8 collective-permute-start.1
  25.6 0.9 collective-permute-start.2
  26.6 5.4 %collective-permute-done = bf16[2,17,16,256]{3,2,1,0:T(8,128)(2,1)S(1)} collective-permute-done((bf16[2,17,16,256]{3,2,1,0:T(8,128)(2,1)S(1)}, bf16[2,17,16,256]{3,2,1,0:T(8,128)(2,1)S(1)}, u32[]{:S(2)}, u32[]{:S(2)}) %collective-permute-start) | collective-permute-done | bytes 278560 | tf_op jit(solution)/shard_map/ppermute | solution.py:52
  32.0 1.0 collective-permute-done.1
  33.0 2.9 %collective-permute-done.2 = bf16[2,17,16,256]{3,2,1,0:T(8,128)(2,1)S(1)} collective-permute-done((bf16[2,17,16,256]{3,2,1,0:T(8,128)(2,1)S(1)}, bf16[2,17,16,256]{3,2,1,0:T(8,128)(2,1)S(1)}, u32[]{:S(2)}, u32[]{:S(2)}) %collective-permute-start.2) | collective-permute-done | bytes 278560 | tf_op jit(solution)/shard_map/ppermute | solution.py:52
  36.0 3.1 %collective-permute-start.3 = (bf16[4,17,16,256]{3,2,1,0:T(8,128)(2,1)S(1)}, bf16[4,17,16,256]{3,2,1,0:T(8,128)(2,1)S(1)}, u32[]{:S(2)}, u32[]{:S(2)}) collective-permute-start(bf16[4,17,16,256]{3,2,1,0:T(8,128)(2,1)S(1)} %pad_maximum_fusion.refs_0_), channel_id=1, source_target_pairs={{0,12},{1,13},{2,14},{3,15},{4,0},{5,1},{6,2},{7,3},{8,4},{9,5},{1... | collective-permute-start | bytes 1671176 | tf_op jit(solution)/shard_map/ppermute | solution.py:52
  39.1 0.6 collective-permute-start.4
  39.7 1.0 collective-permute-start.5
  40.8 2.3 %collective-permute-start.10 = (bf16[4,17,16,256]{3,2,1,0:T(8,128)(2,1)S(1)}, bf16[4,17,16,256]{3,2,1,0:T(8,128)(2,1)}, u32[]{:S(2)}, u32[]{:S(2)}) collective-permute-start(bf16[4,17,16,256]{3,2,1,0:T(8,128)(2,1)S(1)} %pad_maximum_fusion.1.refs_0_), channel_id=1, source_target_pairs={{0,12},{1,13},{2,14},{3,15},{4,0},{5,1},{6,2},{7,3},{8,4},{9,5},{1... | collective-permute-start | bytes 1671176 | tf_op jit(solution)/shard_map/ppermute | solution.py:52
  43.1 9.0 %collective-permute-done.3.refs_1_ = bf16[4,17,16,256]{3,2,1,0:T(8,128)(2,1)S(1)} collective-permute-done((bf16[4,17,16,256]{3,2,1,0:T(8,128)(2,1)S(1)}, bf16[4,17,16,256]{3,2,1,0:T(8,128)(2,1)S(1)}, u32[]{:S(2)}, u32[]{:S(2)}) %collective-permute-start.3) | collective-permute-done | bytes 557088 | tf_op jit(solution)/shard_map/ppermute | solution.py:52
  52.1 4.5 %collective-permute-start.12 = (bf16[4,17,16,256]{3,2,1,0:T(8,128)(2,1)S(1)}, bf16[4,17,16,256]{3,2,1,0:T(8,128)(2,1)}, u32[]{:S(2)}, u32[]{:S(2)}) collective-permute-start(bf16[4,17,16,256]{3,2,1,0:T(8,128)(2,1)S(1)} %pad_maximum_fusion.1.refs_0_), channel_id=1, source_target_pairs={{0,4},{1,5},{2,6},{3,7},{4,8},{5,9},{6,10},{7,11},{8,12},{9,13},{1... | collective-permute-start | bytes 1671176 | tf_op jit(solution)/shard_map/ppermute | solution.py:52
  56.7 0.8 copy-done.2
  57.5 0.8 copy-done.6
  58.8 0.8 copy-done.4
  59.6 4.5 %collective-permute-done.10.refs_1_ = bf16[4,17,16,256]{3,2,1,0:T(8,128)(2,1)} collective-permute-done((bf16[4,17,16,256]{3,2,1,0:T(8,128)(2,1)S(1)}, bf16[4,17,16,256]{3,2,1,0:T(8,128)(2,1)}, u32[]{:S(2)}, u32[]{:S(2)}) %collective-permute-start.10) | collective-permute-done | bytes 557088 | tf_op jit(solution)/shard_map/ppermute | solution.py:52
  64.6 4.6 %collective-permute-done.12.refs_3_ = bf16[4,17,16,256]{3,2,1,0:T(8,128)(2,1)} collective-permute-done((bf16[4,17,16,256]{3,2,1,0:T(8,128)(2,1)S(1)}, bf16[4,17,16,256]{3,2,1,0:T(8,128)(2,1)}, u32[]{:S(2)}, u32[]{:S(2)}) %collective-permute-start.12) | collective-permute-done | bytes 557088 | tf_op jit(solution)/shard_map/ppermute | solution.py:52
  69.2 0.8 copy-done.8
  70.5 0.9 copy-done.10
  71.5 1.1 copy-done.3
  72.5 1.1 copy-done.5
  73.6 1.1 copy-done.7
  74.6 1.1 copy-done.9
  75.7 1.1 copy-done.11
  76.7 9.4 %shard_map.76 = (bf16[128,2048]{1,0:T(8,128)(2,1)S(1)}, bf16[128,2048]{1,0:T(8,128)(2,1)S(1)}, bf16[2,128,16,256]{3,2,1,0:T(8,128)(2,1)S(1)}, bf16[2,9,16,16,256...) custom-call(s32[4]{0:T(128)S(1)} %pad_add_fusion.s_ref, ...), custom_call_target="tpu_custom_call" | custom-call | tf_op jit(solution)/shard_map/pallas_call | solution.py:318
  86.2 13.0 %shard_map.77 = (bf16[128,2048]{1,0:T(8,128)(2,1)S(1)}, bf16[2,144,4608]{2,1,0:T(8,128)(2,1)S(1)}) custom-call(s32[4]{0:T(128)S(1)} %pad_add_fusion.s_ref, bf16[128,2048]{1,0:T(8,128)(2,1)S(1)} %get-tuple-element.12.x2, bf16[2,2,128,2048]{3,2,1,0:T(8,128)(2,1)S(1)} %copy-done.1, bf16[4,17,16,256]{3,2,1,0:T(8,128)(2,1)S(1)} %pad_maximum_fusion.1.refs_0_, ...), custom_call_target="tpu_custom_call" | custom-call | tf_op jit(solution)/shard_map/pallas_call | solution.py:318
  99.2 5.1 %shard_map.78.acts = bf16[2,144,4608]{2,1,0:T(8,128)(2,1)S(1)} custom-call(s32[4]{0:T(128)S(1)} %pad_add_fusion.s_ref, bf16[2,2,128,2048]{3,2,1,0:T(8,128)(2,1)S(1)} %copy-done, bf16[128,2048]{1,0:T(8,128)(2,1)S(1)} %get-tuple-element.11.x1, bf16[128,2048]{1,0:T(8,128)(2,1)S(1)} %get-tuple-element.13.up2, ...), custom_call_target="tpu_custom_call" | custom-call | tf_op jit(solution)/shard_map/pallas_call | solution.py:318
  105.2 2.5 %collective-permute-done.17.got = bf16[144,4608]{1,0:T(8,128)(2,1)S(1)} collective-permute-done((bf16[144,4608]{1,0:T(8,128)(2,1)S(1)}, bf16[144,4608]{1,0:T(8,128)(2,1)S(1)}, u32[]{:S(2)}, u32[]{:S(2)}) %collective-permute-start.17) | collective-permute-done | bytes 1327136 | tf_op jit(solution)/shard_map/ppermute | solution.py:52
  107.7 1.3 shard_map.79
  109.1 0.9 collective-permute-start.18
  110.0 0.7 collective-permute-start.19
  110.6 2.6 %collective-permute-start.20 = (bf16[4,17,16,256]{3,2,1,0:T(8,128)(2,1)S(1)}, bf16[4,17,16,256]{3,2,1,0:T(8,128)(2,1)S(1)}, u32[]{:S(2)}, u32[]{:S(2)}) collective-permute-start(bf16[4,17,16,256]{3,2,1,0:T(8,128)(2,1)S(1)} %get-tuple-element.20), channel_id=1, source_target_pairs={{0,48},{1,49},{2,50},{3,51},{4,52},{5,53},{6,54},{7,55},{8,56},{9,... | collective-permute-start | bytes 1671176 | tf_op jit(solution)/shard_map/ppermute | solution.py:52
  113.2 1.3 shard_map.80
  114.7 1.6 collective-permute-start.25
  116.3 4.1 %collective-permute-done.18 = bf16[4,17,16,256]{3,2,1,0:T(8,128)(2,1)S(1)} collective-permute-done((bf16[4,17,16,256]{3,2,1,0:T(8,128)(2,1)S(1)}, bf16[4,17,16,256]{3,2,1,0:T(8,128)(2,1)S(1)}, u32[]{:S(2)}, u32[]{:S(2)}) %collective-permute-start.18) | collective-permute-done | bytes 557088 | tf_op jit(solution)/shard_map/ppermute | solution.py:52
  120.9 5.3 %collective-permute-done.19 = bf16[4,17,16,256]{3,2,1,0:T(8,128)(2,1)S(1)} collective-permute-done((bf16[4,17,16,256]{3,2,1,0:T(8,128)(2,1)S(1)}, bf16[4,17,16,256]{3,2,1,0:T(8,128)(2,1)S(1)}, u32[]{:S(2)}, u32[]{:S(2)}) %collective-permute-start.19) | collective-permute-done | bytes 557088 | tf_op jit(solution)/shard_map/ppermute | solution.py:52
  126.6 1.5 collective-permute-start.22
  128.1 6.3 %collective-permute-done.25 = bf16[4,17,16,256]{3,2,1,0:T(8,128)(2,1)S(1)} collective-permute-done((bf16[4,17,16,256]{3,2,1,0:T(8,128)(2,1)S(1)}, bf16[4,17,16,256]{3,2,1,0:T(8,128)(2,1)S(1)}, u32[]{:S(2)}, u32[]{:S(2)}) %collective-permute-start.25) | collective-permute-done | bytes 557088 | tf_op jit(solution)/shard_map/ppermute | solution.py:52
  134.8 6.3 %collective-permute-done.26 = bf16[4,17,16,256]{3,2,1,0:T(8,128)(2,1)S(1)} collective-permute-done((bf16[4,17,16,256]{3,2,1,0:T(8,128)(2,1)S(1)}, bf16[4,17,16,256]{3,2,1,0:T(8,128)(2,1)S(1)}, u32[]{:S(2)}, u32[]{:S(2)}) %collective-permute-start.26) | collective-permute-done | bytes 557088 | tf_op jit(solution)/shard_map/ppermute | solution.py:52
  141.6 1.5 collective-permute-start.29
  143.0 1.9 %collective-permute-start.30 = (bf16[17,16,256]{2,1,0:T(8,128)(2,1)S(1)}, bf16[17,16,256]{2,1,0:T(8,128)(2,1)S(1)}, u32[]{:S(2)}, u32[]{:S(2)}) collective-permute-start(bf16[17,16,256]{2,1,0:T(8,128)(2,1)S(1)} %get-tuple-element.29), channel_id=1, source_target_pairs={{0,12},{1,13},{2,14},{3,15},{4,0},{5,1},{6,2},{7,3},{8,4},{9,5},{1... | collective-permute-start | bytes 417800 | tf_op jit(solution)/shard_map/ppermute | solution.py:52
  145.0 3.2 %collective-permute-done.28 = bf16[17,16,256]{2,1,0:T(8,128)(2,1)S(1)} collective-permute-done((bf16[17,16,256]{2,1,0:T(8,128)(2,1)S(1)}, bf16[17,16,256]{2,1,0:T(8,128)(2,1)S(1)}, u32[]{:S(2)}, u32[]{:S(2)}) %collective-permute-start.28) | collective-permute-done | bytes 139296 | tf_op jit(solution)/shard_map/ppermute | solution.py:52
  148.2 1.2 collective-permute-done.29
  149.8 13.9 %all_to_all.11 = bf16[8,72,256]{2,1,0:T(8,128)(2,1)S(1)} all-to-all(bf16[8,72,256]{2,1,0:T(8,128)(2,1)S(1)} %pad_maximum_fusion.2), channel_id=1, replica_groups=mesh['zl'=2,'c'=2,'x'=4,'y'=4,'zh'=4] {'zl','zh'}, dimensions={0} | all-to-all | bytes 589824 | tf_op jit(solution)/shard_map/all_to_all | solution.py:415
  164.9 0.6 broadcast_in_dim_reshape.3
  (88 shorter events, 6.9 us)
Async XLA Ops:
  22.0 9.9 %collective-permute-start = (bf16[2,17,16,256]{3,2,1,0:T(8,128)(2,1)S(1)}, bf16[2,17,16,256]{3,2,1,0:T(8,128)(2,1)S(1)}, u32[]{:S(2)}, u32[]{:S(2)}) collective-permute-start(bf16[2,17,16,256]{3,2,1,0:T(8,128)(2,1)S(1)} %fusion.1), channel_id=1, source_target_pairs={{0,48},{1,49},{2,50},{3,51},{4,52},{5,53},{6,54},{7,55},{8,56},{9,... | collective-permute-start | bytes 835592 | tf_op jit(solution)/shard_map/ppermute | solution.py:52
  24.8 8.2 %collective-permute-start.1 = (bf16[2,17,16,256]{3,2,1,0:T(8,128)(2,1)S(1)}, bf16[2,17,16,256]{3,2,1,0:T(8,128)(2,1)S(1)}, u32[]{:S(2)}, u32[]{:S(2)}) collective-permute-start(bf16[2,17,16,256]{3,2,1,0:T(8,128)(2,1)S(1)} %fusion.1), channel_id=1, source_target_pairs={{0,32},{1,33},{2,34},{3,35},{4,36},{5,37},{6,38},{7,39},{8,40},{9,... | collective-permute-start | bytes 835592 | tf_op jit(solution)/shard_map/ppermute | solution.py:52
  25.6 10.2 %collective-permute-start.2 = (bf16[2,17,16,256]{3,2,1,0:T(8,128)(2,1)S(1)}, bf16[2,17,16,256]{3,2,1,0:T(8,128)(2,1)S(1)}, u32[]{:S(2)}, u32[]{:S(2)}) collective-permute-start(bf16[2,17,16,256]{3,2,1,0:T(8,128)(2,1)S(1)} %fusion.1), channel_id=1, source_target_pairs={{0,16},{1,17},{2,18},{3,19},{4,20},{5,21},{6,22},{7,23},{8,24},{9,... | collective-permute-start | bytes 835592 | tf_op jit(solution)/shard_map/ppermute | solution.py:52
  33.0 38.5 %copy-start = (bf16[2,2,128,2048]{3,2,1,0:T(8,128)(2,1)S(1)}, bf16[2,2,128,2048]{3,2,1,0:T(8,128)(2,1)}, u32[]{:S(2)}) copy-start(bf16[2,2,128,2048]{3,2,1,0:T(8,128)(2,1)} %xs.3) | copy-start | bytes 6291460
  36.0 16.1 %collective-permute-start.3 = (bf16[4,17,16,256]{3,2,1,0:T(8,128)(2,1)S(1)}, bf16[4,17,16,256]{3,2,1,0:T(8,128)(2,1)S(1)}, u32[]{:S(2)}, u32[]{:S(2)}) collective-permute-start(bf16[4,17,16,256]{3,2,1,0:T(8,128)(2,1)S(1)} %pad_maximum_fusion.refs_0_), channel_id=1, source_target_pairs={{0,12},{1,13},{2,14},{3,15},{4,0},{5,1},{6,2},{7,3},{8,4},{9,5},{1... | collective-permute-start | bytes 1671176 | tf_op jit(solution)/shard_map/ppermute | solution.py:52
  39.1 13.0 %collective-permute-start.4 = (bf16[4,17,16,256]{3,2,1,0:T(8,128)(2,1)S(1)}, bf16[4,17,16,256]{3,2,1,0:T(8,128)(2,1)S(1)}, u32[]{:S(2)}, u32[]{:S(2)}) collective-permute-start(bf16[4,17,16,256]{3,2,1,0:T(8,128)(2,1)S(1)} %pad_maximum_fusion.refs_0_), channel_id=1, source_target_pairs={{0,8},{1,9},{2,10},{3,11},{4,12},{5,13},{6,14},{7,15},{8,0},{9,1},... | collective-permute-start | bytes 1671176 | tf_op jit(solution)/shard_map/ppermute | solution.py:52
  39.7 16.9 %collective-permute-start.5 = (bf16[4,17,16,256]{3,2,1,0:T(8,128)(2,1)S(1)}, bf16[4,17,16,256]{3,2,1,0:T(8,128)(2,1)}, u32[]{:S(2)}, u32[]{:S(2)}) collective-permute-start(bf16[4,17,16,256]{3,2,1,0:T(8,128)(2,1)S(1)} %pad_maximum_fusion.refs_0_), channel_id=1, source_target_pairs={{0,4},{1,5},{2,6},{3,7},{4,8},{5,9},{6,10},{7,11},{8,12},{9,13},{1... | collective-permute-start | bytes 1671176 | tf_op jit(solution)/shard_map/ppermute | solution.py:52
  40.7 16.8 %collective-permute-start.6 = (bf16[4,17,16,256]{3,2,1,0:T(8,128)(2,1)S(1)}, bf16[4,17,16,256]{3,2,1,0:T(8,128)(2,1)S(1)}, u32[]{:S(2)}, u32[]{:S(2)}) collective-permute-start(bf16[4,17,16,256]{3,2,1,0:T(8,128)(2,1)S(1)} %pad_maximum_fusion.refs_0_), channel_id=1, source_target_pairs={{0,64},{1,65},{2,66},{3,67},{4,68},{5,69},{6,70},{7,71},{8,72},{9,... | collective-permute-start | bytes 1671176 | tf_op jit(solution)/shard_map/ppermute | solution.py:52
  40.8 23.3 %collective-permute-start.10 = (bf16[4,17,16,256]{3,2,1,0:T(8,128)(2,1)S(1)}, bf16[4,17,16,256]{3,2,1,0:T(8,128)(2,1)}, u32[]{:S(2)}, u32[]{:S(2)}) collective-permute-start(bf16[4,17,16,256]{3,2,1,0:T(8,128)(2,1)S(1)} %pad_maximum_fusion.1.refs_0_), channel_id=1, source_target_pairs={{0,12},{1,13},{2,14},{3,15},{4,0},{5,1},{6,2},{7,3},{8,4},{9,5},{1... | collective-permute-start | bytes 1671176 | tf_op jit(solution)/shard_map/ppermute | solution.py:52
  52.1 12.0 %collective-permute-start.11 = (bf16[4,17,16,256]{3,2,1,0:T(8,128)(2,1)S(1)}, bf16[4,17,16,256]{3,2,1,0:T(8,128)(2,1)}, u32[]{:S(2)}, u32[]{:S(2)}) collective-permute-start(bf16[4,17,16,256]{3,2,1,0:T(8,128)(2,1)S(1)} %pad_maximum_fusion.1.refs_0_), channel_id=1, source_target_pairs={{0,8},{1,9},{2,10},{3,11},{4,12},{5,13},{6,14},{7,15},{8,0},{9,1},... | collective-permute-start | bytes 1671176 | tf_op jit(solution)/shard_map/ppermute | solution.py:52
  52.1 17.1 %collective-permute-start.12 = (bf16[4,17,16,256]{3,2,1,0:T(8,128)(2,1)S(1)}, bf16[4,17,16,256]{3,2,1,0:T(8,128)(2,1)}, u32[]{:S(2)}, u32[]{:S(2)}) collective-permute-start(bf16[4,17,16,256]{3,2,1,0:T(8,128)(2,1)S(1)} %pad_maximum_fusion.1.refs_0_), channel_id=1, source_target_pairs={{0,4},{1,5},{2,6},{3,7},{4,8},{5,9},{6,10},{7,11},{8,12},{9,13},{1... | collective-permute-start | bytes 1671176 | tf_op jit(solution)/shard_map/ppermute | solution.py:52
  56.7 12.6 %collective-permute-start.7 = (bf16[4,17,16,256]{3,2,1,0:T(8,128)(2,1)S(1)}, bf16[4,17,16,256]{3,2,1,0:T(8,128)(2,1)S(1)}, u32[]{:S(2)}, u32[]{:S(2)}) collective-permute-start(bf16[4,17,16,256]{3,2,1,0:T(8,128)(2,1)S(1)} %collective-permute-done.3.refs_1_), channel_id=1, source_target_pairs={{0,64},{1,65},{2,66},{3,67},{4,68},{5,69},{6,70},{7,71},{8,72},{9,... | collective-permute-start | bytes 1671176 | tf_op jit(solution)/shard_map/ppermute | solution.py:52
  56.7 0.8 copy-start.2
  57.5 0.8 copy-start.6
  58.3 12.2 %collective-permute-start.8 = (bf16[4,17,16,256]{3,2,1,0:T(8,128)(2,1)S(1)}, bf16[4,17,16,256]{3,2,1,0:T(8,128)(2,1)S(1)}, u32[]{:S(2)}, u32[]{:S(2)}) collective-permute-start(bf16[4,17,16,256]{3,2,1,0:T(8,128)(2,1)S(1)} %collective-permute-done.4.refs_2_), channel_id=1, source_target_pairs={{0,64},{1,65},{2,66},{3,67},{4,68},{5,69},{6,70},{7,71},{8,72},{9,... | collective-permute-start | bytes 1671176 | tf_op jit(solution)/shard_map/ppermute | solution.py:52
  58.8 0.8 copy-start.4
  64.1 22.1 %collective-permute-start.13 = (bf16[4,17,16,256]{3,2,1,0:T(8,128)(2,1)S(1)}, bf16[4,17,16,256]{3,2,1,0:T(8,128)(2,1)}, u32[]{:S(2)}, u32[]{:S(2)}) collective-permute-start(bf16[4,17,16,256]{3,2,1,0:T(8,128)(2,1)S(1)} %pad_maximum_fusion.1.refs_0_), channel_id=1, source_target_pairs={{0,64},{1,65},{2,66},{3,67},{4,68},{5,69},{6,70},{7,71},{8,72},{9,... | collective-permute-start | bytes 1671176 | tf_op jit(solution)/shard_map/ppermute | solution.py:52
  64.1 7.4 %collective-permute-start.9 = (bf16[4,17,16,256]{3,2,1,0:T(8,128)(2,1)}, bf16[4,17,16,256]{3,2,1,0:T(8,128)(2,1)}, u32[]{:S(2)}, u32[]{:S(2)}) collective-permute-start(bf16[4,17,16,256]{3,2,1,0:T(8,128)(2,1)} %collective-permute-done.5.refs_3_), channel_id=1, source_target_pairs={{0,64},{1,65},{2,66},{3,67},{4,68},{5,69},{6,70},{7,71},{8,72},{9,... | collective-permute-start | bytes 1671176 | tf_op jit(solution)/shard_map/ppermute | solution.py:52
  69.2 16.9 %collective-permute-start.14 = (bf16[4,17,16,256]{3,2,1,0:T(8,128)(2,1)}, bf16[4,17,16,256]{3,2,1,0:T(8,128)(2,1)}, u32[]{:S(2)}, u32[]{:S(2)}) collective-permute-start(bf16[4,17,16,256]{3,2,1,0:T(8,128)(2,1)} %collective-permute-done.10.refs_1_), channel_id=1, source_target_pairs={{0,64},{1,65},{2,66},{3,67},{4,68},{5,69},{6,70},{7,71},{8,72},{9,... | collective-permute-start | bytes 1671176 | tf_op jit(solution)/shard_map/ppermute | solution.py:52
  69.2 0.8 copy-start.8
  70.0 16.1 %collective-permute-start.15 = (bf16[4,17,16,256]{3,2,1,0:T(8,128)(2,1)}, bf16[4,17,16,256]{3,2,1,0:T(8,128)(2,1)}, u32[]{:S(2)}, u32[]{:S(2)}) collective-permute-start(bf16[4,17,16,256]{3,2,1,0:T(8,128)(2,1)} %collective-permute-done.11.refs_2_), channel_id=1, source_target_pairs={{0,64},{1,65},{2,66},{3,67},{4,68},{5,69},{6,70},{7,71},{8,72},{9,... | collective-permute-start | bytes 1671176 | tf_op jit(solution)/shard_map/ppermute | solution.py:52
  70.5 0.9 copy-start.10
  71.4 14.8 %collective-permute-start.16 = (bf16[4,17,16,256]{3,2,1,0:T(8,128)(2,1)}, bf16[4,17,16,256]{3,2,1,0:T(8,128)(2,1)}, u32[]{:S(2)}, u32[]{:S(2)}) collective-permute-start(bf16[4,17,16,256]{3,2,1,0:T(8,128)(2,1)} %collective-permute-done.12.refs_3_), channel_id=1, source_target_pairs={{0,64},{1,65},{2,66},{3,67},{4,68},{5,69},{6,70},{7,71},{8,72},{9,... | collective-permute-start | bytes 1671176 | tf_op jit(solution)/shard_map/ppermute | solution.py:52
  71.5 1.1 copy-start.3
  72.5 1.1 copy-start.5
  73.6 1.1 copy-start.7
  74.6 1.1 copy-start.9
  75.7 1.1 copy-start.11
  76.7 9.4 %copy-start.1 = (bf16[2,2,128,2048]{3,2,1,0:T(8,128)(2,1)S(1)}, bf16[2,2,128,2048]{3,2,1,0:T(8,128)(2,1)}, u32[]{:S(2)}) copy-start(bf16[2,2,128,2048]{3,2,1,0:T(8,128)(2,1)} %cots.1) | copy-start | bytes 6291460
  104.4 3.3 %collective-permute-start.17 = (bf16[144,4608]{1,0:T(8,128)(2,1)S(1)}, bf16[144,4608]{1,0:T(8,128)(2,1)S(1)}, u32[]{:S(2)}, u32[]{:S(2)}) collective-permute-start(bf16[144,4608]{1,0:T(8,128)(2,1)S(1)} %slice_bitcast_fusion), channel_id=1, source_target_pairs={{0,64},{1,65},{2,66},{3,67},{4,68},{5,69},{6,70},{7,71},{8,72},{9,... | collective-permute-start | bytes 3981320 | tf_op jit(solution)/shard_map/ppermute | solution.py:52
  105.1 8.2 %collective-permute-start.24 = (bf16[144,4608]{1,0:T(8,128)(2,1)S(1)}, bf16[144,4608]{1,0:T(8,128)(2,1)S(1)}, u32[]{:S(2)}, u32[]{:S(2)}) collective-permute-start(bf16[144,4608]{1,0:T(8,128)(2,1)S(1)} %slice_bitcast_fusion.1), channel_id=1, source_target_pairs={{0,64},{1,65},{2,66},{3,67},{4,68},{5,69},{6,70},{7,71},{8,72},{9,... | collective-permute-start | bytes 3981320 | tf_op jit(solution)/shard_map/ppermute | solution.py:52
  109.1 11.2 %collective-permute-start.18 = (bf16[4,17,16,256]{3,2,1,0:T(8,128)(2,1)S(1)}, bf16[4,17,16,256]{3,2,1,0:T(8,128)(2,1)S(1)}, u32[]{:S(2)}, u32[]{:S(2)}) collective-permute-start(bf16[4,17,16,256]{3,2,1,0:T(8,128)(2,1)S(1)} %get-tuple-element.19), channel_id=1, source_target_pairs={{0,32},{1,33},{2,34},{3,35},{4,36},{5,37},{6,38},{7,39},{8,40},{9,... | collective-permute-start | bytes 1671176 | tf_op jit(solution)/shard_map/ppermute | solution.py:52
  110.0 16.2 %collective-permute-start.19 = (bf16[4,17,16,256]{3,2,1,0:T(8,128)(2,1)S(1)}, bf16[4,17,16,256]{3,2,1,0:T(8,128)(2,1)S(1)}, u32[]{:S(2)}, u32[]{:S(2)}) collective-permute-start(bf16[4,17,16,256]{3,2,1,0:T(8,128)(2,1)S(1)} %get-tuple-element.21), channel_id=1, source_target_pairs={{0,16},{1,17},{2,18},{3,19},{4,20},{5,21},{6,22},{7,23},{8,24},{9,... | collective-permute-start | bytes 1671176 | tf_op jit(solution)/shard_map/ppermute | solution.py:52
  110.6 15.5 %collective-permute-start.20 = (bf16[4,17,16,256]{3,2,1,0:T(8,128)(2,1)S(1)}, bf16[4,17,16,256]{3,2,1,0:T(8,128)(2,1)S(1)}, u32[]{:S(2)}, u32[]{:S(2)}) collective-permute-start(bf16[4,17,16,256]{3,2,1,0:T(8,128)(2,1)S(1)} %get-tuple-element.20), channel_id=1, source_target_pairs={{0,48},{1,49},{2,50},{3,51},{4,52},{5,53},{6,54},{7,55},{8,56},{9,... | collective-permute-start | bytes 1671176 | tf_op jit(solution)/shard_map/ppermute | solution.py:52
  114.7 19.8 %collective-permute-start.25 = (bf16[4,17,16,256]{3,2,1,0:T(8,128)(2,1)S(1)}, bf16[4,17,16,256]{3,2,1,0:T(8,128)(2,1)S(1)}, u32[]{:S(2)}, u32[]{:S(2)}) collective-permute-start(bf16[4,17,16,256]{3,2,1,0:T(8,128)(2,1)S(1)} %get-tuple-element.22), channel_id=1, source_target_pairs={{0,32},{1,33},{2,34},{3,35},{4,36},{5,37},{6,38},{7,39},{8,40},{9,... | collective-permute-start | bytes 1671176 | tf_op jit(solution)/shard_map/ppermute | solution.py:52
  116.3 24.9 %collective-permute-start.26 = (bf16[4,17,16,256]{3,2,1,0:T(8,128)(2,1)S(1)}, bf16[4,17,16,256]{3,2,1,0:T(8,128)(2,1)S(1)}, u32[]{:S(2)}, u32[]{:S(2)}) collective-permute-start(bf16[4,17,16,256]{3,2,1,0:T(8,128)(2,1)S(1)} %get-tuple-element.24), channel_id=1, source_target_pairs={{0,16},{1,17},{2,18},{3,19},{4,20},{5,21},{6,22},{7,23},{8,24},{9,... | collective-permute-start | bytes 1671176 | tf_op jit(solution)/shard_map/ppermute | solution.py:52
  120.3 20.8 %collective-permute-start.27 = (bf16[4,17,16,256]{3,2,1,0:T(8,128)(2,1)S(1)}, bf16[4,17,16,256]{3,2,1,0:T(8,128)(2,1)S(1)}, u32[]{:S(2)}, u32[]{:S(2)}) collective-permute-start(bf16[4,17,16,256]{3,2,1,0:T(8,128)(2,1)S(1)} %get-tuple-element.23), channel_id=1, source_target_pairs={{0,48},{1,49},{2,50},{3,51},{4,52},{5,53},{6,54},{7,55},{8,56},{9,... | collective-permute-start | bytes 1671176 | tf_op jit(solution)/shard_map/ppermute | solution.py:52
  126.5 16.5 %collective-permute-start.21 = (bf16[17,16,256]{2,1,0:T(8,128)(2,1)S(1)}, bf16[17,16,256]{2,1,0:T(8,128)(2,1)S(1)}, u32[]{:S(2)}, u32[]{:S(2)}) collective-permute-start(bf16[17,16,256]{2,1,0:T(8,128)(2,1)S(1)} %get-tuple-element.25), channel_id=1, source_target_pairs={{0,8},{1,9},{2,10},{3,11},{4,12},{5,13},{6,14},{7,15},{8,0},{9,1},... | collective-permute-start | bytes 417800 | tf_op jit(solution)/shard_map/ppermute | solution.py:52
  126.6 18.2 %collective-permute-start.22 = (bf16[17,16,256]{2,1,0:T(8,128)(2,1)S(1)}, bf16[17,16,256]{2,1,0:T(8,128)(2,1)S(1)}, u32[]{:S(2)}, u32[]{:S(2)}) collective-permute-start(bf16[17,16,256]{2,1,0:T(8,128)(2,1)S(1)} %get-tuple-element.27), channel_id=1, source_target_pairs={{0,4},{1,5},{2,6},{3,7},{4,8},{5,9},{6,10},{7,11},{8,12},{9,13},{1... | collective-permute-start | bytes 417800 | tf_op jit(solution)/shard_map/ppermute | solution.py:52
  134.4 10.5 %collective-permute-start.23 = (bf16[17,16,256]{2,1,0:T(8,128)(2,1)S(1)}, bf16[17,16,256]{2,1,0:T(8,128)(2,1)S(1)}, u32[]{:S(2)}, u32[]{:S(2)}) collective-permute-start(bf16[17,16,256]{2,1,0:T(8,128)(2,1)S(1)} %get-tuple-element.26), channel_id=1, source_target_pairs={{0,12},{1,13},{2,14},{3,15},{4,0},{5,1},{6,2},{7,3},{8,4},{9,5},{1... | collective-permute-start | bytes 417800 | tf_op jit(solution)/shard_map/ppermute | solution.py:52
  141.5 6.7 %collective-permute-start.28 = (bf16[17,16,256]{2,1,0:T(8,128)(2,1)S(1)}, bf16[17,16,256]{2,1,0:T(8,128)(2,1)S(1)}, u32[]{:S(2)}, u32[]{:S(2)}) collective-permute-start(bf16[17,16,256]{2,1,0:T(8,128)(2,1)S(1)} %get-tuple-element.28), channel_id=1, source_target_pairs={{0,8},{1,9},{2,10},{3,11},{4,12},{5,13},{6,14},{7,15},{8,0},{9,1},... | collective-permute-start | bytes 417800 | tf_op jit(solution)/shard_map/ppermute | solution.py:52
  141.6 7.8 %collective-permute-start.29 = (bf16[17,16,256]{2,1,0:T(8,128)(2,1)S(1)}, bf16[17,16,256]{2,1,0:T(8,128)(2,1)S(1)}, u32[]{:S(2)}, u32[]{:S(2)}) collective-permute-start(bf16[17,16,256]{2,1,0:T(8,128)(2,1)S(1)} %get-tuple-element.30), channel_id=1, source_target_pairs={{0,4},{1,5},{2,6},{3,7},{4,8},{5,9},{6,10},{7,11},{8,12},{9,13},{1... | collective-permute-start | bytes 417800 | tf_op jit(solution)/shard_map/ppermute | solution.py:52
  143.0 6.4 %collective-permute-start.30 = (bf16[17,16,256]{2,1,0:T(8,128)(2,1)S(1)}, bf16[17,16,256]{2,1,0:T(8,128)(2,1)S(1)}, u32[]{:S(2)}, u32[]{:S(2)}) collective-permute-start(bf16[17,16,256]{2,1,0:T(8,128)(2,1)S(1)} %get-tuple-element.29), channel_id=1, source_target_pairs={{0,12},{1,13},{2,14},{3,15},{4,0},{5,1},{6,2},{7,3},{8,4},{9,5},{1... | collective-permute-start | bytes 417800 | tf_op jit(solution)/shard_map/ppermute | solution.py:52
where the time goes:
time: 166 us
  waiting for transfers between devices  56.2 us (34%)
  blocking collectives  33.3 us (20%)
  Pallas kernels  30.1 us (18%)
  starting transfers between devices  30 us (18%)
  local copies, waits for them, and re-layouts  13 us (8%)
  other arithmetic  1.89 us (1%)
    ppermute x31, waiting for transfers between devices, shift(): return lax.ppermute(value, AXES, pairs)  56.2 us
    pallas_call x5, Pallas kernels, call(): pl.pallas_call(body, in_specs=[pl.BlockSpec(memory_space=pltpu.SMEM)] + [...  30.1 us
    ppermute x31, starting transfers between devices, shift(): return lax.ppermute(value, AXES, pairs)  30 us
    all_to_all x1, blocking collectives, device_body(): lax.all_to_all(jnp.broadcast_to(shard[None], (8, 72, 256)), ('zl', 'zh'),...  19.5 us
    all_to_all x1, blocking collectives, device_body(): lax.all_to_all(parts, ('zl', 'zh'), 0, 0).astype(F32)  13.9 us
    unnamed x26, local copies, waits for them, and re-layouts  10.2 us
  transfers between devices with their start and end apart: 31, of which 13 were waited for; matrix products, arithmetic and copies ran while one was open for 1% of the time, Pallas kernels for 7%

commit v1 on v0

--- a/solution.py
+++ b/solution.py
@@ -69,9 +69,8 @@
     )
 
 
-def weight_copies(s_ref, pieces, win, wout, sems):
+def place_weights(s_ref, pieces, win, wout):
     mx, my, c = s_ref[0], s_ref[1], s_ref[2]
-    copies = []
     for o in range(2):
         par = c if o == 0 else 1 - c
         for b in range(4):
@@ -80,29 +79,9 @@
                 y = (my + jnp.where(par == 0, b, a)) & 3
                 xy = x * 4 + y
                 src = pieces[o * 4 + b]
-                n = (b * 4 + a) * 2
-                copies.append(
-                    pltpu.make_async_copy(
-                        src.at[a, pl.ds(0, 8)], win.at[par, pl.ds(xy * 8, 8)], sems.at[par, n]
-                    )
-                )
-                copies.append(
-                    pltpu.make_async_copy(
-                        src.at[a, pl.ds(8, 9)], wout.at[par, :, xy], sems.at[par, n + 1]
-                    )
-                )
-    return copies
-
-
-def wait_layer(pieces, win, wout, sems, par):
-    src = pieces[0]
-    for n in range(16):
-        pltpu.make_async_copy(
-            src.at[0, pl.ds(0, 8)], win.at[par, pl.ds(0, 8)], sems.at[par, 2 * n]
-        ).wait()
-        pltpu.make_async_copy(
-            src.at[0, pl.ds(8, 9)], wout.at[par, :, 0], sems.at[par, 2 * n + 1]
-        ).wait()
+                win[par, pl.ds(xy * 8, 8)] = src[a, 0:8]
+                for k in range(9):
+                    wout[par, k, xy] = src[a, 8 + k]
 
 
 def gain_row(wout, par):
@@ -180,14 +159,9 @@
     ).astype(BF16)
 
 
-def start_all(copies):
-    for copy in copies:
-        copy.start()
-
-
 def kernel_low_forward(s_ref, xs, *refs):
-    pieces, (x1, x2, win, wout, stats, pre, normed, hat, sems) = refs[:8], refs[8:]
-    start_all(weight_copies(s_ref, pieces, win, wout, sems))
+    pieces, (x1, x2, win, wout, stats, pre, normed, hat) = refs[:8], refs[8:]
+    place_weights(s_ref, pieces, win, wout)
     c, zl = s_ref[2], s_ref[3]
     for par in range(2):
 
@@ -199,7 +173,6 @@
             stats[par, 1, rows, :] = spread(recip_std)
 
         hat_pass(x_at, hat, keep_stat)
-        wait_layer(pieces, win, wout, sems, par)
         gain = gain_row(wout, par)
 
         def step(rows, gain=gain):
@@ -213,8 +186,8 @@
 
 def kernel_high(s_ref, x2, cots, *refs):
     pieces = refs[:8]
-    up2, acts, win, wout, hat0, hat1, rstd, x3, up3, pre0, gnorm, gsum, sems = refs[8:]
-    start_all(weight_copies(s_ref, pieces, win, wout, sems))
+    up2, acts, win, wout, hat0, hat1, rstd, x3, up3, pre0, gnorm, gsum = refs[8:]
+    place_weights(s_ref, pieces, win, wout)
     c, zl = s_ref[2], s_ref[3]
     gains = []
     for par, (src, hat) in enumerate(((x2, hat0), (x3, hat1))):
@@ -223,7 +196,6 @@
             rstd[par, rows, :] = spread(recip_std)
 
         hat_pass(lambda rows, src=src: src[rows, :], hat, keep_stat)
-        wait_layer(pieces, win, wout, sems, par)
         gain = gain_row(wout, par)
         slot = jnp.where(c == par, 0, 1)
 
@@ -303,14 +275,19 @@
     return jax.ShapeDtypeStruct(shape, kind)
 
 
-UNROLL = 2
+UNROLL = 8
 UP_AT, ACT_AT, PRE_AT, WIDE = D, 2 * D, 2 * D + R, 2 * D + 2 * R
 ACT = (ROWS, D)
 WIN, WOUT = (2, 128, 16, 256), (2, 9, 16, 16, 256)
 ACTS = (2, ROWS + 16, WIDE)
 HAT = vmem(ROWS, D, kind=F32)
 GSUM = vmem(CHUNK, D, kind=F32)
-SEMS = pltpu.SemaphoreType.DMA((2, 32))
+LOW_SCRATCH = [vmem(*ACT), HAT]
+HIGH_SCRATCH = [
+    vmem(*WIN), vmem(*WOUT), HAT, HAT, vmem(2, ROWS, 128, kind=F32),
+    vmem(*ACT), vmem(*ACT), vmem(ROWS, R, kind=F32), HAT, GSUM,
+]
+BACK_SCRATCH = [HAT, vmem(*ACT), HAT, GSUM]
 WHOLE = pl.BlockSpec(memory_space=pltpu.VMEM)
 
 
@@ -363,10 +340,12 @@
         ],
         axis=1,
     )
-    near = [block] + [shift(block, send_first(-k)) for k in (1, 2, 3)]
+    near = []
+    for p in range(2):
+        near.append([block[p]] + [shift(block[p], send_first(-k)) for k in (1, 2, 3)])
     pairs = []
     for p in range(2):
-        row = jnp.stack([v[p] for v in near])
+        row = jnp.stack(near[p])
         rows = [row] + [shift(row, send_second(-k)) for k in (1, 2, 3)]
         pairs.append(rows + [shift(v, SWAP) for v in rows])
     x1, x2, win, wout, stats, pre = call(
@@ -377,17 +356,10 @@
             array(*ACT), array(*ACT), array(*WIN), array(*WOUT),
             array(2, 2, ROWS, 128, kind=F32), array(2, ROWS, R, kind=F32),
         ],
-        [vmem(*ACT), HAT, SEMS],
+        LOW_SCRATCH,
     )
     up2, acts1 = call(
-        kernel_high,
-        scalars,
-        [x2, cotangent, *pairs[1]],
-        [array(*ACT), array(*ACTS)],
-        [
-            vmem(*WIN), vmem(*WOUT), HAT, HAT, vmem(2, ROWS, 128, kind=F32),
-            vmem(*ACT), vmem(*ACT), vmem(ROWS, R, kind=F32), HAT, GSUM, SEMS,
-        ],
+        kernel_high, scalars, [x2, cotangent, *pairs[1]], [array(*ACT), array(*ACTS)], HIGH_SCRATCH
     )
     got1 = shift(acts1[1], SWAP)
     acts0 = call(
@@ -395,7 +367,7 @@
         scalars,
         [inputs, x1, up2, win, wout, stats, pre],
         array(*ACTS),
-        [HAT, vmem(*ACT), HAT, GSUM],
+        BACK_SCRATCH,
     )
     got0 = shift(acts0[1], SWAP)
     grad = array(16, 17, 16, 256)

time: 166 us -> 162 us (0.976)
  Pallas kernels: 30.1 us -> 16.2 us
  waiting for transfers between devices: 56.2 us -> 67.5 us
    pallas_call x5, Pallas kernels: 30.1 us -> 16.2 us  [call(): pl.pallas_call(body, in_specs=[pl.BlockSpec(memory_space=pltpu.SMEM)] + [...]
    ppermute x31 -> x34, waiting for transfers between devices: 56.2 us -> 67.5 us  [shift(): return lax.ppermute(value, AXES, pairs)]
    ppermute x31 -> x34, starting transfers between devices: 30 us -> 29 us  [shift(): return lax.ppermute(value, AXES, pairs)]
  transfers between devices with their start and end apart: 31 -> 34, of which waited for: 13 -> 16; matrix products, arithmetic and copies ran while one was open for 1% -> 1% of each run, Pallas kernels for 7% -> 4%
where the time goes in v1:
time: 162 us; the launch traced here: 161 us
  waiting for transfers between devices  67.5 us (42%)
  blocking collectives  32.5 us (20%)
  starting transfers between devices  29 us (18%)
  Pallas kernels  16.2 us (10%)
  local copies, waits for them, and re-layouts  12.9 us (8%)
  other arithmetic  1.89 us (1%)
    ppermute x34, waiting for transfers between devices, shift(): return lax.ppermute(value, AXES, pairs)  67.5 us
    ppermute x34, starting transfers between devices, shift(): return lax.ppermute(value, AXES, pairs)  29 us
    all_to_all x1, blocking collectives, device_body(): lax.all_to_all(jnp.broadcast_to(shard[None], (8, 72, 256)), ('zl', 'zh'),...  19.5 us
    pallas_call x5, Pallas kernels, call(): pl.pallas_call(body, in_specs=[pl.BlockSpec(memory_space=pltpu.SMEM)] + [...  16.2 us
    all_to_all x1, blocking collectives, device_body(): lax.all_to_all(parts, ('zl', 'zh'), 0, 0).astype(F32)  13 us
    unnamed x26, local copies, waits for them, and re-layouts  10.2 us
  transfers between devices with their start and end apart: 34, of which 16 were waited for; matrix products, arithmetic and copies ran while one was open for 1% of the time, Pallas kernels for 4%

profile of v1, /device:TPU:32, one launch (start us, length us, event | category | flops | bytes accessed | tf_op | source)
XLA Modules:
  0.0 161.0 jit_solution(7260853711368719411)
XLA Ops:
  2.1 19.5 %all_to_all.10 = bf16[8,72,256]{2,1,0:T(8,128)(2,1)S(1)} all-to-all(bf16[8,72,256]{2,1,0:T(8,128)(2,1)S(1)} %broadcast_in_dim.4), channel_id=1, replica_groups=mesh['zl'=2,'c'=2,'x'=4,'y'=4,'zh'=4] {'zl','zh'}, dimensions={0} | all-to-all | bytes 589824 | tf_op jit(solution)/shard_map/all_to_all | solution.py:331
  22.1 2.8 %collective-permute-start = (bf16[17,16,256]{2,1,0:T(8,128)(2,1)S(1)}, bf16[17,16,256]{2,1,0:T(8,128)(2,1)S(1)}, u32[]{:S(2)}, u32[]{:S(2)}) collective-permute-start(bf16[17,16,256]{2,1,0:T(8,128)(2,1)S(1)} %get-tuple-element.36), channel_id=1, source_target_pairs={{0,48},{1,49},{2,50},{3,51},{4,52},{5,53},{6,54},{7,55},{8,56},{9,... | collective-permute-start | bytes 417800 | tf_op jit(solution)/shard_map/ppermute | solution.py:52
  24.9 0.8 collective-permute-start.1
  25.7 0.9 collective-permute-start.2
  26.6 2.4 %collective-permute-done = bf16[17,16,256]{2,1,0:T(8,128)(2,1)S(1)} collective-permute-done((bf16[17,16,256]{2,1,0:T(8,128)(2,1)S(1)}, bf16[17,16,256]{2,1,0:T(8,128)(2,1)S(1)}, u32[]{:S(2)}, u32[]{:S(2)}) %collective-permute-start) | collective-permute-done | bytes 139296 | tf_op jit(solution)/shard_map/ppermute | solution.py:52
  29.0 2.6 %collective-permute-done.1 = bf16[17,16,256]{2,1,0:T(8,128)(2,1)S(1)} collective-permute-done((bf16[17,16,256]{2,1,0:T(8,128)(2,1)S(1)}, bf16[17,16,256]{2,1,0:T(8,128)(2,1)S(1)}, u32[]{:S(2)}, u32[]{:S(2)}) %collective-permute-start.1) | collective-permute-done | bytes 139296 | tf_op jit(solution)/shard_map/ppermute | solution.py:52
  31.6 1.4 collective-permute-done.2
  33.0 3.1 %collective-permute-start.3 = (bf16[4,17,16,256]{3,2,1,0:T(8,128)(2,1)S(1)}, bf16[4,17,16,256]{3,2,1,0:T(8,128)(2,1)S(1)}, u32[]{:S(2)}, u32[]{:S(2)}) collective-permute-start(bf16[4,17,16,256]{3,2,1,0:T(8,128)(2,1)S(1)} %pad_maximum_fusion.refs_0_), channel_id=1, source_target_pairs={{0,12},{1,13},{2,14},{3,15},{4,0},{5,1},{6,2},{7,3},{8,4},{9,5},{1... | collective-permute-start | bytes 1671176 | tf_op jit(solution)/shard_map/ppermute | solution.py:52
  36.8 1.0 collective-permute-start.5
  38.3 9.5 %collective-permute-done.10 = bf16[17,16,256]{2,1,0:T(8,128)(2,1)S(1)} collective-permute-done((bf16[17,16,256]{2,1,0:T(8,128)(2,1)S(1)}, bf16[17,16,256]{2,1,0:T(8,128)(2,1)S(1)}, u32[]{:S(2)}, u32[]{:S(2)}) %collective-permute-start.10) | collective-permute-done | bytes 139296 | tf_op jit(solution)/shard_map/ppermute | solution.py:52
  47.8 6.6 %collective-permute-done.11 = bf16[17,16,256]{2,1,0:T(8,128)(2,1)S(1)} collective-permute-done((bf16[17,16,256]{2,1,0:T(8,128)(2,1)S(1)}, bf16[17,16,256]{2,1,0:T(8,128)(2,1)S(1)}, u32[]{:S(2)}, u32[]{:S(2)}) %collective-permute-start.11) | collective-permute-done | bytes 139296 | tf_op jit(solution)/shard_map/ppermute | solution.py:52
  54.4 1.0 collective-permute-start.12
  55.4 5.7 %collective-permute-done.12 = bf16[17,16,256]{2,1,0:T(8,128)(2,1)S(1)} collective-permute-done((bf16[17,16,256]{2,1,0:T(8,128)(2,1)S(1)}, bf16[17,16,256]{2,1,0:T(8,128)(2,1)S(1)}, u32[]{:S(2)}, u32[]{:S(2)}) %collective-permute-start.12) | collective-permute-done | bytes 139296 | tf_op jit(solution)/shard_map/ppermute | solution.py:52
  61.1 0.9 collective-permute-start.13
  62.7 0.9 collective-permute-start.15
  63.6 0.8 copy-done.2
  64.4 0.8 copy-done.6
  65.7 0.8 copy-done.4
  66.5 4.3 %collective-permute-done.13.refs_1_ = bf16[4,17,16,256]{3,2,1,0:T(8,128)(2,1)} collective-permute-done((bf16[4,17,16,256]{3,2,1,0:T(8,128)(2,1)S(1)}, bf16[4,17,16,256]{3,2,1,0:T(8,128)(2,1)}, u32[]{:S(2)}, u32[]{:S(2)}) %collective-permute-start.13) | collective-permute-done | bytes 557088 | tf_op jit(solution)/shard_map/ppermute | solution.py:52
  70.9 2.5 %collective-permute-done.14.refs_2_ = bf16[4,17,16,256]{3,2,1,0:T(8,128)(2,1)} collective-permute-done((bf16[4,17,16,256]{3,2,1,0:T(8,128)(2,1)S(1)}, bf16[4,17,16,256]{3,2,1,0:T(8,128)(2,1)}, u32[]{:S(2)}, u32[]{:S(2)}) %collective-permute-start.14) | collective-permute-done | bytes 557088 | tf_op jit(solution)/shard_map/ppermute | solution.py:52
  73.3 5.9 %collective-permute-done.15.refs_3_ = bf16[4,17,16,256]{3,2,1,0:T(8,128)(2,1)} collective-permute-done((bf16[4,17,16,256]{3,2,1,0:T(8,128)(2,1)S(1)}, bf16[4,17,16,256]{3,2,1,0:T(8,128)(2,1)}, u32[]{:S(2)}, u32[]{:S(2)}) %collective-permute-start.15) | collective-permute-done | bytes 557088 | tf_op jit(solution)/shard_map/ppermute | solution.py:52
  80.5 0.9 copy-done.10
  81.5 1.1 copy-done.3
  82.5 1.1 copy-done.5
  83.6 1.1 copy-done.7
  84.6 1.1 copy-done.9
  85.7 1.1 copy-done.11
  86.7 3.7 %shard_map.76 = (bf16[128,2048]{1,0:T(8,128)(2,1)S(1)}, bf16[128,2048]{1,0:T(8,128)(2,1)S(1)}, bf16[2,128,16,256]{3,2,1,0:T(8,128)(2,1)S(1)}, bf16[2,9,16,16,256...) custom-call(s32[4]{0:T(128)S(1)} %pad_add_fusion.s_ref, ...), custom_call_target="tpu_custom_call" | custom-call | tf_op jit(solution)/shard_map/pallas_call | solution.py:295
  90.5 6.5 %shard_map.77 = (bf16[128,2048]{1,0:T(8,128)(2,1)S(1)}, bf16[2,144,4608]{2,1,0:T(8,128)(2,1)S(1)}) custom-call(s32[4]{0:T(128)S(1)} %pad_add_fusion.s_ref, bf16[128,2048]{1,0:T(8,128)(2,1)S(1)} %get-tuple-element.12.x2, bf16[2,2,128,2048]{3,2,1,0:T(8,128)(2,1)S(1)} %copy-done.1, bf16[4,17,16,256]{3,2,1,0:T(8,128)(2,1)S(1)} %pad_maximum_fusion.1.refs_0_, ...), custom_call_target="tpu_custom_call" | custom-call | tf_op jit(solution)/shard_map/pallas_call | solution.py:295
  97.0 3.4 %shard_map.78.acts = bf16[2,144,4608]{2,1,0:T(8,128)(2,1)S(1)} custom-call(s32[4]{0:T(128)S(1)} %pad_add_fusion.s_ref, bf16[2,2,128,2048]{3,2,1,0:T(8,128)(2,1)S(1)} %copy-done, bf16[128,2048]{1,0:T(8,128)(2,1)S(1)} %get-tuple-element.11.x1, bf16[128,2048]{1,0:T(8,128)(2,1)S(1)} %get-tuple-element.13.up2, ...), custom_call_target="tpu_custom_call" | custom-call | tf_op jit(solution)/shard_map/pallas_call | solution.py:295
  101.3 2.5 %collective-permute-done.20.got = bf16[144,4608]{1,0:T(8,128)(2,1)S(1)} collective-permute-done((bf16[144,4608]{1,0:T(8,128)(2,1)S(1)}, bf16[144,4608]{1,0:T(8,128)(2,1)S(1)}, u32[]{:S(2)}, u32[]{:S(2)}) %collective-permute-start.20) | collective-permute-done | bytes 1327136 | tf_op jit(solution)/shard_map/ppermute | solution.py:52
  103.8 1.3 shard_map.79
  105.2 1.1 collective-permute-start.21
  106.4 1.9 %collective-permute-start.22 = (bf16[4,17,16,256]{3,2,1,0:T(8,128)(2,1)S(1)}, bf16[4,17,16,256]{3,2,1,0:T(8,128)(2,1)S(1)}, u32[]{:S(2)}, u32[]{:S(2)}) collective-permute-start(bf16[4,17,16,256]{3,2,1,0:T(8,128)(2,1)S(1)} %get-tuple-element.21), channel_id=1, source_target_pairs={{0,16},{1,17},{2,18},{3,19},{4,20},{5,21},{6,22},{7,23},{8,24},{9,... | collective-permute-start | bytes 1671176 | tf_op jit(solution)/shard_map/ppermute | solution.py:52
  108.2 1.4 collective-permute-start.23
  109.6 1.3 shard_map.80
  111.0 1.4 collective-permute-start.28
  112.4 4.1 %collective-permute-done.21 = bf16[4,17,16,256]{3,2,1,0:T(8,128)(2,1)S(1)} collective-permute-done((bf16[4,17,16,256]{3,2,1,0:T(8,128)(2,1)S(1)}, bf16[4,17,16,256]{3,2,1,0:T(8,128)(2,1)S(1)}, u32[]{:S(2)}, u32[]{:S(2)}) %collective-permute-start.21) | collective-permute-done | bytes 557088 | tf_op jit(solution)/shard_map/ppermute | solution.py:52
  116.5 2.0 %collective-permute-start.30 = (bf16[4,17,16,256]{3,2,1,0:T(8,128)(2,1)S(1)}, bf16[4,17,16,256]{3,2,1,0:T(8,128)(2,1)S(1)}, u32[]{:S(2)}, u32[]{:S(2)}) collective-permute-start(bf16[4,17,16,256]{3,2,1,0:T(8,128)(2,1)S(1)} %get-tuple-element.23), channel_id=1, source_target_pairs={{0,48},{1,49},{2,50},{3,51},{4,52},{5,53},{6,54},{7,55},{8,56},{9,... | collective-permute-start | bytes 1671176 | tf_op jit(solution)/shard_map/ppermute | solution.py:52
  118.5 3.8 %collective-permute-done.22 = bf16[4,17,16,256]{3,2,1,0:T(8,128)(2,1)S(1)} collective-permute-done((bf16[4,17,16,256]{3,2,1,0:T(8,128)(2,1)S(1)}, bf16[4,17,16,256]{3,2,1,0:T(8,128)(2,1)S(1)}, u32[]{:S(2)}, u32[]{:S(2)}) %collective-permute-start.22) | collective-permute-done | bytes 557088 | tf_op jit(solution)/shard_map/ppermute | solution.py:52
  123.4 0.9 collective-permute-start.25
  124.3 6.0 %collective-permute-done.28 = bf16[4,17,16,256]{3,2,1,0:T(8,128)(2,1)S(1)} collective-permute-done((bf16[4,17,16,256]{3,2,1,0:T(8,128)(2,1)S(1)}, bf16[4,17,16,256]{3,2,1,0:T(8,128)(2,1)S(1)}, u32[]{:S(2)}, u32[]{:S(2)}) %collective-permute-start.28) | collective-permute-done | bytes 557088 | tf_op jit(solution)/shard_map/ppermute | solution.py:52
  131.1 6.1 %collective-permute-done.29 = bf16[4,17,16,256]{3,2,1,0:T(8,128)(2,1)S(1)} collective-permute-done((bf16[4,17,16,256]{3,2,1,0:T(8,128)(2,1)S(1)}, bf16[4,17,16,256]{3,2,1,0:T(8,128)(2,1)S(1)}, u32[]{:S(2)}, u32[]{:S(2)}) %collective-permute-start.29) | collective-permute-done | bytes 557088 | tf_op jit(solution)/shard_map/ppermute | solution.py:52
  138.3 0.9 collective-permute-start.32
  139.2 2.3 %collective-permute-start.33 = (bf16[17,16,256]{2,1,0:T(8,128)(2,1)S(1)}, bf16[17,16,256]{2,1,0:T(8,128)(2,1)S(1)}, u32[]{:S(2)}, u32[]{:S(2)}) collective-permute-start(bf16[17,16,256]{2,1,0:T(8,128)(2,1)S(1)} %get-tuple-element.29), channel_id=1, source_target_pairs={{0,12},{1,13},{2,14},{3,15},{4,0},{5,1},{6,2},{7,3},{8,4},{9,5},{1... | collective-permute-start | bytes 417800 | tf_op jit(solution)/shard_map/ppermute | solution.py:52
  141.7 2.7 %collective-permute-done.31 = bf16[17,16,256]{2,1,0:T(8,128)(2,1)S(1)} collective-permute-done((bf16[17,16,256]{2,1,0:T(8,128)(2,1)S(1)}, bf16[17,16,256]{2,1,0:T(8,128)(2,1)S(1)}, u32[]{:S(2)}, u32[]{:S(2)}) %collective-permute-start.31) | collective-permute-done | bytes 139296 | tf_op jit(solution)/shard_map/ppermute | solution.py:52
  144.4 1.4 collective-permute-done.32
  146.2 13.0 %all_to_all.11 = bf16[8,72,256]{2,1,0:T(8,128)(2,1)S(1)} all-to-all(bf16[8,72,256]{2,1,0:T(8,128)(2,1)S(1)} %pad_maximum_fusion.2), channel_id=1, replica_groups=mesh['zl'=2,'c'=2,'x'=4,'y'=4,'zh'=4] {'zl','zh'}, dimensions={0} | all-to-all | bytes 589824 | tf_op jit(solution)/shard_map/all_to_all | solution.py:387
  (91 shorter events, 12.1 us)
Async XLA Ops:
  22.1 59.4 %copy-start = (bf16[2,2,128,2048]{3,2,1,0:T(8,128)(2,1)S(1)}, bf16[2,2,128,2048]{3,2,1,0:T(8,128)(2,1)}, u32[]{:S(2)}) copy-start(bf16[2,2,128,2048]{3,2,1,0:T(8,128)(2,1)} %xs.3) | copy-start | bytes 6291460
  22.1 6.9 %collective-permute-start = (bf16[17,16,256]{2,1,0:T(8,128)(2,1)S(1)}, bf16[17,16,256]{2,1,0:T(8,128)(2,1)S(1)}, u32[]{:S(2)}, u32[]{:S(2)}) collective-permute-start(bf16[17,16,256]{2,1,0:T(8,128)(2,1)S(1)} %get-tuple-element.36), channel_id=1, source_target_pairs={{0,48},{1,49},{2,50},{3,51},{4,52},{5,53},{6,54},{7,55},{8,56},{9,... | collective-permute-start | bytes 417800 | tf_op jit(solution)/shard_map/ppermute | solution.py:52
  24.9 6.7 %collective-permute-start.1 = (bf16[17,16,256]{2,1,0:T(8,128)(2,1)S(1)}, bf16[17,16,256]{2,1,0:T(8,128)(2,1)S(1)}, u32[]{:S(2)}, u32[]{:S(2)}) collective-permute-start(bf16[17,16,256]{2,1,0:T(8,128)(2,1)S(1)} %get-tuple-element.36), channel_id=1, source_target_pairs={{0,32},{1,33},{2,34},{3,35},{4,36},{5,37},{6,38},{7,39},{8,40},{9,... | collective-permute-start | bytes 417800 | tf_op jit(solution)/shard_map/ppermute | solution.py:52
  25.7 7.3 %collective-permute-start.2 = (bf16[17,16,256]{2,1,0:T(8,128)(2,1)S(1)}, bf16[17,16,256]{2,1,0:T(8,128)(2,1)S(1)}, u32[]{:S(2)}, u32[]{:S(2)}) collective-permute-start(bf16[17,16,256]{2,1,0:T(8,128)(2,1)S(1)} %get-tuple-element.36), channel_id=1, source_target_pairs={{0,16},{1,17},{2,18},{3,19},{4,20},{5,21},{6,22},{7,23},{8,24},{9,... | collective-permute-start | bytes 417800 | tf_op jit(solution)/shard_map/ppermute | solution.py:52
  33.0 29.0 %collective-permute-start.3 = (bf16[4,17,16,256]{3,2,1,0:T(8,128)(2,1)S(1)}, bf16[4,17,16,256]{3,2,1,0:T(8,128)(2,1)S(1)}, u32[]{:S(2)}, u32[]{:S(2)}) collective-permute-start(bf16[4,17,16,256]{3,2,1,0:T(8,128)(2,1)S(1)} %pad_maximum_fusion.refs_0_), channel_id=1, source_target_pairs={{0,12},{1,13},{2,14},{3,15},{4,0},{5,1},{6,2},{7,3},{8,4},{9,5},{1... | collective-permute-start | bytes 1671176 | tf_op jit(solution)/shard_map/ppermute | solution.py:52
  36.1 26.6 %collective-permute-start.4 = (bf16[4,17,16,256]{3,2,1,0:T(8,128)(2,1)S(1)}, bf16[4,17,16,256]{3,2,1,0:T(8,128)(2,1)S(1)}, u32[]{:S(2)}, u32[]{:S(2)}) collective-permute-start(bf16[4,17,16,256]{3,2,1,0:T(8,128)(2,1)S(1)} %pad_maximum_fusion.refs_0_), channel_id=1, source_target_pairs={{0,8},{1,9},{2,10},{3,11},{4,12},{5,13},{6,14},{7,15},{8,0},{9,1},... | collective-permute-start | bytes 1671176 | tf_op jit(solution)/shard_map/ppermute | solution.py:52
  36.8 26.8 %collective-permute-start.5 = (bf16[4,17,16,256]{3,2,1,0:T(8,128)(2,1)S(1)}, bf16[4,17,16,256]{3,2,1,0:T(8,128)(2,1)}, u32[]{:S(2)}, u32[]{:S(2)}) collective-permute-start(bf16[4,17,16,256]{3,2,1,0:T(8,128)(2,1)S(1)} %pad_maximum_fusion.refs_0_), channel_id=1, source_target_pairs={{0,4},{1,5},{2,6},{3,7},{4,8},{5,9},{6,10},{7,11},{8,12},{9,13},{1... | collective-permute-start | bytes 1671176 | tf_op jit(solution)/shard_map/ppermute | solution.py:52
  37.7 26.7 %collective-permute-start.6 = (bf16[4,17,16,256]{3,2,1,0:T(8,128)(2,1)S(1)}, bf16[4,17,16,256]{3,2,1,0:T(8,128)(2,1)S(1)}, u32[]{:S(2)}, u32[]{:S(2)}) collective-permute-start(bf16[4,17,16,256]{3,2,1,0:T(8,128)(2,1)S(1)} %pad_maximum_fusion.refs_0_), channel_id=1, source_target_pairs={{0,64},{1,65},{2,66},{3,67},{4,68},{5,69},{6,70},{7,71},{8,72},{9,... | collective-permute-start | bytes 1671176 | tf_op jit(solution)/shard_map/ppermute | solution.py:52
  37.7 10.1 %collective-permute-start.10 = (bf16[17,16,256]{2,1,0:T(8,128)(2,1)S(1)}, bf16[17,16,256]{2,1,0:T(8,128)(2,1)S(1)}, u32[]{:S(2)}, u32[]{:S(2)}) collective-permute-start(bf16[17,16,256]{2,1,0:T(8,128)(2,1)S(1)} %get-tuple-element.37), channel_id=1, source_target_pairs={{0,48},{1,49},{2,50},{3,51},{4,52},{5,53},{6,54},{7,55},{8,56},{9,... | collective-permute-start | bytes 417800 | tf_op jit(solution)/shard_map/ppermute | solution.py:52
  47.8 6.6 %collective-permute-start.11 = (bf16[17,16,256]{2,1,0:T(8,128)(2,1)S(1)}, bf16[17,16,256]{2,1,0:T(8,128)(2,1)S(1)}, u32[]{:S(2)}, u32[]{:S(2)}) collective-permute-start(bf16[17,16,256]{2,1,0:T(8,128)(2,1)S(1)} %get-tuple-element.37), channel_id=1, source_target_pairs={{0,32},{1,33},{2,34},{3,35},{4,36},{5,37},{6,38},{7,39},{8,40},{9,... | collective-permute-start | bytes 417800 | tf_op jit(solution)/shard_map/ppermute | solution.py:52
  54.4 6.7 %collective-permute-start.12 = (bf16[17,16,256]{2,1,0:T(8,128)(2,1)S(1)}, bf16[17,16,256]{2,1,0:T(8,128)(2,1)S(1)}, u32[]{:S(2)}, u32[]{:S(2)}) collective-permute-start(bf16[17,16,256]{2,1,0:T(8,128)(2,1)S(1)} %get-tuple-element.37), channel_id=1, source_target_pairs={{0,16},{1,17},{2,18},{3,19},{4,20},{5,21},{6,22},{7,23},{8,24},{9,... | collective-permute-start | bytes 417800 | tf_op jit(solution)/shard_map/ppermute | solution.py:52
  61.1 9.7 %collective-permute-start.13 = (bf16[4,17,16,256]{3,2,1,0:T(8,128)(2,1)S(1)}, bf16[4,17,16,256]{3,2,1,0:T(8,128)(2,1)}, u32[]{:S(2)}, u32[]{:S(2)}) collective-permute-start(bf16[4,17,16,256]{3,2,1,0:T(8,128)(2,1)S(1)} %pad_maximum_fusion.1.refs_0_), channel_id=1, source_target_pairs={{0,12},{1,13},{2,14},{3,15},{4,0},{5,1},{6,2},{7,3},{8,4},{9,5},{1... | collective-permute-start | bytes 1671176 | tf_op jit(solution)/shard_map/ppermute | solution.py:52
  62.1 11.2 %collective-permute-start.14 = (bf16[4,17,16,256]{3,2,1,0:T(8,128)(2,1)S(1)}, bf16[4,17,16,256]{3,2,1,0:T(8,128)(2,1)}, u32[]{:S(2)}, u32[]{:S(2)}) collective-permute-start(bf16[4,17,16,256]{3,2,1,0:T(8,128)(2,1)S(1)} %pad_maximum_fusion.1.refs_0_), channel_id=1, source_target_pairs={{0,8},{1,9},{2,10},{3,11},{4,12},{5,13},{6,14},{7,15},{8,0},{9,1},... | collective-permute-start | bytes 1671176 | tf_op jit(solution)/shard_map/ppermute | solution.py:52
  62.7 16.5 %collective-permute-start.15 = (bf16[4,17,16,256]{3,2,1,0:T(8,128)(2,1)S(1)}, bf16[4,17,16,256]{3,2,1,0:T(8,128)(2,1)}, u32[]{:S(2)}, u32[]{:S(2)}) collective-permute-start(bf16[4,17,16,256]{3,2,1,0:T(8,128)(2,1)S(1)} %pad_maximum_fusion.1.refs_0_), channel_id=1, source_target_pairs={{0,4},{1,5},{2,6},{3,7},{4,8},{5,9},{6,10},{7,11},{8,12},{9,13},{1... | collective-permute-start | bytes 1671176 | tf_op jit(solution)/shard_map/ppermute | solution.py:52
  63.6 15.6 %collective-permute-start.7 = (bf16[4,17,16,256]{3,2,1,0:T(8,128)(2,1)S(1)}, bf16[4,17,16,256]{3,2,1,0:T(8,128)(2,1)S(1)}, u32[]{:S(2)}, u32[]{:S(2)}) collective-permute-start(bf16[4,17,16,256]{3,2,1,0:T(8,128)(2,1)S(1)} %collective-permute-done.3.refs_1_), channel_id=1, source_target_pairs={{0,64},{1,65},{2,66},{3,67},{4,68},{5,69},{6,70},{7,71},{8,72},{9,... | collective-permute-start | bytes 1671176 | tf_op jit(solution)/shard_map/ppermute | solution.py:52
  63.6 0.8 copy-start.2
  64.4 0.8 copy-start.6
  65.2 15.3 %collective-permute-start.8 = (bf16[4,17,16,256]{3,2,1,0:T(8,128)(2,1)S(1)}, bf16[4,17,16,256]{3,2,1,0:T(8,128)(2,1)S(1)}, u32[]{:S(2)}, u32[]{:S(2)}) collective-permute-start(bf16[4,17,16,256]{3,2,1,0:T(8,128)(2,1)S(1)} %collective-permute-done.4.refs_2_), channel_id=1, source_target_pairs={{0,64},{1,65},{2,66},{3,67},{4,68},{5,69},{6,70},{7,71},{8,72},{9,... | collective-permute-start | bytes 1671176 | tf_op jit(solution)/shard_map/ppermute | solution.py:52
  65.7 0.8 copy-start.4
  70.9 19.6 %collective-permute-start.16 = (bf16[4,17,16,256]{3,2,1,0:T(8,128)(2,1)S(1)}, bf16[4,17,16,256]{3,2,1,0:T(8,128)(2,1)}, u32[]{:S(2)}, u32[]{:S(2)}) collective-permute-start(bf16[4,17,16,256]{3,2,1,0:T(8,128)(2,1)S(1)} %pad_maximum_fusion.1.refs_0_), channel_id=1, source_target_pairs={{0,64},{1,65},{2,66},{3,67},{4,68},{5,69},{6,70},{7,71},{8,72},{9,... | collective-permute-start | bytes 1671176 | tf_op jit(solution)/shard_map/ppermute | solution.py:52
  73.3 8.1 %collective-permute-start.9 = (bf16[4,17,16,256]{3,2,1,0:T(8,128)(2,1)}, bf16[4,17,16,256]{3,2,1,0:T(8,128)(2,1)}, u32[]{:S(2)}, u32[]{:S(2)}) collective-permute-start(bf16[4,17,16,256]{3,2,1,0:T(8,128)(2,1)} %collective-permute-done.5.refs_3_), channel_id=1, source_target_pairs={{0,64},{1,65},{2,66},{3,67},{4,68},{5,69},{6,70},{7,71},{8,72},{9,... | collective-permute-start | bytes 1671176 | tf_op jit(solution)/shard_map/ppermute | solution.py:52
  79.2 11.3 %collective-permute-start.17 = (bf16[4,17,16,256]{3,2,1,0:T(8,128)(2,1)}, bf16[4,17,16,256]{3,2,1,0:T(8,128)(2,1)}, u32[]{:S(2)}, u32[]{:S(2)}) collective-permute-start(bf16[4,17,16,256]{3,2,1,0:T(8,128)(2,1)} %collective-permute-done.13.refs_1_), channel_id=1, source_target_pairs={{0,64},{1,65},{2,66},{3,67},{4,68},{5,69},{6,70},{7,71},{8,72},{9,... | collective-permute-start | bytes 1671176 | tf_op jit(solution)/shard_map/ppermute | solution.py:52
  79.2 0.8 copy-start.8
  80.0 10.5 %collective-permute-start.18 = (bf16[4,17,16,256]{3,2,1,0:T(8,128)(2,1)}, bf16[4,17,16,256]{3,2,1,0:T(8,128)(2,1)}, u32[]{:S(2)}, u32[]{:S(2)}) collective-permute-start(bf16[4,17,16,256]{3,2,1,0:T(8,128)(2,1)} %collective-permute-done.14.refs_2_), channel_id=1, source_target_pairs={{0,64},{1,65},{2,66},{3,67},{4,68},{5,69},{6,70},{7,71},{8,72},{9,... | collective-permute-start | bytes 1671176 | tf_op jit(solution)/shard_map/ppermute | solution.py:52
  80.5 0.9 copy-start.10
  81.4 9.1 %collective-permute-start.19 = (bf16[4,17,16,256]{3,2,1,0:T(8,128)(2,1)}, bf16[4,17,16,256]{3,2,1,0:T(8,128)(2,1)}, u32[]{:S(2)}, u32[]{:S(2)}) collective-permute-start(bf16[4,17,16,256]{3,2,1,0:T(8,128)(2,1)} %collective-permute-done.15.refs_3_), channel_id=1, source_target_pairs={{0,64},{1,65},{2,66},{3,67},{4,68},{5,69},{6,70},{7,71},{8,72},{9,... | collective-permute-start | bytes 1671176 | tf_op jit(solution)/shard_map/ppermute | solution.py:52
  81.5 1.1 copy-start.3
  82.5 1.1 copy-start.5
  83.6 1.1 copy-start.7
  84.6 1.1 copy-start.9
  85.7 1.1 copy-start.11
  86.7 3.8 %copy-start.1 = (bf16[2,2,128,2048]{3,2,1,0:T(8,128)(2,1)S(1)}, bf16[2,2,128,2048]{3,2,1,0:T(8,128)(2,1)}, u32[]{:S(2)}) copy-start(bf16[2,2,128,2048]{3,2,1,0:T(8,128)(2,1)} %cots.1) | copy-start | bytes 6291460
  100.5 3.3 %collective-permute-start.20 = (bf16[144,4608]{1,0:T(8,128)(2,1)S(1)}, bf16[144,4608]{1,0:T(8,128)(2,1)S(1)}, u32[]{:S(2)}, u32[]{:S(2)}) collective-permute-start(bf16[144,4608]{1,0:T(8,128)(2,1)S(1)} %slice_bitcast_fusion), channel_id=1, source_target_pairs={{0,64},{1,65},{2,66},{3,67},{4,68},{5,69},{6,70},{7,71},{8,72},{9,... | collective-permute-start | bytes 3981320 | tf_op jit(solution)/shard_map/ppermute | solution.py:52
  101.2 8.4 %collective-permute-start.27 = (bf16[144,4608]{1,0:T(8,128)(2,1)S(1)}, bf16[144,4608]{1,0:T(8,128)(2,1)S(1)}, u32[]{:S(2)}, u32[]{:S(2)}) collective-permute-start(bf16[144,4608]{1,0:T(8,128)(2,1)S(1)} %slice_bitcast_fusion.1), channel_id=1, source_target_pairs={{0,64},{1,65},{2,66},{3,67},{4,68},{5,69},{6,70},{7,71},{8,72},{9,... | collective-permute-start | bytes 3981320 | tf_op jit(solution)/shard_map/ppermute | solution.py:52
  105.2 11.2 %collective-permute-start.21 = (bf16[4,17,16,256]{3,2,1,0:T(8,128)(2,1)S(1)}, bf16[4,17,16,256]{3,2,1,0:T(8,128)(2,1)S(1)}, u32[]{:S(2)}, u32[]{:S(2)}) collective-permute-start(bf16[4,17,16,256]{3,2,1,0:T(8,128)(2,1)S(1)} %get-tuple-element.19), channel_id=1, source_target_pairs={{0,32},{1,33},{2,34},{3,35},{4,36},{5,37},{6,38},{7,39},{8,40},{9,... | collective-permute-start | bytes 1671176 | tf_op jit(solution)/shard_map/ppermute | solution.py:52
  106.4 16.0 %collective-permute-start.22 = (bf16[4,17,16,256]{3,2,1,0:T(8,128)(2,1)S(1)}, bf16[4,17,16,256]{3,2,1,0:T(8,128)(2,1)S(1)}, u32[]{:S(2)}, u32[]{:S(2)}) collective-permute-start(bf16[4,17,16,256]{3,2,1,0:T(8,128)(2,1)S(1)} %get-tuple-element.21), channel_id=1, source_target_pairs={{0,16},{1,17},{2,18},{3,19},{4,20},{5,21},{6,22},{7,23},{8,24},{9,... | collective-permute-start | bytes 1671176 | tf_op jit(solution)/shard_map/ppermute | solution.py:52
  108.2 14.1 %collective-permute-start.23 = (bf16[4,17,16,256]{3,2,1,0:T(8,128)(2,1)S(1)}, bf16[4,17,16,256]{3,2,1,0:T(8,128)(2,1)S(1)}, u32[]{:S(2)}, u32[]{:S(2)}) collective-permute-start(bf16[4,17,16,256]{3,2,1,0:T(8,128)(2,1)S(1)} %get-tuple-element.20), channel_id=1, source_target_pairs={{0,48},{1,49},{2,50},{3,51},{4,52},{5,53},{6,54},{7,55},{8,56},{9,... | collective-permute-start | bytes 1671176 | tf_op jit(solution)/shard_map/ppermute | solution.py:52
  111.0 19.3 %collective-permute-start.28 = (bf16[4,17,16,256]{3,2,1,0:T(8,128)(2,1)S(1)}, bf16[4,17,16,256]{3,2,1,0:T(8,128)(2,1)S(1)}, u32[]{:S(2)}, u32[]{:S(2)}) collective-permute-start(bf16[4,17,16,256]{3,2,1,0:T(8,128)(2,1)S(1)} %get-tuple-element.22), channel_id=1, source_target_pairs={{0,32},{1,33},{2,34},{3,35},{4,36},{5,37},{6,38},{7,39},{8,40},{9,... | collective-permute-start | bytes 1671176 | tf_op jit(solution)/shard_map/ppermute | solution.py:52
  112.4 24.9 %collective-permute-start.29 = (bf16[4,17,16,256]{3,2,1,0:T(8,128)(2,1)S(1)}, bf16[4,17,16,256]{3,2,1,0:T(8,128)(2,1)S(1)}, u32[]{:S(2)}, u32[]{:S(2)}) collective-permute-start(bf16[4,17,16,256]{3,2,1,0:T(8,128)(2,1)S(1)} %get-tuple-element.24), channel_id=1, source_target_pairs={{0,16},{1,17},{2,18},{3,19},{4,20},{5,21},{6,22},{7,23},{8,24},{9,... | collective-permute-start | bytes 1671176 | tf_op jit(solution)/shard_map/ppermute | solution.py:52
  116.5 20.8 %collective-permute-start.30 = (bf16[4,17,16,256]{3,2,1,0:T(8,128)(2,1)S(1)}, bf16[4,17,16,256]{3,2,1,0:T(8,128)(2,1)S(1)}, u32[]{:S(2)}, u32[]{:S(2)}) collective-permute-start(bf16[4,17,16,256]{3,2,1,0:T(8,128)(2,1)S(1)} %get-tuple-element.23), channel_id=1, source_target_pairs={{0,48},{1,49},{2,50},{3,51},{4,52},{5,53},{6,54},{7,55},{8,56},{9,... | collective-permute-start | bytes 1671176 | tf_op jit(solution)/shard_map/ppermute | solution.py:52
  122.7 16.5 %collective-permute-start.24 = (bf16[17,16,256]{2,1,0:T(8,128)(2,1)S(1)}, bf16[17,16,256]{2,1,0:T(8,128)(2,1)S(1)}, u32[]{:S(2)}, u32[]{:S(2)}) collective-permute-start(bf16[17,16,256]{2,1,0:T(8,128)(2,1)S(1)} %get-tuple-element.25), channel_id=1, source_target_pairs={{0,8},{1,9},{2,10},{3,11},{4,12},{5,13},{6,14},{7,15},{8,0},{9,1},... | collective-permute-start | bytes 417800 | tf_op jit(solution)/shard_map/ppermute | solution.py:52
  123.4 18.2 %collective-permute-start.25 = (bf16[17,16,256]{2,1,0:T(8,128)(2,1)S(1)}, bf16[17,16,256]{2,1,0:T(8,128)(2,1)S(1)}, u32[]{:S(2)}, u32[]{:S(2)}) collective-permute-start(bf16[17,16,256]{2,1,0:T(8,128)(2,1)S(1)} %get-tuple-element.27), channel_id=1, source_target_pairs={{0,4},{1,5},{2,6},{3,7},{4,8},{5,9},{6,10},{7,11},{8,12},{9,13},{1... | collective-permute-start | bytes 417800 | tf_op jit(solution)/shard_map/ppermute | solution.py:52
  130.4 11.2 %collective-permute-start.26 = (bf16[17,16,256]{2,1,0:T(8,128)(2,1)S(1)}, bf16[17,16,256]{2,1,0:T(8,128)(2,1)S(1)}, u32[]{:S(2)}, u32[]{:S(2)}) collective-permute-start(bf16[17,16,256]{2,1,0:T(8,128)(2,1)S(1)} %get-tuple-element.26), channel_id=1, source_target_pairs={{0,12},{1,13},{2,14},{3,15},{4,0},{5,1},{6,2},{7,3},{8,4},{9,5},{1... | collective-permute-start | bytes 417800 | tf_op jit(solution)/shard_map/ppermute | solution.py:52
  137.6 6.7 %collective-permute-start.31 = (bf16[17,16,256]{2,1,0:T(8,128)(2,1)S(1)}, bf16[17,16,256]{2,1,0:T(8,128)(2,1)S(1)}, u32[]{:S(2)}, u32[]{:S(2)}) collective-permute-start(bf16[17,16,256]{2,1,0:T(8,128)(2,1)S(1)} %get-tuple-element.28), channel_id=1, source_target_pairs={{0,8},{1,9},{2,10},{3,11},{4,12},{5,13},{6,14},{7,15},{8,0},{9,1},... | collective-permute-start | bytes 417800 | tf_op jit(solution)/shard_map/ppermute | solution.py:52
  138.3 7.4 %collective-permute-start.32 = (bf16[17,16,256]{2,1,0:T(8,128)(2,1)S(1)}, bf16[17,16,256]{2,1,0:T(8,128)(2,1)S(1)}, u32[]{:S(2)}, u32[]{:S(2)}) collective-permute-start(bf16[17,16,256]{2,1,0:T(8,128)(2,1)S(1)} %get-tuple-element.30), channel_id=1, source_target_pairs={{0,4},{1,5},{2,6},{3,7},{4,8},{5,9},{6,10},{7,11},{8,12},{9,13},{1... | collective-permute-start | bytes 417800 | tf_op jit(solution)/shard_map/ppermute | solution.py:52
  139.2 6.5 %collective-permute-start.33 = (bf16[17,16,256]{2,1,0:T(8,128)(2,1)S(1)}, bf16[17,16,256]{2,1,0:T(8,128)(2,1)S(1)}, u32[]{:S(2)}, u32[]{:S(2)}) collective-permute-start(bf16[17,16,256]{2,1,0:T(8,128)(2,1)S(1)} %get-tuple-element.29), channel_id=1, source_target_pairs={{0,12},{1,13},{2,14},{3,15},{4,0},{5,1},{6,2},{7,3},{8,4},{9,5},{1... | collective-permute-start | bytes 417800 | tf_op jit(solution)/shard_map/ppermute | solution.py:52

commit v2 on v1

--- a/solution.py
+++ b/solution.py
@@ -73,15 +73,19 @@
     mx, my, c = s_ref[0], s_ref[1], s_ref[2]
     for o in range(2):
         par = c if o == 0 else 1 - c
-        for b in range(4):
-            for a in range(4):
+        for src, (b, first, count) in zip(pieces[o * PIECES : (o + 1) * PIECES], SPANS):
+
+            def place(i, carry, par=par, src=src, b=b, first=first):
+                a = first + i
                 x = (mx + jnp.where(par == 0, a, b)) & 3
                 y = (my + jnp.where(par == 0, b, a)) & 3
                 xy = x * 4 + y
-                src = pieces[o * 4 + b]
-                win[par, pl.ds(xy * 8, 8)] = src[a, 0:8]
+                win[par, pl.ds(xy * 8, 8)] = src[i, 0:8]
                 for k in range(9):
-                    wout[par, k, xy] = src[a, 8 + k]
+                    wout[par, k, xy] = src[i, 8 + k]
+                return carry
+
+            lax.fori_loop(0, count, place, 0)
 
 
 def gain_row(wout, par):
@@ -160,7 +164,7 @@
 
 
 def kernel_low_forward(s_ref, xs, *refs):
-    pieces, (x1, x2, win, wout, stats, pre, normed, hat) = refs[:8], refs[8:]
+    pieces, (x1, x2, win, wout, stats, pre, normed, hat) = refs[: 2 * PIECES], refs[2 * PIECES :]
     place_weights(s_ref, pieces, win, wout)
     c, zl = s_ref[2], s_ref[3]
     for par in range(2):
@@ -185,8 +189,8 @@
 
 
 def kernel_high(s_ref, x2, cots, *refs):
-    pieces = refs[:8]
-    up2, acts, win, wout, hat0, hat1, rstd, x3, up3, pre0, gnorm, gsum = refs[8:]
+    pieces = refs[: 2 * PIECES]
+    up2, acts, win, wout, hat0, hat1, rstd, x3, up3, pre0, gnorm, gsum = refs[2 * PIECES :]
     place_weights(s_ref, pieces, win, wout)
     c, zl = s_ref[2], s_ref[3]
     gains = []
@@ -240,7 +244,7 @@
         )
 
 
-def kernel_grads(s_ref, acts, got, out):
+def kernel_grads(s_ref, acts, got, out, up, down):
     mx, my, c = s_ref[0], s_ref[1], s_ref[2]
     places = []
     for xy in range(16):
@@ -267,6 +271,40 @@
         out[places[xy], 16] = jnp.concatenate([part, part], axis=1).astype(BF16)
 
 
+    up[...] = out[8:10]
+    down[...] = out[10:12]
+
+
+def over_groups(step):
+    def body(g, carry):
+        step(g)
+        return carry
+
+    lax.fori_loop(0, 17, body, 0)
+
+
+def kernel_sides(s_ref, grads, up, down, after, before):
+    def step(g):
+        for i in range(2):
+            after[i, g] = (grads[4 + i, g].astype(F32) + up[i, g].astype(F32)).astype(BF16)
+            after[2 + i, g] = grads[6 + i, g]
+            before[i, g] = grads[12 + i, g]
+            before[2 + i, g] = (grads[14 + i, g].astype(F32) + down[i, g].astype(F32)).astype(BF16)
+
+    over_groups(step)
+
+
+def kernel_sum(s_ref, low, low_a, low_b, high, high_a, high_b, *pieces):
+    def step(g):
+        for p, (own, a, b) in enumerate(((low, low_a, low_b), (high, high_a, high_b))):
+            for k in range(4):
+                pieces[k][p, g] = (
+                    own[k, g].astype(F32) + a[k, g].astype(F32) + b[k, g].astype(F32)
+                ).astype(BF16)
+
+    over_groups(step)
+
+
 def vmem(*shape, kind=BF16):
     return pltpu.VMEM(shape, kind)
 
@@ -276,6 +314,8 @@
 
 
 UNROLL = 8
+SPANS = ((0, 0, 4), (1, 0, 4), (3, 0, 4), (2, 0, 2), (2, 2, 2))
+PIECES = len(SPANS)
 UP_AT, ACT_AT, PRE_AT, WIDE = D, 2 * D, 2 * D + R, 2 * D + 2 * R
 ACT = (ROWS, D)
 WIN, WOUT = (2, 128, 16, 256), (2, 9, 16, 16, 256)
@@ -306,15 +346,25 @@
     return functools.reduce(lambda p, q: p + q.astype(F32), got, first.astype(F32)).astype(BF16)
 
 
-def scatter_first(grads):
-    both = grads.reshape(4, 4, 17, 16, 256)
-    got = [shift(both[k], send_first(k)) for k in (2, 1, 3)]
-    return both[0], got
-
-
-def scatter_second(row):
-    got = [shift(row[k], send_second(k)) for k in (2, 1, 3)]
-    return add_up(row[0], got)
+def scatter_first(scalars, acts, got):
+    half = array(2, 17, 16, 256)
+    grads, up, down = call(
+        kernel_grads, scalars, [acts, got], [array(16, 17, 16, 256), half, half], []
+    )
+    return grads, shift(up, send_first(1)), shift(down, send_first(-1))
+
+
+def scatter_sides(scalars, grads, up, down):
+    row = array(4, 17, 16, 256)
+    after, before = call(kernel_sides, scalars, [grads, up, down], [row, row], [])
+    return grads, shift(after, send_first(1)), shift(before, send_first(-1))
+
+
+def scatter_second(scalars, low, high):
+    piece = array(2, 17, 16, 256)
+    own, *pieces = call(kernel_sum, scalars, [*low, *high], [piece] * 4, [])
+    got = [shift(pieces[k - 1], send_second(k)) for k in (2, 1, 3)]
+    return add_up(own, got)
 
 
 def device_body(inputs, cotangent, norm_gain, proj_in, proj_out):
@@ -346,7 +396,14 @@
     pairs = []
     for p in range(2):
         row = jnp.stack(near[p])
-        rows = [row] + [shift(row, send_second(-k)) for k in (1, 2, 3)]
+        after, before = shift(row, send_second(-1)), shift(row, send_second(1))
+        rows = [
+            row,
+            after,
+            before,
+            shift(after[:2], send_second(-1)),
+            shift(before[2:], send_second(1)),
+        ]
         pairs.append(rows + [shift(v, SWAP) for v in rows])
     x1, x2, win, wout, stats, pre = call(
         kernel_low_forward,
@@ -370,12 +427,11 @@
         BACK_SCRATCH,
     )
     got0 = shift(acts0[1], SWAP)
-    grad = array(16, 17, 16, 256)
-    own1, first1 = scatter_first(call(kernel_grads, scalars, [acts1, got1], grad, []))
-    own0, first0 = scatter_first(call(kernel_grads, scalars, [acts0, got0], grad, []))
-    high = scatter_second(add_up(own1, first1))
-    low = scatter_second(add_up(own0, first0))
-    grads = jnp.stack([low, high])
+    first1 = scatter_first(scalars, acts1, got1)
+    first0 = scatter_first(scalars, acts0, got0)
+    high = scatter_sides(scalars, *first1)
+    low = scatter_sides(scalars, *first0)
+    grads = scatter_second(scalars, low, high)
     parts = jnp.concatenate(
         [
             grads[:, :8].reshape(2, 4, 32, 256),

time: 162 us -> 147 us (0.907)
  waiting for transfers between devices: 67.5 us -> 28.7 us
  starting transfers between devices: 29 us -> 43.3 us
  local copies, waits for them, and re-layouts: 12.9 us -> 19.8 us
  Pallas kernels: 16.2 us -> 18.4 us
    ppermute x34 -> x37, waiting for transfers between devices: 67.5 us -> 28.7 us  [shift(): return lax.ppermute(value, AXES, pairs)]
    ppermute x34 -> x37, starting transfers between devices: 29 us -> 43.3 us  [shift(): return lax.ppermute(value, AXES, pairs)]
    unnamed x26 -> x42, local copies, waits for them, and re-layouts: 10.2 us -> 15.3 us
    pallas_call x5 -> x8, Pallas kernels: 16.2 us -> 18.4 us  [call(): pl.pallas_call(body, in_specs=[pl.BlockSpec(memory_space=pltpu.SMEM)] + [...]
    slice x2 -> x6, local copies, waits for them, and re-layouts: 0.22 us -> 2.03 us  [the longest x2 0.99 us: device_body(): before[2:]]
  transfers between devices with their start and end apart: 34 -> 37, of which waited for: 16 -> 12; matrix products, arithmetic and copies ran while one was open for 1% -> 2% of each run, Pallas kernels for 4% -> 7%
where the time goes in v2:
time: 147 us; the launch traced here: 145 us
  starting transfers between devices  43.3 us (29%)
  blocking collectives  32.9 us (22%)
  waiting for transfers between devices  28.7 us (20%)
  local copies, waits for them, and re-layouts  19.8 us (13%)
  Pallas kernels  18.4 us (13%)
    ppermute x37, starting transfers between devices, shift(): return lax.ppermute(value, AXES, pairs)  43.3 us
    ppermute x37, waiting for transfers between devices, shift(): return lax.ppermute(value, AXES, pairs)  28.7 us
    all_to_all x1, blocking collectives, device_body(): lax.all_to_all(jnp.broadcast_to(shard[None], (8, 72, 256)), ('zl', 'zh'),...  19.5 us
    pallas_call x8, Pallas kernels, call(): pl.pallas_call(body, in_specs=[pl.BlockSpec(memory_space=pltpu.SMEM)] + [...  18.4 us
    unnamed x42, local copies, waits for them, and re-layouts  15.3 us
    all_to_all x1, blocking collectives, device_body(): lax.all_to_all(parts, ('zl', 'zh'), 0, 0).astype(F32)  13.4 us
  transfers between devices with their start and end apart: 37, of which 12 were waited for; matrix products, arithmetic and copies ran while one was open for 2% of the time, Pallas kernels for 7%

profile of v2, /device:TPU:32, one launch (start us, length us, event | category | flops | bytes accessed | tf_op | source)
XLA Modules:
  0.0 145.2 jit_solution(1184882099229868054)
XLA Ops:
  2.1 19.5 %all_to_all.10 = bf16[8,72,256]{2,1,0:T(8,128)(2,1)S(1)} all-to-all(bf16[8,72,256]{2,1,0:T(8,128)(2,1)S(1)} %broadcast_in_dim.4), channel_id=1, replica_groups=mesh['zl'=2,'c'=2,'x'=4,'y'=4,'zh'=4] {'zl','zh'}, dimensions={0} | all-to-all | bytes 589824 | tf_op jit(solution)/shard_map/all_to_all | solution.py:381
  22.1 2.8 %collective-permute-start = (bf16[17,16,256]{2,1,0:T(8,128)(2,1)S(1)}, bf16[17,16,256]{2,1,0:T(8,128)(2,1)S(1)}, u32[]{:S(2)}, u32[]{:S(2)}) collective-permute-start(bf16[17,16,256]{2,1,0:T(8,128)(2,1)S(1)} %get-tuple-element.52), channel_id=1, source_target_pairs={{0,48},{1,49},{2,50},{3,51},{4,52},{5,53},{6,54},{7,55},{8,56},{9,... | collective-permute-start | bytes 417800 | tf_op jit(solution)/shard_map/ppermute | solution.py:52
  25.7 0.9 collective-permute-start.2
  26.6 2.4 %collective-permute-start.12 = (bf16[17,16,256]{2,1,0:T(8,128)(2,1)S(1)}, bf16[17,16,256]{2,1,0:T(8,128)(2,1)S(1)}, u32[]{:S(2)}, u32[]{:S(2)}) collective-permute-start(bf16[17,16,256]{2,1,0:T(8,128)(2,1)S(1)} %get-tuple-element.53), channel_id=1, source_target_pairs={{0,48},{1,49},{2,50},{3,51},{4,52},{5,53},{6,54},{7,55},{8,56},{9,... | collective-permute-start | bytes 417800 | tf_op jit(solution)/shard_map/ppermute | solution.py:52
  28.9 1.5 %collective-permute-start.13 = (bf16[17,16,256]{2,1,0:T(8,128)(2,1)S(1)}, bf16[17,16,256]{2,1,0:T(8,128)(2,1)S(1)}, u32[]{:S(2)}, u32[]{:S(2)}) collective-permute-start(bf16[17,16,256]{2,1,0:T(8,128)(2,1)S(1)} %get-tuple-element.53), channel_id=1, source_target_pairs={{0,32},{1,33},{2,34},{3,35},{4,36},{5,37},{6,38},{7,39},{8,40},{9,... | collective-permute-start | bytes 417800 | tf_op jit(solution)/shard_map/ppermute | solution.py:52
  30.5 1.1 collective-permute-done.1
  31.6 1.4 collective-permute-done.2
  33.0 3.1 %collective-permute-start.3 = (bf16[4,17,16,256]{3,2,1,0:T(8,128)(2,1)S(1)}, bf16[4,17,16,256]{3,2,1,0:T(8,128)(2,1)S(1)}, u32[]{:S(2)}, u32[]{:S(2)}) collective-permute-start(bf16[4,17,16,256]{3,2,1,0:T(8,128)(2,1)S(1)} %pad_maximum_fusion.refs_0_), channel_id=1, source_target_pairs={{0,12},{1,13},{2,14},{3,15},{4,0},{5,1},{6,2},{7,3},{8,4},{9,5},{1... | collective-permute-start | bytes 1671176 | tf_op jit(solution)/shard_map/ppermute | solution.py:52
  36.1 0.9 collective-permute-done.14
  37.1 4.7 %collective-permute-start.15 = (bf16[4,17,16,256]{3,2,1,0:T(8,128)(2,1)S(1)}, bf16[4,17,16,256]{3,2,1,0:T(8,128)(2,1)}, u32[]{:S(2)}, u32[]{:S(2)}) collective-permute-start(bf16[4,17,16,256]{3,2,1,0:T(8,128)(2,1)S(1)} %pad_maximum_fusion.1.refs_0_), channel_id=1, source_target_pairs={{0,12},{1,13},{2,14},{3,15},{4,0},{5,1},{6,2},{7,3},{8,4},{9,5},{1... | collective-permute-start | bytes 1671176 | tf_op jit(solution)/shard_map/ppermute | solution.py:52
  41.8 1.4 collective-permute-done.3.refs_1_
  43.2 3.8 %collective-permute-start.5 = (bf16[2,17,16,256]{3,2,1,0:T(8,128)(2,1)S(1)}, bf16[2,17,16,256]{3,2,1,0:T(8,128)(2,1)S(1)}, u32[]{:S(2)}, u32[]{:S(2)}) collective-permute-start(bf16[2,17,16,256]{3,2,1,0:T(8,128)(2,1)S(1)} %slice.78), channel_id=1, source_target_pairs={{0,12},{1,13},{2,14},{3,15},{4,0},{5,1},{6,2},{7,3},{8,4},{9,5},{1... | collective-permute-start | bytes 835592 | tf_op jit(solution)/shard_map/ppermute | solution.py:52
  47.1 2.1 %collective-permute-done.15.refs_1_ = bf16[4,17,16,256]{3,2,1,0:T(8,128)(2,1)} collective-permute-done((bf16[4,17,16,256]{3,2,1,0:T(8,128)(2,1)S(1)}, bf16[4,17,16,256]{3,2,1,0:T(8,128)(2,1)}, u32[]{:S(2)}, u32[]{:S(2)}) %collective-permute-start.15) | collective-permute-done | bytes 557088 | tf_op jit(solution)/shard_map/ppermute | solution.py:52
  49.1 1.0 slice.81
  50.1 3.9 %collective-permute-start.17 = (bf16[2,17,16,256]{3,2,1,0:T(8,128)(2,1)S(1)}, bf16[2,17,16,256]{3,2,1,0:T(8,128)(2,1)S(1)}, u32[]{:S(2)}, u32[]{:S(2)}) collective-permute-start(bf16[2,17,16,256]{3,2,1,0:T(8,128)(2,1)S(1)} %slice.81), channel_id=1, source_target_pairs={{0,12},{1,13},{2,14},{3,15},{4,0},{5,1},{6,2},{7,3},{8,4},{9,5},{1... | collective-permute-start | bytes 835592 | tf_op jit(solution)/shard_map/ppermute | solution.py:52
  54.0 1.0 slice.82
  55.1 0.8 copy-done.6
  57.2 0.9 collective-permute-done.17.refs_3_
  58.8 4.1 %collective-permute-done.18.refs_4_ = bf16[2,17,16,256]{3,2,1,0:T(8,128)(2,1)} collective-permute-done((bf16[2,17,16,256]{3,2,1,0:T(8,128)(2,1)S(1)}, bf16[2,17,16,256]{3,2,1,0:T(8,128)(2,1)}, u32[]{:S(2)}, u32[]{:S(2)}) %collective-permute-start.18) | collective-permute-done | bytes 278560 | tf_op jit(solution)/shard_map/ppermute | solution.py:52
  64.9 0.8 copy-done.8
  66.3 0.8 copy-done.10
  67.2 1.1 copy-done.3
  68.2 1.1 copy-done.5
  69.3 1.1 copy-done.7
  70.3 1.1 copy-done.9
  71.4 1.1 copy-done.11
  72.4 1.0 copy-done.13
  73.4 1.0 copy-done.15
  74.3 1.0 copy-done.17
  75.3 1.0 copy-done.19
  76.3 3.2 %shard_map.76 = (bf16[128,2048]{1,0:T(8,128)(2,1)S(1)}, bf16[128,2048]{1,0:T(8,128)(2,1)S(1)}, bf16[2,128,16,256]{3,2,1,0:T(8,128)(2,1)S(1)}, bf16[2,9,16,16,256...) custom-call(s32[4]{0:T(128)S(1)} %pad_add_fusion.s_ref, ...), custom_call_target="tpu_custom_call" | custom-call | tf_op jit(solution)/shard_map/pallas_call | solution.py:335
  79.5 6.7 %shard_map.77 = (bf16[128,2048]{1,0:T(8,128)(2,1)S(1)}, bf16[2,144,4608]{2,1,0:T(8,128)(2,1)S(1)}) custom-call(s32[4]{0:T(128)S(1)} %pad_add_fusion.s_ref, bf16[128,2048]{1,0:T(8,128)(2,1)S(1)} %get-tuple-element.26.x2, bf16[2,2,128,2048]{3,2,1,0:T(8,128)(2,1)S(1)} %copy-done.1, bf16[4,17,16,256]{3,2,1,0:T(8,128)(2,1)S(1)} %pad_maximum_fusion.1.refs_0_, ...), custom_call_target="tpu_custom_call" | custom-call | tf_op jit(solution)/shard_map/pallas_call | solution.py:335
  86.3 0.8 collective-permute-start.29
  87.1 3.4 %shard_map.78.acts = bf16[2,144,4608]{2,1,0:T(8,128)(2,1)S(1)} custom-call(s32[4]{0:T(128)S(1)} %pad_add_fusion.s_ref, bf16[2,2,128,2048]{3,2,1,0:T(8,128)(2,1)S(1)} %copy-done, bf16[128,2048]{1,0:T(8,128)(2,1)S(1)} %get-tuple-element.25.x1, bf16[128,2048]{1,0:T(8,128)(2,1)S(1)} %get-tuple-element.27.up2, ...), custom_call_target="tpu_custom_call" | custom-call | tf_op jit(solution)/shard_map/pallas_call | solution.py:335
  90.7 1.3 shard_map.81
  92.5 2.8 %collective-permute-start.31 = (bf16[2,17,16,256]{3,2,1,0:T(8,128)(2,1)S(1)}, bf16[2,17,16,256]{3,2,1,0:T(8,128)(2,1)S(1)}, u32[]{:S(2)}, u32[]{:S(2)}) collective-permute-start(bf16[2,17,16,256]{3,2,1,0:T(8,128)(2,1)S(1)} %get-tuple-element.40), channel_id=1, source_target_pairs={{0,48},{1,49},{2,50},{3,51},{4,52},{5,53},{6,54},{7,55},{8,56},{9,... | collective-permute-start | bytes 835592 | tf_op jit(solution)/shard_map/ppermute | solution.py:52
  95.3 1.3 shard_map.79
  96.8 3.2 %collective-permute-start.26 = (bf16[2,17,16,256]{3,2,1,0:T(8,128)(2,1)S(1)}, bf16[2,17,16,256]{3,2,1,0:T(8,128)(2,1)S(1)}, u32[]{:S(2)}, u32[]{:S(2)}) collective-permute-start(bf16[2,17,16,256]{3,2,1,0:T(8,128)(2,1)S(1)} %get-tuple-element.34), channel_id=1, source_target_pairs={{0,48},{1,49},{2,50},{3,51},{4,52},{5,53},{6,54},{7,55},{8,56},{9,... | collective-permute-start | bytes 835592 | tf_op jit(solution)/shard_map/ppermute | solution.py:52
  100.8 3.2 %collective-permute-start.33 = (bf16[4,17,16,256]{3,2,1,0:T(8,128)(2,1)S(1)}, bf16[4,17,16,256]{3,2,1,0:T(8,128)(2,1)S(1)}, u32[]{:S(2)}, u32[]{:S(2)}) collective-permute-start(bf16[4,17,16,256]{3,2,1,0:T(8,128)(2,1)S(1)} %get-tuple-element.42), channel_id=1, source_target_pairs={{0,48},{1,49},{2,50},{3,51},{4,52},{5,53},{6,54},{7,55},{8,56},{9,... | collective-permute-start | bytes 1671176 | tf_op jit(solution)/shard_map/ppermute | solution.py:52
  105.4 3.3 %collective-permute-start.28 = (bf16[4,17,16,256]{3,2,1,0:T(8,128)(2,1)S(1)}, bf16[4,17,16,256]{3,2,1,0:T(8,128)(2,1)S(1)}, u32[]{:S(2)}, u32[]{:S(2)}) collective-permute-start(bf16[4,17,16,256]{3,2,1,0:T(8,128)(2,1)S(1)} %get-tuple-element.36), channel_id=1, source_target_pairs={{0,48},{1,49},{2,50},{3,51},{4,52},{5,53},{6,54},{7,55},{8,56},{9,... | collective-permute-start | bytes 1671176 | tf_op jit(solution)/shard_map/ppermute | solution.py:52
  108.7 2.9 %collective-permute-done.32.high_a = bf16[4,17,16,256]{3,2,1,0:T(8,128)(2,1)S(1)} collective-permute-done((bf16[4,17,16,256]{3,2,1,0:T(8,128)(2,1)S(1)}, bf16[4,17,16,256]{3,2,1,0:T(8,128)(2,1)S(1)}, u32[]{:S(2)}, u32[]{:S(2)}) %collective-permute-start.32) | collective-permute-done | bytes 557088 | tf_op jit(solution)/shard_map/ppermute | solution.py:52
  111.6 6.0 %collective-permute-done.27.low_a = bf16[4,17,16,256]{3,2,1,0:T(8,128)(2,1)S(1)} collective-permute-done((bf16[4,17,16,256]{3,2,1,0:T(8,128)(2,1)S(1)}, bf16[4,17,16,256]{3,2,1,0:T(8,128)(2,1)S(1)}, u32[]{:S(2)}, u32[]{:S(2)}) %collective-permute-start.27) | collective-permute-done | bytes 557088 | tf_op jit(solution)/shard_map/ppermute | solution.py:52
  117.5 1.0 shard_map.83
  118.7 0.9 collective-permute-start.35
  119.5 2.4 %collective-permute-start.36 = (bf16[2,17,16,256]{3,2,1,0:T(8,128)(2,1)S(1)}, bf16[2,17,16,256]{3,2,1,0:T(8,128)(2,1)S(1)}, u32[]{:S(2)}, u32[]{:S(2)}) collective-permute-start(bf16[2,17,16,256]{3,2,1,0:T(8,128)(2,1)S(1)} %get-tuple-element.46), channel_id=1, source_target_pairs={{0,12},{1,13},{2,14},{3,15},{4,0},{5,1},{6,2},{7,3},{8,4},{9,5},{1... | collective-permute-start | bytes 835592 | tf_op jit(solution)/shard_map/ppermute | solution.py:52
  122.0 4.8 %collective-permute-done.34 = bf16[2,17,16,256]{3,2,1,0:T(8,128)(2,1)S(1)} collective-permute-done((bf16[2,17,16,256]{3,2,1,0:T(8,128)(2,1)S(1)}, bf16[2,17,16,256]{3,2,1,0:T(8,128)(2,1)S(1)}, u32[]{:S(2)}, u32[]{:S(2)}) %collective-permute-start.34) | collective-permute-done | bytes 278560 | tf_op jit(solution)/shard_map/ppermute | solution.py:52
  126.8 2.7 %collective-permute-done.35 = bf16[2,17,16,256]{3,2,1,0:T(8,128)(2,1)S(1)} collective-permute-done((bf16[2,17,16,256]{3,2,1,0:T(8,128)(2,1)S(1)}, bf16[2,17,16,256]{3,2,1,0:T(8,128)(2,1)S(1)}, u32[]{:S(2)}, u32[]{:S(2)}) %collective-permute-start.35) | collective-permute-done | bytes 278560 | tf_op jit(solution)/shard_map/ppermute | solution.py:52
  130.0 13.4 %all_to_all.11 = bf16[8,72,256]{2,1,0:T(8,128)(2,1)S(1)} all-to-all(bf16[8,72,256]{2,1,0:T(8,128)(2,1)S(1)} %pad_maximum_fusion.2), channel_id=1, replica_groups=mesh['zl'=2,'c'=2,'x'=4,'y'=4,'zh'=4] {'zl','zh'}, dimensions={0} | all-to-all | bytes 589824 | tf_op jit(solution)/shard_map/all_to_all | solution.py:443
  (113 shorter events, 13.0 us)
Async XLA Ops:
  22.1 8.4 %collective-permute-start = (bf16[17,16,256]{2,1,0:T(8,128)(2,1)S(1)}, bf16[17,16,256]{2,1,0:T(8,128)(2,1)S(1)}, u32[]{:S(2)}, u32[]{:S(2)}) collective-permute-start(bf16[17,16,256]{2,1,0:T(8,128)(2,1)S(1)} %get-tuple-element.52), channel_id=1, source_target_pairs={{0,48},{1,49},{2,50},{3,51},{4,52},{5,53},{6,54},{7,55},{8,56},{9,... | collective-permute-start | bytes 417800 | tf_op jit(solution)/shard_map/ppermute | solution.py:52
  24.9 6.7 %collective-permute-start.1 = (bf16[17,16,256]{2,1,0:T(8,128)(2,1)S(1)}, bf16[17,16,256]{2,1,0:T(8,128)(2,1)S(1)}, u32[]{:S(2)}, u32[]{:S(2)}) collective-permute-start(bf16[17,16,256]{2,1,0:T(8,128)(2,1)S(1)} %get-tuple-element.52), channel_id=1, source_target_pairs={{0,32},{1,33},{2,34},{3,35},{4,36},{5,37},{6,38},{7,39},{8,40},{9,... | collective-permute-start | bytes 417800 | tf_op jit(solution)/shard_map/ppermute | solution.py:52
  25.7 7.3 %collective-permute-start.2 = (bf16[17,16,256]{2,1,0:T(8,128)(2,1)S(1)}, bf16[17,16,256]{2,1,0:T(8,128)(2,1)S(1)}, u32[]{:S(2)}, u32[]{:S(2)}) collective-permute-start(bf16[17,16,256]{2,1,0:T(8,128)(2,1)S(1)} %get-tuple-element.52), channel_id=1, source_target_pairs={{0,16},{1,17},{2,18},{3,19},{4,20},{5,21},{6,22},{7,23},{8,24},{9,... | collective-permute-start | bytes 417800 | tf_op jit(solution)/shard_map/ppermute | solution.py:52
  26.6 9.5 %collective-permute-start.12 = (bf16[17,16,256]{2,1,0:T(8,128)(2,1)S(1)}, bf16[17,16,256]{2,1,0:T(8,128)(2,1)S(1)}, u32[]{:S(2)}, u32[]{:S(2)}) collective-permute-start(bf16[17,16,256]{2,1,0:T(8,128)(2,1)S(1)} %get-tuple-element.53), channel_id=1, source_target_pairs={{0,48},{1,49},{2,50},{3,51},{4,52},{5,53},{6,54},{7,55},{8,56},{9,... | collective-permute-start | bytes 417800 | tf_op jit(solution)/shard_map/ppermute | solution.py:52
  28.9 7.2 %collective-permute-start.13 = (bf16[17,16,256]{2,1,0:T(8,128)(2,1)S(1)}, bf16[17,16,256]{2,1,0:T(8,128)(2,1)S(1)}, u32[]{:S(2)}, u32[]{:S(2)}) collective-permute-start(bf16[17,16,256]{2,1,0:T(8,128)(2,1)S(1)} %get-tuple-element.53), channel_id=1, source_target_pairs={{0,32},{1,33},{2,34},{3,35},{4,36},{5,37},{6,38},{7,39},{8,40},{9,... | collective-permute-start | bytes 417800 | tf_op jit(solution)/shard_map/ppermute | solution.py:52
  30.5 6.5 %collective-permute-start.14 = (bf16[17,16,256]{2,1,0:T(8,128)(2,1)S(1)}, bf16[17,16,256]{2,1,0:T(8,128)(2,1)S(1)}, u32[]{:S(2)}, u32[]{:S(2)}) collective-permute-start(bf16[17,16,256]{2,1,0:T(8,128)(2,1)S(1)} %get-tuple-element.53), channel_id=1, source_target_pairs={{0,16},{1,17},{2,18},{3,19},{4,20},{5,21},{6,22},{7,23},{8,24},{9,... | collective-permute-start | bytes 417800 | tf_op jit(solution)/shard_map/ppermute | solution.py:52
  32.9 34.2 %copy-start = (bf16[2,2,128,2048]{3,2,1,0:T(8,128)(2,1)S(1)}, bf16[2,2,128,2048]{3,2,1,0:T(8,128)(2,1)}, u32[]{:S(2)}) copy-start(bf16[2,2,128,2048]{3,2,1,0:T(8,128)(2,1)} %xs.3) | copy-start | bytes 6291460
  33.0 10.1 %collective-permute-start.3 = (bf16[4,17,16,256]{3,2,1,0:T(8,128)(2,1)S(1)}, bf16[4,17,16,256]{3,2,1,0:T(8,128)(2,1)S(1)}, u32[]{:S(2)}, u32[]{:S(2)}) collective-permute-start(bf16[4,17,16,256]{3,2,1,0:T(8,128)(2,1)S(1)} %pad_maximum_fusion.refs_0_), channel_id=1, source_target_pairs={{0,12},{1,13},{2,14},{3,15},{4,0},{5,1},{6,2},{7,3},{8,4},{9,5},{1... | collective-permute-start | bytes 1671176 | tf_op jit(solution)/shard_map/ppermute | solution.py:52
  36.1 10.8 %collective-permute-start.4 = (bf16[4,17,16,256]{3,2,1,0:T(8,128)(2,1)S(1)}, bf16[4,17,16,256]{3,2,1,0:T(8,128)(2,1)S(1)}, u32[]{:S(2)}, u32[]{:S(2)}) collective-permute-start(bf16[4,17,16,256]{3,2,1,0:T(8,128)(2,1)S(1)} %pad_maximum_fusion.refs_0_), channel_id=1, source_target_pairs={{0,4},{1,5},{2,6},{3,7},{4,8},{5,9},{6,10},{7,11},{8,12},{9,13},{1... | collective-permute-start | bytes 1671176 | tf_op jit(solution)/shard_map/ppermute | solution.py:52
  37.1 12.1 %collective-permute-start.15 = (bf16[4,17,16,256]{3,2,1,0:T(8,128)(2,1)S(1)}, bf16[4,17,16,256]{3,2,1,0:T(8,128)(2,1)}, u32[]{:S(2)}, u32[]{:S(2)}) collective-permute-start(bf16[4,17,16,256]{3,2,1,0:T(8,128)(2,1)S(1)} %pad_maximum_fusion.1.refs_0_), channel_id=1, source_target_pairs={{0,12},{1,13},{2,14},{3,15},{4,0},{5,1},{6,2},{7,3},{8,4},{9,5},{1... | collective-permute-start | bytes 1671176 | tf_op jit(solution)/shard_map/ppermute | solution.py:52
  41.8 12.2 %collective-permute-start.16 = (bf16[4,17,16,256]{3,2,1,0:T(8,128)(2,1)S(1)}, bf16[4,17,16,256]{3,2,1,0:T(8,128)(2,1)}, u32[]{:S(2)}, u32[]{:S(2)}) collective-permute-start(bf16[4,17,16,256]{3,2,1,0:T(8,128)(2,1)S(1)} %pad_maximum_fusion.1.refs_0_), channel_id=1, source_target_pairs={{0,4},{1,5},{2,6},{3,7},{4,8},{5,9},{6,10},{7,11},{8,12},{9,13},{1... | collective-permute-start | bytes 1671176 | tf_op jit(solution)/shard_map/ppermute | solution.py:52
  41.8 13.3 %collective-permute-start.7 = (bf16[4,17,16,256]{3,2,1,0:T(8,128)(2,1)S(1)}, bf16[4,17,16,256]{3,2,1,0:T(8,128)(2,1)S(1)}, u32[]{:S(2)}, u32[]{:S(2)}) collective-permute-start(bf16[4,17,16,256]{3,2,1,0:T(8,128)(2,1)S(1)} %pad_maximum_fusion.refs_0_), channel_id=1, source_target_pairs={{0,64},{1,65},{2,66},{3,67},{4,68},{5,69},{6,70},{7,71},{8,72},{9,... | collective-permute-start | bytes 1671176 | tf_op jit(solution)/shard_map/ppermute | solution.py:52
  43.2 14.9 %copy-start.2 = (bf16[4,17,16,256]{3,2,1,0:T(8,128)(2,1)}, bf16[4,17,16,256]{3,2,1,0:T(8,128)(2,1)S(1)}, u32[]{:S(2)}) copy-start(bf16[4,17,16,256]{3,2,1,0:T(8,128)(2,1)S(1)} %collective-permute-done.3.refs_1_) | copy-start | bytes 1671172
  43.2 12.7 %collective-permute-start.5 = (bf16[2,17,16,256]{3,2,1,0:T(8,128)(2,1)S(1)}, bf16[2,17,16,256]{3,2,1,0:T(8,128)(2,1)S(1)}, u32[]{:S(2)}, u32[]{:S(2)}) collective-permute-start(bf16[2,17,16,256]{3,2,1,0:T(8,128)(2,1)S(1)} %slice.78), channel_id=1, source_target_pairs={{0,12},{1,13},{2,14},{3,15},{4,0},{5,1},{6,2},{7,3},{8,4},{9,5},{1... | collective-permute-start | bytes 835592 | tf_op jit(solution)/shard_map/ppermute | solution.py:52
  47.0 17.9 %copy-start.4 = (bf16[4,17,16,256]{3,2,1,0:T(8,128)(2,1)}, bf16[4,17,16,256]{3,2,1,0:T(8,128)(2,1)S(1)}, u32[]{:S(2)}) copy-start(bf16[4,17,16,256]{3,2,1,0:T(8,128)(2,1)S(1)} %collective-permute-done.4.refs_2_) | copy-start | bytes 1671172
  47.0 9.4 %collective-permute-start.6 = (bf16[2,17,16,256]{3,2,1,0:T(8,128)(2,1)S(1)}, bf16[2,17,16,256]{3,2,1,0:T(8,128)(2,1)S(1)}, u32[]{:S(2)}, u32[]{:S(2)}) collective-permute-start(bf16[2,17,16,256]{3,2,1,0:T(8,128)(2,1)S(1)} %slice.79), channel_id=1, source_target_pairs={{0,4},{1,5},{2,6},{3,7},{4,8},{5,9},{6,10},{7,11},{8,12},{9,13},{1... | collective-permute-start | bytes 835592 | tf_op jit(solution)/shard_map/ppermute | solution.py:52
  50.1 7.9 %collective-permute-start.17 = (bf16[2,17,16,256]{3,2,1,0:T(8,128)(2,1)S(1)}, bf16[2,17,16,256]{3,2,1,0:T(8,128)(2,1)S(1)}, u32[]{:S(2)}, u32[]{:S(2)}) collective-permute-start(bf16[2,17,16,256]{3,2,1,0:T(8,128)(2,1)S(1)} %slice.81), channel_id=1, source_target_pairs={{0,12},{1,13},{2,14},{3,15},{4,0},{5,1},{6,2},{7,3},{8,4},{9,5},{1... | collective-permute-start | bytes 835592 | tf_op jit(solution)/shard_map/ppermute | solution.py:52
  55.0 7.9 %collective-permute-start.18 = (bf16[2,17,16,256]{3,2,1,0:T(8,128)(2,1)S(1)}, bf16[2,17,16,256]{3,2,1,0:T(8,128)(2,1)}, u32[]{:S(2)}, u32[]{:S(2)}) collective-permute-start(bf16[2,17,16,256]{3,2,1,0:T(8,128)(2,1)S(1)} %slice.82), channel_id=1, source_target_pairs={{0,4},{1,5},{2,6},{3,7},{4,8},{5,9},{6,10},{7,11},{8,12},{9,13},{1... | collective-permute-start | bytes 835592 | tf_op jit(solution)/shard_map/ppermute | solution.py:52
  55.9 9.0 %collective-permute-start.8 = (bf16[4,17,16,256]{3,2,1,0:T(8,128)(2,1)S(1)}, bf16[4,17,16,256]{3,2,1,0:T(8,128)(2,1)S(1)}, u32[]{:S(2)}, u32[]{:S(2)}) collective-permute-start(bf16[4,17,16,256]{3,2,1,0:T(8,128)(2,1)S(1)} %collective-permute-done.3.refs_1_), channel_id=1, source_target_pairs={{0,64},{1,65},{2,66},{3,67},{4,68},{5,69},{6,70},{7,71},{8,72},{9,... | collective-permute-start | bytes 1671176 | tf_op jit(solution)/shard_map/ppermute | solution.py:52
  55.9 10.4 %collective-permute-start.9 = (bf16[4,17,16,256]{3,2,1,0:T(8,128)(2,1)S(1)}, bf16[4,17,16,256]{3,2,1,0:T(8,128)(2,1)S(1)}, u32[]{:S(2)}, u32[]{:S(2)}) collective-permute-start(bf16[4,17,16,256]{3,2,1,0:T(8,128)(2,1)S(1)} %collective-permute-done.4.refs_2_), channel_id=1, source_target_pairs={{0,64},{1,65},{2,66},{3,67},{4,68},{5,69},{6,70},{7,71},{8,72},{9,... | collective-permute-start | bytes 1671176 | tf_op jit(solution)/shard_map/ppermute | solution.py:52
  56.4 6.5 %collective-permute-start.10 = (bf16[2,17,16,256]{3,2,1,0:T(8,128)(2,1)S(1)}, bf16[2,17,16,256]{3,2,1,0:T(8,128)(2,1)S(1)}, u32[]{:S(2)}, u32[]{:S(2)}) collective-permute-start(bf16[2,17,16,256]{3,2,1,0:T(8,128)(2,1)S(1)} %collective-permute-done.5.refs_3_), channel_id=1, source_target_pairs={{0,64},{1,65},{2,66},{3,67},{4,68},{5,69},{6,70},{7,71},{8,72},{9,... | collective-permute-start | bytes 835592 | tf_op jit(solution)/shard_map/ppermute | solution.py:52
  58.1 6.1 %collective-permute-start.11 = (bf16[2,17,16,256]{3,2,1,0:T(8,128)(2,1)S(1)}, bf16[2,17,16,256]{3,2,1,0:T(8,128)(2,1)S(1)}, u32[]{:S(2)}, u32[]{:S(2)}) collective-permute-start(bf16[2,17,16,256]{3,2,1,0:T(8,128)(2,1)S(1)} %collective-permute-done.6.refs_4_), channel_id=1, source_target_pairs={{0,64},{1,65},{2,66},{3,67},{4,68},{5,69},{6,70},{7,71},{8,72},{9,... | collective-permute-start | bytes 835592 | tf_op jit(solution)/shard_map/ppermute | solution.py:52
  62.9 16.5 %collective-permute-start.19 = (bf16[4,17,16,256]{3,2,1,0:T(8,128)(2,1)S(1)}, bf16[4,17,16,256]{3,2,1,0:T(8,128)(2,1)}, u32[]{:S(2)}, u32[]{:S(2)}) collective-permute-start(bf16[4,17,16,256]{3,2,1,0:T(8,128)(2,1)S(1)} %pad_maximum_fusion.1.refs_0_), channel_id=1, source_target_pairs={{0,64},{1,65},{2,66},{3,67},{4,68},{5,69},{6,70},{7,71},{8,72},{9,... | collective-permute-start | bytes 1671176 | tf_op jit(solution)/shard_map/ppermute | solution.py:52
  63.6 15.8 %collective-permute-start.20 = (bf16[4,17,16,256]{3,2,1,0:T(8,128)(2,1)}, bf16[4,17,16,256]{3,2,1,0:T(8,128)(2,1)}, u32[]{:S(2)}, u32[]{:S(2)}) collective-permute-start(bf16[4,17,16,256]{3,2,1,0:T(8,128)(2,1)} %collective-permute-done.15.refs_1_), channel_id=1, source_target_pairs={{0,64},{1,65},{2,66},{3,67},{4,68},{5,69},{6,70},{7,71},{8,72},{9,... | collective-permute-start | bytes 1671176 | tf_op jit(solution)/shard_map/ppermute | solution.py:52
  64.9 14.6 %collective-permute-start.21 = (bf16[4,17,16,256]{3,2,1,0:T(8,128)(2,1)}, bf16[4,17,16,256]{3,2,1,0:T(8,128)(2,1)}, u32[]{:S(2)}, u32[]{:S(2)}) collective-permute-start(bf16[4,17,16,256]{3,2,1,0:T(8,128)(2,1)} %collective-permute-done.16.refs_2_), channel_id=1, source_target_pairs={{0,64},{1,65},{2,66},{3,67},{4,68},{5,69},{6,70},{7,71},{8,72},{9,... | collective-permute-start | bytes 1671176 | tf_op jit(solution)/shard_map/ppermute | solution.py:52
  65.8 13.7 %collective-permute-start.22 = (bf16[2,17,16,256]{3,2,1,0:T(8,128)(2,1)S(1)}, bf16[2,17,16,256]{3,2,1,0:T(8,128)(2,1)}, u32[]{:S(2)}, u32[]{:S(2)}) collective-permute-start(bf16[2,17,16,256]{3,2,1,0:T(8,128)(2,1)S(1)} %collective-permute-done.17.refs_3_), channel_id=1, source_target_pairs={{0,64},{1,65},{2,66},{3,67},{4,68},{5,69},{6,70},{7,71},{8,72},{9,... | collective-permute-start | bytes 835592 | tf_op jit(solution)/shard_map/ppermute | solution.py:52
  67.1 12.4 %collective-permute-start.23 = (bf16[2,17,16,256]{3,2,1,0:T(8,128)(2,1)}, bf16[2,17,16,256]{3,2,1,0:T(8,128)(2,1)}, u32[]{:S(2)}, u32[]{:S(2)}) collective-permute-start(bf16[2,17,16,256]{3,2,1,0:T(8,128)(2,1)} %collective-permute-done.18.refs_4_), channel_id=1, source_target_pairs={{0,64},{1,65},{2,66},{3,67},{4,68},{5,69},{6,70},{7,71},{8,72},{9,... | collective-permute-start | bytes 835592 | tf_op jit(solution)/shard_map/ppermute | solution.py:52
  67.2 1.1 copy-start.3
  68.2 1.1 copy-start.5
  69.3 1.1 copy-start.7
  70.3 1.1 copy-start.9
  71.4 1.1 copy-start.11
  72.4 1.0 copy-start.13
  73.4 1.0 copy-start.15
  76.3 3.2 %copy-start.1 = (bf16[2,2,128,2048]{3,2,1,0:T(8,128)(2,1)S(1)}, bf16[2,2,128,2048]{3,2,1,0:T(8,128)(2,1)}, u32[]{:S(2)}) copy-start(bf16[2,2,128,2048]{3,2,1,0:T(8,128)(2,1)} %cots.1) | copy-start | bytes 6291460
  86.3 4.4 %collective-permute-start.29 = (bf16[144,4608]{1,0:T(8,128)(2,1)S(1)}, bf16[144,4608]{1,0:T(8,128)(2,1)S(1)}, u32[]{:S(2)}, u32[]{:S(2)}) collective-permute-start(bf16[144,4608]{1,0:T(8,128)(2,1)S(1)} %slice_bitcast_fusion.1), channel_id=1, source_target_pairs={{0,64},{1,65},{2,66},{3,67},{4,68},{5,69},{6,70},{7,71},{8,72},{9,... | collective-permute-start | bytes 3981320 | tf_op jit(solution)/shard_map/ppermute | solution.py:52
  90.6 4.8 %collective-permute-start.24 = (bf16[144,4608]{1,0:T(8,128)(2,1)S(1)}, bf16[144,4608]{1,0:T(8,128)(2,1)S(1)}, u32[]{:S(2)}, u32[]{:S(2)}) collective-permute-start(bf16[144,4608]{1,0:T(8,128)(2,1)S(1)} %slice_bitcast_fusion), channel_id=1, source_target_pairs={{0,64},{1,65},{2,66},{3,67},{4,68},{5,69},{6,70},{7,71},{8,72},{9,... | collective-permute-start | bytes 3981320 | tf_op jit(solution)/shard_map/ppermute | solution.py:52
  92.0 8.0 %collective-permute-start.30 = (bf16[2,17,16,256]{3,2,1,0:T(8,128)(2,1)S(1)}, bf16[2,17,16,256]{3,2,1,0:T(8,128)(2,1)S(1)}, u32[]{:S(2)}, u32[]{:S(2)}) collective-permute-start(bf16[2,17,16,256]{3,2,1,0:T(8,128)(2,1)S(1)} %get-tuple-element.39), channel_id=1, source_target_pairs={{0,16},{1,17},{2,18},{3,19},{4,20},{5,21},{6,22},{7,23},{8,24},{9,... | collective-permute-start | bytes 835592 | tf_op jit(solution)/shard_map/ppermute | solution.py:52
  92.5 7.5 %collective-permute-start.31 = (bf16[2,17,16,256]{3,2,1,0:T(8,128)(2,1)S(1)}, bf16[2,17,16,256]{3,2,1,0:T(8,128)(2,1)S(1)}, u32[]{:S(2)}, u32[]{:S(2)}) collective-permute-start(bf16[2,17,16,256]{3,2,1,0:T(8,128)(2,1)S(1)} %get-tuple-element.40), channel_id=1, source_target_pairs={{0,48},{1,49},{2,50},{3,51},{4,52},{5,53},{6,54},{7,55},{8,56},{9,... | collective-permute-start | bytes 835592 | tf_op jit(solution)/shard_map/ppermute | solution.py:52
  96.7 7.8 %collective-permute-start.25 = (bf16[2,17,16,256]{3,2,1,0:T(8,128)(2,1)S(1)}, bf16[2,17,16,256]{3,2,1,0:T(8,128)(2,1)S(1)}, u32[]{:S(2)}, u32[]{:S(2)}) collective-permute-start(bf16[2,17,16,256]{3,2,1,0:T(8,128)(2,1)S(1)} %get-tuple-element.33), channel_id=1, source_target_pairs={{0,16},{1,17},{2,18},{3,19},{4,20},{5,21},{6,22},{7,23},{8,24},{9,... | collective-permute-start | bytes 835592 | tf_op jit(solution)/shard_map/ppermute | solution.py:52
  96.8 7.7 %collective-permute-start.26 = (bf16[2,17,16,256]{3,2,1,0:T(8,128)(2,1)S(1)}, bf16[2,17,16,256]{3,2,1,0:T(8,128)(2,1)S(1)}, u32[]{:S(2)}, u32[]{:S(2)}) collective-permute-start(bf16[2,17,16,256]{3,2,1,0:T(8,128)(2,1)S(1)} %get-tuple-element.34), channel_id=1, source_target_pairs={{0,48},{1,49},{2,50},{3,51},{4,52},{5,53},{6,54},{7,55},{8,56},{9,... | collective-permute-start | bytes 835592 | tf_op jit(solution)/shard_map/ppermute | solution.py:52
  100.8 10.8 %collective-permute-start.32 = (bf16[4,17,16,256]{3,2,1,0:T(8,128)(2,1)S(1)}, bf16[4,17,16,256]{3,2,1,0:T(8,128)(2,1)S(1)}, u32[]{:S(2)}, u32[]{:S(2)}) collective-permute-start(bf16[4,17,16,256]{3,2,1,0:T(8,128)(2,1)S(1)} %get-tuple-element.41), channel_id=1, source_target_pairs={{0,16},{1,17},{2,18},{3,19},{4,20},{5,21},{6,22},{7,23},{8,24},{9,... | collective-permute-start | bytes 1671176 | tf_op jit(solution)/shard_map/ppermute | solution.py:52
  100.8 10.7 %collective-permute-start.33 = (bf16[4,17,16,256]{3,2,1,0:T(8,128)(2,1)S(1)}, bf16[4,17,16,256]{3,2,1,0:T(8,128)(2,1)S(1)}, u32[]{:S(2)}, u32[]{:S(2)}) collective-permute-start(bf16[4,17,16,256]{3,2,1,0:T(8,128)(2,1)S(1)} %get-tuple-element.42), channel_id=1, source_target_pairs={{0,48},{1,49},{2,50},{3,51},{4,52},{5,53},{6,54},{7,55},{8,56},{9,... | collective-permute-start | bytes 1671176 | tf_op jit(solution)/shard_map/ppermute | solution.py:52
  105.3 12.3 %collective-permute-start.27 = (bf16[4,17,16,256]{3,2,1,0:T(8,128)(2,1)S(1)}, bf16[4,17,16,256]{3,2,1,0:T(8,128)(2,1)S(1)}, u32[]{:S(2)}, u32[]{:S(2)}) collective-permute-start(bf16[4,17,16,256]{3,2,1,0:T(8,128)(2,1)S(1)} %get-tuple-element.35), channel_id=1, source_target_pairs={{0,16},{1,17},{2,18},{3,19},{4,20},{5,21},{6,22},{7,23},{8,24},{9,... | collective-permute-start | bytes 1671176 | tf_op jit(solution)/shard_map/ppermute | solution.py:52
  105.4 12.2 %collective-permute-start.28 = (bf16[4,17,16,256]{3,2,1,0:T(8,128)(2,1)S(1)}, bf16[4,17,16,256]{3,2,1,0:T(8,128)(2,1)S(1)}, u32[]{:S(2)}, u32[]{:S(2)}) collective-permute-start(bf16[4,17,16,256]{3,2,1,0:T(8,128)(2,1)S(1)} %get-tuple-element.36), channel_id=1, source_target_pairs={{0,48},{1,49},{2,50},{3,51},{4,52},{5,53},{6,54},{7,55},{8,56},{9,... | collective-permute-start | bytes 1671176 | tf_op jit(solution)/shard_map/ppermute | solution.py:52
  118.6 8.2 %collective-permute-start.34 = (bf16[2,17,16,256]{3,2,1,0:T(8,128)(2,1)S(1)}, bf16[2,17,16,256]{3,2,1,0:T(8,128)(2,1)S(1)}, u32[]{:S(2)}, u32[]{:S(2)}) collective-permute-start(bf16[2,17,16,256]{3,2,1,0:T(8,128)(2,1)S(1)} %get-tuple-element.44), channel_id=1, source_target_pairs={{0,8},{1,9},{2,10},{3,11},{4,12},{5,13},{6,14},{7,15},{8,0},{9,1},... | collective-permute-start | bytes 835592 | tf_op jit(solution)/shard_map/ppermute | solution.py:52
  118.7 10.8 %collective-permute-start.35 = (bf16[2,17,16,256]{3,2,1,0:T(8,128)(2,1)S(1)}, bf16[2,17,16,256]{3,2,1,0:T(8,128)(2,1)S(1)}, u32[]{:S(2)}, u32[]{:S(2)}) collective-permute-start(bf16[2,17,16,256]{3,2,1,0:T(8,128)(2,1)S(1)} %get-tuple-element.45), channel_id=1, source_target_pairs={{0,4},{1,5},{2,6},{3,7},{4,8},{5,9},{6,10},{7,11},{8,12},{9,13},{1... | collective-permute-start | bytes 835592 | tf_op jit(solution)/shard_map/ppermute | solution.py:52
  119.5 9.9 %collective-permute-start.36 = (bf16[2,17,16,256]{3,2,1,0:T(8,128)(2,1)S(1)}, bf16[2,17,16,256]{3,2,1,0:T(8,128)(2,1)S(1)}, u32[]{:S(2)}, u32[]{:S(2)}) collective-permute-start(bf16[2,17,16,256]{3,2,1,0:T(8,128)(2,1)S(1)} %get-tuple-element.46), channel_id=1, source_target_pairs={{0,12},{1,13},{2,14},{3,15},{4,0},{5,1},{6,2},{7,3},{8,4},{9,5},{1... | collective-permute-start | bytes 835592 | tf_op jit(solution)/shard_map/ppermute | solution.py:52
  (9 other events, 7.3 us)

commit v3 on v2

--- a/solution.py
+++ b/solution.py
@@ -294,13 +294,12 @@
     over_groups(step)
 
 
-def kernel_sum(s_ref, low, low_a, low_b, high, high_a, high_b, *pieces):
+def kernel_sum(s_ref, own, a, b, *pieces):
     def step(g):
-        for p, (own, a, b) in enumerate(((low, low_a, low_b), (high, high_a, high_b))):
-            for k in range(4):
-                pieces[k][p, g] = (
-                    own[k, g].astype(F32) + a[k, g].astype(F32) + b[k, g].astype(F32)
-                ).astype(BF16)
+        for k in range(4):
+            pieces[k][g] = (
+                own[k, g].astype(F32) + a[k, g].astype(F32) + b[k, g].astype(F32)
+            ).astype(BF16)
 
     over_groups(step)
 
@@ -314,7 +313,7 @@
 
 
 UNROLL = 8
-SPANS = ((0, 0, 4), (1, 0, 4), (3, 0, 4), (2, 0, 2), (2, 2, 2))
+SPANS = tuple((b, 0, 4) for b in range(4))
 PIECES = len(SPANS)
 UP_AT, ACT_AT, PRE_AT, WIDE = D, 2 * D, 2 * D + R, 2 * D + 2 * R
 ACT = (ROWS, D)
@@ -360,9 +359,9 @@
     return grads, shift(after, send_first(1)), shift(before, send_first(-1))
 
 
-def scatter_second(scalars, low, high):
-    piece = array(2, 17, 16, 256)
-    own, *pieces = call(kernel_sum, scalars, [*low, *high], [piece] * 4, [])
+def scatter_second(scalars, parts):
+    piece = array(17, 16, 256)
+    own, *pieces = call(kernel_sum, scalars, parts, [piece] * 4, [])
     got = [shift(pieces[k - 1], send_second(k)) for k in (2, 1, 3)]
     return add_up(own, got)
 
@@ -390,20 +389,11 @@
         ],
         axis=1,
     )
-    near = []
-    for p in range(2):
-        near.append([block[p]] + [shift(block[p], send_first(-k)) for k in (1, 2, 3)])
+    near = [block] + [shift(block, send_first(-k)) for k in (1, 2, 3)]
     pairs = []
     for p in range(2):
-        row = jnp.stack(near[p])
-        after, before = shift(row, send_second(-1)), shift(row, send_second(1))
-        rows = [
-            row,
-            after,
-            before,
-            shift(after[:2], send_second(-1)),
-            shift(before[2:], send_second(1)),
-        ]
+        row = jnp.stack([v[p] for v in near])
+        rows = [row] + [shift(row, send_second(-k)) for k in (1, 2, 3)]
         pairs.append(rows + [shift(v, SWAP) for v in rows])
     x1, x2, win, wout, stats, pre = call(
         kernel_low_forward,
@@ -429,9 +419,11 @@
     got0 = shift(acts0[1], SWAP)
     first1 = scatter_first(scalars, acts1, got1)
     first0 = scatter_first(scalars, acts0, got0)
-    high = scatter_sides(scalars, *first1)
-    low = scatter_sides(scalars, *first0)
-    grads = scatter_second(scalars, low, high)
+    sides1 = scatter_sides(scalars, *first1)
+    sides0 = scatter_sides(scalars, *first0)
+    high = scatter_second(scalars, sides1)
+    low = scatter_second(scalars, sides0)
+    grads = jnp.stack([low, high])
     parts = jnp.concatenate(
         [
             grads[:, :8].reshape(2, 4, 32, 256),

time: 147 us -> 153 us (1.041)
  the two profiles are of different devices: /device:TPU:32 before, /device:TPU:4 now
where the time goes in v3:
time: 153 us
  waiting for transfers between devices  49.4 us (32%)
  starting transfers between devices  34.8 us (23%)
  blocking collectives  33.8 us (22%)
  Pallas kernels  19.8 us (13%)
  local copies, waits for them, and re-layouts  12.8 us (8%)
    ppermute x33, waiting for transfers between devices, shift(): return lax.ppermute(value, AXES, pairs)  49.4 us
    ppermute x33, starting transfers between devices, shift(): return lax.ppermute(value, AXES, pairs)  34.8 us
    all_to_all x1, blocking collectives, device_body(): lax.all_to_all(jnp.broadcast_to(shard[None], (8, 72, 256)), ('zl', 'zh'),...  20.7 us
    pallas_call x9, Pallas kernels, call(): pl.pallas_call(body, in_specs=[pl.BlockSpec(memory_space=pltpu.SMEM)] + [...  19.8 us
    all_to_all x1, blocking collectives, device_body(): lax.all_to_all(parts, ('zl', 'zh'), 0, 0).astype(F32)  13.1 us
    unnamed x26, local copies, waits for them, and re-layouts  10.3 us
  transfers between devices with their start and end apart: 33, of which 16 were waited for; matrix products, arithmetic and copies ran while one was open for 0% of the time, Pallas kernels for 6%

profile of v3, /device:TPU:4, one launch (start us, length us, event | category | flops | bytes accessed | tf_op | source)
XLA Modules:
  0.0 152.8 jit_solution(17363887557801753973)
XLA Ops:
  1.4 0.7 fusion.7
  2.1 20.7 %all_to_all.10 = bf16[8,72,256]{2,1,0:T(8,128)(2,1)S(1)} all-to-all(bf16[8,72,256]{2,1,0:T(8,128)(2,1)S(1)} %broadcast_in_dim.4), channel_id=1, replica_groups=mesh['zl'=2,'c'=2,'x'=4,'y'=4,'zh'=4] {'zl','zh'}, dimensions={0} | all-to-all | bytes 589824 | tf_op jit(solution)/shard_map/all_to_all | solution.py:380
  23.8 2.7 %collective-permute-start.1 = (bf16[2,17,16,256]{3,2,1,0:T(8,128)(2,1)S(1)}, bf16[2,17,16,256]{3,2,1,0:T(8,128)(2,1)S(1)}, u32[]{:S(2)}, u32[]{:S(2)}) collective-permute-start(bf16[2,17,16,256]{3,2,1,0:T(8,128)(2,1)S(1)} %fusion.1), channel_id=1, source_target_pairs={{0,32},{1,33},{2,34},{3,35},{4,36},{5,37},{6,38},{7,39},{8,40},{9,... | collective-permute-start | bytes 835592 | tf_op jit(solution)/shard_map/ppermute | solution.py:52
  26.6 3.2 %collective-permute-done = bf16[2,17,16,256]{3,2,1,0:T(8,128)(2,1)S(1)} collective-permute-done((bf16[2,17,16,256]{3,2,1,0:T(8,128)(2,1)S(1)}, bf16[2,17,16,256]{3,2,1,0:T(8,128)(2,1)S(1)}, u32[]{:S(2)}, u32[]{:S(2)}) %collective-permute-start) | collective-permute-done | bytes 278560 | tf_op jit(solution)/shard_map/ppermute | solution.py:52
  29.9 2.1 %collective-permute-done.1 = bf16[2,17,16,256]{3,2,1,0:T(8,128)(2,1)S(1)} collective-permute-done((bf16[2,17,16,256]{3,2,1,0:T(8,128)(2,1)S(1)}, bf16[2,17,16,256]{3,2,1,0:T(8,128)(2,1)S(1)}, u32[]{:S(2)}, u32[]{:S(2)}) %collective-permute-start.1) | collective-permute-done | bytes 278560 | tf_op jit(solution)/shard_map/ppermute | solution.py:52
  32.0 2.9 %collective-permute-done.2 = bf16[2,17,16,256]{3,2,1,0:T(8,128)(2,1)S(1)} collective-permute-done((bf16[2,17,16,256]{3,2,1,0:T(8,128)(2,1)S(1)}, bf16[2,17,16,256]{3,2,1,0:T(8,128)(2,1)S(1)}, u32[]{:S(2)}, u32[]{:S(2)}) %collective-permute-start.2) | collective-permute-done | bytes 278560 | tf_op jit(solution)/shard_map/ppermute | solution.py:52
  35.0 3.1 %collective-permute-start.3 = (bf16[4,17,16,256]{3,2,1,0:T(8,128)(2,1)S(1)}, bf16[4,17,16,256]{3,2,1,0:T(8,128)(2,1)S(1)}, u32[]{:S(2)}, u32[]{:S(2)}) collective-permute-start(bf16[4,17,16,256]{3,2,1,0:T(8,128)(2,1)S(1)} %pad_maximum_fusion.refs_0_), channel_id=1, source_target_pairs={{0,12},{1,13},{2,14},{3,15},{4,0},{5,1},{6,2},{7,3},{8,4},{9,5},{1... | collective-permute-start | bytes 1671176 | tf_op jit(solution)/shard_map/ppermute | solution.py:52
  38.7 1.0 collective-permute-start.5
  39.8 2.3 %collective-permute-start.10 = (bf16[4,17,16,256]{3,2,1,0:T(8,128)(2,1)S(1)}, bf16[4,17,16,256]{3,2,1,0:T(8,128)(2,1)}, u32[]{:S(2)}, u32[]{:S(2)}) collective-permute-start(bf16[4,17,16,256]{3,2,1,0:T(8,128)(2,1)S(1)} %pad_maximum_fusion.1.refs_0_), channel_id=1, source_target_pairs={{0,12},{1,13},{2,14},{3,15},{4,0},{5,1},{6,2},{7,3},{8,4},{9,5},{1... | collective-permute-start | bytes 1671176 | tf_op jit(solution)/shard_map/ppermute | solution.py:52
  42.1 9.0 %collective-permute-done.3.refs_1_ = bf16[4,17,16,256]{3,2,1,0:T(8,128)(2,1)S(1)} collective-permute-done((bf16[4,17,16,256]{3,2,1,0:T(8,128)(2,1)S(1)}, bf16[4,17,16,256]{3,2,1,0:T(8,128)(2,1)S(1)}, u32[]{:S(2)}, u32[]{:S(2)}) %collective-permute-start.3) | collective-permute-done | bytes 557088 | tf_op jit(solution)/shard_map/ppermute | solution.py:52
  51.1 4.5 %collective-permute-start.12 = (bf16[4,17,16,256]{3,2,1,0:T(8,128)(2,1)S(1)}, bf16[4,17,16,256]{3,2,1,0:T(8,128)(2,1)}, u32[]{:S(2)}, u32[]{:S(2)}) collective-permute-start(bf16[4,17,16,256]{3,2,1,0:T(8,128)(2,1)S(1)} %pad_maximum_fusion.1.refs_0_), channel_id=1, source_target_pairs={{0,4},{1,5},{2,6},{3,7},{4,8},{5,9},{6,10},{7,11},{8,12},{9,13},{1... | collective-permute-start | bytes 1671176 | tf_op jit(solution)/shard_map/ppermute | solution.py:52
  55.7 0.8 copy-done.2
  56.5 0.8 copy-done.6
  57.8 0.8 copy-done.4
  58.6 4.5 %collective-permute-done.10.refs_1_ = bf16[4,17,16,256]{3,2,1,0:T(8,128)(2,1)} collective-permute-done((bf16[4,17,16,256]{3,2,1,0:T(8,128)(2,1)S(1)}, bf16[4,17,16,256]{3,2,1,0:T(8,128)(2,1)}, u32[]{:S(2)}, u32[]{:S(2)}) %collective-permute-start.10) | collective-permute-done | bytes 557088 | tf_op jit(solution)/shard_map/ppermute | solution.py:52
  63.6 4.6 %collective-permute-done.12.refs_3_ = bf16[4,17,16,256]{3,2,1,0:T(8,128)(2,1)} collective-permute-done((bf16[4,17,16,256]{3,2,1,0:T(8,128)(2,1)S(1)}, bf16[4,17,16,256]{3,2,1,0:T(8,128)(2,1)}, u32[]{:S(2)}, u32[]{:S(2)}) %collective-permute-start.12) | collective-permute-done | bytes 557088 | tf_op jit(solution)/shard_map/ppermute | solution.py:52
  68.2 0.8 copy-done.8
  69.5 0.8 copy-done.10
  70.5 1.2 copy-done.3
  71.7 1.1 copy-done.5
  72.7 1.1 copy-done.7
  73.8 1.1 copy-done.9
  74.8 1.1 copy-done.11
  75.9 3.9 %shard_map.76 = (bf16[128,2048]{1,0:T(8,128)(2,1)S(1)}, bf16[128,2048]{1,0:T(8,128)(2,1)S(1)}, bf16[2,128,16,256]{3,2,1,0:T(8,128)(2,1)S(1)}, bf16[2,9,16,16,256...) custom-call(s32[4]{0:T(128)S(1)} %pad_add_fusion.s_ref, ...), custom_call_target="tpu_custom_call" | custom-call | tf_op jit(solution)/shard_map/pallas_call | solution.py:334
  79.8 6.8 %shard_map.77 = (bf16[128,2048]{1,0:T(8,128)(2,1)S(1)}, bf16[2,144,4608]{2,1,0:T(8,128)(2,1)S(1)}) custom-call(s32[4]{0:T(128)S(1)} %pad_add_fusion.s_ref, bf16[128,2048]{1,0:T(8,128)(2,1)S(1)} %get-tuple-element.30.x2, bf16[2,2,128,2048]{3,2,1,0:T(8,128)(2,1)S(1)} %copy-done.1, bf16[4,17,16,256]{3,2,1,0:T(8,128)(2,1)S(1)} %pad_maximum_fusion.1.refs_0_, ...), custom_call_target="tpu_custom_call" | custom-call | tf_op jit(solution)/shard_map/pallas_call | solution.py:334
  86.6 3.4 %shard_map.78.acts = bf16[2,144,4608]{2,1,0:T(8,128)(2,1)S(1)} custom-call(s32[4]{0:T(128)S(1)} %pad_add_fusion.s_ref, bf16[2,2,128,2048]{3,2,1,0:T(8,128)(2,1)S(1)} %copy-done, bf16[128,2048]{1,0:T(8,128)(2,1)S(1)} %get-tuple-element.29.x1, bf16[128,2048]{1,0:T(8,128)(2,1)S(1)} %get-tuple-element.31.up2, ...), custom_call_target="tpu_custom_call" | custom-call | tf_op jit(solution)/shard_map/pallas_call | solution.py:334
  90.8 2.5 %collective-permute-done.17.got = bf16[144,4608]{1,0:T(8,128)(2,1)S(1)} collective-permute-done((bf16[144,4608]{1,0:T(8,128)(2,1)S(1)}, bf16[144,4608]{1,0:T(8,128)(2,1)S(1)}, u32[]{:S(2)}, u32[]{:S(2)}) %collective-permute-start.17) | collective-permute-done | bytes 1327136 | tf_op jit(solution)/shard_map/ppermute | solution.py:52
  93.3 1.3 shard_map.79
  94.7 1.3 collective-permute-start.18
  96.0 0.8 collective-permute-start.19
  96.8 1.3 shard_map.82
  98.1 2.0 %collective-permute-start.26 = (bf16[2,17,16,256]{3,2,1,0:T(8,128)(2,1)S(1)}, bf16[2,17,16,256]{3,2,1,0:T(8,128)(2,1)S(1)}, u32[]{:S(2)}, u32[]{:S(2)}) collective-permute-start(bf16[2,17,16,256]{3,2,1,0:T(8,128)(2,1)S(1)} %get-tuple-element.47), channel_id=1, source_target_pairs={{0,16},{1,17},{2,18},{3,19},{4,20},{5,21},{6,22},{7,23},{8,24},{9,... | collective-permute-start | bytes 835592 | tf_op jit(solution)/shard_map/ppermute | solution.py:52
  100.2 1.1 collective-permute-done.18.up
  101.3 1.9 %collective-permute-done.19.down = bf16[2,17,16,256]{3,2,1,0:T(8,128)(2,1)S(1)} collective-permute-done((bf16[2,17,16,256]{3,2,1,0:T(8,128)(2,1)S(1)}, bf16[2,17,16,256]{3,2,1,0:T(8,128)(2,1)S(1)}, u32[]{:S(2)}, u32[]{:S(2)}) %collective-permute-start.19) | collective-permute-done | bytes 278560 | tf_op jit(solution)/shard_map/ppermute | solution.py:52
  103.9 3.3 %collective-permute-start.20 = (bf16[4,17,16,256]{3,2,1,0:T(8,128)(2,1)S(1)}, bf16[4,17,16,256]{3,2,1,0:T(8,128)(2,1)S(1)}, u32[]{:S(2)}, u32[]{:S(2)}) collective-permute-start(bf16[4,17,16,256]{3,2,1,0:T(8,128)(2,1)S(1)} %get-tuple-element.39), channel_id=1, source_target_pairs={{0,16},{1,17},{2,18},{3,19},{4,20},{5,21},{6,22},{7,23},{8,24},{9,... | collective-permute-start | bytes 1671176 | tf_op jit(solution)/shard_map/ppermute | solution.py:52
  108.6 3.3 %collective-permute-start.28 = (bf16[4,17,16,256]{3,2,1,0:T(8,128)(2,1)S(1)}, bf16[4,17,16,256]{3,2,1,0:T(8,128)(2,1)S(1)}, u32[]{:S(2)}, u32[]{:S(2)}) collective-permute-start(bf16[4,17,16,256]{3,2,1,0:T(8,128)(2,1)S(1)} %get-tuple-element.49), channel_id=1, source_target_pairs={{0,16},{1,17},{2,18},{3,19},{4,20},{5,21},{6,22},{7,23},{8,24},{9,... | collective-permute-start | bytes 1671176 | tf_op jit(solution)/shard_map/ppermute | solution.py:52
  111.9 2.4 %collective-permute-done.20.a = bf16[4,17,16,256]{3,2,1,0:T(8,128)(2,1)S(1)} collective-permute-done((bf16[4,17,16,256]{3,2,1,0:T(8,128)(2,1)S(1)}, bf16[4,17,16,256]{3,2,1,0:T(8,128)(2,1)S(1)}, u32[]{:S(2)}, u32[]{:S(2)}) %collective-permute-start.20) | collective-permute-done | bytes 557088 | tf_op jit(solution)/shard_map/ppermute | solution.py:52
  114.3 2.8 %collective-permute-done.21.b = bf16[4,17,16,256]{3,2,1,0:T(8,128)(2,1)S(1)} collective-permute-done((bf16[4,17,16,256]{3,2,1,0:T(8,128)(2,1)S(1)}, bf16[4,17,16,256]{3,2,1,0:T(8,128)(2,1)S(1)}, u32[]{:S(2)}, u32[]{:S(2)}) %collective-permute-start.21) | collective-permute-done | bytes 557088 | tf_op jit(solution)/shard_map/ppermute | solution.py:52
  117.1 0.8 shard_map.81
  118.0 1.2 collective-permute-start.23
  119.2 2.2 %collective-permute-start.24 = (bf16[17,16,256]{2,1,0:T(8,128)(2,1)S(1)}, bf16[17,16,256]{2,1,0:T(8,128)(2,1)S(1)}, u32[]{:S(2)}, u32[]{:S(2)}) collective-permute-start(bf16[17,16,256]{2,1,0:T(8,128)(2,1)S(1)} %get-tuple-element.44), channel_id=1, source_target_pairs={{0,12},{1,13},{2,14},{3,15},{4,0},{5,1},{6,2},{7,3},{8,4},{9,5},{1... | collective-permute-start | bytes 417800 | tf_op jit(solution)/shard_map/ppermute | solution.py:52
  121.3 1.9 %collective-permute-done.28.a = bf16[4,17,16,256]{3,2,1,0:T(8,128)(2,1)S(1)} collective-permute-done((bf16[4,17,16,256]{3,2,1,0:T(8,128)(2,1)S(1)}, bf16[4,17,16,256]{3,2,1,0:T(8,128)(2,1)S(1)}, u32[]{:S(2)}, u32[]{:S(2)}) %collective-permute-start.28) | collective-permute-done | bytes 557088 | tf_op jit(solution)/shard_map/ppermute | solution.py:52
  123.2 5.5 %collective-permute-done.29.b = bf16[4,17,16,256]{3,2,1,0:T(8,128)(2,1)S(1)} collective-permute-done((bf16[4,17,16,256]{3,2,1,0:T(8,128)(2,1)S(1)}, bf16[4,17,16,256]{3,2,1,0:T(8,128)(2,1)S(1)}, u32[]{:S(2)}, u32[]{:S(2)}) %collective-permute-start.29) | collective-permute-done | bytes 557088 | tf_op jit(solution)/shard_map/ppermute | solution.py:52
  128.7 0.8 shard_map.84
  129.7 3.2 %collective-permute-start.32 = (bf16[17,16,256]{2,1,0:T(8,128)(2,1)S(1)}, bf16[17,16,256]{2,1,0:T(8,128)(2,1)S(1)}, u32[]{:S(2)}, u32[]{:S(2)}) collective-permute-start(bf16[17,16,256]{2,1,0:T(8,128)(2,1)S(1)} %get-tuple-element.54), channel_id=1, source_target_pairs={{0,12},{1,13},{2,14},{3,15},{4,0},{5,1},{6,2},{7,3},{8,4},{9,5},{1... | collective-permute-start | bytes 417800 | tf_op jit(solution)/shard_map/ppermute | solution.py:52
  133.1 3.2 %collective-permute-done.30 = bf16[17,16,256]{2,1,0:T(8,128)(2,1)S(1)} collective-permute-done((bf16[17,16,256]{2,1,0:T(8,128)(2,1)S(1)}, bf16[17,16,256]{2,1,0:T(8,128)(2,1)S(1)}, u32[]{:S(2)}, u32[]{:S(2)}) %collective-permute-start.30) | collective-permute-done | bytes 139296 | tf_op jit(solution)/shard_map/ppermute | solution.py:52
  136.3 1.2 collective-permute-done.31
  137.9 13.1 %all_to_all.11 = bf16[8,72,256]{2,1,0:T(8,128)(2,1)S(1)} all-to-all(bf16[8,72,256]{2,1,0:T(8,128)(2,1)S(1)} %pad_maximum_fusion.2), channel_id=1, replica_groups=mesh['zl'=2,'c'=2,'x'=4,'y'=4,'zh'=4] {'zl','zh'}, dimensions={0} | all-to-all | bytes 589824 | tf_op jit(solution)/shard_map/all_to_all | solution.py:435
  (90 shorter events, 9.9 us)
Async XLA Ops:
  23.2 6.6 %collective-permute-start = (bf16[2,17,16,256]{3,2,1,0:T(8,128)(2,1)S(1)}, bf16[2,17,16,256]{3,2,1,0:T(8,128)(2,1)S(1)}, u32[]{:S(2)}, u32[]{:S(2)}) collective-permute-start(bf16[2,17,16,256]{3,2,1,0:T(8,128)(2,1)S(1)} %fusion.1), channel_id=1, source_target_pairs={{0,48},{1,49},{2,50},{3,51},{4,52},{5,53},{6,54},{7,55},{8,56},{9,... | collective-permute-start | bytes 835592 | tf_op jit(solution)/shard_map/ppermute | solution.py:52
  23.8 8.2 %collective-permute-start.1 = (bf16[2,17,16,256]{3,2,1,0:T(8,128)(2,1)S(1)}, bf16[2,17,16,256]{3,2,1,0:T(8,128)(2,1)S(1)}, u32[]{:S(2)}, u32[]{:S(2)}) collective-permute-start(bf16[2,17,16,256]{3,2,1,0:T(8,128)(2,1)S(1)} %fusion.1), channel_id=1, source_target_pairs={{0,32},{1,33},{2,34},{3,35},{4,36},{5,37},{6,38},{7,39},{8,40},{9,... | collective-permute-start | bytes 835592 | tf_op jit(solution)/shard_map/ppermute | solution.py:52
  26.6 8.3 %collective-permute-start.2 = (bf16[2,17,16,256]{3,2,1,0:T(8,128)(2,1)S(1)}, bf16[2,17,16,256]{3,2,1,0:T(8,128)(2,1)S(1)}, u32[]{:S(2)}, u32[]{:S(2)}) collective-permute-start(bf16[2,17,16,256]{3,2,1,0:T(8,128)(2,1)S(1)} %fusion.1), channel_id=1, source_target_pairs={{0,16},{1,17},{2,18},{3,19},{4,20},{5,21},{6,22},{7,23},{8,24},{9,... | collective-permute-start | bytes 835592 | tf_op jit(solution)/shard_map/ppermute | solution.py:52
  26.6 43.9 %copy-start = (bf16[2,2,128,2048]{3,2,1,0:T(8,128)(2,1)S(1)}, bf16[2,2,128,2048]{3,2,1,0:T(8,128)(2,1)}, u32[]{:S(2)}) copy-start(bf16[2,2,128,2048]{3,2,1,0:T(8,128)(2,1)} %xs.3) | copy-start | bytes 6291460
  35.0 16.1 %collective-permute-start.3 = (bf16[4,17,16,256]{3,2,1,0:T(8,128)(2,1)S(1)}, bf16[4,17,16,256]{3,2,1,0:T(8,128)(2,1)S(1)}, u32[]{:S(2)}, u32[]{:S(2)}) collective-permute-start(bf16[4,17,16,256]{3,2,1,0:T(8,128)(2,1)S(1)} %pad_maximum_fusion.refs_0_), channel_id=1, source_target_pairs={{0,12},{1,13},{2,14},{3,15},{4,0},{5,1},{6,2},{7,3},{8,4},{9,5},{1... | collective-permute-start | bytes 1671176 | tf_op jit(solution)/shard_map/ppermute | solution.py:52
  38.1 13.0 %collective-permute-start.4 = (bf16[4,17,16,256]{3,2,1,0:T(8,128)(2,1)S(1)}, bf16[4,17,16,256]{3,2,1,0:T(8,128)(2,1)S(1)}, u32[]{:S(2)}, u32[]{:S(2)}) collective-permute-start(bf16[4,17,16,256]{3,2,1,0:T(8,128)(2,1)S(1)} %pad_maximum_fusion.refs_0_), channel_id=1, source_target_pairs={{0,8},{1,9},{2,10},{3,11},{4,12},{5,13},{6,14},{7,15},{8,0},{9,1},... | collective-permute-start | bytes 1671176 | tf_op jit(solution)/shard_map/ppermute | solution.py:52
  38.7 16.9 %collective-permute-start.5 = (bf16[4,17,16,256]{3,2,1,0:T(8,128)(2,1)S(1)}, bf16[4,17,16,256]{3,2,1,0:T(8,128)(2,1)}, u32[]{:S(2)}, u32[]{:S(2)}) collective-permute-start(bf16[4,17,16,256]{3,2,1,0:T(8,128)(2,1)S(1)} %pad_maximum_fusion.refs_0_), channel_id=1, source_target_pairs={{0,4},{1,5},{2,6},{3,7},{4,8},{5,9},{6,10},{7,11},{8,12},{9,13},{1... | collective-permute-start | bytes 1671176 | tf_op jit(solution)/shard_map/ppermute | solution.py:52
  39.7 16.8 %collective-permute-start.6 = (bf16[4,17,16,256]{3,2,1,0:T(8,128)(2,1)S(1)}, bf16[4,17,16,256]{3,2,1,0:T(8,128)(2,1)S(1)}, u32[]{:S(2)}, u32[]{:S(2)}) collective-permute-start(bf16[4,17,16,256]{3,2,1,0:T(8,128)(2,1)S(1)} %pad_maximum_fusion.refs_0_), channel_id=1, source_target_pairs={{0,64},{1,65},{2,66},{3,67},{4,68},{5,69},{6,70},{7,71},{8,72},{9,... | collective-permute-start | bytes 1671176 | tf_op jit(solution)/shard_map/ppermute | solution.py:52
  39.8 23.3 %collective-permute-start.10 = (bf16[4,17,16,256]{3,2,1,0:T(8,128)(2,1)S(1)}, bf16[4,17,16,256]{3,2,1,0:T(8,128)(2,1)}, u32[]{:S(2)}, u32[]{:S(2)}) collective-permute-start(bf16[4,17,16,256]{3,2,1,0:T(8,128)(2,1)S(1)} %pad_maximum_fusion.1.refs_0_), channel_id=1, source_target_pairs={{0,12},{1,13},{2,14},{3,15},{4,0},{5,1},{6,2},{7,3},{8,4},{9,5},{1... | collective-permute-start | bytes 1671176 | tf_op jit(solution)/shard_map/ppermute | solution.py:52
  51.1 12.0 %collective-permute-start.11 = (bf16[4,17,16,256]{3,2,1,0:T(8,128)(2,1)S(1)}, bf16[4,17,16,256]{3,2,1,0:T(8,128)(2,1)}, u32[]{:S(2)}, u32[]{:S(2)}) collective-permute-start(bf16[4,17,16,256]{3,2,1,0:T(8,128)(2,1)S(1)} %pad_maximum_fusion.1.refs_0_), channel_id=1, source_target_pairs={{0,8},{1,9},{2,10},{3,11},{4,12},{5,13},{6,14},{7,15},{8,0},{9,1},... | collective-permute-start | bytes 1671176 | tf_op jit(solution)/shard_map/ppermute | solution.py:52
  51.1 17.1 %collective-permute-start.12 = (bf16[4,17,16,256]{3,2,1,0:T(8,128)(2,1)S(1)}, bf16[4,17,16,256]{3,2,1,0:T(8,128)(2,1)}, u32[]{:S(2)}, u32[]{:S(2)}) collective-permute-start(bf16[4,17,16,256]{3,2,1,0:T(8,128)(2,1)S(1)} %pad_maximum_fusion.1.refs_0_), channel_id=1, source_target_pairs={{0,4},{1,5},{2,6},{3,7},{4,8},{5,9},{6,10},{7,11},{8,12},{9,13},{1... | collective-permute-start | bytes 1671176 | tf_op jit(solution)/shard_map/ppermute | solution.py:52
  55.7 12.6 %collective-permute-start.7 = (bf16[4,17,16,256]{3,2,1,0:T(8,128)(2,1)S(1)}, bf16[4,17,16,256]{3,2,1,0:T(8,128)(2,1)S(1)}, u32[]{:S(2)}, u32[]{:S(2)}) collective-permute-start(bf16[4,17,16,256]{3,2,1,0:T(8,128)(2,1)S(1)} %collective-permute-done.3.refs_1_), channel_id=1, source_target_pairs={{0,64},{1,65},{2,66},{3,67},{4,68},{5,69},{6,70},{7,71},{8,72},{9,... | collective-permute-start | bytes 1671176 | tf_op jit(solution)/shard_map/ppermute | solution.py:52
  55.7 0.8 copy-start.2
  56.5 0.8 copy-start.6
  57.3 12.2 %collective-permute-start.8 = (bf16[4,17,16,256]{3,2,1,0:T(8,128)(2,1)S(1)}, bf16[4,17,16,256]{3,2,1,0:T(8,128)(2,1)S(1)}, u32[]{:S(2)}, u32[]{:S(2)}) collective-permute-start(bf16[4,17,16,256]{3,2,1,0:T(8,128)(2,1)S(1)} %collective-permute-done.4.refs_2_), channel_id=1, source_target_pairs={{0,64},{1,65},{2,66},{3,67},{4,68},{5,69},{6,70},{7,71},{8,72},{9,... | collective-permute-start | bytes 1671176 | tf_op jit(solution)/shard_map/ppermute | solution.py:52
  57.8 0.8 copy-start.4
  63.1 16.7 %collective-permute-start.13 = (bf16[4,17,16,256]{3,2,1,0:T(8,128)(2,1)S(1)}, bf16[4,17,16,256]{3,2,1,0:T(8,128)(2,1)}, u32[]{:S(2)}, u32[]{:S(2)}) collective-permute-start(bf16[4,17,16,256]{3,2,1,0:T(8,128)(2,1)S(1)} %pad_maximum_fusion.1.refs_0_), channel_id=1, source_target_pairs={{0,64},{1,65},{2,66},{3,67},{4,68},{5,69},{6,70},{7,71},{8,72},{9,... | collective-permute-start | bytes 1671176 | tf_op jit(solution)/shard_map/ppermute | solution.py:52
  63.1 7.4 %collective-permute-start.9 = (bf16[4,17,16,256]{3,2,1,0:T(8,128)(2,1)}, bf16[4,17,16,256]{3,2,1,0:T(8,128)(2,1)}, u32[]{:S(2)}, u32[]{:S(2)}) collective-permute-start(bf16[4,17,16,256]{3,2,1,0:T(8,128)(2,1)} %collective-permute-done.5.refs_3_), channel_id=1, source_target_pairs={{0,64},{1,65},{2,66},{3,67},{4,68},{5,69},{6,70},{7,71},{8,72},{9,... | collective-permute-start | bytes 1671176 | tf_op jit(solution)/shard_map/ppermute | solution.py:52
  68.2 11.5 %collective-permute-start.14 = (bf16[4,17,16,256]{3,2,1,0:T(8,128)(2,1)}, bf16[4,17,16,256]{3,2,1,0:T(8,128)(2,1)}, u32[]{:S(2)}, u32[]{:S(2)}) collective-permute-start(bf16[4,17,16,256]{3,2,1,0:T(8,128)(2,1)} %collective-permute-done.10.refs_1_), channel_id=1, source_target_pairs={{0,64},{1,65},{2,66},{3,67},{4,68},{5,69},{6,70},{7,71},{8,72},{9,... | collective-permute-start | bytes 1671176 | tf_op jit(solution)/shard_map/ppermute | solution.py:52
  68.2 0.8 copy-start.8
  69.0 10.8 %collective-permute-start.15 = (bf16[4,17,16,256]{3,2,1,0:T(8,128)(2,1)}, bf16[4,17,16,256]{3,2,1,0:T(8,128)(2,1)}, u32[]{:S(2)}, u32[]{:S(2)}) collective-permute-start(bf16[4,17,16,256]{3,2,1,0:T(8,128)(2,1)} %collective-permute-done.11.refs_2_), channel_id=1, source_target_pairs={{0,64},{1,65},{2,66},{3,67},{4,68},{5,69},{6,70},{7,71},{8,72},{9,... | collective-permute-start | bytes 1671176 | tf_op jit(solution)/shard_map/ppermute | solution.py:52
  69.5 0.8 copy-start.10
  70.4 9.4 %collective-permute-start.16 = (bf16[4,17,16,256]{3,2,1,0:T(8,128)(2,1)}, bf16[4,17,16,256]{3,2,1,0:T(8,128)(2,1)}, u32[]{:S(2)}, u32[]{:S(2)}) collective-permute-start(bf16[4,17,16,256]{3,2,1,0:T(8,128)(2,1)} %collective-permute-done.12.refs_3_), channel_id=1, source_target_pairs={{0,64},{1,65},{2,66},{3,67},{4,68},{5,69},{6,70},{7,71},{8,72},{9,... | collective-permute-start | bytes 1671176 | tf_op jit(solution)/shard_map/ppermute | solution.py:52
  70.5 9.3 %copy-start.1 = (bf16[2,2,128,2048]{3,2,1,0:T(8,128)(2,1)S(1)}, bf16[2,2,128,2048]{3,2,1,0:T(8,128)(2,1)}, u32[]{:S(2)}) copy-start(bf16[2,2,128,2048]{3,2,1,0:T(8,128)(2,1)} %cots.1) | copy-start | bytes 6291460
  70.5 1.2 copy-start.3
  71.7 1.1 copy-start.5
  72.7 1.1 copy-start.7
  73.8 1.1 copy-start.9
  74.8 1.1 copy-start.11
  90.1 3.3 %collective-permute-start.17 = (bf16[144,4608]{1,0:T(8,128)(2,1)S(1)}, bf16[144,4608]{1,0:T(8,128)(2,1)S(1)}, u32[]{:S(2)}, u32[]{:S(2)}) collective-permute-start(bf16[144,4608]{1,0:T(8,128)(2,1)S(1)} %slice_bitcast_fusion), channel_id=1, source_target_pairs={{0,64},{1,65},{2,66},{3,67},{4,68},{5,69},{6,70},{7,71},{8,72},{9,... | collective-permute-start | bytes 3981320 | tf_op jit(solution)/shard_map/ppermute | solution.py:52
  90.7 6.0 %collective-permute-start.25 = (bf16[144,4608]{1,0:T(8,128)(2,1)S(1)}, bf16[144,4608]{1,0:T(8,128)(2,1)S(1)}, u32[]{:S(2)}, u32[]{:S(2)}) collective-permute-start(bf16[144,4608]{1,0:T(8,128)(2,1)S(1)} %slice_bitcast_fusion.1), channel_id=1, source_target_pairs={{0,64},{1,65},{2,66},{3,67},{4,68},{5,69},{6,70},{7,71},{8,72},{9,... | collective-permute-start | bytes 3981320 | tf_op jit(solution)/shard_map/ppermute | solution.py:52
  94.7 6.6 %collective-permute-start.18 = (bf16[2,17,16,256]{3,2,1,0:T(8,128)(2,1)S(1)}, bf16[2,17,16,256]{3,2,1,0:T(8,128)(2,1)S(1)}, u32[]{:S(2)}, u32[]{:S(2)}) collective-permute-start(bf16[2,17,16,256]{3,2,1,0:T(8,128)(2,1)S(1)} %get-tuple-element.37), channel_id=1, source_target_pairs={{0,16},{1,17},{2,18},{3,19},{4,20},{5,21},{6,22},{7,23},{8,24},{9,... | collective-permute-start | bytes 835592 | tf_op jit(solution)/shard_map/ppermute | solution.py:52
  96.0 7.2 %collective-permute-start.19 = (bf16[2,17,16,256]{3,2,1,0:T(8,128)(2,1)S(1)}, bf16[2,17,16,256]{3,2,1,0:T(8,128)(2,1)S(1)}, u32[]{:S(2)}, u32[]{:S(2)}) collective-permute-start(bf16[2,17,16,256]{3,2,1,0:T(8,128)(2,1)S(1)} %get-tuple-element.38), channel_id=1, source_target_pairs={{0,48},{1,49},{2,50},{3,51},{4,52},{5,53},{6,54},{7,55},{8,56},{9,... | collective-permute-start | bytes 835592 | tf_op jit(solution)/shard_map/ppermute | solution.py:52
  98.1 9.1 %collective-permute-start.26 = (bf16[2,17,16,256]{3,2,1,0:T(8,128)(2,1)S(1)}, bf16[2,17,16,256]{3,2,1,0:T(8,128)(2,1)S(1)}, u32[]{:S(2)}, u32[]{:S(2)}) collective-permute-start(bf16[2,17,16,256]{3,2,1,0:T(8,128)(2,1)S(1)} %get-tuple-element.47), channel_id=1, source_target_pairs={{0,16},{1,17},{2,18},{3,19},{4,20},{5,21},{6,22},{7,23},{8,24},{9,... | collective-permute-start | bytes 835592 | tf_op jit(solution)/shard_map/ppermute | solution.py:52
  100.1 7.8 %collective-permute-start.27 = (bf16[2,17,16,256]{3,2,1,0:T(8,128)(2,1)S(1)}, bf16[2,17,16,256]{3,2,1,0:T(8,128)(2,1)S(1)}, u32[]{:S(2)}, u32[]{:S(2)}) collective-permute-start(bf16[2,17,16,256]{3,2,1,0:T(8,128)(2,1)S(1)} %get-tuple-element.48), channel_id=1, source_target_pairs={{0,48},{1,49},{2,50},{3,51},{4,52},{5,53},{6,54},{7,55},{8,56},{9,... | collective-permute-start | bytes 835592 | tf_op jit(solution)/shard_map/ppermute | solution.py:52
  103.9 10.4 %collective-permute-start.20 = (bf16[4,17,16,256]{3,2,1,0:T(8,128)(2,1)S(1)}, bf16[4,17,16,256]{3,2,1,0:T(8,128)(2,1)S(1)}, u32[]{:S(2)}, u32[]{:S(2)}) collective-permute-start(bf16[4,17,16,256]{3,2,1,0:T(8,128)(2,1)S(1)} %get-tuple-element.39), channel_id=1, source_target_pairs={{0,16},{1,17},{2,18},{3,19},{4,20},{5,21},{6,22},{7,23},{8,24},{9,... | collective-permute-start | bytes 1671176 | tf_op jit(solution)/shard_map/ppermute | solution.py:52
  107.2 9.8 %collective-permute-start.21 = (bf16[4,17,16,256]{3,2,1,0:T(8,128)(2,1)S(1)}, bf16[4,17,16,256]{3,2,1,0:T(8,128)(2,1)S(1)}, u32[]{:S(2)}, u32[]{:S(2)}) collective-permute-start(bf16[4,17,16,256]{3,2,1,0:T(8,128)(2,1)S(1)} %get-tuple-element.40), channel_id=1, source_target_pairs={{0,48},{1,49},{2,50},{3,51},{4,52},{5,53},{6,54},{7,55},{8,56},{9,... | collective-permute-start | bytes 1671176 | tf_op jit(solution)/shard_map/ppermute | solution.py:52
  108.6 14.7 %collective-permute-start.28 = (bf16[4,17,16,256]{3,2,1,0:T(8,128)(2,1)S(1)}, bf16[4,17,16,256]{3,2,1,0:T(8,128)(2,1)S(1)}, u32[]{:S(2)}, u32[]{:S(2)}) collective-permute-start(bf16[4,17,16,256]{3,2,1,0:T(8,128)(2,1)S(1)} %get-tuple-element.49), channel_id=1, source_target_pairs={{0,16},{1,17},{2,18},{3,19},{4,20},{5,21},{6,22},{7,23},{8,24},{9,... | collective-permute-start | bytes 1671176 | tf_op jit(solution)/shard_map/ppermute | solution.py:52
  111.9 16.8 %collective-permute-start.29 = (bf16[4,17,16,256]{3,2,1,0:T(8,128)(2,1)S(1)}, bf16[4,17,16,256]{3,2,1,0:T(8,128)(2,1)S(1)}, u32[]{:S(2)}, u32[]{:S(2)}) collective-permute-start(bf16[4,17,16,256]{3,2,1,0:T(8,128)(2,1)S(1)} %get-tuple-element.50), channel_id=1, source_target_pairs={{0,48},{1,49},{2,50},{3,51},{4,52},{5,53},{6,54},{7,55},{8,56},{9,... | collective-permute-start | bytes 1671176 | tf_op jit(solution)/shard_map/ppermute | solution.py:52
  117.9 11.8 %collective-permute-start.22 = (bf16[17,16,256]{2,1,0:T(8,128)(2,1)S(1)}, bf16[17,16,256]{2,1,0:T(8,128)(2,1)S(1)}, u32[]{:S(2)}, u32[]{:S(2)}) collective-permute-start(bf16[17,16,256]{2,1,0:T(8,128)(2,1)S(1)} %get-tuple-element.42), channel_id=1, source_target_pairs={{0,8},{1,9},{2,10},{3,11},{4,12},{5,13},{6,14},{7,15},{8,0},{9,1},... | collective-permute-start | bytes 417800 | tf_op jit(solution)/shard_map/ppermute | solution.py:52
  118.0 15.0 %collective-permute-start.23 = (bf16[17,16,256]{2,1,0:T(8,128)(2,1)S(1)}, bf16[17,16,256]{2,1,0:T(8,128)(2,1)S(1)}, u32[]{:S(2)}, u32[]{:S(2)}) collective-permute-start(bf16[17,16,256]{2,1,0:T(8,128)(2,1)S(1)} %get-tuple-element.43), channel_id=1, source_target_pairs={{0,4},{1,5},{2,6},{3,7},{4,8},{5,9},{6,10},{7,11},{8,12},{9,13},{1... | collective-permute-start | bytes 417800 | tf_op jit(solution)/shard_map/ppermute | solution.py:52
  119.2 13.8 %collective-permute-start.24 = (bf16[17,16,256]{2,1,0:T(8,128)(2,1)S(1)}, bf16[17,16,256]{2,1,0:T(8,128)(2,1)S(1)}, u32[]{:S(2)}, u32[]{:S(2)}) collective-permute-start(bf16[17,16,256]{2,1,0:T(8,128)(2,1)S(1)} %get-tuple-element.44), channel_id=1, source_target_pairs={{0,12},{1,13},{2,14},{3,15},{4,0},{5,1},{6,2},{7,3},{8,4},{9,5},{1... | collective-permute-start | bytes 417800 | tf_op jit(solution)/shard_map/ppermute | solution.py:52
  129.5 6.7 %collective-permute-start.30 = (bf16[17,16,256]{2,1,0:T(8,128)(2,1)S(1)}, bf16[17,16,256]{2,1,0:T(8,128)(2,1)S(1)}, u32[]{:S(2)}, u32[]{:S(2)}) collective-permute-start(bf16[17,16,256]{2,1,0:T(8,128)(2,1)S(1)} %get-tuple-element.52), channel_id=1, source_target_pairs={{0,8},{1,9},{2,10},{3,11},{4,12},{5,13},{6,14},{7,15},{8,0},{9,1},... | collective-permute-start | bytes 417800 | tf_op jit(solution)/shard_map/ppermute | solution.py:52
  129.6 7.8 %collective-permute-start.31 = (bf16[17,16,256]{2,1,0:T(8,128)(2,1)S(1)}, bf16[17,16,256]{2,1,0:T(8,128)(2,1)S(1)}, u32[]{:S(2)}, u32[]{:S(2)}) collective-permute-start(bf16[17,16,256]{2,1,0:T(8,128)(2,1)S(1)} %get-tuple-element.53), channel_id=1, source_target_pairs={{0,4},{1,5},{2,6},{3,7},{4,8},{5,9},{6,10},{7,11},{8,12},{9,13},{1... | collective-permute-start | bytes 417800 | tf_op jit(solution)/shard_map/ppermute | solution.py:52
  129.7 7.7 %collective-permute-start.32 = (bf16[17,16,256]{2,1,0:T(8,128)(2,1)S(1)}, bf16[17,16,256]{2,1,0:T(8,128)(2,1)S(1)}, u32[]{:S(2)}, u32[]{:S(2)}) collective-permute-start(bf16[17,16,256]{2,1,0:T(8,128)(2,1)S(1)} %get-tuple-element.54), channel_id=1, source_target_pairs={{0,12},{1,13},{2,14},{3,15},{4,0},{5,1},{6,2},{7,3},{8,4},{9,5},{1... | collective-permute-start | bytes 417800 | tf_op jit(solution)/shard_map/ppermute | solution.py:52

commit v4 on v3

--- a/solution.py
+++ b/solution.py
@@ -302,6 +302,16 @@
             ).astype(BF16)
 
     over_groups(step)
+
+
+def kernel_finish(s_ref, parts, gain, grad_in, grad_out):
+    total = parts[0].astype(F32)
+    for i in range(1, 8):
+        total += parts[i].astype(F32)
+    grad_in[0] = total[0:32]
+    for k in range(8):
+        grad_out[0, :, pl.ds(k * 256, 256)] = total[32 + 4 * k : 36 + 4 * k]
+    gain[...] = total[64:65, 0:32]
 
 
 def vmem(*shape, kind=BF16):
@@ -389,10 +399,12 @@
         ],
         axis=1,
     )
-    near = [block] + [shift(block, send_first(-k)) for k in (1, 2, 3)]
+    near = []
+    for p in range(2):
+        near.append([block[p]] + [shift(block[p], send_first(-k)) for k in (1, 2, 3)])
     pairs = []
     for p in range(2):
-        row = jnp.stack([v[p] for v in near])
+        row = jnp.stack(near[p])
         rows = [row] + [shift(row, send_second(-k)) for k in (1, 2, 3)]
         pairs.append(rows + [shift(v, SWAP) for v in rows])
     x1, x2, win, wout, stats, pre = call(
@@ -432,10 +444,13 @@
         ],
         axis=2,
     ).reshape(8, 72, 256)
-    total = jnp.sum(lax.all_to_all(parts, ("zl", "zh"), 0, 0).astype(F32), axis=0)
-    grad_in = total[:32]
-    grad_out = total[32:64].reshape(8, 4, 256).transpose(1, 0, 2).reshape(4, 2048)
-    return (total[64:65, :32], grad_in[None], grad_out[None])
+    return call(
+        kernel_finish,
+        scalars,
+        [lax.all_to_all(parts, ("zl", "zh"), 0, 0)],
+        (array(1, 32, kind=F32), array(1, 32, 256, kind=F32), array(1, 4, 2048, kind=F32)),
+        [],
+    )
 
 
 def solution(mesh):

time: 153 us -> 162 us (1.059)
  the two profiles are of different devices: /device:TPU:4 before, /device:TPU:32 now
where the time goes in v4:
time: 162 us; the launch traced here: 158 us
  waiting for transfers between devices  56.8 us (35%)
  starting transfers between devices  35.6 us (22%)
  blocking collectives  31.9 us (20%)
  Pallas kernels  21 us (13%)
  local copies, waits for them, and re-layouts  11 us (7%)
    ppermute x36, waiting for transfers between devices, shift(): return lax.ppermute(value, AXES, pairs)  56.8 us
    ppermute x36, starting transfers between devices, shift(): return lax.ppermute(value, AXES, pairs)  35.6 us
    pallas_call x10, Pallas kernels, call(): pl.pallas_call(body, in_specs=[pl.BlockSpec(memory_space=pltpu.SMEM)] + [...  21 us
    all_to_all x1, blocking collectives, device_body(): lax.all_to_all(jnp.broadcast_to(shard[None], (8, 72, 256)), ('zl', 'zh'),...  19.5 us
    all_to_all x1, blocking collectives, device_body(): lax.all_to_all(parts, ('zl', 'zh'), 0, 0)  12.4 us
    unnamed x26, local copies, waits for them, and re-layouts  10.3 us
  transfers between devices with their start and end apart: 36, of which 16 were waited for; matrix products, arithmetic and copies ran while one was open for 0% of the time, Pallas kernels for 6%

profile of v4, /device:TPU:32, one launch (start us, length us, event | category | flops | bytes accessed | tf_op | source)
XLA Modules:
  0.0 158.4 jit_solution(11213164344186591288)
XLA Ops:
  2.1 19.5 %all_to_all.10 = bf16[8,72,256]{2,1,0:T(8,128)(2,1)S(1)} all-to-all(bf16[8,72,256]{2,1,0:T(8,128)(2,1)S(1)} %broadcast_in_dim.2), channel_id=1, replica_groups=mesh['zl'=2,'c'=2,'x'=4,'y'=4,'zh'=4] {'zl','zh'}, dimensions={0} | all-to-all | bytes 589824 | tf_op jit(solution)/shard_map/all_to_all | solution.py:390
  22.1 2.8 %collective-permute-start = (bf16[17,16,256]{2,1,0:T(8,128)(2,1)S(1)}, bf16[17,16,256]{2,1,0:T(8,128)(2,1)S(1)}, u32[]{:S(2)}, u32[]{:S(2)}) collective-permute-start(bf16[17,16,256]{2,1,0:T(8,128)(2,1)S(1)} %get-tuple-element.60), channel_id=1, source_target_pairs={{0,48},{1,49},{2,50},{3,51},{4,52},{5,53},{6,54},{7,55},{8,56},{9,... | collective-permute-start | bytes 417800 | tf_op jit(solution)/shard_map/ppermute | solution.py:52
  24.9 0.8 collective-permute-start.1
  25.7 0.9 collective-permute-start.2
  26.6 2.4 %collective-permute-done = bf16[17,16,256]{2,1,0:T(8,128)(2,1)S(1)} collective-permute-done((bf16[17,16,256]{2,1,0:T(8,128)(2,1)S(1)}, bf16[17,16,256]{2,1,0:T(8,128)(2,1)S(1)}, u32[]{:S(2)}, u32[]{:S(2)}) %collective-permute-start) | collective-permute-done | bytes 139296 | tf_op jit(solution)/shard_map/ppermute | solution.py:52
  29.0 2.6 %collective-permute-done.1 = bf16[17,16,256]{2,1,0:T(8,128)(2,1)S(1)} collective-permute-done((bf16[17,16,256]{2,1,0:T(8,128)(2,1)S(1)}, bf16[17,16,256]{2,1,0:T(8,128)(2,1)S(1)}, u32[]{:S(2)}, u32[]{:S(2)}) %collective-permute-start.1) | collective-permute-done | bytes 139296 | tf_op jit(solution)/shard_map/ppermute | solution.py:52
  31.6 1.4 collective-permute-done.2
  33.0 3.1 %collective-permute-start.3 = (bf16[4,17,16,256]{3,2,1,0:T(8,128)(2,1)S(1)}, bf16[4,17,16,256]{3,2,1,0:T(8,128)(2,1)S(1)}, u32[]{:S(2)}, u32[]{:S(2)}) collective-permute-start(bf16[4,17,16,256]{3,2,1,0:T(8,128)(2,1)S(1)} %pad_maximum_fusion.refs_0_), channel_id=1, source_target_pairs={{0,12},{1,13},{2,14},{3,15},{4,0},{5,1},{6,2},{7,3},{8,4},{9,5},{1... | collective-permute-start | bytes 1671176 | tf_op jit(solution)/shard_map/ppermute | solution.py:52
  36.8 1.0 collective-permute-start.5
  38.3 9.5 %collective-permute-done.10 = bf16[17,16,256]{2,1,0:T(8,128)(2,1)S(1)} collective-permute-done((bf16[17,16,256]{2,1,0:T(8,128)(2,1)S(1)}, bf16[17,16,256]{2,1,0:T(8,128)(2,1)S(1)}, u32[]{:S(2)}, u32[]{:S(2)}) %collective-permute-start.10) | collective-permute-done | bytes 139296 | tf_op jit(solution)/shard_map/ppermute | solution.py:52
  47.8 6.6 %collective-permute-done.11 = bf16[17,16,256]{2,1,0:T(8,128)(2,1)S(1)} collective-permute-done((bf16[17,16,256]{2,1,0:T(8,128)(2,1)S(1)}, bf16[17,16,256]{2,1,0:T(8,128)(2,1)S(1)}, u32[]{:S(2)}, u32[]{:S(2)}) %collective-permute-start.11) | collective-permute-done | bytes 139296 | tf_op jit(solution)/shard_map/ppermute | solution.py:52
  54.4 1.0 collective-permute-start.12
  55.4 5.7 %collective-permute-done.12 = bf16[17,16,256]{2,1,0:T(8,128)(2,1)S(1)} collective-permute-done((bf16[17,16,256]{2,1,0:T(8,128)(2,1)S(1)}, bf16[17,16,256]{2,1,0:T(8,128)(2,1)S(1)}, u32[]{:S(2)}, u32[]{:S(2)}) %collective-permute-start.12) | collective-permute-done | bytes 139296 | tf_op jit(solution)/shard_map/ppermute | solution.py:52
  61.1 0.9 collective-permute-start.13
  62.7 0.9 collective-permute-start.15
  63.6 0.8 copy-done.2
  66.5 4.4 %collective-permute-done.13.refs_1_ = bf16[4,17,16,256]{3,2,1,0:T(8,128)(2,1)} collective-permute-done((bf16[4,17,16,256]{3,2,1,0:T(8,128)(2,1)S(1)}, bf16[4,17,16,256]{3,2,1,0:T(8,128)(2,1)}, u32[]{:S(2)}, u32[]{:S(2)}) %collective-permute-start.13) | collective-permute-done | bytes 557088 | tf_op jit(solution)/shard_map/ppermute | solution.py:52
  70.9 2.5 %collective-permute-done.14.refs_2_ = bf16[4,17,16,256]{3,2,1,0:T(8,128)(2,1)} collective-permute-done((bf16[4,17,16,256]{3,2,1,0:T(8,128)(2,1)S(1)}, bf16[4,17,16,256]{3,2,1,0:T(8,128)(2,1)}, u32[]{:S(2)}, u32[]{:S(2)}) %collective-permute-start.14) | collective-permute-done | bytes 557088 | tf_op jit(solution)/shard_map/ppermute | solution.py:52
  73.3 5.9 %collective-permute-done.15.refs_3_ = bf16[4,17,16,256]{3,2,1,0:T(8,128)(2,1)} collective-permute-done((bf16[4,17,16,256]{3,2,1,0:T(8,128)(2,1)S(1)}, bf16[4,17,16,256]{3,2,1,0:T(8,128)(2,1)}, u32[]{:S(2)}, u32[]{:S(2)}) %collective-permute-start.15) | collective-permute-done | bytes 557088 | tf_op jit(solution)/shard_map/ppermute | solution.py:52
  79.2 0.8 copy-done.8
  80.5 0.9 copy-done.10
  81.5 1.2 copy-done.3
  82.7 1.1 copy-done.5
  83.7 1.1 copy-done.7
  84.8 1.1 copy-done.9
  85.8 1.1 copy-done.11
  86.9 3.9 %shard_map.76 = (bf16[128,2048]{1,0:T(8,128)(2,1)S(1)}, bf16[128,2048]{1,0:T(8,128)(2,1)S(1)}, bf16[2,128,16,256]{3,2,1,0:T(8,128)(2,1)S(1)}, bf16[2,9,16,16,256...) custom-call(s32[4]{0:T(128)S(1)} %pad_add_fusion.s_ref, ...), custom_call_target="tpu_custom_call" | custom-call | tf_op jit(solution)/shard_map/pallas_call | solution.py:344
  90.8 6.8 %shard_map.77 = (bf16[128,2048]{1,0:T(8,128)(2,1)S(1)}, bf16[2,144,4608]{2,1,0:T(8,128)(2,1)S(1)}) custom-call(s32[4]{0:T(128)S(1)} %pad_add_fusion.s_ref, bf16[128,2048]{1,0:T(8,128)(2,1)S(1)} %get-tuple-element.30.x2, bf16[2,2,128,2048]{3,2,1,0:T(8,128)(2,1)S(1)} %copy-done.1, bf16[4,17,16,256]{3,2,1,0:T(8,128)(2,1)S(1)} %pad_maximum_fusion.1.refs_0_, ...), custom_call_target="tpu_custom_call" | custom-call | tf_op jit(solution)/shard_map/pallas_call | solution.py:344
  97.5 3.4 %shard_map.78.acts = bf16[2,144,4608]{2,1,0:T(8,128)(2,1)S(1)} custom-call(s32[4]{0:T(128)S(1)} %pad_add_fusion.s_ref, bf16[2,2,128,2048]{3,2,1,0:T(8,128)(2,1)S(1)} %copy-done, bf16[128,2048]{1,0:T(8,128)(2,1)S(1)} %get-tuple-element.29.x1, bf16[128,2048]{1,0:T(8,128)(2,1)S(1)} %get-tuple-element.31.up2, ...), custom_call_target="tpu_custom_call" | custom-call | tf_op jit(solution)/shard_map/pallas_call | solution.py:344
  101.8 2.5 %collective-permute-done.20.got = bf16[144,4608]{1,0:T(8,128)(2,1)S(1)} collective-permute-done((bf16[144,4608]{1,0:T(8,128)(2,1)S(1)}, bf16[144,4608]{1,0:T(8,128)(2,1)S(1)}, u32[]{:S(2)}, u32[]{:S(2)}) %collective-permute-start.20) | collective-permute-done | bytes 1327136 | tf_op jit(solution)/shard_map/ppermute | solution.py:52
  104.3 1.3 shard_map.79
  105.8 3.2 %collective-permute-start.22 = (bf16[2,17,16,256]{3,2,1,0:T(8,128)(2,1)S(1)}, bf16[2,17,16,256]{3,2,1,0:T(8,128)(2,1)S(1)}, u32[]{:S(2)}, u32[]{:S(2)}) collective-permute-start(bf16[2,17,16,256]{3,2,1,0:T(8,128)(2,1)S(1)} %get-tuple-element.38), channel_id=1, source_target_pairs={{0,48},{1,49},{2,50},{3,51},{4,52},{5,53},{6,54},{7,55},{8,56},{9,... | collective-permute-start | bytes 835592 | tf_op jit(solution)/shard_map/ppermute | solution.py:52
  109.0 1.3 shard_map.82
  110.4 3.2 %collective-permute-start.30 = (bf16[2,17,16,256]{3,2,1,0:T(8,128)(2,1)S(1)}, bf16[2,17,16,256]{3,2,1,0:T(8,128)(2,1)S(1)}, u32[]{:S(2)}, u32[]{:S(2)}) collective-permute-start(bf16[2,17,16,256]{3,2,1,0:T(8,128)(2,1)S(1)} %get-tuple-element.48), channel_id=1, source_target_pairs={{0,48},{1,49},{2,50},{3,51},{4,52},{5,53},{6,54},{7,55},{8,56},{9,... | collective-permute-start | bytes 835592 | tf_op jit(solution)/shard_map/ppermute | solution.py:52
  114.5 3.2 %collective-permute-start.24 = (bf16[4,17,16,256]{3,2,1,0:T(8,128)(2,1)S(1)}, bf16[4,17,16,256]{3,2,1,0:T(8,128)(2,1)S(1)}, u32[]{:S(2)}, u32[]{:S(2)}) collective-permute-start(bf16[4,17,16,256]{3,2,1,0:T(8,128)(2,1)S(1)} %get-tuple-element.40), channel_id=1, source_target_pairs={{0,48},{1,49},{2,50},{3,51},{4,52},{5,53},{6,54},{7,55},{8,56},{9,... | collective-permute-start | bytes 1671176 | tf_op jit(solution)/shard_map/ppermute | solution.py:52
  119.0 3.3 %collective-permute-start.32 = (bf16[4,17,16,256]{3,2,1,0:T(8,128)(2,1)S(1)}, bf16[4,17,16,256]{3,2,1,0:T(8,128)(2,1)S(1)}, u32[]{:S(2)}, u32[]{:S(2)}) collective-permute-start(bf16[4,17,16,256]{3,2,1,0:T(8,128)(2,1)S(1)} %get-tuple-element.50), channel_id=1, source_target_pairs={{0,48},{1,49},{2,50},{3,51},{4,52},{5,53},{6,54},{7,55},{8,56},{9,... | collective-permute-start | bytes 1671176 | tf_op jit(solution)/shard_map/ppermute | solution.py:52
  122.3 2.9 %collective-permute-done.23.a = bf16[4,17,16,256]{3,2,1,0:T(8,128)(2,1)S(1)} collective-permute-done((bf16[4,17,16,256]{3,2,1,0:T(8,128)(2,1)S(1)}, bf16[4,17,16,256]{3,2,1,0:T(8,128)(2,1)S(1)}, u32[]{:S(2)}, u32[]{:S(2)}) %collective-permute-start.23) | collective-permute-done | bytes 557088 | tf_op jit(solution)/shard_map/ppermute | solution.py:52
  125.2 0.8 shard_map.81
  126.8 0.9 collective-permute-start.26
  127.7 2.3 %collective-permute-start.27 = (bf16[17,16,256]{2,1,0:T(8,128)(2,1)S(1)}, bf16[17,16,256]{2,1,0:T(8,128)(2,1)S(1)}, u32[]{:S(2)}, u32[]{:S(2)}) collective-permute-start(bf16[17,16,256]{2,1,0:T(8,128)(2,1)S(1)} %get-tuple-element.44), channel_id=1, source_target_pairs={{0,12},{1,13},{2,14},{3,15},{4,0},{5,1},{6,2},{7,3},{8,4},{9,5},{1... | collective-permute-start | bytes 417800 | tf_op jit(solution)/shard_map/ppermute | solution.py:52
  130.0 4.2 %collective-permute-done.31.a = bf16[4,17,16,256]{3,2,1,0:T(8,128)(2,1)S(1)} collective-permute-done((bf16[4,17,16,256]{3,2,1,0:T(8,128)(2,1)S(1)}, bf16[4,17,16,256]{3,2,1,0:T(8,128)(2,1)S(1)}, u32[]{:S(2)}, u32[]{:S(2)}) %collective-permute-start.31) | collective-permute-done | bytes 557088 | tf_op jit(solution)/shard_map/ppermute | solution.py:52
  134.2 1.5 collective-permute-done.32.b
  135.6 0.8 shard_map.84
  136.7 3.2 %collective-permute-start.35 = (bf16[17,16,256]{2,1,0:T(8,128)(2,1)S(1)}, bf16[17,16,256]{2,1,0:T(8,128)(2,1)S(1)}, u32[]{:S(2)}, u32[]{:S(2)}) collective-permute-start(bf16[17,16,256]{2,1,0:T(8,128)(2,1)S(1)} %get-tuple-element.54), channel_id=1, source_target_pairs={{0,12},{1,13},{2,14},{3,15},{4,0},{5,1},{6,2},{7,3},{8,4},{9,5},{1... | collective-permute-start | bytes 417800 | tf_op jit(solution)/shard_map/ppermute | solution.py:52
  140.0 3.2 %collective-permute-done.33 = bf16[17,16,256]{2,1,0:T(8,128)(2,1)S(1)} collective-permute-done((bf16[17,16,256]{2,1,0:T(8,128)(2,1)S(1)}, bf16[17,16,256]{2,1,0:T(8,128)(2,1)S(1)}, u32[]{:S(2)}, u32[]{:S(2)}) %collective-permute-start.33) | collective-permute-done | bytes 139296 | tf_op jit(solution)/shard_map/ppermute | solution.py:52
  143.2 1.2 collective-permute-done.34
  144.8 12.4 %all_to_all.11.parts = bf16[8,72,256]{2,1,0:T(8,128)(2,1)S(1)} all-to-all(bf16[8,72,256]{2,1,0:T(8,128)(2,1)S(1)} %pad_maximum_fusion.2), channel_id=1, replica_groups=mesh['zl'=2,'c'=2,'x'=4,'y'=4,'zh'=4] {'zl','zh'}, dimensions={0} | all-to-all | bytes 589824 | tf_op jit(solution)/shard_map/all_to_all | solution.py:450
  157.2 1.2 shard_map.85
  (88 shorter events, 11.2 us)
Async XLA Ops:
  21.8 59.7 %copy-start = (bf16[2,2,128,2048]{3,2,1,0:T(8,128)(2,1)S(1)}, bf16[2,2,128,2048]{3,2,1,0:T(8,128)(2,1)}, u32[]{:S(2)}) copy-start(bf16[2,2,128,2048]{3,2,1,0:T(8,128)(2,1)} %xs.3) | copy-start | bytes 6291460
  22.1 6.9 %collective-permute-start = (bf16[17,16,256]{2,1,0:T(8,128)(2,1)S(1)}, bf16[17,16,256]{2,1,0:T(8,128)(2,1)S(1)}, u32[]{:S(2)}, u32[]{:S(2)}) collective-permute-start(bf16[17,16,256]{2,1,0:T(8,128)(2,1)S(1)} %get-tuple-element.60), channel_id=1, source_target_pairs={{0,48},{1,49},{2,50},{3,51},{4,52},{5,53},{6,54},{7,55},{8,56},{9,... | collective-permute-start | bytes 417800 | tf_op jit(solution)/shard_map/ppermute | solution.py:52
  24.9 6.7 %collective-permute-start.1 = (bf16[17,16,256]{2,1,0:T(8,128)(2,1)S(1)}, bf16[17,16,256]{2,1,0:T(8,128)(2,1)S(1)}, u32[]{:S(2)}, u32[]{:S(2)}) collective-permute-start(bf16[17,16,256]{2,1,0:T(8,128)(2,1)S(1)} %get-tuple-element.60), channel_id=1, source_target_pairs={{0,32},{1,33},{2,34},{3,35},{4,36},{5,37},{6,38},{7,39},{8,40},{9,... | collective-permute-start | bytes 417800 | tf_op jit(solution)/shard_map/ppermute | solution.py:52
  25.7 7.3 %collective-permute-start.2 = (bf16[17,16,256]{2,1,0:T(8,128)(2,1)S(1)}, bf16[17,16,256]{2,1,0:T(8,128)(2,1)S(1)}, u32[]{:S(2)}, u32[]{:S(2)}) collective-permute-start(bf16[17,16,256]{2,1,0:T(8,128)(2,1)S(1)} %get-tuple-element.60), channel_id=1, source_target_pairs={{0,16},{1,17},{2,18},{3,19},{4,20},{5,21},{6,22},{7,23},{8,24},{9,... | collective-permute-start | bytes 417800 | tf_op jit(solution)/shard_map/ppermute | solution.py:52
  33.0 29.0 %collective-permute-start.3 = (bf16[4,17,16,256]{3,2,1,0:T(8,128)(2,1)S(1)}, bf16[4,17,16,256]{3,2,1,0:T(8,128)(2,1)S(1)}, u32[]{:S(2)}, u32[]{:S(2)}) collective-permute-start(bf16[4,17,16,256]{3,2,1,0:T(8,128)(2,1)S(1)} %pad_maximum_fusion.refs_0_), channel_id=1, source_target_pairs={{0,12},{1,13},{2,14},{3,15},{4,0},{5,1},{6,2},{7,3},{8,4},{9,5},{1... | collective-permute-start | bytes 1671176 | tf_op jit(solution)/shard_map/ppermute | solution.py:52
  36.1 26.6 %collective-permute-start.4 = (bf16[4,17,16,256]{3,2,1,0:T(8,128)(2,1)S(1)}, bf16[4,17,16,256]{3,2,1,0:T(8,128)(2,1)S(1)}, u32[]{:S(2)}, u32[]{:S(2)}) collective-permute-start(bf16[4,17,16,256]{3,2,1,0:T(8,128)(2,1)S(1)} %pad_maximum_fusion.refs_0_), channel_id=1, source_target_pairs={{0,8},{1,9},{2,10},{3,11},{4,12},{5,13},{6,14},{7,15},{8,0},{9,1},... | collective-permute-start | bytes 1671176 | tf_op jit(solution)/shard_map/ppermute | solution.py:52
  36.8 26.8 %collective-permute-start.5 = (bf16[4,17,16,256]{3,2,1,0:T(8,128)(2,1)S(1)}, bf16[4,17,16,256]{3,2,1,0:T(8,128)(2,1)}, u32[]{:S(2)}, u32[]{:S(2)}) collective-permute-start(bf16[4,17,16,256]{3,2,1,0:T(8,128)(2,1)S(1)} %pad_maximum_fusion.refs_0_), channel_id=1, source_target_pairs={{0,4},{1,5},{2,6},{3,7},{4,8},{5,9},{6,10},{7,11},{8,12},{9,13},{1... | collective-permute-start | bytes 1671176 | tf_op jit(solution)/shard_map/ppermute | solution.py:52
  37.7 26.7 %collective-permute-start.6 = (bf16[4,17,16,256]{3,2,1,0:T(8,128)(2,1)S(1)}, bf16[4,17,16,256]{3,2,1,0:T(8,128)(2,1)S(1)}, u32[]{:S(2)}, u32[]{:S(2)}) collective-permute-start(bf16[4,17,16,256]{3,2,1,0:T(8,128)(2,1)S(1)} %pad_maximum_fusion.refs_0_), channel_id=1, source_target_pairs={{0,64},{1,65},{2,66},{3,67},{4,68},{5,69},{6,70},{7,71},{8,72},{9,... | collective-permute-start | bytes 1671176 | tf_op jit(solution)/shard_map/ppermute | solution.py:52
  37.7 10.1 %collective-permute-start.10 = (bf16[17,16,256]{2,1,0:T(8,128)(2,1)S(1)}, bf16[17,16,256]{2,1,0:T(8,128)(2,1)S(1)}, u32[]{:S(2)}, u32[]{:S(2)}) collective-permute-start(bf16[17,16,256]{2,1,0:T(8,128)(2,1)S(1)} %get-tuple-element.61), channel_id=1, source_target_pairs={{0,48},{1,49},{2,50},{3,51},{4,52},{5,53},{6,54},{7,55},{8,56},{9,... | collective-permute-start | bytes 417800 | tf_op jit(solution)/shard_map/ppermute | solution.py:52
  47.8 6.6 %collective-permute-start.11 = (bf16[17,16,256]{2,1,0:T(8,128)(2,1)S(1)}, bf16[17,16,256]{2,1,0:T(8,128)(2,1)S(1)}, u32[]{:S(2)}, u32[]{:S(2)}) collective-permute-start(bf16[17,16,256]{2,1,0:T(8,128)(2,1)S(1)} %get-tuple-element.61), channel_id=1, source_target_pairs={{0,32},{1,33},{2,34},{3,35},{4,36},{5,37},{6,38},{7,39},{8,40},{9,... | collective-permute-start | bytes 417800 | tf_op jit(solution)/shard_map/ppermute | solution.py:52
  54.4 6.7 %collective-permute-start.12 = (bf16[17,16,256]{2,1,0:T(8,128)(2,1)S(1)}, bf16[17,16,256]{2,1,0:T(8,128)(2,1)S(1)}, u32[]{:S(2)}, u32[]{:S(2)}) collective-permute-start(bf16[17,16,256]{2,1,0:T(8,128)(2,1)S(1)} %get-tuple-element.61), channel_id=1, source_target_pairs={{0,16},{1,17},{2,18},{3,19},{4,20},{5,21},{6,22},{7,23},{8,24},{9,... | collective-permute-start | bytes 417800 | tf_op jit(solution)/shard_map/ppermute | solution.py:52
  61.1 9.7 %collective-permute-start.13 = (bf16[4,17,16,256]{3,2,1,0:T(8,128)(2,1)S(1)}, bf16[4,17,16,256]{3,2,1,0:T(8,128)(2,1)}, u32[]{:S(2)}, u32[]{:S(2)}) collective-permute-start(bf16[4,17,16,256]{3,2,1,0:T(8,128)(2,1)S(1)} %pad_maximum_fusion.1.refs_0_), channel_id=1, source_target_pairs={{0,12},{1,13},{2,14},{3,15},{4,0},{5,1},{6,2},{7,3},{8,4},{9,5},{1... | collective-permute-start | bytes 1671176 | tf_op jit(solution)/shard_map/ppermute | solution.py:52
  62.1 11.2 %collective-permute-start.14 = (bf16[4,17,16,256]{3,2,1,0:T(8,128)(2,1)S(1)}, bf16[4,17,16,256]{3,2,1,0:T(8,128)(2,1)}, u32[]{:S(2)}, u32[]{:S(2)}) collective-permute-start(bf16[4,17,16,256]{3,2,1,0:T(8,128)(2,1)S(1)} %pad_maximum_fusion.1.refs_0_), channel_id=1, source_target_pairs={{0,8},{1,9},{2,10},{3,11},{4,12},{5,13},{6,14},{7,15},{8,0},{9,1},... | collective-permute-start | bytes 1671176 | tf_op jit(solution)/shard_map/ppermute | solution.py:52
  62.7 16.5 %collective-permute-start.15 = (bf16[4,17,16,256]{3,2,1,0:T(8,128)(2,1)S(1)}, bf16[4,17,16,256]{3,2,1,0:T(8,128)(2,1)}, u32[]{:S(2)}, u32[]{:S(2)}) collective-permute-start(bf16[4,17,16,256]{3,2,1,0:T(8,128)(2,1)S(1)} %pad_maximum_fusion.1.refs_0_), channel_id=1, source_target_pairs={{0,4},{1,5},{2,6},{3,7},{4,8},{5,9},{6,10},{7,11},{8,12},{9,13},{1... | collective-permute-start | bytes 1671176 | tf_op jit(solution)/shard_map/ppermute | solution.py:52
  63.6 15.6 %collective-permute-start.7 = (bf16[4,17,16,256]{3,2,1,0:T(8,128)(2,1)S(1)}, bf16[4,17,16,256]{3,2,1,0:T(8,128)(2,1)S(1)}, u32[]{:S(2)}, u32[]{:S(2)}) collective-permute-start(bf16[4,17,16,256]{3,2,1,0:T(8,128)(2,1)S(1)} %collective-permute-done.3.refs_1_), channel_id=1, source_target_pairs={{0,64},{1,65},{2,66},{3,67},{4,68},{5,69},{6,70},{7,71},{8,72},{9,... | collective-permute-start | bytes 1671176 | tf_op jit(solution)/shard_map/ppermute | solution.py:52
  63.6 0.8 copy-start.2
  64.4 0.8 copy-start.6
  65.2 15.3 %collective-permute-start.8 = (bf16[4,17,16,256]{3,2,1,0:T(8,128)(2,1)S(1)}, bf16[4,17,16,256]{3,2,1,0:T(8,128)(2,1)S(1)}, u32[]{:S(2)}, u32[]{:S(2)}) collective-permute-start(bf16[4,17,16,256]{3,2,1,0:T(8,128)(2,1)S(1)} %collective-permute-done.4.refs_2_), channel_id=1, source_target_pairs={{0,64},{1,65},{2,66},{3,67},{4,68},{5,69},{6,70},{7,71},{8,72},{9,... | collective-permute-start | bytes 1671176 | tf_op jit(solution)/shard_map/ppermute | solution.py:52
  65.7 0.8 copy-start.4
  70.9 19.9 %collective-permute-start.16 = (bf16[4,17,16,256]{3,2,1,0:T(8,128)(2,1)S(1)}, bf16[4,17,16,256]{3,2,1,0:T(8,128)(2,1)}, u32[]{:S(2)}, u32[]{:S(2)}) collective-permute-start(bf16[4,17,16,256]{3,2,1,0:T(8,128)(2,1)S(1)} %pad_maximum_fusion.1.refs_0_), channel_id=1, source_target_pairs={{0,64},{1,65},{2,66},{3,67},{4,68},{5,69},{6,70},{7,71},{8,72},{9,... | collective-permute-start | bytes 1671176 | tf_op jit(solution)/shard_map/ppermute | solution.py:52
  73.3 8.1 %collective-permute-start.9 = (bf16[4,17,16,256]{3,2,1,0:T(8,128)(2,1)}, bf16[4,17,16,256]{3,2,1,0:T(8,128)(2,1)}, u32[]{:S(2)}, u32[]{:S(2)}) collective-permute-start(bf16[4,17,16,256]{3,2,1,0:T(8,128)(2,1)} %collective-permute-done.5.refs_3_), channel_id=1, source_target_pairs={{0,64},{1,65},{2,66},{3,67},{4,68},{5,69},{6,70},{7,71},{8,72},{9,... | collective-permute-start | bytes 1671176 | tf_op jit(solution)/shard_map/ppermute | solution.py:52
  79.2 11.6 %collective-permute-start.17 = (bf16[4,17,16,256]{3,2,1,0:T(8,128)(2,1)}, bf16[4,17,16,256]{3,2,1,0:T(8,128)(2,1)}, u32[]{:S(2)}, u32[]{:S(2)}) collective-permute-start(bf16[4,17,16,256]{3,2,1,0:T(8,128)(2,1)} %collective-permute-done.13.refs_1_), channel_id=1, source_target_pairs={{0,64},{1,65},{2,66},{3,67},{4,68},{5,69},{6,70},{7,71},{8,72},{9,... | collective-permute-start | bytes 1671176 | tf_op jit(solution)/shard_map/ppermute | solution.py:52
  79.2 0.8 copy-start.8
  80.0 10.8 %collective-permute-start.18 = (bf16[4,17,16,256]{3,2,1,0:T(8,128)(2,1)}, bf16[4,17,16,256]{3,2,1,0:T(8,128)(2,1)}, u32[]{:S(2)}, u32[]{:S(2)}) collective-permute-start(bf16[4,17,16,256]{3,2,1,0:T(8,128)(2,1)} %collective-permute-done.14.refs_2_), channel_id=1, source_target_pairs={{0,64},{1,65},{2,66},{3,67},{4,68},{5,69},{6,70},{7,71},{8,72},{9,... | collective-permute-start | bytes 1671176 | tf_op jit(solution)/shard_map/ppermute | solution.py:52
  80.5 0.9 copy-start.10
  81.4 9.4 %collective-permute-start.19 = (bf16[4,17,16,256]{3,2,1,0:T(8,128)(2,1)}, bf16[4,17,16,256]{3,2,1,0:T(8,128)(2,1)}, u32[]{:S(2)}, u32[]{:S(2)}) collective-permute-start(bf16[4,17,16,256]{3,2,1,0:T(8,128)(2,1)} %collective-permute-done.15.refs_3_), channel_id=1, source_target_pairs={{0,64},{1,65},{2,66},{3,67},{4,68},{5,69},{6,70},{7,71},{8,72},{9,... | collective-permute-start | bytes 1671176 | tf_op jit(solution)/shard_map/ppermute | solution.py:52
  81.5 9.3 %copy-start.1 = (bf16[2,2,128,2048]{3,2,1,0:T(8,128)(2,1)S(1)}, bf16[2,2,128,2048]{3,2,1,0:T(8,128)(2,1)}, u32[]{:S(2)}) copy-start(bf16[2,2,128,2048]{3,2,1,0:T(8,128)(2,1)} %cots.1) | copy-start | bytes 6291460
  81.5 1.2 copy-start.3
  82.7 1.1 copy-start.5
  83.7 1.1 copy-start.7
  84.8 1.1 copy-start.9
  85.8 1.1 copy-start.11
  101.0 3.3 %collective-permute-start.20 = (bf16[144,4608]{1,0:T(8,128)(2,1)S(1)}, bf16[144,4608]{1,0:T(8,128)(2,1)S(1)}, u32[]{:S(2)}, u32[]{:S(2)}) collective-permute-start(bf16[144,4608]{1,0:T(8,128)(2,1)S(1)} %slice_bitcast_fusion), channel_id=1, source_target_pairs={{0,64},{1,65},{2,66},{3,67},{4,68},{5,69},{6,70},{7,71},{8,72},{9,... | collective-permute-start | bytes 3981320 | tf_op jit(solution)/shard_map/ppermute | solution.py:52
  101.7 7.3 %collective-permute-start.28 = (bf16[144,4608]{1,0:T(8,128)(2,1)S(1)}, bf16[144,4608]{1,0:T(8,128)(2,1)S(1)}, u32[]{:S(2)}, u32[]{:S(2)}) collective-permute-start(bf16[144,4608]{1,0:T(8,128)(2,1)S(1)} %slice_bitcast_fusion.1), channel_id=1, source_target_pairs={{0,64},{1,65},{2,66},{3,67},{4,68},{5,69},{6,70},{7,71},{8,72},{9,... | collective-permute-start | bytes 3981320 | tf_op jit(solution)/shard_map/ppermute | solution.py:52
  105.7 8.0 %collective-permute-start.21 = (bf16[2,17,16,256]{3,2,1,0:T(8,128)(2,1)S(1)}, bf16[2,17,16,256]{3,2,1,0:T(8,128)(2,1)S(1)}, u32[]{:S(2)}, u32[]{:S(2)}) collective-permute-start(bf16[2,17,16,256]{3,2,1,0:T(8,128)(2,1)S(1)} %get-tuple-element.37), channel_id=1, source_target_pairs={{0,16},{1,17},{2,18},{3,19},{4,20},{5,21},{6,22},{7,23},{8,24},{9,... | collective-permute-start | bytes 835592 | tf_op jit(solution)/shard_map/ppermute | solution.py:52
  105.8 7.9 %collective-permute-start.22 = (bf16[2,17,16,256]{3,2,1,0:T(8,128)(2,1)S(1)}, bf16[2,17,16,256]{3,2,1,0:T(8,128)(2,1)S(1)}, u32[]{:S(2)}, u32[]{:S(2)}) collective-permute-start(bf16[2,17,16,256]{3,2,1,0:T(8,128)(2,1)S(1)} %get-tuple-element.38), channel_id=1, source_target_pairs={{0,48},{1,49},{2,50},{3,51},{4,52},{5,53},{6,54},{7,55},{8,56},{9,... | collective-permute-start | bytes 835592 | tf_op jit(solution)/shard_map/ppermute | solution.py:52
  110.3 7.8 %collective-permute-start.29 = (bf16[2,17,16,256]{3,2,1,0:T(8,128)(2,1)S(1)}, bf16[2,17,16,256]{3,2,1,0:T(8,128)(2,1)S(1)}, u32[]{:S(2)}, u32[]{:S(2)}) collective-permute-start(bf16[2,17,16,256]{3,2,1,0:T(8,128)(2,1)S(1)} %get-tuple-element.47), channel_id=1, source_target_pairs={{0,16},{1,17},{2,18},{3,19},{4,20},{5,21},{6,22},{7,23},{8,24},{9,... | collective-permute-start | bytes 835592 | tf_op jit(solution)/shard_map/ppermute | solution.py:52
  110.4 7.7 %collective-permute-start.30 = (bf16[2,17,16,256]{3,2,1,0:T(8,128)(2,1)S(1)}, bf16[2,17,16,256]{3,2,1,0:T(8,128)(2,1)S(1)}, u32[]{:S(2)}, u32[]{:S(2)}) collective-permute-start(bf16[2,17,16,256]{3,2,1,0:T(8,128)(2,1)S(1)} %get-tuple-element.48), channel_id=1, source_target_pairs={{0,48},{1,49},{2,50},{3,51},{4,52},{5,53},{6,54},{7,55},{8,56},{9,... | collective-permute-start | bytes 835592 | tf_op jit(solution)/shard_map/ppermute | solution.py:52
  114.4 10.8 %collective-permute-start.23 = (bf16[4,17,16,256]{3,2,1,0:T(8,128)(2,1)S(1)}, bf16[4,17,16,256]{3,2,1,0:T(8,128)(2,1)S(1)}, u32[]{:S(2)}, u32[]{:S(2)}) collective-permute-start(bf16[4,17,16,256]{3,2,1,0:T(8,128)(2,1)S(1)} %get-tuple-element.39), channel_id=1, source_target_pairs={{0,16},{1,17},{2,18},{3,19},{4,20},{5,21},{6,22},{7,23},{8,24},{9,... | collective-permute-start | bytes 1671176 | tf_op jit(solution)/shard_map/ppermute | solution.py:52
  114.5 10.7 %collective-permute-start.24 = (bf16[4,17,16,256]{3,2,1,0:T(8,128)(2,1)S(1)}, bf16[4,17,16,256]{3,2,1,0:T(8,128)(2,1)S(1)}, u32[]{:S(2)}, u32[]{:S(2)}) collective-permute-start(bf16[4,17,16,256]{3,2,1,0:T(8,128)(2,1)S(1)} %get-tuple-element.40), channel_id=1, source_target_pairs={{0,48},{1,49},{2,50},{3,51},{4,52},{5,53},{6,54},{7,55},{8,56},{9,... | collective-permute-start | bytes 1671176 | tf_op jit(solution)/shard_map/ppermute | solution.py:52
  118.9 15.3 %collective-permute-start.31 = (bf16[4,17,16,256]{3,2,1,0:T(8,128)(2,1)S(1)}, bf16[4,17,16,256]{3,2,1,0:T(8,128)(2,1)S(1)}, u32[]{:S(2)}, u32[]{:S(2)}) collective-permute-start(bf16[4,17,16,256]{3,2,1,0:T(8,128)(2,1)S(1)} %get-tuple-element.49), channel_id=1, source_target_pairs={{0,16},{1,17},{2,18},{3,19},{4,20},{5,21},{6,22},{7,23},{8,24},{9,... | collective-permute-start | bytes 1671176 | tf_op jit(solution)/shard_map/ppermute | solution.py:52
  119.0 16.6 %collective-permute-start.32 = (bf16[4,17,16,256]{3,2,1,0:T(8,128)(2,1)S(1)}, bf16[4,17,16,256]{3,2,1,0:T(8,128)(2,1)S(1)}, u32[]{:S(2)}, u32[]{:S(2)}) collective-permute-start(bf16[4,17,16,256]{3,2,1,0:T(8,128)(2,1)S(1)} %get-tuple-element.50), channel_id=1, source_target_pairs={{0,48},{1,49},{2,50},{3,51},{4,52},{5,53},{6,54},{7,55},{8,56},{9,... | collective-permute-start | bytes 1671176 | tf_op jit(solution)/shard_map/ppermute | solution.py:52
  126.1 10.6 %collective-permute-start.25 = (bf16[17,16,256]{2,1,0:T(8,128)(2,1)S(1)}, bf16[17,16,256]{2,1,0:T(8,128)(2,1)S(1)}, u32[]{:S(2)}, u32[]{:S(2)}) collective-permute-start(bf16[17,16,256]{2,1,0:T(8,128)(2,1)S(1)} %get-tuple-element.42), channel_id=1, source_target_pairs={{0,8},{1,9},{2,10},{3,11},{4,12},{5,13},{6,14},{7,15},{8,0},{9,1},... | collective-permute-start | bytes 417800 | tf_op jit(solution)/shard_map/ppermute | solution.py:52
  126.8 13.1 %collective-permute-start.26 = (bf16[17,16,256]{2,1,0:T(8,128)(2,1)S(1)}, bf16[17,16,256]{2,1,0:T(8,128)(2,1)S(1)}, u32[]{:S(2)}, u32[]{:S(2)}) collective-permute-start(bf16[17,16,256]{2,1,0:T(8,128)(2,1)S(1)} %get-tuple-element.43), channel_id=1, source_target_pairs={{0,4},{1,5},{2,6},{3,7},{4,8},{5,9},{6,10},{7,11},{8,12},{9,13},{1... | collective-permute-start | bytes 417800 | tf_op jit(solution)/shard_map/ppermute | solution.py:52
  127.7 12.2 %collective-permute-start.27 = (bf16[17,16,256]{2,1,0:T(8,128)(2,1)S(1)}, bf16[17,16,256]{2,1,0:T(8,128)(2,1)S(1)}, u32[]{:S(2)}, u32[]{:S(2)}) collective-permute-start(bf16[17,16,256]{2,1,0:T(8,128)(2,1)S(1)} %get-tuple-element.44), channel_id=1, source_target_pairs={{0,12},{1,13},{2,14},{3,15},{4,0},{5,1},{6,2},{7,3},{8,4},{9,5},{1... | collective-permute-start | bytes 417800 | tf_op jit(solution)/shard_map/ppermute | solution.py:52
  136.5 6.7 %collective-permute-start.33 = (bf16[17,16,256]{2,1,0:T(8,128)(2,1)S(1)}, bf16[17,16,256]{2,1,0:T(8,128)(2,1)S(1)}, u32[]{:S(2)}, u32[]{:S(2)}) collective-permute-start(bf16[17,16,256]{2,1,0:T(8,128)(2,1)S(1)} %get-tuple-element.52), channel_id=1, source_target_pairs={{0,8},{1,9},{2,10},{3,11},{4,12},{5,13},{6,14},{7,15},{8,0},{9,1},... | collective-permute-start | bytes 417800 | tf_op jit(solution)/shard_map/ppermute | solution.py:52
  136.6 7.8 %collective-permute-start.34 = (bf16[17,16,256]{2,1,0:T(8,128)(2,1)S(1)}, bf16[17,16,256]{2,1,0:T(8,128)(2,1)S(1)}, u32[]{:S(2)}, u32[]{:S(2)}) collective-permute-start(bf16[17,16,256]{2,1,0:T(8,128)(2,1)S(1)} %get-tuple-element.53), channel_id=1, source_target_pairs={{0,4},{1,5},{2,6},{3,7},{4,8},{5,9},{6,10},{7,11},{8,12},{9,13},{1... | collective-permute-start | bytes 417800 | tf_op jit(solution)/shard_map/ppermute | solution.py:52
  136.7 7.7 %collective-permute-start.35 = (bf16[17,16,256]{2,1,0:T(8,128)(2,1)S(1)}, bf16[17,16,256]{2,1,0:T(8,128)(2,1)S(1)}, u32[]{:S(2)}, u32[]{:S(2)}) collective-permute-start(bf16[17,16,256]{2,1,0:T(8,128)(2,1)S(1)} %get-tuple-element.54), channel_id=1, source_target_pairs={{0,12},{1,13},{2,14},{3,15},{4,0},{5,1},{6,2},{7,3},{8,4},{9,5},{1... | collective-permute-start | bytes 417800 | tf_op jit(solution)/shard_map/ppermute | solution.py:52

commit v5 on v4

--- a/solution.py
+++ b/solution.py
@@ -163,29 +163,51 @@
     ).astype(BF16)
 
 
-def kernel_low_forward(s_ref, xs, *refs):
-    pieces, (x1, x2, win, wout, stats, pre, normed, hat) = refs[: 2 * PIECES], refs[2 * PIECES :]
+def kernel_pack(s_ref, gain, weight_in, weight_out, out):
+    groups = [weight_out[0, :, pl.ds(k * 256, 256)].astype(F32) for k in range(8)]
+    across = jnp.concatenate(groups, axis=0).astype(BF16)
+    along = jnp.broadcast_to(gain[...].astype(F32), (8, 32)).astype(BF16)
+    for i in range(8):
+        out[i, 0:32] = weight_in[0]
+        out[i, 32:64] = across
+        out[i, 64:72, 0:32] = along
+
+
+def kernel_stats(s_ref, xs, hat, stat):
+    c, zl = s_ref[2], s_ref[3]
+
+    def keep_stat(rows, mean, recip_std):
+        stat[0, rows, :] = spread(mean)
+        stat[1, rows, :] = spread(recip_std)
+
+    hat_pass(lambda rows: xs[zl, c, rows, :], hat, keep_stat)
+
+
+def kernel_low_forward(s_ref, xs, hat0, *refs):
+    pieces = refs[: 2 * PIECES]
+    x1, x2, win, wout, stat1, pre, normed, hat1 = refs[2 * PIECES :]
     place_weights(s_ref, pieces, win, wout)
     c, zl = s_ref[2], s_ref[3]
-    for par in range(2):
-
-        def x_at(rows=slice(None), cols=slice(None), par=par):
-            return xs[zl, c, rows, cols] if par == 0 else x1[rows, cols]
-
-        def keep_stat(rows, mean, recip_std, par=par):
-            stats[par, 0, rows, :] = spread(mean)
-            stats[par, 1, rows, :] = spread(recip_std)
-
-        hat_pass(x_at, hat, keep_stat)
+
+    def keep_stat(rows, mean, recip_std):
+        stat1[0, rows, :] = spread(mean)
+        stat1[1, rows, :] = spread(recip_std)
+
+    for par, hat in enumerate((hat0, hat1)):
+        if par:
+            hat_pass(lambda rows: x1[rows, :], hat1, keep_stat)
         gain = gain_row(wout, par)
 
-        def step(rows, gain=gain):
+        def step(rows, gain=gain, hat=hat):
             normed[rows, :] = (hat[rows, :] * gain).astype(BF16)
 
         over_rows(step)
         pre[par] = dot(normed[...], win[par].reshape(D, R))
         act = gelu_parts(pre[par])[1]
-        layer_out(lambda cols: x_at(slice(None), cols), act, wout, par, x2 if par else x1)
+        if par:
+            layer_out(lambda cols: x1[:, cols], act, wout, par, x2)
+        else:
+            layer_out(lambda cols: xs[zl, c, :, cols], act, wout, par, x1)
 
 
 def kernel_high(s_ref, x2, cots, *refs):
@@ -224,27 +246,27 @@
     )
 
 
-def kernel_low_back(s_ref, xs, x1, up2, win, wout, stats, pre, acts, hat, up1, gnorm, gsum):
+def kernel_low_back(s_ref, xs, x1, up2, win, wout, stat0, stat1, pre, acts, hat, up1, gnorm, gsum):
     c, zl = s_ref[2], s_ref[3]
-    for par, up, up_out in ((1, up2, up1), (0, up1, None)):
+    for par, stat, up, up_out in ((1, stat1, up2, up1), (0, stat0, up1, None)):
         gain = gain_row(wout, par)
         slot = jnp.where(c == par, 0, 1)
 
-        def step(rows, par=par, gain=gain, slot=slot):
+        def step(rows, par=par, stat=stat, gain=gain, slot=slot):
             xf = (x1[rows, :] if par else xs[zl, c, rows, :]).astype(F32)
-            hatted = (xf - stats[par, 0, rows, 0:1]) * stats[par, 1, rows, 0:1]
+            hatted = (xf - stat[0, rows, 0:1]) * stat[1, rows, 0:1]
             hat[rows, :] = hatted
             acts[slot, rows, 0:D] = (hatted * gain).astype(BF16)
 
         over_rows(step)
         layer_back(
             lambda rows, cols, up=up: up[rows, cols],
-            acts, slot, hat, lambda rows, par=par: stats[par, 1, rows, 0:1],
+            acts, slot, hat, lambda rows, stat=stat: stat[1, rows, 0:1],
             pre[par], win, wout, par, gain, gnorm, gsum, up_out,
         )
 
 
-def kernel_grads(s_ref, acts, got, out, up, down):
+def kernel_grads(s_ref, acts, got, out, *pieces):
     mx, my, c = s_ref[0], s_ref[1], s_ref[2]
     places = []
     for xy in range(16):
@@ -271,8 +293,12 @@
         out[places[xy], 16] = jnp.concatenate([part, part], axis=1).astype(BF16)
 
 
-    up[...] = out[8:10]
-    down[...] = out[10:12]
+    if len(pieces) == 2:
+        pieces[0][...] = out[8:10]
+        pieces[1][...] = out[10:12]
+    else:
+        for k in range(3):
+            pieces[k][...] = out[4 * k + 4 : 4 * k + 8]
 
 
 def over_groups(step):
@@ -294,12 +320,15 @@
     over_groups(step)
 
 
-def kernel_sum(s_ref, own, a, b, *pieces):
+def kernel_sum(s_ref, own, *refs):
+    got, pieces = refs[:-4], refs[-4:]
+
     def step(g):
         for k in range(4):
-            pieces[k][g] = (
-                own[k, g].astype(F32) + a[k, g].astype(F32) + b[k, g].astype(F32)
-            ).astype(BF16)
+            total = own[k, g].astype(F32)
+            for part in got:
+                total += part[k, g].astype(F32)
+            pieces[k][g] = total.astype(BF16)
 
     over_groups(step)
 
@@ -363,6 +392,14 @@
     return grads, shift(up, send_first(1)), shift(down, send_first(-1))
 
 
+def scatter_direct(scalars, acts, got):
+    row = array(4, 17, 16, 256)
+    grads, *pieces = call(
+        kernel_grads, scalars, [acts, got], [array(16, 17, 16, 256)] + [row] * 3, []
+    )
+    return [grads] + [shift(pieces[k - 1], send_first(k)) for k in (2, 1, 3)]
+
+
 def scatter_sides(scalars, grads, up, down):
     row = array(4, 17, 16, 256)
     after, before = call(kernel_sides, scalars, [grads, up, down], [row, row], [])
@@ -379,17 +416,8 @@
 def device_body(inputs, cotangent, norm_gain, proj_in, proj_out):
     where = [lax.axis_index(n).astype(jnp.int32) for n in ("x", "y", "c", "zl")]
     scalars = jnp.stack(where)
-    shard = jnp.concatenate(
-        [
-            proj_in[0],
-            proj_out[0].reshape(4, 8, 256).transpose(1, 0, 2).reshape(32, 256),
-            jnp.pad(norm_gain, ((0, 7), (0, 224))),
-        ],
-        axis=0,
-    )
-    column = lax.all_to_all(
-        jnp.broadcast_to(shard[None], (8, 72, 256)), ("zl", "zh"), 0, 0
-    ).reshape(2, 4, 72, 256)
+    shard = call(kernel_pack, scalars, [norm_gain, proj_in, proj_out], array(8, 72, 256), [])
+    column = lax.all_to_all(shard, ("zl", "zh"), 0, 0).reshape(2, 4, 72, 256)
     gain = jnp.pad(column[:, :, 64, :32].reshape(2, 1, 1, 128), ((0, 0), (0, 0), (0, 15), (0, 128)))
     block = jnp.concatenate(
         [
@@ -399,6 +427,9 @@
         ],
         axis=1,
     )
+    hat0, stat0 = call(
+        kernel_stats, scalars, [inputs], [array(*ACT, kind=F32), array(2, ROWS, 128, kind=F32)], []
+    )
     near = []
     for p in range(2):
         near.append([block[p]] + [shift(block[p], send_first(-k)) for k in (1, 2, 3)])
@@ -407,13 +438,13 @@
         row = jnp.stack(near[p])
         rows = [row] + [shift(row, send_second(-k)) for k in (1, 2, 3)]
         pairs.append(rows + [shift(v, SWAP) for v in rows])
-    x1, x2, win, wout, stats, pre = call(
+    x1, x2, win, wout, stat1, pre = call(
         kernel_low_forward,
         scalars,
-        [inputs, *pairs[0]],
+        [inputs, hat0, *pairs[0]],
         [
             array(*ACT), array(*ACT), array(*WIN), array(*WOUT),
-            array(2, 2, ROWS, 128, kind=F32), array(2, ROWS, R, kind=F32),
+            array(2, ROWS, 128, kind=F32), array(2, ROWS, R, kind=F32),
         ],
         LOW_SCRATCH,
     )
@@ -424,14 +455,13 @@
     acts0 = call(
         kernel_low_back,
         scalars,
-        [inputs, x1, up2, win, wout, stats, pre],
+        [inputs, x1, up2, win, wout, stat0, stat1, pre],
         array(*ACTS),
         BACK_SCRATCH,
     )
     got0 = shift(acts0[1], SWAP)
-    first1 = scatter_first(scalars, acts1, got1)
+    sides1 = scatter_direct(scalars, acts1, got1)
     first0 = scatter_first(scalars, acts0, got0)
-    sides1 = scatter_sides(scalars, *first1)
     sides0 = scatter_sides(scalars, *first0)
     high = scatter_second(scalars, sides1)
     low = scatter_second(scalars, sides0)

time: 162 us -> 153 us (0.944); the launches traced: 158 us -> 152 us
  local copies, waits for them, and re-layouts: 11 us -> 2.85 us
  starting transfers between devices: 35.6 us -> 39.4 us
    unnamed x26 -> x11, local copies, waits for them, and re-layouts: 10.3 us -> 2.21 us
    ppermute x36 -> x35, starting transfers between devices: 35.6 us -> 39.4 us  [shift(): return lax.ppermute(value, AXES, pairs)]
    pallas_call x10 -> x11, Pallas kernels: 21 us -> 19.4 us  [call(): pl.pallas_call(body, in_specs=[pl.BlockSpec(memory_space=pltpu.SMEM)] + [...]
    ppermute x36 -> x35, waiting for transfers between devices: 56.8 us -> 57.1 us  [shift(): return lax.ppermute(value, AXES, pairs)]
  transfers between devices with their start and end apart: 36 -> 35, of which waited for: 16 -> 13; matrix products, arithmetic and copies ran while one was open for 0% -> 0% of each run, Pallas kernels for 6% -> 6%
where the time goes in v5:
time: 153 us; the launch traced here: 152 us
  waiting for transfers between devices  57.1 us (37%)
  starting transfers between devices  39.4 us (26%)
  blocking collectives  32.1 us (21%)
  Pallas kernels  19.4 us (13%)
  local copies, waits for them, and re-layouts  2.85 us (2%)
    ppermute x35, waiting for transfers between devices, shift(): return lax.ppermute(value, AXES, pairs)  57.1 us
    ppermute x35, starting transfers between devices, shift(): return lax.ppermute(value, AXES, pairs)  39.4 us
    all_to_all x1, blocking collectives, device_body(): column = lax.all_to_all(shard, ('zl', 'zh'), 0, 0).reshape(2, 4, 72, 256)  19.5 us
    pallas_call x11, Pallas kernels, call(): pl.pallas_call(body, in_specs=[pl.BlockSpec(memory_space=pltpu.SMEM)] + [...  19.4 us
    all_to_all x1, blocking collectives, device_body(): lax.all_to_all(parts, ('zl', 'zh'), 0, 0)  12.6 us
  transfers between devices with their start and end apart: 35, of which 13 were waited for; matrix products, arithmetic and copies ran while one was open for 0% of the time, Pallas kernels for 6%

profile of v5, /device:TPU:32, one launch (start us, length us, event | category | flops | bytes accessed | tf_op | source)
XLA Modules:
  0.0 152.2 jit_solution(16091862228570872924)
XLA Ops:
  0.7 0.7 copy-done.2
  1.4 0.7 copy-done.3
  2.2 0.7 copy-done.4
  2.8 0.6 shard_map.77
  3.4 19.5 %all_to_all.10 = bf16[8,72,256]{2,1,0:T(8,128)(2,1)S(1)} all-to-all(bf16[8,72,256]{2,1,0:T(8,128)(2,1)S(1)} %shard_map.77), channel_id=1, replica_groups=mesh['zl'=2,'c'=2,'x'=4,'y'=4,'zh'=4] {'zl','zh'}, dimensions={0} | all-to-all | bytes 589824 | tf_op jit(solution)/shard_map/all_to_all | solution.py:420
  23.3 3.1 %collective-permute-start.1 = (bf16[17,16,256]{2,1,0:T(8,128)(2,1)S(1)}, bf16[17,16,256]{2,1,0:T(8,128)(2,1)S(1)}, u32[]{:S(2)}, u32[]{:S(2)}) collective-permute-start(bf16[17,16,256]{2,1,0:T(8,128)(2,1)S(1)} %get-tuple-element.62), channel_id=1, source_target_pairs={{0,32},{1,33},{2,34},{3,35},{4,36},{5,37},{6,38},{7,39},{8,40},{9,... | collective-permute-start | bytes 417800 | tf_op jit(solution)/shard_map/ppermute | solution.py:52
  26.4 0.6 collective-permute-start.2
  27.0 2.6 %collective-permute-start = (bf16[17,16,256]{2,1,0:T(8,128)(2,1)S(1)}, bf16[17,16,256]{2,1,0:T(8,128)(2,1)S(1)}, u32[]{:S(2)}, u32[]{:S(2)}) collective-permute-start(bf16[17,16,256]{2,1,0:T(8,128)(2,1)S(1)} %get-tuple-element.62), channel_id=1, source_target_pairs={{0,48},{1,49},{2,50},{3,51},{4,52},{5,53},{6,54},{7,55},{8,56},{9,... | collective-permute-start | bytes 417800 | tf_op jit(solution)/shard_map/ppermute | solution.py:52
  29.9 2.7 %collective-permute-done.2 = bf16[17,16,256]{2,1,0:T(8,128)(2,1)S(1)} collective-permute-done((bf16[17,16,256]{2,1,0:T(8,128)(2,1)S(1)}, bf16[17,16,256]{2,1,0:T(8,128)(2,1)S(1)}, u32[]{:S(2)}, u32[]{:S(2)}) %collective-permute-start.2) | collective-permute-done | bytes 139296 | tf_op jit(solution)/shard_map/ppermute | solution.py:52
  32.8 3.1 %collective-permute-start.3 = (bf16[4,17,16,256]{3,2,1,0:T(8,128)(2,1)S(1)}, bf16[4,17,16,256]{3,2,1,0:T(8,128)(2,1)S(1)}, u32[]{:S(2)}, u32[]{:S(2)}) collective-permute-start(bf16[4,17,16,256]{3,2,1,0:T(8,128)(2,1)S(1)} %pad_maximum_fusion.refs_0_), channel_id=1, source_target_pairs={{0,12},{1,13},{2,14},{3,15},{4,0},{5,1},{6,2},{7,3},{8,4},{9,5},{1... | collective-permute-start | bytes 1671176 | tf_op jit(solution)/shard_map/ppermute | solution.py:52
  35.8 0.6 collective-permute-start.4
  36.5 1.0 collective-permute-start.5
  37.5 3.2 %collective-permute-start.10 = (bf16[17,16,256]{2,1,0:T(8,128)(2,1)S(1)}, bf16[17,16,256]{2,1,0:T(8,128)(2,1)S(1)}, u32[]{:S(2)}, u32[]{:S(2)}) collective-permute-start(bf16[17,16,256]{2,1,0:T(8,128)(2,1)S(1)} %get-tuple-element.63), channel_id=1, source_target_pairs={{0,48},{1,49},{2,50},{3,51},{4,52},{5,53},{6,54},{7,55},{8,56},{9,... | collective-permute-start | bytes 417800 | tf_op jit(solution)/shard_map/ppermute | solution.py:52
  40.7 6.7 %collective-permute-done.10 = bf16[17,16,256]{2,1,0:T(8,128)(2,1)S(1)} collective-permute-done((bf16[17,16,256]{2,1,0:T(8,128)(2,1)S(1)}, bf16[17,16,256]{2,1,0:T(8,128)(2,1)S(1)}, u32[]{:S(2)}, u32[]{:S(2)}) %collective-permute-start.10) | collective-permute-done | bytes 139296 | tf_op jit(solution)/shard_map/ppermute | solution.py:52
  47.4 6.6 %collective-permute-done.11 = bf16[17,16,256]{2,1,0:T(8,128)(2,1)S(1)} collective-permute-done((bf16[17,16,256]{2,1,0:T(8,128)(2,1)S(1)}, bf16[17,16,256]{2,1,0:T(8,128)(2,1)S(1)}, u32[]{:S(2)}, u32[]{:S(2)}) %collective-permute-start.11) | collective-permute-done | bytes 139296 | tf_op jit(solution)/shard_map/ppermute | solution.py:52
  54.0 1.0 collective-permute-start.12
  55.0 5.7 %collective-permute-done.12 = bf16[17,16,256]{2,1,0:T(8,128)(2,1)S(1)} collective-permute-done((bf16[17,16,256]{2,1,0:T(8,128)(2,1)S(1)}, bf16[17,16,256]{2,1,0:T(8,128)(2,1)S(1)}, u32[]{:S(2)}, u32[]{:S(2)}) %collective-permute-start.12) | collective-permute-done | bytes 139296 | tf_op jit(solution)/shard_map/ppermute | solution.py:52
  60.8 3.0 %collective-permute-start.13 = (bf16[4,17,16,256]{3,2,1,0:T(8,128)(2,1)S(1)}, bf16[4,17,16,256]{3,2,1,0:T(8,128)(2,1)S(1)}, u32[]{:S(2)}, u32[]{:S(2)}) collective-permute-start(bf16[4,17,16,256]{3,2,1,0:T(8,128)(2,1)S(1)} %pad_maximum_fusion.1.refs_0_), channel_id=1, source_target_pairs={{0,12},{1,13},{2,14},{3,15},{4,0},{5,1},{6,2},{7,3},{8,4},{9,5},{1... | collective-permute-start | bytes 1671176 | tf_op jit(solution)/shard_map/ppermute | solution.py:52
  63.8 1.0 collective-permute-start.15
  65.3 11.5 %collective-permute-done.13.refs_1_ = bf16[4,17,16,256]{3,2,1,0:T(8,128)(2,1)S(1)} collective-permute-done((bf16[4,17,16,256]{3,2,1,0:T(8,128)(2,1)S(1)}, bf16[4,17,16,256]{3,2,1,0:T(8,128)(2,1)S(1)}, u32[]{:S(2)}, u32[]{:S(2)}) %collective-permute-start.13) | collective-permute-done | bytes 557088 | tf_op jit(solution)/shard_map/ppermute | solution.py:52
  76.8 0.5 collective-permute-start.9
  77.3 3.3 %collective-permute-done.15.refs_3_ = bf16[4,17,16,256]{3,2,1,0:T(8,128)(2,1)S(1)} collective-permute-done((bf16[4,17,16,256]{3,2,1,0:T(8,128)(2,1)S(1)}, bf16[4,17,16,256]{3,2,1,0:T(8,128)(2,1)S(1)}, u32[]{:S(2)}, u32[]{:S(2)}) %collective-permute-start.15) | collective-permute-done | bytes 557088 | tf_op jit(solution)/shard_map/ppermute | solution.py:52
  80.6 0.5 collective-permute-start.18
  81.2 0.9 shard_map.76
  82.1 2.9 %shard_map.78 = (bf16[128,2048]{1,0:T(8,128)(2,1)S(1)}, bf16[128,2048]{1,0:T(8,128)(2,1)S(1)}, bf16[2,128,16,256]{3,2,1,0:T(8,128)(2,1)S(1)}, bf16[2,9,16,16,256...) custom-call(s32[4]{0:T(128)S(1)} %pad_add_fusion.s_ref, ...), custom_call_target="tpu_custom_call" | custom-call | tf_op jit(solution)/shard_map/pallas_call | solution.py:373
  85.1 5.2 %shard_map.79 = (bf16[128,2048]{1,0:T(8,128)(2,1)S(1)}, bf16[2,144,4608]{2,1,0:T(8,128)(2,1)S(1)}) custom-call(s32[4]{0:T(128)S(1)} %pad_add_fusion.s_ref, bf16[128,2048]{1,0:T(8,128)(2,1)S(1)} %get-tuple-element.32.x2, bf16[2,2,128,2048]{3,2,1,0:T(8,128)(2,1)S(1)} %copy-done.1, bf16[4,17,16,256]{3,2,1,0:T(8,128)(2,1)S(1)} %pad_maximum_fusion.1.refs_0_, ...), custom_call_target="tpu_custom_call" | custom-call | tf_op jit(solution)/shard_map/pallas_call | solution.py:373
  90.3 3.4 %shard_map.80.acts = bf16[2,144,4608]{2,1,0:T(8,128)(2,1)S(1)} custom-call(s32[4]{0:T(128)S(1)} %pad_add_fusion.s_ref, bf16[2,2,128,2048]{3,2,1,0:T(8,128)(2,1)S(1)} %copy-done, bf16[128,2048]{1,0:T(8,128)(2,1)S(1)} %get-tuple-element.31.x1, bf16[128,2048]{1,0:T(8,128)(2,1)S(1)} %get-tuple-element.33.up2, ...), custom_call_target="tpu_custom_call" | custom-call | tf_op jit(solution)/shard_map/pallas_call | solution.py:373
  94.6 2.4 %collective-permute-done.20.got = bf16[144,4608]{1,0:T(8,128)(2,1)S(1)} collective-permute-done((bf16[144,4608]{1,0:T(8,128)(2,1)S(1)}, bf16[144,4608]{1,0:T(8,128)(2,1)S(1)}, u32[]{:S(2)}, u32[]{:S(2)}) %collective-permute-start.20) | collective-permute-done | bytes 1327136 | tf_op jit(solution)/shard_map/ppermute | solution.py:52
  97.0 1.3 shard_map.81
  98.5 3.2 %collective-permute-start.22 = (bf16[2,17,16,256]{3,2,1,0:T(8,128)(2,1)S(1)}, bf16[2,17,16,256]{3,2,1,0:T(8,128)(2,1)S(1)}, u32[]{:S(2)}, u32[]{:S(2)}) collective-permute-start(bf16[2,17,16,256]{3,2,1,0:T(8,128)(2,1)S(1)} %get-tuple-element.41), channel_id=1, source_target_pairs={{0,48},{1,49},{2,50},{3,51},{4,52},{5,53},{6,54},{7,55},{8,56},{9,... | collective-permute-start | bytes 835592 | tf_op jit(solution)/shard_map/ppermute | solution.py:52
  101.7 1.4 shard_map.84
  103.4 1.4 collective-permute-start.30
  104.9 1.8 %collective-permute-start.31 = (bf16[4,17,16,256]{3,2,1,0:T(8,128)(2,1)S(1)}, bf16[4,17,16,256]{3,2,1,0:T(8,128)(2,1)S(1)}, u32[]{:S(2)}, u32[]{:S(2)}) collective-permute-start(bf16[4,17,16,256]{3,2,1,0:T(8,128)(2,1)S(1)} %get-tuple-element.52), channel_id=1, source_target_pairs={{0,48},{1,49},{2,50},{3,51},{4,52},{5,53},{6,54},{7,55},{8,56},{9,... | collective-permute-start | bytes 1671176 | tf_op jit(solution)/shard_map/ppermute | solution.py:52
  106.7 5.1 %collective-permute-done.22.down = bf16[2,17,16,256]{3,2,1,0:T(8,128)(2,1)S(1)} collective-permute-done((bf16[2,17,16,256]{3,2,1,0:T(8,128)(2,1)S(1)}, bf16[2,17,16,256]{3,2,1,0:T(8,128)(2,1)S(1)}, u32[]{:S(2)}, u32[]{:S(2)}) %collective-permute-start.22) | collective-permute-done | bytes 278560 | tf_op jit(solution)/shard_map/ppermute | solution.py:52
  111.7 0.7 shard_map.82
  112.6 3.7 %collective-permute-start.24 = (bf16[4,17,16,256]{3,2,1,0:T(8,128)(2,1)S(1)}, bf16[4,17,16,256]{3,2,1,0:T(8,128)(2,1)S(1)}, u32[]{:S(2)}, u32[]{:S(2)}) collective-permute-start(bf16[4,17,16,256]{3,2,1,0:T(8,128)(2,1)S(1)} %get-tuple-element.43), channel_id=1, source_target_pairs={{0,48},{1,49},{2,50},{3,51},{4,52},{5,53},{6,54},{7,55},{8,56},{9,... | collective-permute-start | bytes 1671176 | tf_op jit(solution)/shard_map/ppermute | solution.py:52
  116.3 3.8 %collective-permute-done.30.refs_1_ = bf16[4,17,16,256]{3,2,1,0:T(8,128)(2,1)S(1)} collective-permute-done((bf16[4,17,16,256]{3,2,1,0:T(8,128)(2,1)S(1)}, bf16[4,17,16,256]{3,2,1,0:T(8,128)(2,1)S(1)}, u32[]{:S(2)}, u32[]{:S(2)}) %collective-permute-start.30) | collective-permute-done | bytes 557088 | tf_op jit(solution)/shard_map/ppermute | solution.py:52
  120.2 0.9 shard_map.85
  121.4 1.7 %collective-permute-start.33 = (bf16[17,16,256]{2,1,0:T(8,128)(2,1)S(1)}, bf16[17,16,256]{2,1,0:T(8,128)(2,1)S(1)}, u32[]{:S(2)}, u32[]{:S(2)}) collective-permute-start(bf16[17,16,256]{2,1,0:T(8,128)(2,1)S(1)} %get-tuple-element.55), channel_id=1, source_target_pairs={{0,4},{1,5},{2,6},{3,7},{4,8},{5,9},{6,10},{7,11},{8,12},{9,13},{1... | collective-permute-start | bytes 417800 | tf_op jit(solution)/shard_map/ppermute | solution.py:52
  123.1 1.5 collective-permute-start.34
  124.6 4.5 %collective-permute-done.23.refs_0_ = bf16[4,17,16,256]{3,2,1,0:T(8,128)(2,1)S(1)} collective-permute-done((bf16[4,17,16,256]{3,2,1,0:T(8,128)(2,1)S(1)}, bf16[4,17,16,256]{3,2,1,0:T(8,128)(2,1)S(1)}, u32[]{:S(2)}, u32[]{:S(2)}) %collective-permute-start.23) | collective-permute-done | bytes 557088 | tf_op jit(solution)/shard_map/ppermute | solution.py:52
  129.1 0.8 shard_map.83
  130.2 1.6 %collective-permute-start.26 = (bf16[17,16,256]{2,1,0:T(8,128)(2,1)S(1)}, bf16[17,16,256]{2,1,0:T(8,128)(2,1)S(1)}, u32[]{:S(2)}, u32[]{:S(2)}) collective-permute-start(bf16[17,16,256]{2,1,0:T(8,128)(2,1)S(1)} %get-tuple-element.46), channel_id=1, source_target_pairs={{0,4},{1,5},{2,6},{3,7},{4,8},{5,9},{6,10},{7,11},{8,12},{9,13},{1... | collective-permute-start | bytes 417800 | tf_op jit(solution)/shard_map/ppermute | solution.py:52
  131.9 1.6 %collective-permute-start.27 = (bf16[17,16,256]{2,1,0:T(8,128)(2,1)S(1)}, bf16[17,16,256]{2,1,0:T(8,128)(2,1)S(1)}, u32[]{:S(2)}, u32[]{:S(2)}) collective-permute-start(bf16[17,16,256]{2,1,0:T(8,128)(2,1)S(1)} %get-tuple-element.47), channel_id=1, source_target_pairs={{0,12},{1,13},{2,14},{3,15},{4,0},{5,1},{6,2},{7,3},{8,4},{9,5},{1... | collective-permute-start | bytes 417800 | tf_op jit(solution)/shard_map/ppermute | solution.py:52
  133.6 3.1 %collective-permute-done.25 = bf16[17,16,256]{2,1,0:T(8,128)(2,1)S(1)} collective-permute-done((bf16[17,16,256]{2,1,0:T(8,128)(2,1)S(1)}, bf16[17,16,256]{2,1,0:T(8,128)(2,1)S(1)}, u32[]{:S(2)}, u32[]{:S(2)}) %collective-permute-start.25) | collective-permute-done | bytes 139296 | tf_op jit(solution)/shard_map/ppermute | solution.py:52
  136.7 1.3 collective-permute-done.26
  138.4 12.6 %all_to_all.11.parts = bf16[8,72,256]{2,1,0:T(8,128)(2,1)S(1)} all-to-all(bf16[8,72,256]{2,1,0:T(8,128)(2,1)S(1)} %pad_maximum_fusion.2), channel_id=1, replica_groups=mesh['zl'=2,'c'=2,'x'=4,'y'=4,'zh'=4] {'zl','zh'}, dimensions={0} | all-to-all | bytes 589824 | tf_op jit(solution)/shard_map/all_to_all | solution.py:480
  151.0 1.2 shard_map.86
  (68 shorter events, 4.0 us)
Async XLA Ops:
  0.7 0.7 copy-start.2
  1.4 0.7 copy-start.3
  2.2 0.7 copy-start.4
  23.0 58.2 %copy-start = (bf16[2,2,128,2048]{3,2,1,0:T(8,128)(2,1)S(1)}, bf16[2,2,128,2048]{3,2,1,0:T(8,128)(2,1)}, u32[]{:S(2)}) copy-start(bf16[2,2,128,2048]{3,2,1,0:T(8,128)(2,1)} %xs.5) | copy-start | bytes 6291460
  23.3 6.6 %collective-permute-start.1 = (bf16[17,16,256]{2,1,0:T(8,128)(2,1)S(1)}, bf16[17,16,256]{2,1,0:T(8,128)(2,1)S(1)}, u32[]{:S(2)}, u32[]{:S(2)}) collective-permute-start(bf16[17,16,256]{2,1,0:T(8,128)(2,1)S(1)} %get-tuple-element.62), channel_id=1, source_target_pairs={{0,32},{1,33},{2,34},{3,35},{4,36},{5,37},{6,38},{7,39},{8,40},{9,... | collective-permute-start | bytes 417800 | tf_op jit(solution)/shard_map/ppermute | solution.py:52
  26.4 6.3 %collective-permute-start.2 = (bf16[17,16,256]{2,1,0:T(8,128)(2,1)S(1)}, bf16[17,16,256]{2,1,0:T(8,128)(2,1)S(1)}, u32[]{:S(2)}, u32[]{:S(2)}) collective-permute-start(bf16[17,16,256]{2,1,0:T(8,128)(2,1)S(1)} %get-tuple-element.62), channel_id=1, source_target_pairs={{0,16},{1,17},{2,18},{3,19},{4,20},{5,21},{6,22},{7,23},{8,24},{9,... | collective-permute-start | bytes 417800 | tf_op jit(solution)/shard_map/ppermute | solution.py:52
  27.0 5.7 %collective-permute-start = (bf16[17,16,256]{2,1,0:T(8,128)(2,1)S(1)}, bf16[17,16,256]{2,1,0:T(8,128)(2,1)S(1)}, u32[]{:S(2)}, u32[]{:S(2)}) collective-permute-start(bf16[17,16,256]{2,1,0:T(8,128)(2,1)S(1)} %get-tuple-element.62), channel_id=1, source_target_pairs={{0,48},{1,49},{2,50},{3,51},{4,52},{5,53},{6,54},{7,55},{8,56},{9,... | collective-permute-start | bytes 417800 | tf_op jit(solution)/shard_map/ppermute | solution.py:52
  32.8 31.1 %collective-permute-start.3 = (bf16[4,17,16,256]{3,2,1,0:T(8,128)(2,1)S(1)}, bf16[4,17,16,256]{3,2,1,0:T(8,128)(2,1)S(1)}, u32[]{:S(2)}, u32[]{:S(2)}) collective-permute-start(bf16[4,17,16,256]{3,2,1,0:T(8,128)(2,1)S(1)} %pad_maximum_fusion.refs_0_), channel_id=1, source_target_pairs={{0,12},{1,13},{2,14},{3,15},{4,0},{5,1},{6,2},{7,3},{8,4},{9,5},{1... | collective-permute-start | bytes 1671176 | tf_op jit(solution)/shard_map/ppermute | solution.py:52
  35.8 28.0 %collective-permute-start.4 = (bf16[4,17,16,256]{3,2,1,0:T(8,128)(2,1)S(1)}, bf16[4,17,16,256]{3,2,1,0:T(8,128)(2,1)S(1)}, u32[]{:S(2)}, u32[]{:S(2)}) collective-permute-start(bf16[4,17,16,256]{3,2,1,0:T(8,128)(2,1)S(1)} %pad_maximum_fusion.refs_0_), channel_id=1, source_target_pairs={{0,8},{1,9},{2,10},{3,11},{4,12},{5,13},{6,14},{7,15},{8,0},{9,1},... | collective-permute-start | bytes 1671176 | tf_op jit(solution)/shard_map/ppermute | solution.py:52
  36.5 28.3 %collective-permute-start.5 = (bf16[4,17,16,256]{3,2,1,0:T(8,128)(2,1)S(1)}, bf16[4,17,16,256]{3,2,1,0:T(8,128)(2,1)S(1)}, u32[]{:S(2)}, u32[]{:S(2)}) collective-permute-start(bf16[4,17,16,256]{3,2,1,0:T(8,128)(2,1)S(1)} %pad_maximum_fusion.refs_0_), channel_id=1, source_target_pairs={{0,4},{1,5},{2,6},{3,7},{4,8},{5,9},{6,10},{7,11},{8,12},{9,13},{1... | collective-permute-start | bytes 1671176 | tf_op jit(solution)/shard_map/ppermute | solution.py:52
  37.4 27.3 %collective-permute-start.6 = (bf16[4,17,16,256]{3,2,1,0:T(8,128)(2,1)S(1)}, bf16[4,17,16,256]{3,2,1,0:T(8,128)(2,1)S(1)}, u32[]{:S(2)}, u32[]{:S(2)}) collective-permute-start(bf16[4,17,16,256]{3,2,1,0:T(8,128)(2,1)S(1)} %pad_maximum_fusion.refs_0_), channel_id=1, source_target_pairs={{0,64},{1,65},{2,66},{3,67},{4,68},{5,69},{6,70},{7,71},{8,72},{9,... | collective-permute-start | bytes 1671176 | tf_op jit(solution)/shard_map/ppermute | solution.py:52
  37.5 10.0 %collective-permute-start.10 = (bf16[17,16,256]{2,1,0:T(8,128)(2,1)S(1)}, bf16[17,16,256]{2,1,0:T(8,128)(2,1)S(1)}, u32[]{:S(2)}, u32[]{:S(2)}) collective-permute-start(bf16[17,16,256]{2,1,0:T(8,128)(2,1)S(1)} %get-tuple-element.63), channel_id=1, source_target_pairs={{0,48},{1,49},{2,50},{3,51},{4,52},{5,53},{6,54},{7,55},{8,56},{9,... | collective-permute-start | bytes 417800 | tf_op jit(solution)/shard_map/ppermute | solution.py:52
  47.4 6.6 %collective-permute-start.11 = (bf16[17,16,256]{2,1,0:T(8,128)(2,1)S(1)}, bf16[17,16,256]{2,1,0:T(8,128)(2,1)S(1)}, u32[]{:S(2)}, u32[]{:S(2)}) collective-permute-start(bf16[17,16,256]{2,1,0:T(8,128)(2,1)S(1)} %get-tuple-element.63), channel_id=1, source_target_pairs={{0,32},{1,33},{2,34},{3,35},{4,36},{5,37},{6,38},{7,39},{8,40},{9,... | collective-permute-start | bytes 417800 | tf_op jit(solution)/shard_map/ppermute | solution.py:52
  54.0 6.7 %collective-permute-start.12 = (bf16[17,16,256]{2,1,0:T(8,128)(2,1)S(1)}, bf16[17,16,256]{2,1,0:T(8,128)(2,1)S(1)}, u32[]{:S(2)}, u32[]{:S(2)}) collective-permute-start(bf16[17,16,256]{2,1,0:T(8,128)(2,1)S(1)} %get-tuple-element.63), channel_id=1, source_target_pairs={{0,16},{1,17},{2,18},{3,19},{4,20},{5,21},{6,22},{7,23},{8,24},{9,... | collective-permute-start | bytes 417800 | tf_op jit(solution)/shard_map/ppermute | solution.py:52
  60.8 16.0 %collective-permute-start.13 = (bf16[4,17,16,256]{3,2,1,0:T(8,128)(2,1)S(1)}, bf16[4,17,16,256]{3,2,1,0:T(8,128)(2,1)S(1)}, u32[]{:S(2)}, u32[]{:S(2)}) collective-permute-start(bf16[4,17,16,256]{3,2,1,0:T(8,128)(2,1)S(1)} %pad_maximum_fusion.1.refs_0_), channel_id=1, source_target_pairs={{0,12},{1,13},{2,14},{3,15},{4,0},{5,1},{6,2},{7,3},{8,4},{9,5},{1... | collective-permute-start | bytes 1671176 | tf_op jit(solution)/shard_map/ppermute | solution.py:52
  63.8 13.0 %collective-permute-start.14 = (bf16[4,17,16,256]{3,2,1,0:T(8,128)(2,1)S(1)}, bf16[4,17,16,256]{3,2,1,0:T(8,128)(2,1)S(1)}, u32[]{:S(2)}, u32[]{:S(2)}) collective-permute-start(bf16[4,17,16,256]{3,2,1,0:T(8,128)(2,1)S(1)} %pad_maximum_fusion.1.refs_0_), channel_id=1, source_target_pairs={{0,8},{1,9},{2,10},{3,11},{4,12},{5,13},{6,14},{7,15},{8,0},{9,1},... | collective-permute-start | bytes 1671176 | tf_op jit(solution)/shard_map/ppermute | solution.py:52
  63.8 16.8 %collective-permute-start.15 = (bf16[4,17,16,256]{3,2,1,0:T(8,128)(2,1)S(1)}, bf16[4,17,16,256]{3,2,1,0:T(8,128)(2,1)S(1)}, u32[]{:S(2)}, u32[]{:S(2)}) collective-permute-start(bf16[4,17,16,256]{3,2,1,0:T(8,128)(2,1)S(1)} %pad_maximum_fusion.1.refs_0_), channel_id=1, source_target_pairs={{0,4},{1,5},{2,6},{3,7},{4,8},{5,9},{6,10},{7,11},{8,12},{9,13},{1... | collective-permute-start | bytes 1671176 | tf_op jit(solution)/shard_map/ppermute | solution.py:52
  64.8 15.8 %collective-permute-start.7 = (bf16[4,17,16,256]{3,2,1,0:T(8,128)(2,1)S(1)}, bf16[4,17,16,256]{3,2,1,0:T(8,128)(2,1)S(1)}, u32[]{:S(2)}, u32[]{:S(2)}) collective-permute-start(bf16[4,17,16,256]{3,2,1,0:T(8,128)(2,1)S(1)} %collective-permute-done.3.refs_1_), channel_id=1, source_target_pairs={{0,64},{1,65},{2,66},{3,67},{4,68},{5,69},{6,70},{7,71},{8,72},{9,... | collective-permute-start | bytes 1671176 | tf_op jit(solution)/shard_map/ppermute | solution.py:52
  64.8 16.3 %collective-permute-start.8 = (bf16[4,17,16,256]{3,2,1,0:T(8,128)(2,1)S(1)}, bf16[4,17,16,256]{3,2,1,0:T(8,128)(2,1)S(1)}, u32[]{:S(2)}, u32[]{:S(2)}) collective-permute-start(bf16[4,17,16,256]{3,2,1,0:T(8,128)(2,1)S(1)} %collective-permute-done.4.refs_2_), channel_id=1, source_target_pairs={{0,64},{1,65},{2,66},{3,67},{4,68},{5,69},{6,70},{7,71},{8,72},{9,... | collective-permute-start | bytes 1671176 | tf_op jit(solution)/shard_map/ppermute | solution.py:52
  76.8 8.2 %collective-permute-start.16 = (bf16[4,17,16,256]{3,2,1,0:T(8,128)(2,1)S(1)}, bf16[4,17,16,256]{3,2,1,0:T(8,128)(2,1)S(1)}, u32[]{:S(2)}, u32[]{:S(2)}) collective-permute-start(bf16[4,17,16,256]{3,2,1,0:T(8,128)(2,1)S(1)} %pad_maximum_fusion.1.refs_0_), channel_id=1, source_target_pairs={{0,64},{1,65},{2,66},{3,67},{4,68},{5,69},{6,70},{7,71},{8,72},{9,... | collective-permute-start | bytes 1671176 | tf_op jit(solution)/shard_map/ppermute | solution.py:52
  76.8 5.3 %collective-permute-start.9 = (bf16[4,17,16,256]{3,2,1,0:T(8,128)(2,1)S(1)}, bf16[4,17,16,256]{3,2,1,0:T(8,128)(2,1)S(1)}, u32[]{:S(2)}, u32[]{:S(2)}) collective-permute-start(bf16[4,17,16,256]{3,2,1,0:T(8,128)(2,1)S(1)} %collective-permute-done.5.refs_3_), channel_id=1, source_target_pairs={{0,64},{1,65},{2,66},{3,67},{4,68},{5,69},{6,70},{7,71},{8,72},{9,... | collective-permute-start | bytes 1671176 | tf_op jit(solution)/shard_map/ppermute | solution.py:52
  80.6 4.4 %collective-permute-start.17 = (bf16[4,17,16,256]{3,2,1,0:T(8,128)(2,1)S(1)}, bf16[4,17,16,256]{3,2,1,0:T(8,128)(2,1)S(1)}, u32[]{:S(2)}, u32[]{:S(2)}) collective-permute-start(bf16[4,17,16,256]{3,2,1,0:T(8,128)(2,1)S(1)} %collective-permute-done.13.refs_1_), channel_id=1, source_target_pairs={{0,64},{1,65},{2,66},{3,67},{4,68},{5,69},{6,70},{7,71},{8,72},{9,... | collective-permute-start | bytes 1671176 | tf_op jit(solution)/shard_map/ppermute | solution.py:52
  80.6 4.5 %collective-permute-start.18 = (bf16[4,17,16,256]{3,2,1,0:T(8,128)(2,1)S(1)}, bf16[4,17,16,256]{3,2,1,0:T(8,128)(2,1)S(1)}, u32[]{:S(2)}, u32[]{:S(2)}) collective-permute-start(bf16[4,17,16,256]{3,2,1,0:T(8,128)(2,1)S(1)} %collective-permute-done.14.refs_2_), channel_id=1, source_target_pairs={{0,64},{1,65},{2,66},{3,67},{4,68},{5,69},{6,70},{7,71},{8,72},{9,... | collective-permute-start | bytes 1671176 | tf_op jit(solution)/shard_map/ppermute | solution.py:52
  81.1 4.0 %collective-permute-start.19 = (bf16[4,17,16,256]{3,2,1,0:T(8,128)(2,1)S(1)}, bf16[4,17,16,256]{3,2,1,0:T(8,128)(2,1)S(1)}, u32[]{:S(2)}, u32[]{:S(2)}) collective-permute-start(bf16[4,17,16,256]{3,2,1,0:T(8,128)(2,1)S(1)} %collective-permute-done.15.refs_3_), channel_id=1, source_target_pairs={{0,64},{1,65},{2,66},{3,67},{4,68},{5,69},{6,70},{7,71},{8,72},{9,... | collective-permute-start | bytes 1671176 | tf_op jit(solution)/shard_map/ppermute | solution.py:52
  82.1 3.0 %copy-start.1 = (bf16[2,2,128,2048]{3,2,1,0:T(8,128)(2,1)S(1)}, bf16[2,2,128,2048]{3,2,1,0:T(8,128)(2,1)}, u32[]{:S(2)}) copy-start(bf16[2,2,128,2048]{3,2,1,0:T(8,128)(2,1)} %cots.1) | copy-start | bytes 6291460
  93.8 3.2 %collective-permute-start.20 = (bf16[144,4608]{1,0:T(8,128)(2,1)S(1)}, bf16[144,4608]{1,0:T(8,128)(2,1)S(1)}, u32[]{:S(2)}, u32[]{:S(2)}) collective-permute-start(bf16[144,4608]{1,0:T(8,128)(2,1)S(1)} %slice_bitcast_fusion), channel_id=1, source_target_pairs={{0,64},{1,65},{2,66},{3,67},{4,68},{5,69},{6,70},{7,71},{8,72},{9,... | collective-permute-start | bytes 3981320 | tf_op jit(solution)/shard_map/ppermute | solution.py:52
  94.4 7.3 %collective-permute-start.28 = (bf16[144,4608]{1,0:T(8,128)(2,1)S(1)}, bf16[144,4608]{1,0:T(8,128)(2,1)S(1)}, u32[]{:S(2)}, u32[]{:S(2)}) collective-permute-start(bf16[144,4608]{1,0:T(8,128)(2,1)S(1)} %slice_bitcast_fusion.1), channel_id=1, source_target_pairs={{0,64},{1,65},{2,66},{3,67},{4,68},{5,69},{6,70},{7,71},{8,72},{9,... | collective-permute-start | bytes 3981320 | tf_op jit(solution)/shard_map/ppermute | solution.py:52
  98.4 8.3 %collective-permute-start.21 = (bf16[2,17,16,256]{3,2,1,0:T(8,128)(2,1)S(1)}, bf16[2,17,16,256]{3,2,1,0:T(8,128)(2,1)S(1)}, u32[]{:S(2)}, u32[]{:S(2)}) collective-permute-start(bf16[2,17,16,256]{3,2,1,0:T(8,128)(2,1)S(1)} %get-tuple-element.40), channel_id=1, source_target_pairs={{0,16},{1,17},{2,18},{3,19},{4,20},{5,21},{6,22},{7,23},{8,24},{9,... | collective-permute-start | bytes 835592 | tf_op jit(solution)/shard_map/ppermute | solution.py:52
  98.5 13.3 %collective-permute-start.22 = (bf16[2,17,16,256]{3,2,1,0:T(8,128)(2,1)S(1)}, bf16[2,17,16,256]{3,2,1,0:T(8,128)(2,1)S(1)}, u32[]{:S(2)}, u32[]{:S(2)}) collective-permute-start(bf16[2,17,16,256]{3,2,1,0:T(8,128)(2,1)S(1)} %get-tuple-element.41), channel_id=1, source_target_pairs={{0,48},{1,49},{2,50},{3,51},{4,52},{5,53},{6,54},{7,55},{8,56},{9,... | collective-permute-start | bytes 835592 | tf_op jit(solution)/shard_map/ppermute | solution.py:52
  103.1 13.2 %collective-permute-start.29 = (bf16[4,17,16,256]{3,2,1,0:T(8,128)(2,1)S(1)}, bf16[4,17,16,256]{3,2,1,0:T(8,128)(2,1)S(1)}, u32[]{:S(2)}, u32[]{:S(2)}) collective-permute-start(bf16[4,17,16,256]{3,2,1,0:T(8,128)(2,1)S(1)} %get-tuple-element.50), channel_id=1, source_target_pairs={{0,32},{1,33},{2,34},{3,35},{4,36},{5,37},{6,38},{7,39},{8,40},{9,... | collective-permute-start | bytes 1671176 | tf_op jit(solution)/shard_map/ppermute | solution.py:52
  103.4 16.7 %collective-permute-start.30 = (bf16[4,17,16,256]{3,2,1,0:T(8,128)(2,1)S(1)}, bf16[4,17,16,256]{3,2,1,0:T(8,128)(2,1)S(1)}, u32[]{:S(2)}, u32[]{:S(2)}) collective-permute-start(bf16[4,17,16,256]{3,2,1,0:T(8,128)(2,1)S(1)} %get-tuple-element.51), channel_id=1, source_target_pairs={{0,16},{1,17},{2,18},{3,19},{4,20},{5,21},{6,22},{7,23},{8,24},{9,... | collective-permute-start | bytes 1671176 | tf_op jit(solution)/shard_map/ppermute | solution.py:52
  104.9 15.3 %collective-permute-start.31 = (bf16[4,17,16,256]{3,2,1,0:T(8,128)(2,1)S(1)}, bf16[4,17,16,256]{3,2,1,0:T(8,128)(2,1)S(1)}, u32[]{:S(2)}, u32[]{:S(2)}) collective-permute-start(bf16[4,17,16,256]{3,2,1,0:T(8,128)(2,1)S(1)} %get-tuple-element.52), channel_id=1, source_target_pairs={{0,48},{1,49},{2,50},{3,51},{4,52},{5,53},{6,54},{7,55},{8,56},{9,... | collective-permute-start | bytes 1671176 | tf_op jit(solution)/shard_map/ppermute | solution.py:52
  112.5 16.6 %collective-permute-start.23 = (bf16[4,17,16,256]{3,2,1,0:T(8,128)(2,1)S(1)}, bf16[4,17,16,256]{3,2,1,0:T(8,128)(2,1)S(1)}, u32[]{:S(2)}, u32[]{:S(2)}) collective-permute-start(bf16[4,17,16,256]{3,2,1,0:T(8,128)(2,1)S(1)} %get-tuple-element.42), channel_id=1, source_target_pairs={{0,16},{1,17},{2,18},{3,19},{4,20},{5,21},{6,22},{7,23},{8,24},{9,... | collective-permute-start | bytes 1671176 | tf_op jit(solution)/shard_map/ppermute | solution.py:52
  112.6 16.5 %collective-permute-start.24 = (bf16[4,17,16,256]{3,2,1,0:T(8,128)(2,1)S(1)}, bf16[4,17,16,256]{3,2,1,0:T(8,128)(2,1)S(1)}, u32[]{:S(2)}, u32[]{:S(2)}) collective-permute-start(bf16[4,17,16,256]{3,2,1,0:T(8,128)(2,1)S(1)} %get-tuple-element.43), channel_id=1, source_target_pairs={{0,48},{1,49},{2,50},{3,51},{4,52},{5,53},{6,54},{7,55},{8,56},{9,... | collective-permute-start | bytes 1671176 | tf_op jit(solution)/shard_map/ppermute | solution.py:52
  121.1 10.8 %collective-permute-start.32 = (bf16[17,16,256]{2,1,0:T(8,128)(2,1)S(1)}, bf16[17,16,256]{2,1,0:T(8,128)(2,1)S(1)}, u32[]{:S(2)}, u32[]{:S(2)}) collective-permute-start(bf16[17,16,256]{2,1,0:T(8,128)(2,1)S(1)} %get-tuple-element.54), channel_id=1, source_target_pairs={{0,8},{1,9},{2,10},{3,11},{4,12},{5,13},{6,14},{7,15},{8,0},{9,1},... | collective-permute-start | bytes 417800 | tf_op jit(solution)/shard_map/ppermute | solution.py:52
  121.4 12.1 %collective-permute-start.33 = (bf16[17,16,256]{2,1,0:T(8,128)(2,1)S(1)}, bf16[17,16,256]{2,1,0:T(8,128)(2,1)S(1)}, u32[]{:S(2)}, u32[]{:S(2)}) collective-permute-start(bf16[17,16,256]{2,1,0:T(8,128)(2,1)S(1)} %get-tuple-element.55), channel_id=1, source_target_pairs={{0,4},{1,5},{2,6},{3,7},{4,8},{5,9},{6,10},{7,11},{8,12},{9,13},{1... | collective-permute-start | bytes 417800 | tf_op jit(solution)/shard_map/ppermute | solution.py:52
  123.1 10.4 %collective-permute-start.34 = (bf16[17,16,256]{2,1,0:T(8,128)(2,1)S(1)}, bf16[17,16,256]{2,1,0:T(8,128)(2,1)S(1)}, u32[]{:S(2)}, u32[]{:S(2)}) collective-permute-start(bf16[17,16,256]{2,1,0:T(8,128)(2,1)S(1)} %get-tuple-element.56), channel_id=1, source_target_pairs={{0,12},{1,13},{2,14},{3,15},{4,0},{5,1},{6,2},{7,3},{8,4},{9,5},{1... | collective-permute-start | bytes 417800 | tf_op jit(solution)/shard_map/ppermute | solution.py:52
  129.9 6.7 %collective-permute-start.25 = (bf16[17,16,256]{2,1,0:T(8,128)(2,1)S(1)}, bf16[17,16,256]{2,1,0:T(8,128)(2,1)S(1)}, u32[]{:S(2)}, u32[]{:S(2)}) collective-permute-start(bf16[17,16,256]{2,1,0:T(8,128)(2,1)S(1)} %get-tuple-element.45), channel_id=1, source_target_pairs={{0,8},{1,9},{2,10},{3,11},{4,12},{5,13},{6,14},{7,15},{8,0},{9,1},... | collective-permute-start | bytes 417800 | tf_op jit(solution)/shard_map/ppermute | solution.py:52
  130.2 7.8 %collective-permute-start.26 = (bf16[17,16,256]{2,1,0:T(8,128)(2,1)S(1)}, bf16[17,16,256]{2,1,0:T(8,128)(2,1)S(1)}, u32[]{:S(2)}, u32[]{:S(2)}) collective-permute-start(bf16[17,16,256]{2,1,0:T(8,128)(2,1)S(1)} %get-tuple-element.46), channel_id=1, source_target_pairs={{0,4},{1,5},{2,6},{3,7},{4,8},{5,9},{6,10},{7,11},{8,12},{9,13},{1... | collective-permute-start | bytes 417800 | tf_op jit(solution)/shard_map/ppermute | solution.py:52
  131.9 6.1 %collective-permute-start.27 = (bf16[17,16,256]{2,1,0:T(8,128)(2,1)S(1)}, bf16[17,16,256]{2,1,0:T(8,128)(2,1)S(1)}, u32[]{:S(2)}, u32[]{:S(2)}) collective-permute-start(bf16[17,16,256]{2,1,0:T(8,128)(2,1)S(1)} %get-tuple-element.47), channel_id=1, source_target_pairs={{0,12},{1,13},{2,14},{3,15},{4,0},{5,1},{6,2},{7,3},{8,4},{9,5},{1... | collective-permute-start | bytes 417800 | tf_op jit(solution)/shard_map/ppermute | solution.py:52

commit v6 on v5

--- a/solution.py
+++ b/solution.py
@@ -163,16 +163,6 @@
     ).astype(BF16)
 
 
-def kernel_pack(s_ref, gain, weight_in, weight_out, out):
-    groups = [weight_out[0, :, pl.ds(k * 256, 256)].astype(F32) for k in range(8)]
-    across = jnp.concatenate(groups, axis=0).astype(BF16)
-    along = jnp.broadcast_to(gain[...].astype(F32), (8, 32)).astype(BF16)
-    for i in range(8):
-        out[i, 0:32] = weight_in[0]
-        out[i, 32:64] = across
-        out[i, 64:72, 0:32] = along
-
-
 def kernel_stats(s_ref, xs, hat, stat):
     c, zl = s_ref[2], s_ref[3]
 
@@ -266,7 +256,7 @@
         )
 
 
-def kernel_grads(s_ref, acts, got, out, *pieces):
+def kernel_grads(s_ref, acts, got, out, up, down):
     mx, my, c = s_ref[0], s_ref[1], s_ref[2]
     places = []
     for xy in range(16):
@@ -293,12 +283,8 @@
         out[places[xy], 16] = jnp.concatenate([part, part], axis=1).astype(BF16)
 
 
-    if len(pieces) == 2:
-        pieces[0][...] = out[8:10]
-        pieces[1][...] = out[10:12]
-    else:
-        for k in range(3):
-            pieces[k][...] = out[4 * k + 4 : 4 * k + 8]
+    up[...] = out[8:10]
+    down[...] = out[10:12]
 
 
 def over_groups(step):
@@ -320,15 +306,12 @@
     over_groups(step)
 
 
-def kernel_sum(s_ref, own, *refs):
-    got, pieces = refs[:-4], refs[-4:]
-
+def kernel_sum(s_ref, own, a, b, *pieces):
     def step(g):
         for k in range(4):
-            total = own[k, g].astype(F32)
-            for part in got:
-                total += part[k, g].astype(F32)
-            pieces[k][g] = total.astype(BF16)
+            pieces[k][g] = (
+                own[k, g].astype(F32) + a[k, g].astype(F32) + b[k, g].astype(F32)
+            ).astype(BF16)
 
     over_groups(step)
 
@@ -392,14 +375,6 @@
     return grads, shift(up, send_first(1)), shift(down, send_first(-1))
 
 
-def scatter_direct(scalars, acts, got):
-    row = array(4, 17, 16, 256)
-    grads, *pieces = call(
-        kernel_grads, scalars, [acts, got], [array(16, 17, 16, 256)] + [row] * 3, []
-    )
-    return [grads] + [shift(pieces[k - 1], send_first(k)) for k in (2, 1, 3)]
-
-
 def scatter_sides(scalars, grads, up, down):
     row = array(4, 17, 16, 256)
     after, before = call(kernel_sides, scalars, [grads, up, down], [row, row], [])
@@ -416,8 +391,17 @@
 def device_body(inputs, cotangent, norm_gain, proj_in, proj_out):
     where = [lax.axis_index(n).astype(jnp.int32) for n in ("x", "y", "c", "zl")]
     scalars = jnp.stack(where)
-    shard = call(kernel_pack, scalars, [norm_gain, proj_in, proj_out], array(8, 72, 256), [])
-    column = lax.all_to_all(shard, ("zl", "zh"), 0, 0).reshape(2, 4, 72, 256)
+    shard = jnp.concatenate(
+        [
+            proj_in[0],
+            proj_out[0].reshape(4, 8, 256).transpose(1, 0, 2).reshape(32, 256),
+            jnp.pad(norm_gain, ((0, 7), (0, 224))),
+        ],
+        axis=0,
+    )
+    column = lax.all_to_all(
+        jnp.broadcast_to(shard[None], (8, 72, 256)), ("zl", "zh"), 0, 0
+    ).reshape(2, 4, 72, 256)
     gain = jnp.pad(column[:, :, 64, :32].reshape(2, 1, 1, 128), ((0, 0), (0, 0), (0, 15), (0, 128)))
     block = jnp.concatenate(
         [
@@ -460,8 +444,9 @@
         BACK_SCRATCH,
     )
     got0 = shift(acts0[1], SWAP)
-    sides1 = scatter_direct(scalars, acts1, got1)
+    first1 = scatter_first(scalars, acts1, got1)
     first0 = scatter_first(scalars, acts0, got0)
+    sides1 = scatter_sides(scalars, *first1)
     sides0 = scatter_sides(scalars, *first0)
     high = scatter_second(scalars, sides1)
     low = scatter_second(scalars, sides0)

time: 153 us -> 159 us (1.039); the launches traced: 152 us -> 156 us
  local copies, waits for them, and re-layouts: 2.85 us -> 8.11 us
  starting transfers between devices: 39.4 us -> 35.6 us
  Pallas kernels: 19.4 us -> 21.7 us
    unnamed x11 -> x26, local copies, waits for them, and re-layouts: 2.21 us -> 7.42 us
    ppermute x35 -> x36, starting transfers between devices: 39.4 us -> 35.6 us  [shift(): return lax.ppermute(value, AXES, pairs)]
    pallas_call x11, Pallas kernels: 19.4 us -> 21.7 us  [call(): pl.pallas_call(body, in_specs=[pl.BlockSpec(memory_space=pltpu.SMEM)] + [...]
    ppermute x35 -> x36, waiting for transfers between devices: 57.1 us -> 56.8 us  [shift(): return lax.ppermute(value, AXES, pairs)]
  transfers between devices with their start and end apart: 35 -> 36, of which waited for: 13 -> 16; matrix products, arithmetic and copies ran while one was open for 0% -> 0% of each run, Pallas kernels for 6% -> 7%
where the time goes in v6:
time: 159 us; the launch traced here: 156 us
  waiting for transfers between devices  56.8 us (36%)
  starting transfers between devices  35.6 us (22%)
  blocking collectives  31.9 us (20%)
  Pallas kernels  21.7 us (14%)
  local copies, waits for them, and re-layouts  8.11 us (5%)
    ppermute x36, waiting for transfers between devices, shift(): return lax.ppermute(value, AXES, pairs)  56.8 us
    ppermute x36, starting transfers between devices, shift(): return lax.ppermute(value, AXES, pairs)  35.6 us
    pallas_call x11, Pallas kernels, call(): pl.pallas_call(body, in_specs=[pl.BlockSpec(memory_space=pltpu.SMEM)] + [...  21.7 us
    all_to_all x1, blocking collectives, device_body(): lax.all_to_all(jnp.broadcast_to(shard[None], (8, 72, 256)), ('zl', 'zh'),...  19.5 us
    all_to_all x1, blocking collectives, device_body(): lax.all_to_all(parts, ('zl', 'zh'), 0, 0)  12.4 us
    unnamed x26, local copies, waits for them, and re-layouts  7.42 us
  transfers between devices with their start and end apart: 36, of which 16 were waited for; matrix products, arithmetic and copies ran while one was open for 0% of the time, Pallas kernels for 7%

profile of v6, /device:TPU:32, one launch (start us, length us, event | category | flops | bytes accessed | tf_op | source)
XLA Modules:
  0.0 156.3 jit_solution(16672913701449738739)
XLA Ops:
  2.1 19.5 %all_to_all.10 = bf16[8,72,256]{2,1,0:T(8,128)(2,1)S(1)} all-to-all(bf16[8,72,256]{2,1,0:T(8,128)(2,1)S(1)} %broadcast_in_dim.2), channel_id=1, replica_groups=mesh['zl'=2,'c'=2,'x'=4,'y'=4,'zh'=4] {'zl','zh'}, dimensions={0} | all-to-all | bytes 589824 | tf_op jit(solution)/shard_map/all_to_all | solution.py:402
  22.1 2.8 %collective-permute-start = (bf16[17,16,256]{2,1,0:T(8,128)(2,1)S(1)}, bf16[17,16,256]{2,1,0:T(8,128)(2,1)S(1)}, u32[]{:S(2)}, u32[]{:S(2)}) collective-permute-start(bf16[17,16,256]{2,1,0:T(8,128)(2,1)S(1)} %get-tuple-element.64), channel_id=1, source_target_pairs={{0,48},{1,49},{2,50},{3,51},{4,52},{5,53},{6,54},{7,55},{8,56},{9,... | collective-permute-start | bytes 417800 | tf_op jit(solution)/shard_map/ppermute | solution.py:52
  24.9 0.8 collective-permute-start.1
  25.7 0.9 collective-permute-start.2
  26.6 2.4 %collective-permute-done = bf16[17,16,256]{2,1,0:T(8,128)(2,1)S(1)} collective-permute-done((bf16[17,16,256]{2,1,0:T(8,128)(2,1)S(1)}, bf16[17,16,256]{2,1,0:T(8,128)(2,1)S(1)}, u32[]{:S(2)}, u32[]{:S(2)}) %collective-permute-start) | collective-permute-done | bytes 139296 | tf_op jit(solution)/shard_map/ppermute | solution.py:52
  29.0 2.6 %collective-permute-done.1 = bf16[17,16,256]{2,1,0:T(8,128)(2,1)S(1)} collective-permute-done((bf16[17,16,256]{2,1,0:T(8,128)(2,1)S(1)}, bf16[17,16,256]{2,1,0:T(8,128)(2,1)S(1)}, u32[]{:S(2)}, u32[]{:S(2)}) %collective-permute-start.1) | collective-permute-done | bytes 139296 | tf_op jit(solution)/shard_map/ppermute | solution.py:52
  31.6 1.4 collective-permute-done.2
  33.0 3.1 %collective-permute-start.3 = (bf16[4,17,16,256]{3,2,1,0:T(8,128)(2,1)S(1)}, bf16[4,17,16,256]{3,2,1,0:T(8,128)(2,1)S(1)}, u32[]{:S(2)}, u32[]{:S(2)}) collective-permute-start(bf16[4,17,16,256]{3,2,1,0:T(8,128)(2,1)S(1)} %pad_maximum_fusion.refs_0_), channel_id=1, source_target_pairs={{0,12},{1,13},{2,14},{3,15},{4,0},{5,1},{6,2},{7,3},{8,4},{9,5},{1... | collective-permute-start | bytes 1671176 | tf_op jit(solution)/shard_map/ppermute | solution.py:52
  36.8 1.0 collective-permute-start.5
  38.3 9.5 %collective-permute-done.10 = bf16[17,16,256]{2,1,0:T(8,128)(2,1)S(1)} collective-permute-done((bf16[17,16,256]{2,1,0:T(8,128)(2,1)S(1)}, bf16[17,16,256]{2,1,0:T(8,128)(2,1)S(1)}, u32[]{:S(2)}, u32[]{:S(2)}) %collective-permute-start.10) | collective-permute-done | bytes 139296 | tf_op jit(solution)/shard_map/ppermute | solution.py:52
  47.8 6.6 %collective-permute-done.11 = bf16[17,16,256]{2,1,0:T(8,128)(2,1)S(1)} collective-permute-done((bf16[17,16,256]{2,1,0:T(8,128)(2,1)S(1)}, bf16[17,16,256]{2,1,0:T(8,128)(2,1)S(1)}, u32[]{:S(2)}, u32[]{:S(2)}) %collective-permute-start.11) | collective-permute-done | bytes 139296 | tf_op jit(solution)/shard_map/ppermute | solution.py:52
  54.4 1.0 collective-permute-start.12
  55.4 5.7 %collective-permute-done.12 = bf16[17,16,256]{2,1,0:T(8,128)(2,1)S(1)} collective-permute-done((bf16[17,16,256]{2,1,0:T(8,128)(2,1)S(1)}, bf16[17,16,256]{2,1,0:T(8,128)(2,1)S(1)}, u32[]{:S(2)}, u32[]{:S(2)}) %collective-permute-start.12) | collective-permute-done | bytes 139296 | tf_op jit(solution)/shard_map/ppermute | solution.py:52
  61.1 0.9 collective-permute-start.13
  62.7 0.9 collective-permute-start.15
  63.6 0.8 copy-done.2
  64.4 0.8 copy-done.6
  65.7 0.8 copy-done.4
  66.5 4.3 %collective-permute-done.13.refs_1_ = bf16[4,17,16,256]{3,2,1,0:T(8,128)(2,1)} collective-permute-done((bf16[4,17,16,256]{3,2,1,0:T(8,128)(2,1)S(1)}, bf16[4,17,16,256]{3,2,1,0:T(8,128)(2,1)}, u32[]{:S(2)}, u32[]{:S(2)}) %collective-permute-start.13) | collective-permute-done | bytes 557088 | tf_op jit(solution)/shard_map/ppermute | solution.py:52
  70.9 2.5 %collective-permute-done.14.refs_2_ = bf16[4,17,16,256]{3,2,1,0:T(8,128)(2,1)} collective-permute-done((bf16[4,17,16,256]{3,2,1,0:T(8,128)(2,1)S(1)}, bf16[4,17,16,256]{3,2,1,0:T(8,128)(2,1)}, u32[]{:S(2)}, u32[]{:S(2)}) %collective-permute-start.14) | collective-permute-done | bytes 557088 | tf_op jit(solution)/shard_map/ppermute | solution.py:52
  73.3 5.9 %collective-permute-done.15.refs_3_ = bf16[4,17,16,256]{3,2,1,0:T(8,128)(2,1)} collective-permute-done((bf16[4,17,16,256]{3,2,1,0:T(8,128)(2,1)S(1)}, bf16[4,17,16,256]{3,2,1,0:T(8,128)(2,1)}, u32[]{:S(2)}, u32[]{:S(2)}) %collective-permute-start.15) | collective-permute-done | bytes 557088 | tf_op jit(solution)/shard_map/ppermute | solution.py:52
  79.2 0.8 copy-done.8
  80.5 0.9 copy-done.10
  81.5 0.9 shard_map.76
  82.8 1.1 copy-done.9
  83.8 1.1 copy-done.11
  84.9 3.7 %shard_map.77 = (bf16[128,2048]{1,0:T(8,128)(2,1)S(1)}, bf16[128,2048]{1,0:T(8,128)(2,1)S(1)}, bf16[2,128,16,256]{3,2,1,0:T(8,128)(2,1)S(1)}, bf16[2,9,16,16,256...) custom-call(s32[4]{0:T(128)S(1)} %pad_add_fusion.s_ref, ...), custom_call_target="tpu_custom_call" | custom-call | tf_op jit(solution)/shard_map/pallas_call | solution.py:356
  88.6 6.8 %shard_map.78 = (bf16[128,2048]{1,0:T(8,128)(2,1)S(1)}, bf16[2,144,4608]{2,1,0:T(8,128)(2,1)S(1)}) custom-call(s32[4]{0:T(128)S(1)} %pad_add_fusion.s_ref, bf16[128,2048]{1,0:T(8,128)(2,1)S(1)} %get-tuple-element.33.x2, bf16[2,2,128,2048]{3,2,1,0:T(8,128)(2,1)S(1)} %copy-done.1, bf16[4,17,16,256]{3,2,1,0:T(8,128)(2,1)S(1)} %pad_maximum_fusion.1.refs_0_, ...), custom_call_target="tpu_custom_call" | custom-call | tf_op jit(solution)/shard_map/pallas_call | solution.py:356
  95.4 3.4 %shard_map.79.acts = bf16[2,144,4608]{2,1,0:T(8,128)(2,1)S(1)} custom-call(s32[4]{0:T(128)S(1)} %pad_add_fusion.s_ref, bf16[2,2,128,2048]{3,2,1,0:T(8,128)(2,1)S(1)} %copy-done, bf16[128,2048]{1,0:T(8,128)(2,1)S(1)} %get-tuple-element.32.x1, bf16[128,2048]{1,0:T(8,128)(2,1)S(1)} %get-tuple-element.34.up2, ...), custom_call_target="tpu_custom_call" | custom-call | tf_op jit(solution)/shard_map/pallas_call | solution.py:356
  99.7 2.5 %collective-permute-done.20.got = bf16[144,4608]{1,0:T(8,128)(2,1)S(1)} collective-permute-done((bf16[144,4608]{1,0:T(8,128)(2,1)S(1)}, bf16[144,4608]{1,0:T(8,128)(2,1)S(1)}, u32[]{:S(2)}, u32[]{:S(2)}) %collective-permute-start.20) | collective-permute-done | bytes 1327136 | tf_op jit(solution)/shard_map/ppermute | solution.py:52
  102.2 1.3 shard_map.80
  103.6 3.2 %collective-permute-start.22 = (bf16[2,17,16,256]{3,2,1,0:T(8,128)(2,1)S(1)}, bf16[2,17,16,256]{3,2,1,0:T(8,128)(2,1)S(1)}, u32[]{:S(2)}, u32[]{:S(2)}) collective-permute-start(bf16[2,17,16,256]{3,2,1,0:T(8,128)(2,1)S(1)} %get-tuple-element.42), channel_id=1, source_target_pairs={{0,48},{1,49},{2,50},{3,51},{4,52},{5,53},{6,54},{7,55},{8,56},{9,... | collective-permute-start | bytes 835592 | tf_op jit(solution)/shard_map/ppermute | solution.py:52
  106.9 1.3 shard_map.83
  108.3 3.2 %collective-permute-start.30 = (bf16[2,17,16,256]{3,2,1,0:T(8,128)(2,1)S(1)}, bf16[2,17,16,256]{3,2,1,0:T(8,128)(2,1)S(1)}, u32[]{:S(2)}, u32[]{:S(2)}) collective-permute-start(bf16[2,17,16,256]{3,2,1,0:T(8,128)(2,1)S(1)} %get-tuple-element.52), channel_id=1, source_target_pairs={{0,48},{1,49},{2,50},{3,51},{4,52},{5,53},{6,54},{7,55},{8,56},{9,... | collective-permute-start | bytes 835592 | tf_op jit(solution)/shard_map/ppermute | solution.py:52
  112.4 3.2 %collective-permute-start.24 = (bf16[4,17,16,256]{3,2,1,0:T(8,128)(2,1)S(1)}, bf16[4,17,16,256]{3,2,1,0:T(8,128)(2,1)S(1)}, u32[]{:S(2)}, u32[]{:S(2)}) collective-permute-start(bf16[4,17,16,256]{3,2,1,0:T(8,128)(2,1)S(1)} %get-tuple-element.44), channel_id=1, source_target_pairs={{0,48},{1,49},{2,50},{3,51},{4,52},{5,53},{6,54},{7,55},{8,56},{9,... | collective-permute-start | bytes 1671176 | tf_op jit(solution)/shard_map/ppermute | solution.py:52
  116.9 3.3 %collective-permute-start.32 = (bf16[4,17,16,256]{3,2,1,0:T(8,128)(2,1)S(1)}, bf16[4,17,16,256]{3,2,1,0:T(8,128)(2,1)S(1)}, u32[]{:S(2)}, u32[]{:S(2)}) collective-permute-start(bf16[4,17,16,256]{3,2,1,0:T(8,128)(2,1)S(1)} %get-tuple-element.54), channel_id=1, source_target_pairs={{0,48},{1,49},{2,50},{3,51},{4,52},{5,53},{6,54},{7,55},{8,56},{9,... | collective-permute-start | bytes 1671176 | tf_op jit(solution)/shard_map/ppermute | solution.py:52
  120.2 2.9 %collective-permute-done.23.a = bf16[4,17,16,256]{3,2,1,0:T(8,128)(2,1)S(1)} collective-permute-done((bf16[4,17,16,256]{3,2,1,0:T(8,128)(2,1)S(1)}, bf16[4,17,16,256]{3,2,1,0:T(8,128)(2,1)S(1)}, u32[]{:S(2)}, u32[]{:S(2)}) %collective-permute-start.23) | collective-permute-done | bytes 557088 | tf_op jit(solution)/shard_map/ppermute | solution.py:52
  123.1 0.8 shard_map.82
  124.6 0.9 collective-permute-start.26
  125.5 2.3 %collective-permute-start.27 = (bf16[17,16,256]{2,1,0:T(8,128)(2,1)S(1)}, bf16[17,16,256]{2,1,0:T(8,128)(2,1)S(1)}, u32[]{:S(2)}, u32[]{:S(2)}) collective-permute-start(bf16[17,16,256]{2,1,0:T(8,128)(2,1)S(1)} %get-tuple-element.48), channel_id=1, source_target_pairs={{0,12},{1,13},{2,14},{3,15},{4,0},{5,1},{6,2},{7,3},{8,4},{9,5},{1... | collective-permute-start | bytes 417800 | tf_op jit(solution)/shard_map/ppermute | solution.py:52
  127.9 4.2 %collective-permute-done.31.a = bf16[4,17,16,256]{3,2,1,0:T(8,128)(2,1)S(1)} collective-permute-done((bf16[4,17,16,256]{3,2,1,0:T(8,128)(2,1)S(1)}, bf16[4,17,16,256]{3,2,1,0:T(8,128)(2,1)S(1)}, u32[]{:S(2)}, u32[]{:S(2)}) %collective-permute-start.31) | collective-permute-done | bytes 557088 | tf_op jit(solution)/shard_map/ppermute | solution.py:52
  132.0 1.5 collective-permute-done.32.b
  133.5 0.8 shard_map.85
  134.5 3.2 %collective-permute-start.35 = (bf16[17,16,256]{2,1,0:T(8,128)(2,1)S(1)}, bf16[17,16,256]{2,1,0:T(8,128)(2,1)S(1)}, u32[]{:S(2)}, u32[]{:S(2)}) collective-permute-start(bf16[17,16,256]{2,1,0:T(8,128)(2,1)S(1)} %get-tuple-element.58), channel_id=1, source_target_pairs={{0,12},{1,13},{2,14},{3,15},{4,0},{5,1},{6,2},{7,3},{8,4},{9,5},{1... | collective-permute-start | bytes 417800 | tf_op jit(solution)/shard_map/ppermute | solution.py:52
  137.9 3.2 %collective-permute-done.33 = bf16[17,16,256]{2,1,0:T(8,128)(2,1)S(1)} collective-permute-done((bf16[17,16,256]{2,1,0:T(8,128)(2,1)S(1)}, bf16[17,16,256]{2,1,0:T(8,128)(2,1)S(1)}, u32[]{:S(2)}, u32[]{:S(2)}) %collective-permute-start.33) | collective-permute-done | bytes 139296 | tf_op jit(solution)/shard_map/ppermute | solution.py:52
  141.1 1.2 collective-permute-done.34
  142.7 12.4 %all_to_all.11.parts = bf16[8,72,256]{2,1,0:T(8,128)(2,1)S(1)} all-to-all(bf16[8,72,256]{2,1,0:T(8,128)(2,1)S(1)} %pad_maximum_fusion.2), channel_id=1, replica_groups=mesh['zl'=2,'c'=2,'x'=4,'y'=4,'zh'=4] {'zl','zh'}, dimensions={0} | all-to-all | bytes 589824 | tf_op jit(solution)/shard_map/all_to_all | solution.py:465
  155.1 1.2 shard_map.86
  (89 shorter events, 10.0 us)
Async XLA Ops:
  21.8 59.7 %copy-start = (bf16[2,2,128,2048]{3,2,1,0:T(8,128)(2,1)S(1)}, bf16[2,2,128,2048]{3,2,1,0:T(8,128)(2,1)}, u32[]{:S(2)}) copy-start(bf16[2,2,128,2048]{3,2,1,0:T(8,128)(2,1)} %xs.5) | copy-start | bytes 6291460
  22.1 6.9 %collective-permute-start = (bf16[17,16,256]{2,1,0:T(8,128)(2,1)S(1)}, bf16[17,16,256]{2,1,0:T(8,128)(2,1)S(1)}, u32[]{:S(2)}, u32[]{:S(2)}) collective-permute-start(bf16[17,16,256]{2,1,0:T(8,128)(2,1)S(1)} %get-tuple-element.64), channel_id=1, source_target_pairs={{0,48},{1,49},{2,50},{3,51},{4,52},{5,53},{6,54},{7,55},{8,56},{9,... | collective-permute-start | bytes 417800 | tf_op jit(solution)/shard_map/ppermute | solution.py:52
  24.9 6.7 %collective-permute-start.1 = (bf16[17,16,256]{2,1,0:T(8,128)(2,1)S(1)}, bf16[17,16,256]{2,1,0:T(8,128)(2,1)S(1)}, u32[]{:S(2)}, u32[]{:S(2)}) collective-permute-start(bf16[17,16,256]{2,1,0:T(8,128)(2,1)S(1)} %get-tuple-element.64), channel_id=1, source_target_pairs={{0,32},{1,33},{2,34},{3,35},{4,36},{5,37},{6,38},{7,39},{8,40},{9,... | collective-permute-start | bytes 417800 | tf_op jit(solution)/shard_map/ppermute | solution.py:52
  25.7 7.3 %collective-permute-start.2 = (bf16[17,16,256]{2,1,0:T(8,128)(2,1)S(1)}, bf16[17,16,256]{2,1,0:T(8,128)(2,1)S(1)}, u32[]{:S(2)}, u32[]{:S(2)}) collective-permute-start(bf16[17,16,256]{2,1,0:T(8,128)(2,1)S(1)} %get-tuple-element.64), channel_id=1, source_target_pairs={{0,16},{1,17},{2,18},{3,19},{4,20},{5,21},{6,22},{7,23},{8,24},{9,... | collective-permute-start | bytes 417800 | tf_op jit(solution)/shard_map/ppermute | solution.py:52
  33.0 29.0 %collective-permute-start.3 = (bf16[4,17,16,256]{3,2,1,0:T(8,128)(2,1)S(1)}, bf16[4,17,16,256]{3,2,1,0:T(8,128)(2,1)S(1)}, u32[]{:S(2)}, u32[]{:S(2)}) collective-permute-start(bf16[4,17,16,256]{3,2,1,0:T(8,128)(2,1)S(1)} %pad_maximum_fusion.refs_0_), channel_id=1, source_target_pairs={{0,12},{1,13},{2,14},{3,15},{4,0},{5,1},{6,2},{7,3},{8,4},{9,5},{1... | collective-permute-start | bytes 1671176 | tf_op jit(solution)/shard_map/ppermute | solution.py:52
  36.1 26.6 %collective-permute-start.4 = (bf16[4,17,16,256]{3,2,1,0:T(8,128)(2,1)S(1)}, bf16[4,17,16,256]{3,2,1,0:T(8,128)(2,1)S(1)}, u32[]{:S(2)}, u32[]{:S(2)}) collective-permute-start(bf16[4,17,16,256]{3,2,1,0:T(8,128)(2,1)S(1)} %pad_maximum_fusion.refs_0_), channel_id=1, source_target_pairs={{0,8},{1,9},{2,10},{3,11},{4,12},{5,13},{6,14},{7,15},{8,0},{9,1},... | collective-permute-start | bytes 1671176 | tf_op jit(solution)/shard_map/ppermute | solution.py:52
  36.8 26.8 %collective-permute-start.5 = (bf16[4,17,16,256]{3,2,1,0:T(8,128)(2,1)S(1)}, bf16[4,17,16,256]{3,2,1,0:T(8,128)(2,1)}, u32[]{:S(2)}, u32[]{:S(2)}) collective-permute-start(bf16[4,17,16,256]{3,2,1,0:T(8,128)(2,1)S(1)} %pad_maximum_fusion.refs_0_), channel_id=1, source_target_pairs={{0,4},{1,5},{2,6},{3,7},{4,8},{5,9},{6,10},{7,11},{8,12},{9,13},{1... | collective-permute-start | bytes 1671176 | tf_op jit(solution)/shard_map/ppermute | solution.py:52
  37.7 26.7 %collective-permute-start.6 = (bf16[4,17,16,256]{3,2,1,0:T(8,128)(2,1)S(1)}, bf16[4,17,16,256]{3,2,1,0:T(8,128)(2,1)S(1)}, u32[]{:S(2)}, u32[]{:S(2)}) collective-permute-start(bf16[4,17,16,256]{3,2,1,0:T(8,128)(2,1)S(1)} %pad_maximum_fusion.refs_0_), channel_id=1, source_target_pairs={{0,64},{1,65},{2,66},{3,67},{4,68},{5,69},{6,70},{7,71},{8,72},{9,... | collective-permute-start | bytes 1671176 | tf_op jit(solution)/shard_map/ppermute | solution.py:52
  37.7 10.1 %collective-permute-start.10 = (bf16[17,16,256]{2,1,0:T(8,128)(2,1)S(1)}, bf16[17,16,256]{2,1,0:T(8,128)(2,1)S(1)}, u32[]{:S(2)}, u32[]{:S(2)}) collective-permute-start(bf16[17,16,256]{2,1,0:T(8,128)(2,1)S(1)} %get-tuple-element.65), channel_id=1, source_target_pairs={{0,48},{1,49},{2,50},{3,51},{4,52},{5,53},{6,54},{7,55},{8,56},{9,... | collective-permute-start | bytes 417800 | tf_op jit(solution)/shard_map/ppermute | solution.py:52
  47.8 6.6 %collective-permute-start.11 = (bf16[17,16,256]{2,1,0:T(8,128)(2,1)S(1)}, bf16[17,16,256]{2,1,0:T(8,128)(2,1)S(1)}, u32[]{:S(2)}, u32[]{:S(2)}) collective-permute-start(bf16[17,16,256]{2,1,0:T(8,128)(2,1)S(1)} %get-tuple-element.65), channel_id=1, source_target_pairs={{0,32},{1,33},{2,34},{3,35},{4,36},{5,37},{6,38},{7,39},{8,40},{9,... | collective-permute-start | bytes 417800 | tf_op jit(solution)/shard_map/ppermute | solution.py:52
  54.4 6.7 %collective-permute-start.12 = (bf16[17,16,256]{2,1,0:T(8,128)(2,1)S(1)}, bf16[17,16,256]{2,1,0:T(8,128)(2,1)S(1)}, u32[]{:S(2)}, u32[]{:S(2)}) collective-permute-start(bf16[17,16,256]{2,1,0:T(8,128)(2,1)S(1)} %get-tuple-element.65), channel_id=1, source_target_pairs={{0,16},{1,17},{2,18},{3,19},{4,20},{5,21},{6,22},{7,23},{8,24},{9,... | collective-permute-start | bytes 417800 | tf_op jit(solution)/shard_map/ppermute | solution.py:52
  61.1 9.7 %collective-permute-start.13 = (bf16[4,17,16,256]{3,2,1,0:T(8,128)(2,1)S(1)}, bf16[4,17,16,256]{3,2,1,0:T(8,128)(2,1)}, u32[]{:S(2)}, u32[]{:S(2)}) collective-permute-start(bf16[4,17,16,256]{3,2,1,0:T(8,128)(2,1)S(1)} %pad_maximum_fusion.1.refs_0_), channel_id=1, source_target_pairs={{0,12},{1,13},{2,14},{3,15},{4,0},{5,1},{6,2},{7,3},{8,4},{9,5},{1... | collective-permute-start | bytes 1671176 | tf_op jit(solution)/shard_map/ppermute | solution.py:52
  62.1 11.2 %collective-permute-start.14 = (bf16[4,17,16,256]{3,2,1,0:T(8,128)(2,1)S(1)}, bf16[4,17,16,256]{3,2,1,0:T(8,128)(2,1)}, u32[]{:S(2)}, u32[]{:S(2)}) collective-permute-start(bf16[4,17,16,256]{3,2,1,0:T(8,128)(2,1)S(1)} %pad_maximum_fusion.1.refs_0_), channel_id=1, source_target_pairs={{0,8},{1,9},{2,10},{3,11},{4,12},{5,13},{6,14},{7,15},{8,0},{9,1},... | collective-permute-start | bytes 1671176 | tf_op jit(solution)/shard_map/ppermute | solution.py:52
  62.7 16.5 %collective-permute-start.15 = (bf16[4,17,16,256]{3,2,1,0:T(8,128)(2,1)S(1)}, bf16[4,17,16,256]{3,2,1,0:T(8,128)(2,1)}, u32[]{:S(2)}, u32[]{:S(2)}) collective-permute-start(bf16[4,17,16,256]{3,2,1,0:T(8,128)(2,1)S(1)} %pad_maximum_fusion.1.refs_0_), channel_id=1, source_target_pairs={{0,4},{1,5},{2,6},{3,7},{4,8},{5,9},{6,10},{7,11},{8,12},{9,13},{1... | collective-permute-start | bytes 1671176 | tf_op jit(solution)/shard_map/ppermute | solution.py:52
  63.6 15.6 %collective-permute-start.7 = (bf16[4,17,16,256]{3,2,1,0:T(8,128)(2,1)S(1)}, bf16[4,17,16,256]{3,2,1,0:T(8,128)(2,1)S(1)}, u32[]{:S(2)}, u32[]{:S(2)}) collective-permute-start(bf16[4,17,16,256]{3,2,1,0:T(8,128)(2,1)S(1)} %collective-permute-done.3.refs_1_), channel_id=1, source_target_pairs={{0,64},{1,65},{2,66},{3,67},{4,68},{5,69},{6,70},{7,71},{8,72},{9,... | collective-permute-start | bytes 1671176 | tf_op jit(solution)/shard_map/ppermute | solution.py:52
  63.6 0.8 copy-start.2
  64.4 0.8 copy-start.6
  65.2 15.3 %collective-permute-start.8 = (bf16[4,17,16,256]{3,2,1,0:T(8,128)(2,1)S(1)}, bf16[4,17,16,256]{3,2,1,0:T(8,128)(2,1)S(1)}, u32[]{:S(2)}, u32[]{:S(2)}) collective-permute-start(bf16[4,17,16,256]{3,2,1,0:T(8,128)(2,1)S(1)} %collective-permute-done.4.refs_2_), channel_id=1, source_target_pairs={{0,64},{1,65},{2,66},{3,67},{4,68},{5,69},{6,70},{7,71},{8,72},{9,... | collective-permute-start | bytes 1671176 | tf_op jit(solution)/shard_map/ppermute | solution.py:52
  65.7 0.8 copy-start.4
  70.9 17.7 %collective-permute-start.16 = (bf16[4,17,16,256]{3,2,1,0:T(8,128)(2,1)S(1)}, bf16[4,17,16,256]{3,2,1,0:T(8,128)(2,1)}, u32[]{:S(2)}, u32[]{:S(2)}) collective-permute-start(bf16[4,17,16,256]{3,2,1,0:T(8,128)(2,1)S(1)} %pad_maximum_fusion.1.refs_0_), channel_id=1, source_target_pairs={{0,64},{1,65},{2,66},{3,67},{4,68},{5,69},{6,70},{7,71},{8,72},{9,... | collective-permute-start | bytes 1671176 | tf_op jit(solution)/shard_map/ppermute | solution.py:52
  73.3 9.1 %collective-permute-start.9 = (bf16[4,17,16,256]{3,2,1,0:T(8,128)(2,1)}, bf16[4,17,16,256]{3,2,1,0:T(8,128)(2,1)}, u32[]{:S(2)}, u32[]{:S(2)}) collective-permute-start(bf16[4,17,16,256]{3,2,1,0:T(8,128)(2,1)} %collective-permute-done.5.refs_3_), channel_id=1, source_target_pairs={{0,64},{1,65},{2,66},{3,67},{4,68},{5,69},{6,70},{7,71},{8,72},{9,... | collective-permute-start | bytes 1671176 | tf_op jit(solution)/shard_map/ppermute | solution.py:52
  79.2 9.4 %collective-permute-start.17 = (bf16[4,17,16,256]{3,2,1,0:T(8,128)(2,1)}, bf16[4,17,16,256]{3,2,1,0:T(8,128)(2,1)}, u32[]{:S(2)}, u32[]{:S(2)}) collective-permute-start(bf16[4,17,16,256]{3,2,1,0:T(8,128)(2,1)} %collective-permute-done.13.refs_1_), channel_id=1, source_target_pairs={{0,64},{1,65},{2,66},{3,67},{4,68},{5,69},{6,70},{7,71},{8,72},{9,... | collective-permute-start | bytes 1671176 | tf_op jit(solution)/shard_map/ppermute | solution.py:52
  79.2 0.8 copy-start.8
  80.0 8.6 %collective-permute-start.18 = (bf16[4,17,16,256]{3,2,1,0:T(8,128)(2,1)}, bf16[4,17,16,256]{3,2,1,0:T(8,128)(2,1)}, u32[]{:S(2)}, u32[]{:S(2)}) collective-permute-start(bf16[4,17,16,256]{3,2,1,0:T(8,128)(2,1)} %collective-permute-done.14.refs_2_), channel_id=1, source_target_pairs={{0,64},{1,65},{2,66},{3,67},{4,68},{5,69},{6,70},{7,71},{8,72},{9,... | collective-permute-start | bytes 1671176 | tf_op jit(solution)/shard_map/ppermute | solution.py:52
  80.5 0.9 copy-start.10
  81.4 7.3 %collective-permute-start.19 = (bf16[4,17,16,256]{3,2,1,0:T(8,128)(2,1)}, bf16[4,17,16,256]{3,2,1,0:T(8,128)(2,1)}, u32[]{:S(2)}, u32[]{:S(2)}) collective-permute-start(bf16[4,17,16,256]{3,2,1,0:T(8,128)(2,1)} %collective-permute-done.15.refs_3_), channel_id=1, source_target_pairs={{0,64},{1,65},{2,66},{3,67},{4,68},{5,69},{6,70},{7,71},{8,72},{9,... | collective-permute-start | bytes 1671176 | tf_op jit(solution)/shard_map/ppermute | solution.py:52
  81.4 1.1 copy-start.3
  81.4 1.2 copy-start.5
  81.4 1.4 copy-start.7
  82.8 1.1 copy-start.9
  83.8 1.1 copy-start.11
  84.9 3.8 %copy-start.1 = (bf16[2,2,128,2048]{3,2,1,0:T(8,128)(2,1)S(1)}, bf16[2,2,128,2048]{3,2,1,0:T(8,128)(2,1)}, u32[]{:S(2)}) copy-start(bf16[2,2,128,2048]{3,2,1,0:T(8,128)(2,1)} %cots.1) | copy-start | bytes 6291460
  98.9 3.3 %collective-permute-start.20 = (bf16[144,4608]{1,0:T(8,128)(2,1)S(1)}, bf16[144,4608]{1,0:T(8,128)(2,1)S(1)}, u32[]{:S(2)}, u32[]{:S(2)}) collective-permute-start(bf16[144,4608]{1,0:T(8,128)(2,1)S(1)} %slice_bitcast_fusion), channel_id=1, source_target_pairs={{0,64},{1,65},{2,66},{3,67},{4,68},{5,69},{6,70},{7,71},{8,72},{9,... | collective-permute-start | bytes 3981320 | tf_op jit(solution)/shard_map/ppermute | solution.py:52
  99.6 7.3 %collective-permute-start.28 = (bf16[144,4608]{1,0:T(8,128)(2,1)S(1)}, bf16[144,4608]{1,0:T(8,128)(2,1)S(1)}, u32[]{:S(2)}, u32[]{:S(2)}) collective-permute-start(bf16[144,4608]{1,0:T(8,128)(2,1)S(1)} %slice_bitcast_fusion.1), channel_id=1, source_target_pairs={{0,64},{1,65},{2,66},{3,67},{4,68},{5,69},{6,70},{7,71},{8,72},{9,... | collective-permute-start | bytes 3981320 | tf_op jit(solution)/shard_map/ppermute | solution.py:52
  103.5 8.0 %collective-permute-start.21 = (bf16[2,17,16,256]{3,2,1,0:T(8,128)(2,1)S(1)}, bf16[2,17,16,256]{3,2,1,0:T(8,128)(2,1)S(1)}, u32[]{:S(2)}, u32[]{:S(2)}) collective-permute-start(bf16[2,17,16,256]{3,2,1,0:T(8,128)(2,1)S(1)} %get-tuple-element.41), channel_id=1, source_target_pairs={{0,16},{1,17},{2,18},{3,19},{4,20},{5,21},{6,22},{7,23},{8,24},{9,... | collective-permute-start | bytes 835592 | tf_op jit(solution)/shard_map/ppermute | solution.py:52
  103.6 7.9 %collective-permute-start.22 = (bf16[2,17,16,256]{3,2,1,0:T(8,128)(2,1)S(1)}, bf16[2,17,16,256]{3,2,1,0:T(8,128)(2,1)S(1)}, u32[]{:S(2)}, u32[]{:S(2)}) collective-permute-start(bf16[2,17,16,256]{3,2,1,0:T(8,128)(2,1)S(1)} %get-tuple-element.42), channel_id=1, source_target_pairs={{0,48},{1,49},{2,50},{3,51},{4,52},{5,53},{6,54},{7,55},{8,56},{9,... | collective-permute-start | bytes 835592 | tf_op jit(solution)/shard_map/ppermute | solution.py:52
  108.2 7.8 %collective-permute-start.29 = (bf16[2,17,16,256]{3,2,1,0:T(8,128)(2,1)S(1)}, bf16[2,17,16,256]{3,2,1,0:T(8,128)(2,1)S(1)}, u32[]{:S(2)}, u32[]{:S(2)}) collective-permute-start(bf16[2,17,16,256]{3,2,1,0:T(8,128)(2,1)S(1)} %get-tuple-element.51), channel_id=1, source_target_pairs={{0,16},{1,17},{2,18},{3,19},{4,20},{5,21},{6,22},{7,23},{8,24},{9,... | collective-permute-start | bytes 835592 | tf_op jit(solution)/shard_map/ppermute | solution.py:52
  108.3 7.7 %collective-permute-start.30 = (bf16[2,17,16,256]{3,2,1,0:T(8,128)(2,1)S(1)}, bf16[2,17,16,256]{3,2,1,0:T(8,128)(2,1)S(1)}, u32[]{:S(2)}, u32[]{:S(2)}) collective-permute-start(bf16[2,17,16,256]{3,2,1,0:T(8,128)(2,1)S(1)} %get-tuple-element.52), channel_id=1, source_target_pairs={{0,48},{1,49},{2,50},{3,51},{4,52},{5,53},{6,54},{7,55},{8,56},{9,... | collective-permute-start | bytes 835592 | tf_op jit(solution)/shard_map/ppermute | solution.py:52
  112.3 10.8 %collective-permute-start.23 = (bf16[4,17,16,256]{3,2,1,0:T(8,128)(2,1)S(1)}, bf16[4,17,16,256]{3,2,1,0:T(8,128)(2,1)S(1)}, u32[]{:S(2)}, u32[]{:S(2)}) collective-permute-start(bf16[4,17,16,256]{3,2,1,0:T(8,128)(2,1)S(1)} %get-tuple-element.43), channel_id=1, source_target_pairs={{0,16},{1,17},{2,18},{3,19},{4,20},{5,21},{6,22},{7,23},{8,24},{9,... | collective-permute-start | bytes 1671176 | tf_op jit(solution)/shard_map/ppermute | solution.py:52
  112.4 10.7 %collective-permute-start.24 = (bf16[4,17,16,256]{3,2,1,0:T(8,128)(2,1)S(1)}, bf16[4,17,16,256]{3,2,1,0:T(8,128)(2,1)S(1)}, u32[]{:S(2)}, u32[]{:S(2)}) collective-permute-start(bf16[4,17,16,256]{3,2,1,0:T(8,128)(2,1)S(1)} %get-tuple-element.44), channel_id=1, source_target_pairs={{0,48},{1,49},{2,50},{3,51},{4,52},{5,53},{6,54},{7,55},{8,56},{9,... | collective-permute-start | bytes 1671176 | tf_op jit(solution)/shard_map/ppermute | solution.py:52
  116.8 15.3 %collective-permute-start.31 = (bf16[4,17,16,256]{3,2,1,0:T(8,128)(2,1)S(1)}, bf16[4,17,16,256]{3,2,1,0:T(8,128)(2,1)S(1)}, u32[]{:S(2)}, u32[]{:S(2)}) collective-permute-start(bf16[4,17,16,256]{3,2,1,0:T(8,128)(2,1)S(1)} %get-tuple-element.53), channel_id=1, source_target_pairs={{0,16},{1,17},{2,18},{3,19},{4,20},{5,21},{6,22},{7,23},{8,24},{9,... | collective-permute-start | bytes 1671176 | tf_op jit(solution)/shard_map/ppermute | solution.py:52
  116.9 16.6 %collective-permute-start.32 = (bf16[4,17,16,256]{3,2,1,0:T(8,128)(2,1)S(1)}, bf16[4,17,16,256]{3,2,1,0:T(8,128)(2,1)S(1)}, u32[]{:S(2)}, u32[]{:S(2)}) collective-permute-start(bf16[4,17,16,256]{3,2,1,0:T(8,128)(2,1)S(1)} %get-tuple-element.54), channel_id=1, source_target_pairs={{0,48},{1,49},{2,50},{3,51},{4,52},{5,53},{6,54},{7,55},{8,56},{9,... | collective-permute-start | bytes 1671176 | tf_op jit(solution)/shard_map/ppermute | solution.py:52
  123.9 10.6 %collective-permute-start.25 = (bf16[17,16,256]{2,1,0:T(8,128)(2,1)S(1)}, bf16[17,16,256]{2,1,0:T(8,128)(2,1)S(1)}, u32[]{:S(2)}, u32[]{:S(2)}) collective-permute-start(bf16[17,16,256]{2,1,0:T(8,128)(2,1)S(1)} %get-tuple-element.46), channel_id=1, source_target_pairs={{0,8},{1,9},{2,10},{3,11},{4,12},{5,13},{6,14},{7,15},{8,0},{9,1},... | collective-permute-start | bytes 417800 | tf_op jit(solution)/shard_map/ppermute | solution.py:52
  124.6 13.1 %collective-permute-start.26 = (bf16[17,16,256]{2,1,0:T(8,128)(2,1)S(1)}, bf16[17,16,256]{2,1,0:T(8,128)(2,1)S(1)}, u32[]{:S(2)}, u32[]{:S(2)}) collective-permute-start(bf16[17,16,256]{2,1,0:T(8,128)(2,1)S(1)} %get-tuple-element.47), channel_id=1, source_target_pairs={{0,4},{1,5},{2,6},{3,7},{4,8},{5,9},{6,10},{7,11},{8,12},{9,13},{1... | collective-permute-start | bytes 417800 | tf_op jit(solution)/shard_map/ppermute | solution.py:52
  125.5 12.2 %collective-permute-start.27 = (bf16[17,16,256]{2,1,0:T(8,128)(2,1)S(1)}, bf16[17,16,256]{2,1,0:T(8,128)(2,1)S(1)}, u32[]{:S(2)}, u32[]{:S(2)}) collective-permute-start(bf16[17,16,256]{2,1,0:T(8,128)(2,1)S(1)} %get-tuple-element.48), channel_id=1, source_target_pairs={{0,12},{1,13},{2,14},{3,15},{4,0},{5,1},{6,2},{7,3},{8,4},{9,5},{1... | collective-permute-start | bytes 417800 | tf_op jit(solution)/shard_map/ppermute | solution.py:52
  134.3 6.7 %collective-permute-start.33 = (bf16[17,16,256]{2,1,0:T(8,128)(2,1)S(1)}, bf16[17,16,256]{2,1,0:T(8,128)(2,1)S(1)}, u32[]{:S(2)}, u32[]{:S(2)}) collective-permute-start(bf16[17,16,256]{2,1,0:T(8,128)(2,1)S(1)} %get-tuple-element.56), channel_id=1, source_target_pairs={{0,8},{1,9},{2,10},{3,11},{4,12},{5,13},{6,14},{7,15},{8,0},{9,1},... | collective-permute-start | bytes 417800 | tf_op jit(solution)/shard_map/ppermute | solution.py:52
  134.4 7.8 %collective-permute-start.34 = (bf16[17,16,256]{2,1,0:T(8,128)(2,1)S(1)}, bf16[17,16,256]{2,1,0:T(8,128)(2,1)S(1)}, u32[]{:S(2)}, u32[]{:S(2)}) collective-permute-start(bf16[17,16,256]{2,1,0:T(8,128)(2,1)S(1)} %get-tuple-element.57), channel_id=1, source_target_pairs={{0,4},{1,5},{2,6},{3,7},{4,8},{5,9},{6,10},{7,11},{8,12},{9,13},{1... | collective-permute-start | bytes 417800 | tf_op jit(solution)/shard_map/ppermute | solution.py:52
  134.5 7.7 %collective-permute-start.35 = (bf16[17,16,256]{2,1,0:T(8,128)(2,1)S(1)}, bf16[17,16,256]{2,1,0:T(8,128)(2,1)S(1)}, u32[]{:S(2)}, u32[]{:S(2)}) collective-permute-start(bf16[17,16,256]{2,1,0:T(8,128)(2,1)S(1)} %get-tuple-element.58), channel_id=1, source_target_pairs={{0,12},{1,13},{2,14},{3,15},{4,0},{5,1},{6,2},{7,3},{8,4},{9,5},{1... | collective-permute-start | bytes 417800 | tf_op jit(solution)/shard_map/ppermute | solution.py:52

commit v7 on v6

--- a/solution.py
+++ b/solution.py
@@ -173,6 +173,11 @@
     hat_pass(lambda rows: xs[zl, c, rows, :], hat, keep_stat)
 
 
+def kernel_halves(s_ref, after, before, low, high):
+    low[...] = after[0:2]
+    high[...] = before[2:4]
+
+
 def kernel_low_forward(s_ref, xs, hat0, *refs):
     pieces = refs[: 2 * PIECES]
     x1, x2, win, wout, stat1, pre, normed, hat1 = refs[2 * PIECES :]
@@ -306,12 +311,13 @@
     over_groups(step)
 
 
-def kernel_sum(s_ref, own, a, b, *pieces):
+def kernel_sum(s_ref, low, low_a, low_b, high, high_a, high_b, *pieces):
     def step(g):
-        for k in range(4):
-            pieces[k][g] = (
-                own[k, g].astype(F32) + a[k, g].astype(F32) + b[k, g].astype(F32)
-            ).astype(BF16)
+        for p, (own, a, b) in enumerate(((low, low_a, low_b), (high, high_a, high_b))):
+            for k in range(4):
+                pieces[k][p, g] = (
+                    own[k, g].astype(F32) + a[k, g].astype(F32) + b[k, g].astype(F32)
+                ).astype(BF16)
 
     over_groups(step)
 
@@ -335,7 +341,7 @@
 
 
 UNROLL = 8
-SPANS = tuple((b, 0, 4) for b in range(4))
+SPANS = ((0, 0, 4), (1, 0, 4), (3, 0, 4), (2, 0, 2), (2, 2, 2))
 PIECES = len(SPANS)
 UP_AT, ACT_AT, PRE_AT, WIDE = D, 2 * D, 2 * D + R, 2 * D + 2 * R
 ACT = (ROWS, D)
@@ -381,9 +387,9 @@
     return grads, shift(after, send_first(1)), shift(before, send_first(-1))
 
 
-def scatter_second(scalars, parts):
-    piece = array(17, 16, 256)
-    own, *pieces = call(kernel_sum, scalars, parts, [piece] * 4, [])
+def scatter_second(scalars, low, high):
+    piece = array(2, 17, 16, 256)
+    own, *pieces = call(kernel_sum, scalars, [*low, *high], [piece] * 4, [])
     got = [shift(pieces[k - 1], send_second(k)) for k in (2, 1, 3)]
     return add_up(own, got)
 
@@ -418,9 +424,13 @@
     for p in range(2):
         near.append([block[p]] + [shift(block[p], send_first(-k)) for k in (1, 2, 3)])
     pairs = []
+    half = array(2, 17, 16, 256)
     for p in range(2):
         row = jnp.stack(near[p])
-        rows = [row] + [shift(row, send_second(-k)) for k in (1, 2, 3)]
+        after, before = shift(row, send_second(-1)), shift(row, send_second(1))
+        low, high = call(kernel_halves, scalars, [after, before], [half, half], [])
+        across = [shift(low, send_second(-1)), shift(high, send_second(1))]
+        rows = [row, after, before, *across]
         pairs.append(rows + [shift(v, SWAP) for v in rows])
     x1, x2, win, wout, stat1, pre = call(
         kernel_low_forward,
@@ -448,9 +458,7 @@
     first0 = scatter_first(scalars, acts0, got0)
     sides1 = scatter_sides(scalars, *first1)
     sides0 = scatter_sides(scalars, *first0)
-    high = scatter_second(scalars, sides1)
-    low = scatter_second(scalars, sides0)
-    grads = jnp.stack([low, high])
+    grads = scatter_second(scalars, sides0, sides1)
     parts = jnp.concatenate(
         [
             grads[:, :8].reshape(2, 4, 32, 256),

time: 159 us -> 135 us (0.85)
  waiting for transfers between devices: 56.8 us -> 34.1 us
  local copies, waits for them, and re-layouts: 8.11 us -> 1.57 us
  starting transfers between devices: 35.6 us -> 39.1 us
    ppermute x36 -> x37, waiting for transfers between devices: 56.8 us -> 34.1 us  [shift(): return lax.ppermute(value, AXES, pairs)]
    unnamed x26 -> x6, local copies, waits for them, and re-layouts: 7.42 us -> 0.84 us
    ppermute x36 -> x37, starting transfers between devices: 35.6 us -> 39.1 us  [shift(): return lax.ppermute(value, AXES, pairs)]
    pallas_call x11 -> x12, Pallas kernels: 21.7 us -> 22.8 us  [call(): pl.pallas_call(body, in_specs=[pl.BlockSpec(memory_space=pltpu.SMEM)] + [...]
  transfers between devices with their start and end apart: 36 -> 37, of which waited for: 16 -> 13; matrix products, arithmetic and copies ran while one was open for 0% -> 1% of each run, Pallas kernels for 7% -> 11%
where the time goes in v7:
time: 135 us; the launch traced here: 133 us
  starting transfers between devices  39.1 us (29%)
  waiting for transfers between devices  34.1 us (25%)
  blocking collectives  32.5 us (24%)
  Pallas kernels  22.8 us (17%)
  other arithmetic  2 us (1%)
  local copies, waits for them, and re-layouts  1.57 us (1%)
    ppermute x37, starting transfers between devices, shift(): return lax.ppermute(value, AXES, pairs)  39.1 us
    ppermute x37, waiting for transfers between devices, shift(): return lax.ppermute(value, AXES, pairs)  34.1 us
    pallas_call x12, Pallas kernels, call(): pl.pallas_call(body, in_specs=[pl.BlockSpec(memory_space=pltpu.SMEM)] + [...  22.8 us
    all_to_all x1, blocking collectives, device_body(): lax.all_to_all(jnp.broadcast_to(shard[None], (8, 72, 256)), ('zl', 'zh'),...  19.5 us
    all_to_all x1, blocking collectives, device_body(): lax.all_to_all(parts, ('zl', 'zh'), 0, 0)  13.1 us
  transfers between devices with their start and end apart: 37, of which 13 were waited for; matrix products, arithmetic and copies ran while one was open for 1% of the time, Pallas kernels for 11%

profile of v7, /device:TPU:32, one launch (start us, length us, event | category | flops | bytes accessed | tf_op | source)
XLA Modules:
  0.0 133.1 jit_solution(6931982269547172184)
XLA Ops:
  0.6 0.7 copy.39
  1.4 0.7 fusion.3
  2.1 19.5 %all_to_all.10 = bf16[8,72,256]{2,1,0:T(8,128)(2,1)S(1)} all-to-all(bf16[8,72,256]{2,1,0:T(8,128)(2,1)S(1)} %broadcast_in_dim.2), channel_id=1, replica_groups=mesh['zl'=2,'c'=2,'x'=4,'y'=4,'zh'=4] {'zl','zh'}, dimensions={0} | all-to-all | bytes 589824 | tf_op jit(solution)/shard_map/all_to_all | solution.py:408
  22.1 2.8 %collective-permute-start = (bf16[17,16,256]{2,1,0:T(8,128)(2,1)S(1)}, bf16[17,16,256]{2,1,0:T(8,128)(2,1)S(1)}, u32[]{:S(2)}, u32[]{:S(2)}) collective-permute-start(bf16[17,16,256]{2,1,0:T(8,128)(2,1)S(1)} %get-tuple-element.64), channel_id=1, source_target_pairs={{0,48},{1,49},{2,50},{3,51},{4,52},{5,53},{6,54},{7,55},{8,56},{9,... | collective-permute-start | bytes 417800 | tf_op jit(solution)/shard_map/ppermute | solution.py:52
  24.9 0.8 collective-permute-start.1
  25.7 0.9 collective-permute-start.2
  26.6 2.4 %collective-permute-start.12 = (bf16[17,16,256]{2,1,0:T(8,128)(2,1)S(1)}, bf16[17,16,256]{2,1,0:T(8,128)(2,1)S(1)}, u32[]{:S(2)}, u32[]{:S(2)}) collective-permute-start(bf16[17,16,256]{2,1,0:T(8,128)(2,1)S(1)} %get-tuple-element.65), channel_id=1, source_target_pairs={{0,48},{1,49},{2,50},{3,51},{4,52},{5,53},{6,54},{7,55},{8,56},{9,... | collective-permute-start | bytes 417800 | tf_op jit(solution)/shard_map/ppermute | solution.py:52
  28.9 1.5 %collective-permute-start.13 = (bf16[17,16,256]{2,1,0:T(8,128)(2,1)S(1)}, bf16[17,16,256]{2,1,0:T(8,128)(2,1)S(1)}, u32[]{:S(2)}, u32[]{:S(2)}) collective-permute-start(bf16[17,16,256]{2,1,0:T(8,128)(2,1)S(1)} %get-tuple-element.65), channel_id=1, source_target_pairs={{0,32},{1,33},{2,34},{3,35},{4,36},{5,37},{6,38},{7,39},{8,40},{9,... | collective-permute-start | bytes 417800 | tf_op jit(solution)/shard_map/ppermute | solution.py:52
  30.5 1.1 collective-permute-done.1
  31.6 1.4 %collective-permute-done.2 = bf16[17,16,256]{2,1,0:T(8,128)(2,1)S(1)} collective-permute-done((bf16[17,16,256]{2,1,0:T(8,128)(2,1)S(1)}, bf16[17,16,256]{2,1,0:T(8,128)(2,1)S(1)}, u32[]{:S(2)}, u32[]{:S(2)}) %collective-permute-start.2) | collective-permute-done | bytes 139296 | tf_op jit(solution)/shard_map/ppermute | solution.py:52
  32.9 0.9 pad_maximum_fusion.refs_0_
  33.9 3.0 %collective-permute-start.3 = (bf16[4,17,16,256]{3,2,1,0:T(8,128)(2,1)}, bf16[4,17,16,256]{3,2,1,0:T(8,128)(2,1)}, u32[]{:S(2)}, u32[]{:S(2)}) collective-permute-start(bf16[4,17,16,256]{3,2,1,0:T(8,128)(2,1)} %pad_maximum_fusion.refs_0_), channel_id=1, source_target_pairs={{0,12},{1,13},{2,14},{3,15},{4,0},{5,1},{6,2},{7,3},{8,4},{9,5},{1... | collective-permute-start | bytes 1671176 | tf_op jit(solution)/shard_map/ppermute | solution.py:52
  37.1 3.5 %collective-permute-start.15 = (bf16[4,17,16,256]{3,2,1,0:T(8,128)(2,1)S(1)}, bf16[4,17,16,256]{3,2,1,0:T(8,128)(2,1)S(1)}, u32[]{:S(2)}, u32[]{:S(2)}) collective-permute-start(bf16[4,17,16,256]{3,2,1,0:T(8,128)(2,1)S(1)} %pad_maximum_fusion.1.refs_0_), channel_id=1, source_target_pairs={{0,12},{1,13},{2,14},{3,15},{4,0},{5,1},{6,2},{7,3},{8,4},{9,5},{1... | collective-permute-start | bytes 1671176 | tf_op jit(solution)/shard_map/ppermute | solution.py:52
  40.6 3.6 %collective-permute-done.3.after.refs_1_ = bf16[4,17,16,256]{3,2,1,0:T(8,128)(2,1)} collective-permute-done((bf16[4,17,16,256]{3,2,1,0:T(8,128)(2,1)}, bf16[4,17,16,256]{3,2,1,0:T(8,128)(2,1)}, u32[]{:S(2)}, u32[]{:S(2)}) %collective-permute-start.3) | collective-permute-done | bytes 557088 | tf_op jit(solution)/shard_map/ppermute | solution.py:52
  44.2 3.7 %collective-permute-done.4.before.refs_2_ = bf16[4,17,16,256]{3,2,1,0:T(8,128)(2,1)} collective-permute-done((bf16[4,17,16,256]{3,2,1,0:T(8,128)(2,1)}, bf16[4,17,16,256]{3,2,1,0:T(8,128)(2,1)}, u32[]{:S(2)}, u32[]{:S(2)}) %collective-permute-start.4) | collective-permute-done | bytes 557088 | tf_op jit(solution)/shard_map/ppermute | solution.py:52
  47.9 1.3 shard_map.77
  49.3 2.0 %collective-permute-start.6 = (bf16[2,17,16,256]{3,2,1,0:T(8,128)(2,1)S(1)}, bf16[2,17,16,256]{3,2,1,0:T(8,128)(2,1)S(1)}, u32[]{:S(2)}, u32[]{:S(2)}) collective-permute-start(bf16[2,17,16,256]{3,2,1,0:T(8,128)(2,1)S(1)} %get-tuple-element.33), channel_id=1, source_target_pairs={{0,4},{1,5},{2,6},{3,7},{4,8},{5,9},{6,10},{7,11},{8,12},{9,13},{1... | collective-permute-start | bytes 835592 | tf_op jit(solution)/shard_map/ppermute | solution.py:52
  51.3 2.6 %collective-permute-done.16.before.refs_2_ = bf16[4,17,16,256]{3,2,1,0:T(8,128)(2,1)} collective-permute-done((bf16[4,17,16,256]{3,2,1,0:T(8,128)(2,1)S(1)}, bf16[4,17,16,256]{3,2,1,0:T(8,128)(2,1)}, u32[]{:S(2)}, u32[]{:S(2)}) %collective-permute-start.16) | collective-permute-done | bytes 557088 | tf_op jit(solution)/shard_map/ppermute | solution.py:52
  53.9 1.1 shard_map.79
  55.1 2.0 %collective-permute-start.18 = (bf16[2,17,16,256]{3,2,1,0:T(8,128)(2,1)S(1)}, bf16[2,17,16,256]{3,2,1,0:T(8,128)(2,1)S(1)}, u32[]{:S(2)}, u32[]{:S(2)}) collective-permute-start(bf16[2,17,16,256]{3,2,1,0:T(8,128)(2,1)S(1)} %get-tuple-element.37), channel_id=1, source_target_pairs={{0,4},{1,5},{2,6},{3,7},{4,8},{5,9},{6,10},{7,11},{8,12},{9,13},{1... | collective-permute-start | bytes 835592 | tf_op jit(solution)/shard_map/ppermute | solution.py:52
  57.1 0.5 collective-permute-start.9
  57.7 3.9 %collective-permute-done.17.refs_3_ = bf16[2,17,16,256]{3,2,1,0:T(8,128)(2,1)S(1)} collective-permute-done((bf16[2,17,16,256]{3,2,1,0:T(8,128)(2,1)S(1)}, bf16[2,17,16,256]{3,2,1,0:T(8,128)(2,1)S(1)}, u32[]{:S(2)}, u32[]{:S(2)}) %collective-permute-start.17) | collective-permute-done | bytes 278560 | tf_op jit(solution)/shard_map/ppermute | solution.py:52
  61.6 1.3 collective-permute-done.18.refs_4_
  62.9 0.5 collective-permute-start.20
  64.1 0.9 shard_map.76
  65.0 4.1 %shard_map.78 = (bf16[128,2048]{1,0:T(8,128)(2,1)S(1)}, bf16[128,2048]{1,0:T(8,128)(2,1)S(1)}, bf16[2,128,16,256]{3,2,1,0:T(8,128)(2,1)S(1)}, bf16[2,9,16,16,256...) custom-call(s32[4]{0:T(128)S(1)} %pad_add_fusion.s_ref, ...), custom_call_target="tpu_custom_call" | custom-call | tf_op jit(solution)/shard_map/pallas_call | solution.py:362
  69.1 5.7 %shard_map.80 = (bf16[128,2048]{1,0:T(8,128)(2,1)S(1)}, bf16[2,144,4608]{2,1,0:T(8,128)(2,1)S(1)}) custom-call(s32[4]{0:T(128)S(1)} %pad_add_fusion.s_ref, bf16[128,2048]{1,0:T(8,128)(2,1)S(1)} %get-tuple-element.35.x2, bf16[2,2,128,2048]{3,2,1,0:T(8,128)(2,1)S(1)} %copy-done.1, bf16[4,17,16,256]{3,2,1,0:T(8,128)(2,1)S(1)} %pad_maximum_fusion.1.refs_0_, ...), custom_call_target="tpu_custom_call" | custom-call | tf_op jit(solution)/shard_map/pallas_call | solution.py:362
  74.9 0.7 collective-permute-start.29
  75.7 3.4 %shard_map.81.acts = bf16[2,144,4608]{2,1,0:T(8,128)(2,1)S(1)} custom-call(s32[4]{0:T(128)S(1)} %pad_add_fusion.s_ref, bf16[2,2,128,2048]{3,2,1,0:T(8,128)(2,1)S(1)} %copy-done, bf16[128,2048]{1,0:T(8,128)(2,1)S(1)} %get-tuple-element.34.x1, bf16[128,2048]{1,0:T(8,128)(2,1)S(1)} %get-tuple-element.38.up2, ...), custom_call_target="tpu_custom_call" | custom-call | tf_op jit(solution)/shard_map/pallas_call | solution.py:362
  79.3 1.3 %shard_map.84 = (bf16[16,17,16,256]{3,2,1,0:T(8,128)(2,1)S(1)}, bf16[2,17,16,256]{3,2,1,0:T(8,128)(2,1)S(1)}, bf16[2,17,16,256]{3,2,1,0:T(8,128)(2,1)S(1)}) custom-call(s32[4]{0:T(128)S(1)} %pad_add_fusion.s_ref, bf16[2,144,4608]{2,1,0:T(8,128)(2,1)S(1)} %get-tuple-element.49.acts, bf16[144,4608]{1,0:T(8,128)(2,1)S(1)} %collective-permute-done.29.got), custom_call_target="tpu_custom_call" | custom-call | tf_op jit(solution)/shard_map/pallas_call | solution.py:362
  80.8 3.2 %collective-permute-start.31 = (bf16[2,17,16,256]{3,2,1,0:T(8,128)(2,1)S(1)}, bf16[2,17,16,256]{3,2,1,0:T(8,128)(2,1)S(1)}, u32[]{:S(2)}, u32[]{:S(2)}) collective-permute-start(bf16[2,17,16,256]{3,2,1,0:T(8,128)(2,1)S(1)} %get-tuple-element.52), channel_id=1, source_target_pairs={{0,48},{1,49},{2,50},{3,51},{4,52},{5,53},{6,54},{7,55},{8,56},{9,... | collective-permute-start | bytes 835592 | tf_op jit(solution)/shard_map/ppermute | solution.py:52
  84.0 1.3 %shard_map.82 = (bf16[16,17,16,256]{3,2,1,0:T(8,128)(2,1)S(1)}, bf16[2,17,16,256]{3,2,1,0:T(8,128)(2,1)S(1)}, bf16[2,17,16,256]{3,2,1,0:T(8,128)(2,1)S(1)}) custom-call(s32[4]{0:T(128)S(1)} %pad_add_fusion.s_ref, bf16[2,144,4608]{2,1,0:T(8,128)(2,1)S(1)} %shard_map.81.acts, bf16[144,4608]{1,0:T(8,128)(2,1)S(1)} %collective-permute-done.24.got), custom_call_target="tpu_custom_call" | custom-call | tf_op jit(solution)/shard_map/pallas_call | solution.py:362
  85.5 3.2 %collective-permute-start.26 = (bf16[2,17,16,256]{3,2,1,0:T(8,128)(2,1)S(1)}, bf16[2,17,16,256]{3,2,1,0:T(8,128)(2,1)S(1)}, u32[]{:S(2)}, u32[]{:S(2)}) collective-permute-start(bf16[2,17,16,256]{3,2,1,0:T(8,128)(2,1)S(1)} %get-tuple-element.46), channel_id=1, source_target_pairs={{0,48},{1,49},{2,50},{3,51},{4,52},{5,53},{6,54},{7,55},{8,56},{9,... | collective-permute-start | bytes 835592 | tf_op jit(solution)/shard_map/ppermute | solution.py:52
  88.7 0.7 shard_map.85
  89.5 3.2 %collective-permute-start.33 = (bf16[4,17,16,256]{3,2,1,0:T(8,128)(2,1)S(1)}, bf16[4,17,16,256]{3,2,1,0:T(8,128)(2,1)S(1)}, u32[]{:S(2)}, u32[]{:S(2)}) collective-permute-start(bf16[4,17,16,256]{3,2,1,0:T(8,128)(2,1)S(1)} %get-tuple-element.54), channel_id=1, source_target_pairs={{0,48},{1,49},{2,50},{3,51},{4,52},{5,53},{6,54},{7,55},{8,56},{9,... | collective-permute-start | bytes 1671176 | tf_op jit(solution)/shard_map/ppermute | solution.py:52
  92.7 0.5 collective-permute-done.25.up
  93.2 0.7 shard_map.83
  94.0 3.3 %collective-permute-start.28 = (bf16[4,17,16,256]{3,2,1,0:T(8,128)(2,1)S(1)}, bf16[4,17,16,256]{3,2,1,0:T(8,128)(2,1)S(1)}, u32[]{:S(2)}, u32[]{:S(2)}) collective-permute-start(bf16[4,17,16,256]{3,2,1,0:T(8,128)(2,1)S(1)} %get-tuple-element.48), channel_id=1, source_target_pairs={{0,48},{1,49},{2,50},{3,51},{4,52},{5,53},{6,54},{7,55},{8,56},{9,... | collective-permute-start | bytes 1671176 | tf_op jit(solution)/shard_map/ppermute | solution.py:52
  97.3 2.9 %collective-permute-done.32.high_a = bf16[4,17,16,256]{3,2,1,0:T(8,128)(2,1)S(1)} collective-permute-done((bf16[4,17,16,256]{3,2,1,0:T(8,128)(2,1)S(1)}, bf16[4,17,16,256]{3,2,1,0:T(8,128)(2,1)S(1)}, u32[]{:S(2)}, u32[]{:S(2)}) %collective-permute-start.32) | collective-permute-done | bytes 557088 | tf_op jit(solution)/shard_map/ppermute | solution.py:52
  100.3 6.0 %collective-permute-done.27.low_a = bf16[4,17,16,256]{3,2,1,0:T(8,128)(2,1)S(1)} collective-permute-done((bf16[4,17,16,256]{3,2,1,0:T(8,128)(2,1)S(1)}, bf16[4,17,16,256]{3,2,1,0:T(8,128)(2,1)S(1)}, u32[]{:S(2)}, u32[]{:S(2)}) %collective-permute-start.27) | collective-permute-done | bytes 557088 | tf_op jit(solution)/shard_map/ppermute | solution.py:52
  106.2 1.0 shard_map.86
  107.2 0.8 collective-permute-start.34
  108.1 1.1 collective-permute-start.35
  109.2 2.1 %collective-permute-start.36 = (bf16[2,17,16,256]{3,2,1,0:T(8,128)(2,1)S(1)}, bf16[2,17,16,256]{3,2,1,0:T(8,128)(2,1)S(1)}, u32[]{:S(2)}, u32[]{:S(2)}) collective-permute-start(bf16[2,17,16,256]{3,2,1,0:T(8,128)(2,1)S(1)} %get-tuple-element.58), channel_id=1, source_target_pairs={{0,12},{1,13},{2,14},{3,15},{4,0},{5,1},{6,2},{7,3},{8,4},{9,5},{1... | collective-permute-start | bytes 835592 | tf_op jit(solution)/shard_map/ppermute | solution.py:52
  111.3 4.2 %collective-permute-done.34 = bf16[2,17,16,256]{3,2,1,0:T(8,128)(2,1)S(1)} collective-permute-done((bf16[2,17,16,256]{3,2,1,0:T(8,128)(2,1)S(1)}, bf16[2,17,16,256]{3,2,1,0:T(8,128)(2,1)S(1)}, u32[]{:S(2)}, u32[]{:S(2)}) %collective-permute-start.34) | collective-permute-done | bytes 278560 | tf_op jit(solution)/shard_map/ppermute | solution.py:52
  115.5 2.9 %collective-permute-done.35 = bf16[2,17,16,256]{3,2,1,0:T(8,128)(2,1)S(1)} collective-permute-done((bf16[2,17,16,256]{3,2,1,0:T(8,128)(2,1)S(1)}, bf16[2,17,16,256]{3,2,1,0:T(8,128)(2,1)S(1)}, u32[]{:S(2)}, u32[]{:S(2)}) %collective-permute-start.35) | collective-permute-done | bytes 278560 | tf_op jit(solution)/shard_map/ppermute | solution.py:52
  118.8 13.1 %all_to_all.11.parts = bf16[8,72,256]{2,1,0:T(8,128)(2,1)S(1)} all-to-all(bf16[8,72,256]{2,1,0:T(8,128)(2,1)S(1)} %pad_maximum_fusion.2), channel_id=1, replica_groups=mesh['zl'=2,'c'=2,'x'=4,'y'=4,'zh'=4] {'zl','zh'}, dimensions={0} | all-to-all | bytes 589824 | tf_op jit(solution)/shard_map/all_to_all | solution.py:473
  131.9 1.2 shard_map.87
  (71 shorter events, 2.7 us)
Async XLA Ops:
  22.1 8.4 %collective-permute-start = (bf16[17,16,256]{2,1,0:T(8,128)(2,1)S(1)}, bf16[17,16,256]{2,1,0:T(8,128)(2,1)S(1)}, u32[]{:S(2)}, u32[]{:S(2)}) collective-permute-start(bf16[17,16,256]{2,1,0:T(8,128)(2,1)S(1)} %get-tuple-element.64), channel_id=1, source_target_pairs={{0,48},{1,49},{2,50},{3,51},{4,52},{5,53},{6,54},{7,55},{8,56},{9,... | collective-permute-start | bytes 417800 | tf_op jit(solution)/shard_map/ppermute | solution.py:52
  24.9 6.7 %collective-permute-start.1 = (bf16[17,16,256]{2,1,0:T(8,128)(2,1)S(1)}, bf16[17,16,256]{2,1,0:T(8,128)(2,1)S(1)}, u32[]{:S(2)}, u32[]{:S(2)}) collective-permute-start(bf16[17,16,256]{2,1,0:T(8,128)(2,1)S(1)} %get-tuple-element.64), channel_id=1, source_target_pairs={{0,32},{1,33},{2,34},{3,35},{4,36},{5,37},{6,38},{7,39},{8,40},{9,... | collective-permute-start | bytes 417800 | tf_op jit(solution)/shard_map/ppermute | solution.py:52
  25.7 7.3 %collective-permute-start.2 = (bf16[17,16,256]{2,1,0:T(8,128)(2,1)S(1)}, bf16[17,16,256]{2,1,0:T(8,128)(2,1)S(1)}, u32[]{:S(2)}, u32[]{:S(2)}) collective-permute-start(bf16[17,16,256]{2,1,0:T(8,128)(2,1)S(1)} %get-tuple-element.64), channel_id=1, source_target_pairs={{0,16},{1,17},{2,18},{3,19},{4,20},{5,21},{6,22},{7,23},{8,24},{9,... | collective-permute-start | bytes 417800 | tf_op jit(solution)/shard_map/ppermute | solution.py:52
  26.6 10.3 %collective-permute-start.12 = (bf16[17,16,256]{2,1,0:T(8,128)(2,1)S(1)}, bf16[17,16,256]{2,1,0:T(8,128)(2,1)S(1)}, u32[]{:S(2)}, u32[]{:S(2)}) collective-permute-start(bf16[17,16,256]{2,1,0:T(8,128)(2,1)S(1)} %get-tuple-element.65), channel_id=1, source_target_pairs={{0,48},{1,49},{2,50},{3,51},{4,52},{5,53},{6,54},{7,55},{8,56},{9,... | collective-permute-start | bytes 417800 | tf_op jit(solution)/shard_map/ppermute | solution.py:52
  28.9 8.0 %collective-permute-start.13 = (bf16[17,16,256]{2,1,0:T(8,128)(2,1)S(1)}, bf16[17,16,256]{2,1,0:T(8,128)(2,1)S(1)}, u32[]{:S(2)}, u32[]{:S(2)}) collective-permute-start(bf16[17,16,256]{2,1,0:T(8,128)(2,1)S(1)} %get-tuple-element.65), channel_id=1, source_target_pairs={{0,32},{1,33},{2,34},{3,35},{4,36},{5,37},{6,38},{7,39},{8,40},{9,... | collective-permute-start | bytes 417800 | tf_op jit(solution)/shard_map/ppermute | solution.py:52
  30.5 6.5 %collective-permute-start.14 = (bf16[17,16,256]{2,1,0:T(8,128)(2,1)S(1)}, bf16[17,16,256]{2,1,0:T(8,128)(2,1)S(1)}, u32[]{:S(2)}, u32[]{:S(2)}) collective-permute-start(bf16[17,16,256]{2,1,0:T(8,128)(2,1)S(1)} %get-tuple-element.65), channel_id=1, source_target_pairs={{0,16},{1,17},{2,18},{3,19},{4,20},{5,21},{6,22},{7,23},{8,24},{9,... | collective-permute-start | bytes 417800 | tf_op jit(solution)/shard_map/ppermute | solution.py:52
  32.9 31.1 %copy-start = (bf16[2,2,128,2048]{3,2,1,0:T(8,128)(2,1)S(1)}, bf16[2,2,128,2048]{3,2,1,0:T(8,128)(2,1)}, u32[]{:S(2)}) copy-start(bf16[2,2,128,2048]{3,2,1,0:T(8,128)(2,1)} %xs.5) | copy-start | bytes 6291460
  33.9 10.4 %collective-permute-start.3 = (bf16[4,17,16,256]{3,2,1,0:T(8,128)(2,1)}, bf16[4,17,16,256]{3,2,1,0:T(8,128)(2,1)}, u32[]{:S(2)}, u32[]{:S(2)}) collective-permute-start(bf16[4,17,16,256]{3,2,1,0:T(8,128)(2,1)} %pad_maximum_fusion.refs_0_), channel_id=1, source_target_pairs={{0,12},{1,13},{2,14},{3,15},{4,0},{5,1},{6,2},{7,3},{8,4},{9,5},{1... | collective-permute-start | bytes 1671176 | tf_op jit(solution)/shard_map/ppermute | solution.py:52
  36.9 11.1 %collective-permute-start.4 = (bf16[4,17,16,256]{3,2,1,0:T(8,128)(2,1)}, bf16[4,17,16,256]{3,2,1,0:T(8,128)(2,1)}, u32[]{:S(2)}, u32[]{:S(2)}) collective-permute-start(bf16[4,17,16,256]{3,2,1,0:T(8,128)(2,1)} %pad_maximum_fusion.refs_0_), channel_id=1, source_target_pairs={{0,4},{1,5},{2,6},{3,7},{4,8},{5,9},{6,10},{7,11},{8,12},{9,13},{1... | collective-permute-start | bytes 1671176 | tf_op jit(solution)/shard_map/ppermute | solution.py:52
  37.1 14.3 %collective-permute-start.15 = (bf16[4,17,16,256]{3,2,1,0:T(8,128)(2,1)S(1)}, bf16[4,17,16,256]{3,2,1,0:T(8,128)(2,1)S(1)}, u32[]{:S(2)}, u32[]{:S(2)}) collective-permute-start(bf16[4,17,16,256]{3,2,1,0:T(8,128)(2,1)S(1)} %pad_maximum_fusion.1.refs_0_), channel_id=1, source_target_pairs={{0,12},{1,13},{2,14},{3,15},{4,0},{5,1},{6,2},{7,3},{8,4},{9,5},{1... | collective-permute-start | bytes 1671176 | tf_op jit(solution)/shard_map/ppermute | solution.py:52
  40.6 13.3 %collective-permute-start.16 = (bf16[4,17,16,256]{3,2,1,0:T(8,128)(2,1)S(1)}, bf16[4,17,16,256]{3,2,1,0:T(8,128)(2,1)}, u32[]{:S(2)}, u32[]{:S(2)}) collective-permute-start(bf16[4,17,16,256]{3,2,1,0:T(8,128)(2,1)S(1)} %pad_maximum_fusion.1.refs_0_), channel_id=1, source_target_pairs={{0,4},{1,5},{2,6},{3,7},{4,8},{5,9},{6,10},{7,11},{8,12},{9,13},{1... | collective-permute-start | bytes 1671176 | tf_op jit(solution)/shard_map/ppermute | solution.py:52
  40.6 16.5 %collective-permute-start.7 = (bf16[4,17,16,256]{3,2,1,0:T(8,128)(2,1)}, bf16[4,17,16,256]{3,2,1,0:T(8,128)(2,1)}, u32[]{:S(2)}, u32[]{:S(2)}) collective-permute-start(bf16[4,17,16,256]{3,2,1,0:T(8,128)(2,1)} %pad_maximum_fusion.refs_0_), channel_id=1, source_target_pairs={{0,64},{1,65},{2,66},{3,67},{4,68},{5,69},{6,70},{7,71},{8,72},{9,... | collective-permute-start | bytes 1671176 | tf_op jit(solution)/shard_map/ppermute | solution.py:52
  49.2 7.9 %collective-permute-start.5 = (bf16[2,17,16,256]{3,2,1,0:T(8,128)(2,1)S(1)}, bf16[2,17,16,256]{3,2,1,0:T(8,128)(2,1)S(1)}, u32[]{:S(2)}, u32[]{:S(2)}) collective-permute-start(bf16[2,17,16,256]{3,2,1,0:T(8,128)(2,1)S(1)} %get-tuple-element.32), channel_id=1, source_target_pairs={{0,12},{1,13},{2,14},{3,15},{4,0},{5,1},{6,2},{7,3},{8,4},{9,5},{1... | collective-permute-start | bytes 835592 | tf_op jit(solution)/shard_map/ppermute | solution.py:52
  49.3 8.3 %collective-permute-start.6 = (bf16[2,17,16,256]{3,2,1,0:T(8,128)(2,1)S(1)}, bf16[2,17,16,256]{3,2,1,0:T(8,128)(2,1)S(1)}, u32[]{:S(2)}, u32[]{:S(2)}) collective-permute-start(bf16[2,17,16,256]{3,2,1,0:T(8,128)(2,1)S(1)} %get-tuple-element.33), channel_id=1, source_target_pairs={{0,4},{1,5},{2,6},{3,7},{4,8},{5,9},{6,10},{7,11},{8,12},{9,13},{1... | collective-permute-start | bytes 835592 | tf_op jit(solution)/shard_map/ppermute | solution.py:52
  55.0 6.6 %collective-permute-start.17 = (bf16[2,17,16,256]{3,2,1,0:T(8,128)(2,1)S(1)}, bf16[2,17,16,256]{3,2,1,0:T(8,128)(2,1)S(1)}, u32[]{:S(2)}, u32[]{:S(2)}) collective-permute-start(bf16[2,17,16,256]{3,2,1,0:T(8,128)(2,1)S(1)} %get-tuple-element.36), channel_id=1, source_target_pairs={{0,12},{1,13},{2,14},{3,15},{4,0},{5,1},{6,2},{7,3},{8,4},{9,5},{1... | collective-permute-start | bytes 835592 | tf_op jit(solution)/shard_map/ppermute | solution.py:52
  55.1 7.8 %collective-permute-start.18 = (bf16[2,17,16,256]{3,2,1,0:T(8,128)(2,1)S(1)}, bf16[2,17,16,256]{3,2,1,0:T(8,128)(2,1)S(1)}, u32[]{:S(2)}, u32[]{:S(2)}) collective-permute-start(bf16[2,17,16,256]{3,2,1,0:T(8,128)(2,1)S(1)} %get-tuple-element.37), channel_id=1, source_target_pairs={{0,4},{1,5},{2,6},{3,7},{4,8},{5,9},{6,10},{7,11},{8,12},{9,13},{1... | collective-permute-start | bytes 835592 | tf_op jit(solution)/shard_map/ppermute | solution.py:52
  57.1 6.4 %collective-permute-start.8 = (bf16[4,17,16,256]{3,2,1,0:T(8,128)(2,1)}, bf16[4,17,16,256]{3,2,1,0:T(8,128)(2,1)S(1)}, u32[]{:S(2)}, u32[]{:S(2)}) collective-permute-start(bf16[4,17,16,256]{3,2,1,0:T(8,128)(2,1)} %collective-permute-done.3.after.refs_1_), channel_id=1, source_target_pairs={{0,64},{1,65},{2,66},{3,67},{4,68},{5,69},{6,70},{7,71},{8,72},{9,... | collective-permute-start | bytes 1671176 | tf_op jit(solution)/shard_map/ppermute | solution.py:52
  57.1 6.8 %collective-permute-start.9 = (bf16[4,17,16,256]{3,2,1,0:T(8,128)(2,1)}, bf16[4,17,16,256]{3,2,1,0:T(8,128)(2,1)S(1)}, u32[]{:S(2)}, u32[]{:S(2)}) collective-permute-start(bf16[4,17,16,256]{3,2,1,0:T(8,128)(2,1)} %collective-permute-done.4.before.refs_2_), channel_id=1, source_target_pairs={{0,64},{1,65},{2,66},{3,67},{4,68},{5,69},{6,70},{7,71},{8,72},{9,... | collective-permute-start | bytes 1671176 | tf_op jit(solution)/shard_map/ppermute | solution.py:52
  57.6 5.3 %collective-permute-start.10 = (bf16[2,17,16,256]{3,2,1,0:T(8,128)(2,1)S(1)}, bf16[2,17,16,256]{3,2,1,0:T(8,128)(2,1)S(1)}, u32[]{:S(2)}, u32[]{:S(2)}) collective-permute-start(bf16[2,17,16,256]{3,2,1,0:T(8,128)(2,1)S(1)} %collective-permute-done.5.refs_3_), channel_id=1, source_target_pairs={{0,64},{1,65},{2,66},{3,67},{4,68},{5,69},{6,70},{7,71},{8,72},{9,... | collective-permute-start | bytes 835592 | tf_op jit(solution)/shard_map/ppermute | solution.py:52
  61.6 1.8 %collective-permute-start.11 = (bf16[2,17,16,256]{3,2,1,0:T(8,128)(2,1)S(1)}, bf16[2,17,16,256]{3,2,1,0:T(8,128)(2,1)S(1)}, u32[]{:S(2)}, u32[]{:S(2)}) collective-permute-start(bf16[2,17,16,256]{3,2,1,0:T(8,128)(2,1)S(1)} %collective-permute-done.6.refs_4_), channel_id=1, source_target_pairs={{0,64},{1,65},{2,66},{3,67},{4,68},{5,69},{6,70},{7,71},{8,72},{9,... | collective-permute-start | bytes 835592 | tf_op jit(solution)/shard_map/ppermute | solution.py:52
  62.9 6.1 %collective-permute-start.19 = (bf16[4,17,16,256]{3,2,1,0:T(8,128)(2,1)S(1)}, bf16[4,17,16,256]{3,2,1,0:T(8,128)(2,1)S(1)}, u32[]{:S(2)}, u32[]{:S(2)}) collective-permute-start(bf16[4,17,16,256]{3,2,1,0:T(8,128)(2,1)S(1)} %pad_maximum_fusion.1.refs_0_), channel_id=1, source_target_pairs={{0,64},{1,65},{2,66},{3,67},{4,68},{5,69},{6,70},{7,71},{8,72},{9,... | collective-permute-start | bytes 1671176 | tf_op jit(solution)/shard_map/ppermute | solution.py:52
  62.9 6.1 %collective-permute-start.20 = (bf16[4,17,16,256]{3,2,1,0:T(8,128)(2,1)S(1)}, bf16[4,17,16,256]{3,2,1,0:T(8,128)(2,1)S(1)}, u32[]{:S(2)}, u32[]{:S(2)}) collective-permute-start(bf16[4,17,16,256]{3,2,1,0:T(8,128)(2,1)S(1)} %collective-permute-done.15.after.refs_1_), channel_id=1, source_target_pairs={{0,64},{1,65},{2,66},{3,67},{4,68},{5,69},{6,70},{7,71},{8,72},{9,... | collective-permute-start | bytes 1671176 | tf_op jit(solution)/shard_map/ppermute | solution.py:52
  63.5 5.6 %collective-permute-start.21 = (bf16[4,17,16,256]{3,2,1,0:T(8,128)(2,1)}, bf16[4,17,16,256]{3,2,1,0:T(8,128)(2,1)S(1)}, u32[]{:S(2)}, u32[]{:S(2)}) collective-permute-start(bf16[4,17,16,256]{3,2,1,0:T(8,128)(2,1)} %collective-permute-done.16.before.refs_2_), channel_id=1, source_target_pairs={{0,64},{1,65},{2,66},{3,67},{4,68},{5,69},{6,70},{7,71},{8,72},{9,... | collective-permute-start | bytes 1671176 | tf_op jit(solution)/shard_map/ppermute | solution.py:52
  63.5 5.5 %collective-permute-start.22 = (bf16[2,17,16,256]{3,2,1,0:T(8,128)(2,1)S(1)}, bf16[2,17,16,256]{3,2,1,0:T(8,128)(2,1)S(1)}, u32[]{:S(2)}, u32[]{:S(2)}) collective-permute-start(bf16[2,17,16,256]{3,2,1,0:T(8,128)(2,1)S(1)} %collective-permute-done.17.refs_3_), channel_id=1, source_target_pairs={{0,64},{1,65},{2,66},{3,67},{4,68},{5,69},{6,70},{7,71},{8,72},{9,... | collective-permute-start | bytes 835592 | tf_op jit(solution)/shard_map/ppermute | solution.py:52
  64.0 5.1 %collective-permute-start.23 = (bf16[2,17,16,256]{3,2,1,0:T(8,128)(2,1)S(1)}, bf16[2,17,16,256]{3,2,1,0:T(8,128)(2,1)S(1)}, u32[]{:S(2)}, u32[]{:S(2)}) collective-permute-start(bf16[2,17,16,256]{3,2,1,0:T(8,128)(2,1)S(1)} %collective-permute-done.18.refs_4_), channel_id=1, source_target_pairs={{0,64},{1,65},{2,66},{3,67},{4,68},{5,69},{6,70},{7,71},{8,72},{9,... | collective-permute-start | bytes 835592 | tf_op jit(solution)/shard_map/ppermute | solution.py:52
  65.0 4.1 %copy-start.1 = (bf16[2,2,128,2048]{3,2,1,0:T(8,128)(2,1)S(1)}, bf16[2,2,128,2048]{3,2,1,0:T(8,128)(2,1)}, u32[]{:S(2)}) copy-start(bf16[2,2,128,2048]{3,2,1,0:T(8,128)(2,1)} %cots.1) | copy-start | bytes 6291460
  74.9 4.4 %collective-permute-start.29 = (bf16[144,4608]{1,0:T(8,128)(2,1)S(1)}, bf16[144,4608]{1,0:T(8,128)(2,1)S(1)}, u32[]{:S(2)}, u32[]{:S(2)}) collective-permute-start(bf16[144,4608]{1,0:T(8,128)(2,1)S(1)} %slice_bitcast_fusion.1), channel_id=1, source_target_pairs={{0,64},{1,65},{2,66},{3,67},{4,68},{5,69},{6,70},{7,71},{8,72},{9,... | collective-permute-start | bytes 3981320 | tf_op jit(solution)/shard_map/ppermute | solution.py:52
  79.2 4.8 %collective-permute-start.24 = (bf16[144,4608]{1,0:T(8,128)(2,1)S(1)}, bf16[144,4608]{1,0:T(8,128)(2,1)S(1)}, u32[]{:S(2)}, u32[]{:S(2)}) collective-permute-start(bf16[144,4608]{1,0:T(8,128)(2,1)S(1)} %slice_bitcast_fusion), channel_id=1, source_target_pairs={{0,64},{1,65},{2,66},{3,67},{4,68},{5,69},{6,70},{7,71},{8,72},{9,... | collective-permute-start | bytes 3981320 | tf_op jit(solution)/shard_map/ppermute | solution.py:52
  80.7 8.0 %collective-permute-start.30 = (bf16[2,17,16,256]{3,2,1,0:T(8,128)(2,1)S(1)}, bf16[2,17,16,256]{3,2,1,0:T(8,128)(2,1)S(1)}, u32[]{:S(2)}, u32[]{:S(2)}) collective-permute-start(bf16[2,17,16,256]{3,2,1,0:T(8,128)(2,1)S(1)} %get-tuple-element.51), channel_id=1, source_target_pairs={{0,16},{1,17},{2,18},{3,19},{4,20},{5,21},{6,22},{7,23},{8,24},{9,... | collective-permute-start | bytes 835592 | tf_op jit(solution)/shard_map/ppermute | solution.py:52
  80.8 7.9 %collective-permute-start.31 = (bf16[2,17,16,256]{3,2,1,0:T(8,128)(2,1)S(1)}, bf16[2,17,16,256]{3,2,1,0:T(8,128)(2,1)S(1)}, u32[]{:S(2)}, u32[]{:S(2)}) collective-permute-start(bf16[2,17,16,256]{3,2,1,0:T(8,128)(2,1)S(1)} %get-tuple-element.52), channel_id=1, source_target_pairs={{0,48},{1,49},{2,50},{3,51},{4,52},{5,53},{6,54},{7,55},{8,56},{9,... | collective-permute-start | bytes 835592 | tf_op jit(solution)/shard_map/ppermute | solution.py:52
  85.4 7.8 %collective-permute-start.25 = (bf16[2,17,16,256]{3,2,1,0:T(8,128)(2,1)S(1)}, bf16[2,17,16,256]{3,2,1,0:T(8,128)(2,1)S(1)}, u32[]{:S(2)}, u32[]{:S(2)}) collective-permute-start(bf16[2,17,16,256]{3,2,1,0:T(8,128)(2,1)S(1)} %get-tuple-element.45), channel_id=1, source_target_pairs={{0,16},{1,17},{2,18},{3,19},{4,20},{5,21},{6,22},{7,23},{8,24},{9,... | collective-permute-start | bytes 835592 | tf_op jit(solution)/shard_map/ppermute | solution.py:52
  85.5 7.7 %collective-permute-start.26 = (bf16[2,17,16,256]{3,2,1,0:T(8,128)(2,1)S(1)}, bf16[2,17,16,256]{3,2,1,0:T(8,128)(2,1)S(1)}, u32[]{:S(2)}, u32[]{:S(2)}) collective-permute-start(bf16[2,17,16,256]{3,2,1,0:T(8,128)(2,1)S(1)} %get-tuple-element.46), channel_id=1, source_target_pairs={{0,48},{1,49},{2,50},{3,51},{4,52},{5,53},{6,54},{7,55},{8,56},{9,... | collective-permute-start | bytes 835592 | tf_op jit(solution)/shard_map/ppermute | solution.py:52
  89.4 10.8 %collective-permute-start.32 = (bf16[4,17,16,256]{3,2,1,0:T(8,128)(2,1)S(1)}, bf16[4,17,16,256]{3,2,1,0:T(8,128)(2,1)S(1)}, u32[]{:S(2)}, u32[]{:S(2)}) collective-permute-start(bf16[4,17,16,256]{3,2,1,0:T(8,128)(2,1)S(1)} %get-tuple-element.53), channel_id=1, source_target_pairs={{0,16},{1,17},{2,18},{3,19},{4,20},{5,21},{6,22},{7,23},{8,24},{9,... | collective-permute-start | bytes 1671176 | tf_op jit(solution)/shard_map/ppermute | solution.py:52
  89.5 10.7 %collective-permute-start.33 = (bf16[4,17,16,256]{3,2,1,0:T(8,128)(2,1)S(1)}, bf16[4,17,16,256]{3,2,1,0:T(8,128)(2,1)S(1)}, u32[]{:S(2)}, u32[]{:S(2)}) collective-permute-start(bf16[4,17,16,256]{3,2,1,0:T(8,128)(2,1)S(1)} %get-tuple-element.54), channel_id=1, source_target_pairs={{0,48},{1,49},{2,50},{3,51},{4,52},{5,53},{6,54},{7,55},{8,56},{9,... | collective-permute-start | bytes 1671176 | tf_op jit(solution)/shard_map/ppermute | solution.py:52
  93.9 12.3 %collective-permute-start.27 = (bf16[4,17,16,256]{3,2,1,0:T(8,128)(2,1)S(1)}, bf16[4,17,16,256]{3,2,1,0:T(8,128)(2,1)S(1)}, u32[]{:S(2)}, u32[]{:S(2)}) collective-permute-start(bf16[4,17,16,256]{3,2,1,0:T(8,128)(2,1)S(1)} %get-tuple-element.47), channel_id=1, source_target_pairs={{0,16},{1,17},{2,18},{3,19},{4,20},{5,21},{6,22},{7,23},{8,24},{9,... | collective-permute-start | bytes 1671176 | tf_op jit(solution)/shard_map/ppermute | solution.py:52
  94.0 12.2 %collective-permute-start.28 = (bf16[4,17,16,256]{3,2,1,0:T(8,128)(2,1)S(1)}, bf16[4,17,16,256]{3,2,1,0:T(8,128)(2,1)S(1)}, u32[]{:S(2)}, u32[]{:S(2)}) collective-permute-start(bf16[4,17,16,256]{3,2,1,0:T(8,128)(2,1)S(1)} %get-tuple-element.48), channel_id=1, source_target_pairs={{0,48},{1,49},{2,50},{3,51},{4,52},{5,53},{6,54},{7,55},{8,56},{9,... | collective-permute-start | bytes 1671176 | tf_op jit(solution)/shard_map/ppermute | solution.py:52
  107.2 8.2 %collective-permute-start.34 = (bf16[2,17,16,256]{3,2,1,0:T(8,128)(2,1)S(1)}, bf16[2,17,16,256]{3,2,1,0:T(8,128)(2,1)S(1)}, u32[]{:S(2)}, u32[]{:S(2)}) collective-permute-start(bf16[2,17,16,256]{3,2,1,0:T(8,128)(2,1)S(1)} %get-tuple-element.56), channel_id=1, source_target_pairs={{0,8},{1,9},{2,10},{3,11},{4,12},{5,13},{6,14},{7,15},{8,0},{9,1},... | collective-permute-start | bytes 835592 | tf_op jit(solution)/shard_map/ppermute | solution.py:52
  108.1 10.3 %collective-permute-start.35 = (bf16[2,17,16,256]{3,2,1,0:T(8,128)(2,1)S(1)}, bf16[2,17,16,256]{3,2,1,0:T(8,128)(2,1)S(1)}, u32[]{:S(2)}, u32[]{:S(2)}) collective-permute-start(bf16[2,17,16,256]{3,2,1,0:T(8,128)(2,1)S(1)} %get-tuple-element.57), channel_id=1, source_target_pairs={{0,4},{1,5},{2,6},{3,7},{4,8},{5,9},{6,10},{7,11},{8,12},{9,13},{1... | collective-permute-start | bytes 835592 | tf_op jit(solution)/shard_map/ppermute | solution.py:52
  109.2 9.2 %collective-permute-start.36 = (bf16[2,17,16,256]{3,2,1,0:T(8,128)(2,1)S(1)}, bf16[2,17,16,256]{3,2,1,0:T(8,128)(2,1)S(1)}, u32[]{:S(2)}, u32[]{:S(2)}) collective-permute-start(bf16[2,17,16,256]{3,2,1,0:T(8,128)(2,1)S(1)} %get-tuple-element.58), channel_id=1, source_target_pairs={{0,12},{1,13},{2,14},{3,15},{4,0},{5,1},{6,2},{7,3},{8,4},{9,5},{1... | collective-permute-start | bytes 835592 | tf_op jit(solution)/shard_map/ppermute | solution.py:52

commit v8 on v7

--- a/solution.py
+++ b/solution.py
@@ -173,11 +173,6 @@
     hat_pass(lambda rows: xs[zl, c, rows, :], hat, keep_stat)
 
 
-def kernel_halves(s_ref, after, before, low, high):
-    low[...] = after[0:2]
-    high[...] = before[2:4]
-
-
 def kernel_low_forward(s_ref, xs, hat0, *refs):
     pieces = refs[: 2 * PIECES]
     x1, x2, win, wout, stat1, pre, normed, hat1 = refs[2 * PIECES :]
@@ -341,7 +336,7 @@
 
 
 UNROLL = 8
-SPANS = ((0, 0, 4), (1, 0, 4), (3, 0, 4), (2, 0, 2), (2, 2, 2))
+SPANS = tuple((b, 0, 4) for b in range(4))
 PIECES = len(SPANS)
 UP_AT, ACT_AT, PRE_AT, WIDE = D, 2 * D, 2 * D + R, 2 * D + 2 * R
 ACT = (ROWS, D)
@@ -424,13 +419,9 @@
     for p in range(2):
         near.append([block[p]] + [shift(block[p], send_first(-k)) for k in (1, 2, 3)])
     pairs = []
-    half = array(2, 17, 16, 256)
     for p in range(2):
         row = jnp.stack(near[p])
-        after, before = shift(row, send_second(-1)), shift(row, send_second(1))
-        low, high = call(kernel_halves, scalars, [after, before], [half, half], [])
-        across = [shift(low, send_second(-1)), shift(high, send_second(1))]
-        rows = [row, after, before, *across]
+        rows = [row] + [shift(row, send_second(-k)) for k in (1, 2, 3)]
         pairs.append(rows + [shift(v, SWAP) for v in rows])
     x1, x2, win, wout, stat1, pre = call(
         kernel_low_forward,

time: 135 us -> 155 us (1.15)
  waiting for transfers between devices: 34.1 us -> 57.3 us
  starting transfers between devices: 39.1 us -> 32.2 us
  local copies, waits for them, and re-layouts: 1.57 us -> 8.14 us
  Pallas kernels: 22.8 us -> 21.1 us
    ppermute x37 -> x33, waiting for transfers between devices: 34.1 us -> 57.3 us  [shift(): return lax.ppermute(value, AXES, pairs)]
    ppermute x37 -> x33, starting transfers between devices: 39.1 us -> 32.2 us  [shift(): return lax.ppermute(value, AXES, pairs)]
    unnamed x6 -> x26, local copies, waits for them, and re-layouts: 0.84 us -> 7.41 us
    pallas_call x12 -> x10, Pallas kernels: 22.8 us -> 21.1 us  [call(): pl.pallas_call(body, in_specs=[pl.BlockSpec(memory_space=pltpu.SMEM)] + [...]
  transfers between devices with their start and end apart: 37 -> 33, of which waited for: 13 -> 14; matrix products, arithmetic and copies ran while one was open for 1% -> 0% of each run, Pallas kernels for 11% -> 8%
where the time goes in v8:
time: 155 us; the launch traced here: 153 us
  waiting for transfers between devices  57.3 us (37%)
  starting transfers between devices  32.2 us (21%)
  blocking collectives  31.9 us (21%)
  Pallas kernels  21.1 us (14%)
  local copies, waits for them, and re-layouts  8.14 us (5%)
    ppermute x33, waiting for transfers between devices, shift(): return lax.ppermute(value, AXES, pairs)  57.3 us
    ppermute x33, starting transfers between devices, shift(): return lax.ppermute(value, AXES, pairs)  32.2 us
    pallas_call x10, Pallas kernels, call(): pl.pallas_call(body, in_specs=[pl.BlockSpec(memory_space=pltpu.SMEM)] + [...  21.1 us
    all_to_all x1, blocking collectives, device_body(): lax.all_to_all(jnp.broadcast_to(shard[None], (8, 72, 256)), ('zl', 'zh'),...  19.5 us
    all_to_all x1, blocking collectives, device_body(): lax.all_to_all(parts, ('zl', 'zh'), 0, 0)  12.4 us
    unnamed x26, local copies, waits for them, and re-layouts  7.41 us
  transfers between devices with their start and end apart: 33, of which 14 were waited for; matrix products, arithmetic and copies ran while one was open for 0% of the time, Pallas kernels for 8%

profile of v8, /device:TPU:32, one launch (start us, length us, event | category | flops | bytes accessed | tf_op | source)
XLA Modules:
  0.0 152.8 jit_solution(4855835004574272381)
XLA Ops:
  0.6 0.7 copy.39
  1.4 0.7 fusion.3
  2.1 19.5 %all_to_all.10 = bf16[8,72,256]{2,1,0:T(8,128)(2,1)S(1)} all-to-all(bf16[8,72,256]{2,1,0:T(8,128)(2,1)S(1)} %broadcast_in_dim.2), channel_id=1, replica_groups=mesh['zl'=2,'c'=2,'x'=4,'y'=4,'zh'=4] {'zl','zh'}, dimensions={0} | all-to-all | bytes 589824 | tf_op jit(solution)/shard_map/all_to_all | solution.py:403
  22.1 2.8 %collective-permute-start = (bf16[17,16,256]{2,1,0:T(8,128)(2,1)S(1)}, bf16[17,16,256]{2,1,0:T(8,128)(2,1)S(1)}, u32[]{:S(2)}, u32[]{:S(2)}) collective-permute-start(bf16[17,16,256]{2,1,0:T(8,128)(2,1)S(1)} %get-tuple-element.56), channel_id=1, source_target_pairs={{0,48},{1,49},{2,50},{3,51},{4,52},{5,53},{6,54},{7,55},{8,56},{9,... | collective-permute-start | bytes 417800 | tf_op jit(solution)/shard_map/ppermute | solution.py:52
  24.9 0.8 collective-permute-start.1
  25.7 0.9 collective-permute-start.2
  26.6 2.4 %collective-permute-done = bf16[17,16,256]{2,1,0:T(8,128)(2,1)S(1)} collective-permute-done((bf16[17,16,256]{2,1,0:T(8,128)(2,1)S(1)}, bf16[17,16,256]{2,1,0:T(8,128)(2,1)S(1)}, u32[]{:S(2)}, u32[]{:S(2)}) %collective-permute-start) | collective-permute-done | bytes 139296 | tf_op jit(solution)/shard_map/ppermute | solution.py:52
  29.0 2.6 %collective-permute-done.1 = bf16[17,16,256]{2,1,0:T(8,128)(2,1)S(1)} collective-permute-done((bf16[17,16,256]{2,1,0:T(8,128)(2,1)S(1)}, bf16[17,16,256]{2,1,0:T(8,128)(2,1)S(1)}, u32[]{:S(2)}, u32[]{:S(2)}) %collective-permute-start.1) | collective-permute-done | bytes 139296 | tf_op jit(solution)/shard_map/ppermute | solution.py:52
  31.6 1.4 collective-permute-done.2
  33.0 3.1 %collective-permute-start.3 = (bf16[4,17,16,256]{3,2,1,0:T(8,128)(2,1)S(1)}, bf16[4,17,16,256]{3,2,1,0:T(8,128)(2,1)S(1)}, u32[]{:S(2)}, u32[]{:S(2)}) collective-permute-start(bf16[4,17,16,256]{3,2,1,0:T(8,128)(2,1)S(1)} %pad_maximum_fusion.refs_0_), channel_id=1, source_target_pairs={{0,12},{1,13},{2,14},{3,15},{4,0},{5,1},{6,2},{7,3},{8,4},{9,5},{1... | collective-permute-start | bytes 1671176 | tf_op jit(solution)/shard_map/ppermute | solution.py:52
  36.8 1.0 collective-permute-start.5
  38.3 9.5 %collective-permute-done.10 = bf16[17,16,256]{2,1,0:T(8,128)(2,1)S(1)} collective-permute-done((bf16[17,16,256]{2,1,0:T(8,128)(2,1)S(1)}, bf16[17,16,256]{2,1,0:T(8,128)(2,1)S(1)}, u32[]{:S(2)}, u32[]{:S(2)}) %collective-permute-start.10) | collective-permute-done | bytes 139296 | tf_op jit(solution)/shard_map/ppermute | solution.py:52
  47.8 6.6 %collective-permute-done.11 = bf16[17,16,256]{2,1,0:T(8,128)(2,1)S(1)} collective-permute-done((bf16[17,16,256]{2,1,0:T(8,128)(2,1)S(1)}, bf16[17,16,256]{2,1,0:T(8,128)(2,1)S(1)}, u32[]{:S(2)}, u32[]{:S(2)}) %collective-permute-start.11) | collective-permute-done | bytes 139296 | tf_op jit(solution)/shard_map/ppermute | solution.py:52
  54.4 1.0 collective-permute-start.12
  55.4 5.7 %collective-permute-done.12 = bf16[17,16,256]{2,1,0:T(8,128)(2,1)S(1)} collective-permute-done((bf16[17,16,256]{2,1,0:T(8,128)(2,1)S(1)}, bf16[17,16,256]{2,1,0:T(8,128)(2,1)S(1)}, u32[]{:S(2)}, u32[]{:S(2)}) %collective-permute-start.12) | collective-permute-done | bytes 139296 | tf_op jit(solution)/shard_map/ppermute | solution.py:52
  61.1 0.9 collective-permute-start.13
  62.7 0.9 collective-permute-start.15
  63.6 0.8 copy-done.2
  64.4 0.8 copy-done.6
  65.7 0.8 copy-done.4
  66.5 4.3 %collective-permute-done.13.refs_1_ = bf16[4,17,16,256]{3,2,1,0:T(8,128)(2,1)} collective-permute-done((bf16[4,17,16,256]{3,2,1,0:T(8,128)(2,1)S(1)}, bf16[4,17,16,256]{3,2,1,0:T(8,128)(2,1)}, u32[]{:S(2)}, u32[]{:S(2)}) %collective-permute-start.13) | collective-permute-done | bytes 557088 | tf_op jit(solution)/shard_map/ppermute | solution.py:52
  70.9 2.5 %collective-permute-done.14.refs_2_ = bf16[4,17,16,256]{3,2,1,0:T(8,128)(2,1)} collective-permute-done((bf16[4,17,16,256]{3,2,1,0:T(8,128)(2,1)S(1)}, bf16[4,17,16,256]{3,2,1,0:T(8,128)(2,1)}, u32[]{:S(2)}, u32[]{:S(2)}) %collective-permute-start.14) | collective-permute-done | bytes 557088 | tf_op jit(solution)/shard_map/ppermute | solution.py:52
  73.3 5.9 %collective-permute-done.15.refs_3_ = bf16[4,17,16,256]{3,2,1,0:T(8,128)(2,1)} collective-permute-done((bf16[4,17,16,256]{3,2,1,0:T(8,128)(2,1)S(1)}, bf16[4,17,16,256]{3,2,1,0:T(8,128)(2,1)}, u32[]{:S(2)}, u32[]{:S(2)}) %collective-permute-start.15) | collective-permute-done | bytes 557088 | tf_op jit(solution)/shard_map/ppermute | solution.py:52
  79.2 0.8 copy-done.8
  80.5 0.8 copy-done.10
  81.4 0.9 shard_map.76
  82.8 1.1 copy-done.9
  83.8 1.1 copy-done.11
  84.9 3.7 %shard_map.77 = (bf16[128,2048]{1,0:T(8,128)(2,1)S(1)}, bf16[128,2048]{1,0:T(8,128)(2,1)S(1)}, bf16[2,128,16,256]{3,2,1,0:T(8,128)(2,1)S(1)}, bf16[2,9,16,16,256...) custom-call(s32[4]{0:T(128)S(1)} %pad_add_fusion.s_ref, ...), custom_call_target="tpu_custom_call" | custom-call | tf_op jit(solution)/shard_map/pallas_call | solution.py:357
  88.6 6.8 %shard_map.78 = (bf16[128,2048]{1,0:T(8,128)(2,1)S(1)}, bf16[2,144,4608]{2,1,0:T(8,128)(2,1)S(1)}) custom-call(s32[4]{0:T(128)S(1)} %pad_add_fusion.s_ref, bf16[128,2048]{1,0:T(8,128)(2,1)S(1)} %get-tuple-element.29.x2, bf16[2,2,128,2048]{3,2,1,0:T(8,128)(2,1)S(1)} %copy-done.1, bf16[4,17,16,256]{3,2,1,0:T(8,128)(2,1)S(1)} %pad_maximum_fusion.1.refs_0_, ...), custom_call_target="tpu_custom_call" | custom-call | tf_op jit(solution)/shard_map/pallas_call | solution.py:357
  96.1 3.4 %shard_map.79.acts = bf16[2,144,4608]{2,1,0:T(8,128)(2,1)S(1)} custom-call(s32[4]{0:T(128)S(1)} %pad_add_fusion.s_ref, bf16[2,2,128,2048]{3,2,1,0:T(8,128)(2,1)S(1)} %copy-done, bf16[128,2048]{1,0:T(8,128)(2,1)S(1)} %get-tuple-element.28.x1, bf16[128,2048]{1,0:T(8,128)(2,1)S(1)} %get-tuple-element.30.up2, ...), custom_call_target="tpu_custom_call" | custom-call | tf_op jit(solution)/shard_map/pallas_call | solution.py:357
  99.7 1.3 shard_map.82
  101.1 3.2 %collective-permute-start.27 = (bf16[2,17,16,256]{3,2,1,0:T(8,128)(2,1)S(1)}, bf16[2,17,16,256]{3,2,1,0:T(8,128)(2,1)S(1)}, u32[]{:S(2)}, u32[]{:S(2)}) collective-permute-start(bf16[2,17,16,256]{3,2,1,0:T(8,128)(2,1)S(1)} %get-tuple-element.44), channel_id=1, source_target_pairs={{0,48},{1,49},{2,50},{3,51},{4,52},{5,53},{6,54},{7,55},{8,56},{9,... | collective-permute-start | bytes 835592 | tf_op jit(solution)/shard_map/ppermute | solution.py:52
  104.4 1.3 shard_map.80
  105.8 3.2 %collective-permute-start.22 = (bf16[2,17,16,256]{3,2,1,0:T(8,128)(2,1)S(1)}, bf16[2,17,16,256]{3,2,1,0:T(8,128)(2,1)S(1)}, u32[]{:S(2)}, u32[]{:S(2)}) collective-permute-start(bf16[2,17,16,256]{3,2,1,0:T(8,128)(2,1)S(1)} %get-tuple-element.38), channel_id=1, source_target_pairs={{0,48},{1,49},{2,50},{3,51},{4,52},{5,53},{6,54},{7,55},{8,56},{9,... | collective-permute-start | bytes 835592 | tf_op jit(solution)/shard_map/ppermute | solution.py:52
  109.0 0.7 shard_map.83
  109.9 3.2 %collective-permute-start.29 = (bf16[4,17,16,256]{3,2,1,0:T(8,128)(2,1)S(1)}, bf16[4,17,16,256]{3,2,1,0:T(8,128)(2,1)S(1)}, u32[]{:S(2)}, u32[]{:S(2)}) collective-permute-start(bf16[4,17,16,256]{3,2,1,0:T(8,128)(2,1)S(1)} %get-tuple-element.46), channel_id=1, source_target_pairs={{0,48},{1,49},{2,50},{3,51},{4,52},{5,53},{6,54},{7,55},{8,56},{9,... | collective-permute-start | bytes 1671176 | tf_op jit(solution)/shard_map/ppermute | solution.py:52
  113.5 0.7 shard_map.81
  114.4 3.3 %collective-permute-start.24 = (bf16[4,17,16,256]{3,2,1,0:T(8,128)(2,1)S(1)}, bf16[4,17,16,256]{3,2,1,0:T(8,128)(2,1)S(1)}, u32[]{:S(2)}, u32[]{:S(2)}) collective-permute-start(bf16[4,17,16,256]{3,2,1,0:T(8,128)(2,1)S(1)} %get-tuple-element.40), channel_id=1, source_target_pairs={{0,48},{1,49},{2,50},{3,51},{4,52},{5,53},{6,54},{7,55},{8,56},{9,... | collective-permute-start | bytes 1671176 | tf_op jit(solution)/shard_map/ppermute | solution.py:52
  117.7 2.9 %collective-permute-done.28.high_a = bf16[4,17,16,256]{3,2,1,0:T(8,128)(2,1)S(1)} collective-permute-done((bf16[4,17,16,256]{3,2,1,0:T(8,128)(2,1)S(1)}, bf16[4,17,16,256]{3,2,1,0:T(8,128)(2,1)S(1)}, u32[]{:S(2)}, u32[]{:S(2)}) %collective-permute-start.28) | collective-permute-done | bytes 557088 | tf_op jit(solution)/shard_map/ppermute | solution.py:52
  120.6 6.0 %collective-permute-done.23.low_a = bf16[4,17,16,256]{3,2,1,0:T(8,128)(2,1)S(1)} collective-permute-done((bf16[4,17,16,256]{3,2,1,0:T(8,128)(2,1)S(1)}, bf16[4,17,16,256]{3,2,1,0:T(8,128)(2,1)S(1)}, u32[]{:S(2)}, u32[]{:S(2)}) %collective-permute-start.23) | collective-permute-done | bytes 557088 | tf_op jit(solution)/shard_map/ppermute | solution.py:52
  126.6 1.0 shard_map.84
  128.3 1.0 collective-permute-start.31
  129.3 2.2 %collective-permute-start.32 = (bf16[2,17,16,256]{3,2,1,0:T(8,128)(2,1)S(1)}, bf16[2,17,16,256]{3,2,1,0:T(8,128)(2,1)S(1)}, u32[]{:S(2)}, u32[]{:S(2)}) collective-permute-start(bf16[2,17,16,256]{3,2,1,0:T(8,128)(2,1)S(1)} %get-tuple-element.50), channel_id=1, source_target_pairs={{0,12},{1,13},{2,14},{3,15},{4,0},{5,1},{6,2},{7,3},{8,4},{9,5},{1... | collective-permute-start | bytes 835592 | tf_op jit(solution)/shard_map/ppermute | solution.py:52
  131.6 4.3 %collective-permute-done.30 = bf16[2,17,16,256]{3,2,1,0:T(8,128)(2,1)S(1)} collective-permute-done((bf16[2,17,16,256]{3,2,1,0:T(8,128)(2,1)S(1)}, bf16[2,17,16,256]{3,2,1,0:T(8,128)(2,1)S(1)}, u32[]{:S(2)}, u32[]{:S(2)}) %collective-permute-start.30) | collective-permute-done | bytes 278560 | tf_op jit(solution)/shard_map/ppermute | solution.py:52
  135.8 2.9 %collective-permute-done.31 = bf16[2,17,16,256]{3,2,1,0:T(8,128)(2,1)S(1)} collective-permute-done((bf16[2,17,16,256]{3,2,1,0:T(8,128)(2,1)S(1)}, bf16[2,17,16,256]{3,2,1,0:T(8,128)(2,1)S(1)}, u32[]{:S(2)}, u32[]{:S(2)}) %collective-permute-start.31) | collective-permute-done | bytes 278560 | tf_op jit(solution)/shard_map/ppermute | solution.py:52
  139.2 12.4 %all_to_all.11.parts = bf16[8,72,256]{2,1,0:T(8,128)(2,1)S(1)} all-to-all(bf16[8,72,256]{2,1,0:T(8,128)(2,1)S(1)} %pad_maximum_fusion.2), channel_id=1, replica_groups=mesh['zl'=2,'c'=2,'x'=4,'y'=4,'zh'=4] {'zl','zh'}, dimensions={0} | all-to-all | bytes 589824 | tf_op jit(solution)/shard_map/all_to_all | solution.py:464
  151.6 1.2 shard_map.85
  (81 shorter events, 6.8 us)
Async XLA Ops:
  21.8 59.7 %copy-start = (bf16[2,2,128,2048]{3,2,1,0:T(8,128)(2,1)S(1)}, bf16[2,2,128,2048]{3,2,1,0:T(8,128)(2,1)}, u32[]{:S(2)}) copy-start(bf16[2,2,128,2048]{3,2,1,0:T(8,128)(2,1)} %xs.5) | copy-start | bytes 6291460
  22.1 6.9 %collective-permute-start = (bf16[17,16,256]{2,1,0:T(8,128)(2,1)S(1)}, bf16[17,16,256]{2,1,0:T(8,128)(2,1)S(1)}, u32[]{:S(2)}, u32[]{:S(2)}) collective-permute-start(bf16[17,16,256]{2,1,0:T(8,128)(2,1)S(1)} %get-tuple-element.56), channel_id=1, source_target_pairs={{0,48},{1,49},{2,50},{3,51},{4,52},{5,53},{6,54},{7,55},{8,56},{9,... | collective-permute-start | bytes 417800 | tf_op jit(solution)/shard_map/ppermute | solution.py:52
  24.9 6.7 %collective-permute-start.1 = (bf16[17,16,256]{2,1,0:T(8,128)(2,1)S(1)}, bf16[17,16,256]{2,1,0:T(8,128)(2,1)S(1)}, u32[]{:S(2)}, u32[]{:S(2)}) collective-permute-start(bf16[17,16,256]{2,1,0:T(8,128)(2,1)S(1)} %get-tuple-element.56), channel_id=1, source_target_pairs={{0,32},{1,33},{2,34},{3,35},{4,36},{5,37},{6,38},{7,39},{8,40},{9,... | collective-permute-start | bytes 417800 | tf_op jit(solution)/shard_map/ppermute | solution.py:52
  25.7 7.3 %collective-permute-start.2 = (bf16[17,16,256]{2,1,0:T(8,128)(2,1)S(1)}, bf16[17,16,256]{2,1,0:T(8,128)(2,1)S(1)}, u32[]{:S(2)}, u32[]{:S(2)}) collective-permute-start(bf16[17,16,256]{2,1,0:T(8,128)(2,1)S(1)} %get-tuple-element.56), channel_id=1, source_target_pairs={{0,16},{1,17},{2,18},{3,19},{4,20},{5,21},{6,22},{7,23},{8,24},{9,... | collective-permute-start | bytes 417800 | tf_op jit(solution)/shard_map/ppermute | solution.py:52
  33.0 29.0 %collective-permute-start.3 = (bf16[4,17,16,256]{3,2,1,0:T(8,128)(2,1)S(1)}, bf16[4,17,16,256]{3,2,1,0:T(8,128)(2,1)S(1)}, u32[]{:S(2)}, u32[]{:S(2)}) collective-permute-start(bf16[4,17,16,256]{3,2,1,0:T(8,128)(2,1)S(1)} %pad_maximum_fusion.refs_0_), channel_id=1, source_target_pairs={{0,12},{1,13},{2,14},{3,15},{4,0},{5,1},{6,2},{7,3},{8,4},{9,5},{1... | collective-permute-start | bytes 1671176 | tf_op jit(solution)/shard_map/ppermute | solution.py:52
  36.1 26.6 %collective-permute-start.4 = (bf16[4,17,16,256]{3,2,1,0:T(8,128)(2,1)S(1)}, bf16[4,17,16,256]{3,2,1,0:T(8,128)(2,1)S(1)}, u32[]{:S(2)}, u32[]{:S(2)}) collective-permute-start(bf16[4,17,16,256]{3,2,1,0:T(8,128)(2,1)S(1)} %pad_maximum_fusion.refs_0_), channel_id=1, source_target_pairs={{0,8},{1,9},{2,10},{3,11},{4,12},{5,13},{6,14},{7,15},{8,0},{9,1},... | collective-permute-start | bytes 1671176 | tf_op jit(solution)/shard_map/ppermute | solution.py:52
  36.8 26.8 %collective-permute-start.5 = (bf16[4,17,16,256]{3,2,1,0:T(8,128)(2,1)S(1)}, bf16[4,17,16,256]{3,2,1,0:T(8,128)(2,1)}, u32[]{:S(2)}, u32[]{:S(2)}) collective-permute-start(bf16[4,17,16,256]{3,2,1,0:T(8,128)(2,1)S(1)} %pad_maximum_fusion.refs_0_), channel_id=1, source_target_pairs={{0,4},{1,5},{2,6},{3,7},{4,8},{5,9},{6,10},{7,11},{8,12},{9,13},{1... | collective-permute-start | bytes 1671176 | tf_op jit(solution)/shard_map/ppermute | solution.py:52
  37.7 26.7 %collective-permute-start.6 = (bf16[4,17,16,256]{3,2,1,0:T(8,128)(2,1)S(1)}, bf16[4,17,16,256]{3,2,1,0:T(8,128)(2,1)S(1)}, u32[]{:S(2)}, u32[]{:S(2)}) collective-permute-start(bf16[4,17,16,256]{3,2,1,0:T(8,128)(2,1)S(1)} %pad_maximum_fusion.refs_0_), channel_id=1, source_target_pairs={{0,64},{1,65},{2,66},{3,67},{4,68},{5,69},{6,70},{7,71},{8,72},{9,... | collective-permute-start | bytes 1671176 | tf_op jit(solution)/shard_map/ppermute | solution.py:52
  37.7 10.1 %collective-permute-start.10 = (bf16[17,16,256]{2,1,0:T(8,128)(2,1)S(1)}, bf16[17,16,256]{2,1,0:T(8,128)(2,1)S(1)}, u32[]{:S(2)}, u32[]{:S(2)}) collective-permute-start(bf16[17,16,256]{2,1,0:T(8,128)(2,1)S(1)} %get-tuple-element.57), channel_id=1, source_target_pairs={{0,48},{1,49},{2,50},{3,51},{4,52},{5,53},{6,54},{7,55},{8,56},{9,... | collective-permute-start | bytes 417800 | tf_op jit(solution)/shard_map/ppermute | solution.py:52
  47.8 6.6 %collective-permute-start.11 = (bf16[17,16,256]{2,1,0:T(8,128)(2,1)S(1)}, bf16[17,16,256]{2,1,0:T(8,128)(2,1)S(1)}, u32[]{:S(2)}, u32[]{:S(2)}) collective-permute-start(bf16[17,16,256]{2,1,0:T(8,128)(2,1)S(1)} %get-tuple-element.57), channel_id=1, source_target_pairs={{0,32},{1,33},{2,34},{3,35},{4,36},{5,37},{6,38},{7,39},{8,40},{9,... | collective-permute-start | bytes 417800 | tf_op jit(solution)/shard_map/ppermute | solution.py:52
  54.4 6.7 %collective-permute-start.12 = (bf16[17,16,256]{2,1,0:T(8,128)(2,1)S(1)}, bf16[17,16,256]{2,1,0:T(8,128)(2,1)S(1)}, u32[]{:S(2)}, u32[]{:S(2)}) collective-permute-start(bf16[17,16,256]{2,1,0:T(8,128)(2,1)S(1)} %get-tuple-element.57), channel_id=1, source_target_pairs={{0,16},{1,17},{2,18},{3,19},{4,20},{5,21},{6,22},{7,23},{8,24},{9,... | collective-permute-start | bytes 417800 | tf_op jit(solution)/shard_map/ppermute | solution.py:52
  61.1 9.7 %collective-permute-start.13 = (bf16[4,17,16,256]{3,2,1,0:T(8,128)(2,1)S(1)}, bf16[4,17,16,256]{3,2,1,0:T(8,128)(2,1)}, u32[]{:S(2)}, u32[]{:S(2)}) collective-permute-start(bf16[4,17,16,256]{3,2,1,0:T(8,128)(2,1)S(1)} %pad_maximum_fusion.1.refs_0_), channel_id=1, source_target_pairs={{0,12},{1,13},{2,14},{3,15},{4,0},{5,1},{6,2},{7,3},{8,4},{9,5},{1... | collective-permute-start | bytes 1671176 | tf_op jit(solution)/shard_map/ppermute | solution.py:52
  62.1 11.2 %collective-permute-start.14 = (bf16[4,17,16,256]{3,2,1,0:T(8,128)(2,1)S(1)}, bf16[4,17,16,256]{3,2,1,0:T(8,128)(2,1)}, u32[]{:S(2)}, u32[]{:S(2)}) collective-permute-start(bf16[4,17,16,256]{3,2,1,0:T(8,128)(2,1)S(1)} %pad_maximum_fusion.1.refs_0_), channel_id=1, source_target_pairs={{0,8},{1,9},{2,10},{3,11},{4,12},{5,13},{6,14},{7,15},{8,0},{9,1},... | collective-permute-start | bytes 1671176 | tf_op jit(solution)/shard_map/ppermute | solution.py:52
  62.7 16.5 %collective-permute-start.15 = (bf16[4,17,16,256]{3,2,1,0:T(8,128)(2,1)S(1)}, bf16[4,17,16,256]{3,2,1,0:T(8,128)(2,1)}, u32[]{:S(2)}, u32[]{:S(2)}) collective-permute-start(bf16[4,17,16,256]{3,2,1,0:T(8,128)(2,1)S(1)} %pad_maximum_fusion.1.refs_0_), channel_id=1, source_target_pairs={{0,4},{1,5},{2,6},{3,7},{4,8},{5,9},{6,10},{7,11},{8,12},{9,13},{1... | collective-permute-start | bytes 1671176 | tf_op jit(solution)/shard_map/ppermute | solution.py:52
  63.6 15.6 %collective-permute-start.7 = (bf16[4,17,16,256]{3,2,1,0:T(8,128)(2,1)S(1)}, bf16[4,17,16,256]{3,2,1,0:T(8,128)(2,1)S(1)}, u32[]{:S(2)}, u32[]{:S(2)}) collective-permute-start(bf16[4,17,16,256]{3,2,1,0:T(8,128)(2,1)S(1)} %collective-permute-done.3.refs_1_), channel_id=1, source_target_pairs={{0,64},{1,65},{2,66},{3,67},{4,68},{5,69},{6,70},{7,71},{8,72},{9,... | collective-permute-start | bytes 1671176 | tf_op jit(solution)/shard_map/ppermute | solution.py:52
  63.6 0.8 copy-start.2
  64.4 0.8 copy-start.6
  65.2 15.3 %collective-permute-start.8 = (bf16[4,17,16,256]{3,2,1,0:T(8,128)(2,1)S(1)}, bf16[4,17,16,256]{3,2,1,0:T(8,128)(2,1)S(1)}, u32[]{:S(2)}, u32[]{:S(2)}) collective-permute-start(bf16[4,17,16,256]{3,2,1,0:T(8,128)(2,1)S(1)} %collective-permute-done.4.refs_2_), channel_id=1, source_target_pairs={{0,64},{1,65},{2,66},{3,67},{4,68},{5,69},{6,70},{7,71},{8,72},{9,... | collective-permute-start | bytes 1671176 | tf_op jit(solution)/shard_map/ppermute | solution.py:52
  65.7 0.8 copy-start.4
  70.9 17.7 %collective-permute-start.16 = (bf16[4,17,16,256]{3,2,1,0:T(8,128)(2,1)S(1)}, bf16[4,17,16,256]{3,2,1,0:T(8,128)(2,1)}, u32[]{:S(2)}, u32[]{:S(2)}) collective-permute-start(bf16[4,17,16,256]{3,2,1,0:T(8,128)(2,1)S(1)} %pad_maximum_fusion.1.refs_0_), channel_id=1, source_target_pairs={{0,64},{1,65},{2,66},{3,67},{4,68},{5,69},{6,70},{7,71},{8,72},{9,... | collective-permute-start | bytes 1671176 | tf_op jit(solution)/shard_map/ppermute | solution.py:52
  73.3 9.0 %collective-permute-start.9 = (bf16[4,17,16,256]{3,2,1,0:T(8,128)(2,1)}, bf16[4,17,16,256]{3,2,1,0:T(8,128)(2,1)}, u32[]{:S(2)}, u32[]{:S(2)}) collective-permute-start(bf16[4,17,16,256]{3,2,1,0:T(8,128)(2,1)} %collective-permute-done.5.refs_3_), channel_id=1, source_target_pairs={{0,64},{1,65},{2,66},{3,67},{4,68},{5,69},{6,70},{7,71},{8,72},{9,... | collective-permute-start | bytes 1671176 | tf_op jit(solution)/shard_map/ppermute | solution.py:52
  79.2 9.4 %collective-permute-start.17 = (bf16[4,17,16,256]{3,2,1,0:T(8,128)(2,1)}, bf16[4,17,16,256]{3,2,1,0:T(8,128)(2,1)}, u32[]{:S(2)}, u32[]{:S(2)}) collective-permute-start(bf16[4,17,16,256]{3,2,1,0:T(8,128)(2,1)} %collective-permute-done.13.refs_1_), channel_id=1, source_target_pairs={{0,64},{1,65},{2,66},{3,67},{4,68},{5,69},{6,70},{7,71},{8,72},{9,... | collective-permute-start | bytes 1671176 | tf_op jit(solution)/shard_map/ppermute | solution.py:52
  79.2 0.8 copy-start.8
  80.0 8.6 %collective-permute-start.18 = (bf16[4,17,16,256]{3,2,1,0:T(8,128)(2,1)}, bf16[4,17,16,256]{3,2,1,0:T(8,128)(2,1)}, u32[]{:S(2)}, u32[]{:S(2)}) collective-permute-start(bf16[4,17,16,256]{3,2,1,0:T(8,128)(2,1)} %collective-permute-done.14.refs_2_), channel_id=1, source_target_pairs={{0,64},{1,65},{2,66},{3,67},{4,68},{5,69},{6,70},{7,71},{8,72},{9,... | collective-permute-start | bytes 1671176 | tf_op jit(solution)/shard_map/ppermute | solution.py:52
  80.5 0.8 copy-start.10
  81.4 7.3 %collective-permute-start.19 = (bf16[4,17,16,256]{3,2,1,0:T(8,128)(2,1)}, bf16[4,17,16,256]{3,2,1,0:T(8,128)(2,1)}, u32[]{:S(2)}, u32[]{:S(2)}) collective-permute-start(bf16[4,17,16,256]{3,2,1,0:T(8,128)(2,1)} %collective-permute-done.15.refs_3_), channel_id=1, source_target_pairs={{0,64},{1,65},{2,66},{3,67},{4,68},{5,69},{6,70},{7,71},{8,72},{9,... | collective-permute-start | bytes 1671176 | tf_op jit(solution)/shard_map/ppermute | solution.py:52
  81.4 1.1 copy-start.3
  81.4 1.2 copy-start.5
  81.4 1.4 copy-start.7
  82.7 1.1 copy-start.9
  83.8 1.1 copy-start.11
  84.9 3.8 %copy-start.1 = (bf16[2,2,128,2048]{3,2,1,0:T(8,128)(2,1)S(1)}, bf16[2,2,128,2048]{3,2,1,0:T(8,128)(2,1)}, u32[]{:S(2)}) copy-start(bf16[2,2,128,2048]{3,2,1,0:T(8,128)(2,1)} %cots.1) | copy-start | bytes 6291460
  95.5 4.2 %collective-permute-start.25 = (bf16[144,4608]{1,0:T(8,128)(2,1)S(1)}, bf16[144,4608]{1,0:T(8,128)(2,1)S(1)}, u32[]{:S(2)}, u32[]{:S(2)}) collective-permute-start(bf16[144,4608]{1,0:T(8,128)(2,1)S(1)} %slice_bitcast_fusion.1), channel_id=1, source_target_pairs={{0,64},{1,65},{2,66},{3,67},{4,68},{5,69},{6,70},{7,71},{8,72},{9,... | collective-permute-start | bytes 3981320 | tf_op jit(solution)/shard_map/ppermute | solution.py:52
  99.6 4.8 %collective-permute-start.20 = (bf16[144,4608]{1,0:T(8,128)(2,1)S(1)}, bf16[144,4608]{1,0:T(8,128)(2,1)S(1)}, u32[]{:S(2)}, u32[]{:S(2)}) collective-permute-start(bf16[144,4608]{1,0:T(8,128)(2,1)S(1)} %slice_bitcast_fusion), channel_id=1, source_target_pairs={{0,64},{1,65},{2,66},{3,67},{4,68},{5,69},{6,70},{7,71},{8,72},{9,... | collective-permute-start | bytes 3981320 | tf_op jit(solution)/shard_map/ppermute | solution.py:52
  101.0 8.0 %collective-permute-start.26 = (bf16[2,17,16,256]{3,2,1,0:T(8,128)(2,1)S(1)}, bf16[2,17,16,256]{3,2,1,0:T(8,128)(2,1)S(1)}, u32[]{:S(2)}, u32[]{:S(2)}) collective-permute-start(bf16[2,17,16,256]{3,2,1,0:T(8,128)(2,1)S(1)} %get-tuple-element.43), channel_id=1, source_target_pairs={{0,16},{1,17},{2,18},{3,19},{4,20},{5,21},{6,22},{7,23},{8,24},{9,... | collective-permute-start | bytes 835592 | tf_op jit(solution)/shard_map/ppermute | solution.py:52
  101.1 7.9 %collective-permute-start.27 = (bf16[2,17,16,256]{3,2,1,0:T(8,128)(2,1)S(1)}, bf16[2,17,16,256]{3,2,1,0:T(8,128)(2,1)S(1)}, u32[]{:S(2)}, u32[]{:S(2)}) collective-permute-start(bf16[2,17,16,256]{3,2,1,0:T(8,128)(2,1)S(1)} %get-tuple-element.44), channel_id=1, source_target_pairs={{0,48},{1,49},{2,50},{3,51},{4,52},{5,53},{6,54},{7,55},{8,56},{9,... | collective-permute-start | bytes 835592 | tf_op jit(solution)/shard_map/ppermute | solution.py:52
  105.7 7.8 %collective-permute-start.21 = (bf16[2,17,16,256]{3,2,1,0:T(8,128)(2,1)S(1)}, bf16[2,17,16,256]{3,2,1,0:T(8,128)(2,1)S(1)}, u32[]{:S(2)}, u32[]{:S(2)}) collective-permute-start(bf16[2,17,16,256]{3,2,1,0:T(8,128)(2,1)S(1)} %get-tuple-element.37), channel_id=1, source_target_pairs={{0,16},{1,17},{2,18},{3,19},{4,20},{5,21},{6,22},{7,23},{8,24},{9,... | collective-permute-start | bytes 835592 | tf_op jit(solution)/shard_map/ppermute | solution.py:52
  105.8 7.7 %collective-permute-start.22 = (bf16[2,17,16,256]{3,2,1,0:T(8,128)(2,1)S(1)}, bf16[2,17,16,256]{3,2,1,0:T(8,128)(2,1)S(1)}, u32[]{:S(2)}, u32[]{:S(2)}) collective-permute-start(bf16[2,17,16,256]{3,2,1,0:T(8,128)(2,1)S(1)} %get-tuple-element.38), channel_id=1, source_target_pairs={{0,48},{1,49},{2,50},{3,51},{4,52},{5,53},{6,54},{7,55},{8,56},{9,... | collective-permute-start | bytes 835592 | tf_op jit(solution)/shard_map/ppermute | solution.py:52
  109.8 10.8 %collective-permute-start.28 = (bf16[4,17,16,256]{3,2,1,0:T(8,128)(2,1)S(1)}, bf16[4,17,16,256]{3,2,1,0:T(8,128)(2,1)S(1)}, u32[]{:S(2)}, u32[]{:S(2)}) collective-permute-start(bf16[4,17,16,256]{3,2,1,0:T(8,128)(2,1)S(1)} %get-tuple-element.45), channel_id=1, source_target_pairs={{0,16},{1,17},{2,18},{3,19},{4,20},{5,21},{6,22},{7,23},{8,24},{9,... | collective-permute-start | bytes 1671176 | tf_op jit(solution)/shard_map/ppermute | solution.py:52
  109.9 10.7 %collective-permute-start.29 = (bf16[4,17,16,256]{3,2,1,0:T(8,128)(2,1)S(1)}, bf16[4,17,16,256]{3,2,1,0:T(8,128)(2,1)S(1)}, u32[]{:S(2)}, u32[]{:S(2)}) collective-permute-start(bf16[4,17,16,256]{3,2,1,0:T(8,128)(2,1)S(1)} %get-tuple-element.46), channel_id=1, source_target_pairs={{0,48},{1,49},{2,50},{3,51},{4,52},{5,53},{6,54},{7,55},{8,56},{9,... | collective-permute-start | bytes 1671176 | tf_op jit(solution)/shard_map/ppermute | solution.py:52
  114.3 12.3 %collective-permute-start.23 = (bf16[4,17,16,256]{3,2,1,0:T(8,128)(2,1)S(1)}, bf16[4,17,16,256]{3,2,1,0:T(8,128)(2,1)S(1)}, u32[]{:S(2)}, u32[]{:S(2)}) collective-permute-start(bf16[4,17,16,256]{3,2,1,0:T(8,128)(2,1)S(1)} %get-tuple-element.39), channel_id=1, source_target_pairs={{0,16},{1,17},{2,18},{3,19},{4,20},{5,21},{6,22},{7,23},{8,24},{9,... | collective-permute-start | bytes 1671176 | tf_op jit(solution)/shard_map/ppermute | solution.py:52
  114.4 12.2 %collective-permute-start.24 = (bf16[4,17,16,256]{3,2,1,0:T(8,128)(2,1)S(1)}, bf16[4,17,16,256]{3,2,1,0:T(8,128)(2,1)S(1)}, u32[]{:S(2)}, u32[]{:S(2)}) collective-permute-start(bf16[4,17,16,256]{3,2,1,0:T(8,128)(2,1)S(1)} %get-tuple-element.40), channel_id=1, source_target_pairs={{0,48},{1,49},{2,50},{3,51},{4,52},{5,53},{6,54},{7,55},{8,56},{9,... | collective-permute-start | bytes 1671176 | tf_op jit(solution)/shard_map/ppermute | solution.py:52
  127.6 8.2 %collective-permute-start.30 = (bf16[2,17,16,256]{3,2,1,0:T(8,128)(2,1)S(1)}, bf16[2,17,16,256]{3,2,1,0:T(8,128)(2,1)S(1)}, u32[]{:S(2)}, u32[]{:S(2)}) collective-permute-start(bf16[2,17,16,256]{3,2,1,0:T(8,128)(2,1)S(1)} %get-tuple-element.48), channel_id=1, source_target_pairs={{0,8},{1,9},{2,10},{3,11},{4,12},{5,13},{6,14},{7,15},{8,0},{9,1},... | collective-permute-start | bytes 835592 | tf_op jit(solution)/shard_map/ppermute | solution.py:52
  128.3 10.4 %collective-permute-start.31 = (bf16[2,17,16,256]{3,2,1,0:T(8,128)(2,1)S(1)}, bf16[2,17,16,256]{3,2,1,0:T(8,128)(2,1)S(1)}, u32[]{:S(2)}, u32[]{:S(2)}) collective-permute-start(bf16[2,17,16,256]{3,2,1,0:T(8,128)(2,1)S(1)} %get-tuple-element.49), channel_id=1, source_target_pairs={{0,4},{1,5},{2,6},{3,7},{4,8},{5,9},{6,10},{7,11},{8,12},{9,13},{1... | collective-permute-start | bytes 835592 | tf_op jit(solution)/shard_map/ppermute | solution.py:52
  129.3 9.4 %collective-permute-start.32 = (bf16[2,17,16,256]{3,2,1,0:T(8,128)(2,1)S(1)}, bf16[2,17,16,256]{3,2,1,0:T(8,128)(2,1)S(1)}, u32[]{:S(2)}, u32[]{:S(2)}) collective-permute-start(bf16[2,17,16,256]{3,2,1,0:T(8,128)(2,1)S(1)} %get-tuple-element.50), channel_id=1, source_target_pairs={{0,12},{1,13},{2,14},{3,15},{4,0},{5,1},{6,2},{7,3},{8,4},{9,5},{1... | collective-permute-start | bytes 835592 | tf_op jit(solution)/shard_map/ppermute | solution.py:52

commit v9 on v8

--- a/solution.py
+++ b/solution.py
@@ -50,6 +50,11 @@
 
 def shift(value, pairs):
     return lax.ppermute(value, AXES, pairs)
+
+
+def around(value, send):
+    across = shift(value, send(-2))
+    return [shift(value, send(-1)), across, shift(value, send(-3))]
 
 
 def dot(left, right, left_dim=1, right_dim=0):
@@ -175,7 +180,7 @@
 
 def kernel_low_forward(s_ref, xs, hat0, *refs):
     pieces = refs[: 2 * PIECES]
-    x1, x2, win, wout, stat1, pre, normed, hat1 = refs[2 * PIECES :]
+    x1, x2, win, wout, stat1, pre, hat2, rstd2, normed, hat1 = refs[2 * PIECES :]
     place_weights(s_ref, pieces, win, wout)
     c, zl = s_ref[2], s_ref[3]
 
@@ -199,19 +204,25 @@
         else:
             layer_out(lambda cols: xs[zl, c, :, cols], act, wout, par, x1)
 
-
-def kernel_high(s_ref, x2, cots, *refs):
+    def keep_rstd(rows, mean, recip_std):
+        rstd2[rows, :] = spread(recip_std)
+
+    hat_pass(lambda rows: x2[rows, :], hat2, keep_rstd)
+
+
+def kernel_high(s_ref, x2, hat0, rstd0, cots, *refs):
     pieces = refs[: 2 * PIECES]
-    up2, acts, win, wout, hat0, hat1, rstd, x3, up3, pre0, gnorm, gsum = refs[2 * PIECES :]
+    up2, acts, win, wout, hat1, rstd1, x3, up3, pre0, gnorm, gsum = refs[2 * PIECES :]
     place_weights(s_ref, pieces, win, wout)
     c, zl = s_ref[2], s_ref[3]
     gains = []
-    for par, (src, hat) in enumerate(((x2, hat0), (x3, hat1))):
-
-        def keep_stat(rows, mean, recip_std, par=par):
-            rstd[par, rows, :] = spread(recip_std)
-
-        hat_pass(lambda rows, src=src: src[rows, :], hat, keep_stat)
+
+    def keep_rstd(rows, mean, recip_std):
+        rstd1[rows, :] = spread(recip_std)
+
+    for par, hat in enumerate((hat0, hat1)):
+        if par:
+            hat_pass(lambda rows: x3[rows, :], hat1, keep_rstd)
         gain = gain_row(wout, par)
         slot = jnp.where(c == par, 0, 1)
 
@@ -226,12 +237,12 @@
             layer_out(lambda cols: x2[:, cols], gelu_parts(preact)[1], wout, 0, x3)
     layer_back(
         lambda rows, cols: cots[zl, c, rows, cols],
-        acts, jnp.where(c == 1, 0, 1), hat1, lambda rows: rstd[1, rows, 0:1],
+        acts, jnp.where(c == 1, 0, 1), hat1, lambda rows: rstd1[rows, 0:1],
         preact, win, wout, 1, gains[1], gnorm, gsum, up3,
     )
     layer_back(
         lambda rows, cols: up3[rows, cols],
-        acts, jnp.where(c == 0, 0, 1), hat0, lambda rows: rstd[0, rows, 0:1],
+        acts, jnp.where(c == 0, 0, 1), hat0, lambda rows: rstd0[rows, 0:1],
         pre0[...], win, wout, 0, gains[0], gnorm, gsum, up2,
     )
 
@@ -346,7 +357,7 @@
 GSUM = vmem(CHUNK, D, kind=F32)
 LOW_SCRATCH = [vmem(*ACT), HAT]
 HIGH_SCRATCH = [
-    vmem(*WIN), vmem(*WOUT), HAT, HAT, vmem(2, ROWS, 128, kind=F32),
+    vmem(*WIN), vmem(*WOUT), HAT, vmem(ROWS, 128, kind=F32),
     vmem(*ACT), vmem(*ACT), vmem(ROWS, R, kind=F32), HAT, GSUM,
 ]
 BACK_SCRATCH = [HAT, vmem(*ACT), HAT, GSUM]
@@ -417,24 +428,29 @@
     )
     near = []
     for p in range(2):
-        near.append([block[p]] + [shift(block[p], send_first(-k)) for k in (1, 2, 3)])
+        near.append([block[p]] + around(block[p], send_first))
     pairs = []
     for p in range(2):
         row = jnp.stack(near[p])
-        rows = [row] + [shift(row, send_second(-k)) for k in (1, 2, 3)]
+        rows = [row] + around(row, send_second)
         pairs.append(rows + [shift(v, SWAP) for v in rows])
-    x1, x2, win, wout, stat1, pre = call(
+    x1, x2, win, wout, stat1, pre, hat2, rstd2 = call(
         kernel_low_forward,
         scalars,
         [inputs, hat0, *pairs[0]],
         [
             array(*ACT), array(*ACT), array(*WIN), array(*WOUT),
             array(2, ROWS, 128, kind=F32), array(2, ROWS, R, kind=F32),
+            array(*ACT, kind=F32), array(ROWS, 128, kind=F32),
         ],
         LOW_SCRATCH,
     )
     up2, acts1 = call(
-        kernel_high, scalars, [x2, cotangent, *pairs[1]], [array(*ACT), array(*ACTS)], HIGH_SCRATCH
+        kernel_high,
+        scalars,
+        [x2, hat2, rstd2, cotangent, *pairs[1]],
+        [array(*ACT), array(*ACTS)],
+        HIGH_SCRATCH,
     )
     got1 = shift(acts1[1], SWAP)
     acts0 = call(

time: 155 us -> 155 us (level)
  no operation moved by 1% of the time
where the time goes in v9:
time: 155 us; the launch traced here: 153 us
  waiting for transfers between devices  57.3 us (37%)
  starting transfers between devices  32.2 us (21%)
  blocking collectives  31.9 us (21%)
  Pallas kernels  21.2 us (14%)
  local copies, waits for them, and re-layouts  8.14 us (5%)
    ppermute x33, waiting for transfers between devices, shift(): return lax.ppermute(value, AXES, pairs)  57.3 us
    ppermute x33, starting transfers between devices, shift(): return lax.ppermute(value, AXES, pairs)  32.2 us
    pallas_call x10, Pallas kernels, call(): pl.pallas_call(body, in_specs=[pl.BlockSpec(memory_space=pltpu.SMEM)] + [...  21.2 us
    all_to_all x1, blocking collectives, device_body(): lax.all_to_all(jnp.broadcast_to(shard[None], (8, 72, 256)), ('zl', 'zh'),...  19.5 us
    all_to_all x1, blocking collectives, device_body(): lax.all_to_all(parts, ('zl', 'zh'), 0, 0)  12.4 us
    unnamed x26, local copies, waits for them, and re-layouts  7.41 us
  transfers between devices with their start and end apart: 33, of which 14 were waited for; matrix products, arithmetic and copies ran while one was open for 0% of the time, Pallas kernels for 8%

profile of v9, /device:TPU:32, one launch (start us, length us, event | category | flops | bytes accessed | tf_op | source)
XLA Modules:
  0.0 152.8 jit_solution(14560075935157891045)
XLA Ops:
  0.6 0.7 copy.39
  1.4 0.7 fusion.3
  2.1 19.5 %all_to_all.10 = bf16[8,72,256]{2,1,0:T(8,128)(2,1)S(1)} all-to-all(bf16[8,72,256]{2,1,0:T(8,128)(2,1)S(1)} %broadcast_in_dim.2), channel_id=1, replica_groups=mesh['zl'=2,'c'=2,'x'=4,'y'=4,'zh'=4] {'zl','zh'}, dimensions={0} | all-to-all | bytes 589824 | tf_op jit(solution)/shard_map/all_to_all | solution.py:414
  22.1 2.8 %collective-permute-start = (bf16[17,16,256]{2,1,0:T(8,128)(2,1)S(1)}, bf16[17,16,256]{2,1,0:T(8,128)(2,1)S(1)}, u32[]{:S(2)}, u32[]{:S(2)}) collective-permute-start(bf16[17,16,256]{2,1,0:T(8,128)(2,1)S(1)} %get-tuple-element.60), channel_id=1, source_target_pairs={{0,48},{1,49},{2,50},{3,51},{4,52},{5,53},{6,54},{7,55},{8,56},{9,... | collective-permute-start | bytes 417800 | tf_op jit(solution)/shard_map/ppermute | solution.py:52
  24.9 0.8 collective-permute-start.1
  25.7 0.9 collective-permute-start.2
  26.6 2.4 %collective-permute-done = bf16[17,16,256]{2,1,0:T(8,128)(2,1)S(1)} collective-permute-done((bf16[17,16,256]{2,1,0:T(8,128)(2,1)S(1)}, bf16[17,16,256]{2,1,0:T(8,128)(2,1)S(1)}, u32[]{:S(2)}, u32[]{:S(2)}) %collective-permute-start) | collective-permute-done | bytes 139296 | tf_op jit(solution)/shard_map/ppermute | solution.py:52
  29.0 2.6 %collective-permute-done.1 = bf16[17,16,256]{2,1,0:T(8,128)(2,1)S(1)} collective-permute-done((bf16[17,16,256]{2,1,0:T(8,128)(2,1)S(1)}, bf16[17,16,256]{2,1,0:T(8,128)(2,1)S(1)}, u32[]{:S(2)}, u32[]{:S(2)}) %collective-permute-start.1) | collective-permute-done | bytes 139296 | tf_op jit(solution)/shard_map/ppermute | solution.py:52
  31.6 1.4 collective-permute-done.2
  33.0 3.1 %collective-permute-start.3 = (bf16[4,17,16,256]{3,2,1,0:T(8,128)(2,1)S(1)}, bf16[4,17,16,256]{3,2,1,0:T(8,128)(2,1)S(1)}, u32[]{:S(2)}, u32[]{:S(2)}) collective-permute-start(bf16[4,17,16,256]{3,2,1,0:T(8,128)(2,1)S(1)} %pad_maximum_fusion.refs_0_), channel_id=1, source_target_pairs={{0,12},{1,13},{2,14},{3,15},{4,0},{5,1},{6,2},{7,3},{8,4},{9,5},{1... | collective-permute-start | bytes 1671176 | tf_op jit(solution)/shard_map/ppermute | solution.py:52
  36.8 1.0 collective-permute-start.5
  38.3 9.5 %collective-permute-done.10 = bf16[17,16,256]{2,1,0:T(8,128)(2,1)S(1)} collective-permute-done((bf16[17,16,256]{2,1,0:T(8,128)(2,1)S(1)}, bf16[17,16,256]{2,1,0:T(8,128)(2,1)S(1)}, u32[]{:S(2)}, u32[]{:S(2)}) %collective-permute-start.10) | collective-permute-done | bytes 139296 | tf_op jit(solution)/shard_map/ppermute | solution.py:52
  47.8 6.6 %collective-permute-done.11 = bf16[17,16,256]{2,1,0:T(8,128)(2,1)S(1)} collective-permute-done((bf16[17,16,256]{2,1,0:T(8,128)(2,1)S(1)}, bf16[17,16,256]{2,1,0:T(8,128)(2,1)S(1)}, u32[]{:S(2)}, u32[]{:S(2)}) %collective-permute-start.11) | collective-permute-done | bytes 139296 | tf_op jit(solution)/shard_map/ppermute | solution.py:52
  54.4 1.0 collective-permute-start.12
  55.4 5.7 %collective-permute-done.12 = bf16[17,16,256]{2,1,0:T(8,128)(2,1)S(1)} collective-permute-done((bf16[17,16,256]{2,1,0:T(8,128)(2,1)S(1)}, bf16[17,16,256]{2,1,0:T(8,128)(2,1)S(1)}, u32[]{:S(2)}, u32[]{:S(2)}) %collective-permute-start.12) | collective-permute-done | bytes 139296 | tf_op jit(solution)/shard_map/ppermute | solution.py:52
  61.1 0.9 collective-permute-start.13
  62.7 0.9 collective-permute-start.15
  63.6 0.8 copy-done.2
  64.4 0.8 copy-done.6
  65.7 0.8 copy-done.4
  66.5 4.3 %collective-permute-done.13.refs_1_ = bf16[4,17,16,256]{3,2,1,0:T(8,128)(2,1)} collective-permute-done((bf16[4,17,16,256]{3,2,1,0:T(8,128)(2,1)S(1)}, bf16[4,17,16,256]{3,2,1,0:T(8,128)(2,1)}, u32[]{:S(2)}, u32[]{:S(2)}) %collective-permute-start.13) | collective-permute-done | bytes 557088 | tf_op jit(solution)/shard_map/ppermute | solution.py:52
  70.9 2.5 %collective-permute-done.14.refs_2_ = bf16[4,17,16,256]{3,2,1,0:T(8,128)(2,1)} collective-permute-done((bf16[4,17,16,256]{3,2,1,0:T(8,128)(2,1)S(1)}, bf16[4,17,16,256]{3,2,1,0:T(8,128)(2,1)}, u32[]{:S(2)}, u32[]{:S(2)}) %collective-permute-start.14) | collective-permute-done | bytes 557088 | tf_op jit(solution)/shard_map/ppermute | solution.py:52
  73.3 5.9 %collective-permute-done.15.refs_3_ = bf16[4,17,16,256]{3,2,1,0:T(8,128)(2,1)} collective-permute-done((bf16[4,17,16,256]{3,2,1,0:T(8,128)(2,1)S(1)}, bf16[4,17,16,256]{3,2,1,0:T(8,128)(2,1)}, u32[]{:S(2)}, u32[]{:S(2)}) %collective-permute-start.15) | collective-permute-done | bytes 557088 | tf_op jit(solution)/shard_map/ppermute | solution.py:52
  79.2 0.8 copy-done.8
  80.5 0.8 copy-done.10
  81.4 0.9 shard_map.76
  82.8 1.1 copy-done.9
  83.8 1.1 copy-done.11
  84.9 4.0 %shard_map.77 = (bf16[128,2048]{1,0:T(8,128)(2,1)S(1)}, bf16[128,2048]{1,0:T(8,128)(2,1)S(1)}, bf16[2,128,16,256]{3,2,1,0:T(8,128)(2,1)S(1)}, bf16[2,9,16,16,256...) custom-call(s32[4]{0:T(128)S(1)} %pad_add_fusion.s_ref, ...), custom_call_target="tpu_custom_call" | custom-call | tf_op jit(solution)/shard_map/pallas_call | solution.py:368
  89.0 6.5 %shard_map.78 = (bf16[128,2048]{1,0:T(8,128)(2,1)S(1)}, bf16[2,144,4608]{2,1,0:T(8,128)(2,1)S(1)}) custom-call(s32[4]{0:T(128)S(1)} %pad_add_fusion.s_ref, bf16[128,2048]{1,0:T(8,128)(2,1)S(1)} %get-tuple-element.31.x2, f32[128,2048]{1,0:T(8,128)S(1)} %get-tuple-element.32.hat0, f32[128,128]{1,0:T(8,128)S(1)} %get-tuple-element.33.rstd0, ...), custom_call_target="tpu_custom_call" | custom-call | tf_op jit(solution)/shard_map/pallas_call | solution.py:368
  96.1 3.4 %shard_map.79.acts = bf16[2,144,4608]{2,1,0:T(8,128)(2,1)S(1)} custom-call(s32[4]{0:T(128)S(1)} %pad_add_fusion.s_ref, bf16[2,2,128,2048]{3,2,1,0:T(8,128)(2,1)S(1)} %copy-done, bf16[128,2048]{1,0:T(8,128)(2,1)S(1)} %get-tuple-element.30.x1, bf16[128,2048]{1,0:T(8,128)(2,1)S(1)} %get-tuple-element.34.up2, ...), custom_call_target="tpu_custom_call" | custom-call | tf_op jit(solution)/shard_map/pallas_call | solution.py:368
  99.7 1.3 shard_map.82
  101.2 3.2 %collective-permute-start.27 = (bf16[2,17,16,256]{3,2,1,0:T(8,128)(2,1)S(1)}, bf16[2,17,16,256]{3,2,1,0:T(8,128)(2,1)S(1)}, u32[]{:S(2)}, u32[]{:S(2)}) collective-permute-start(bf16[2,17,16,256]{3,2,1,0:T(8,128)(2,1)S(1)} %get-tuple-element.48), channel_id=1, source_target_pairs={{0,48},{1,49},{2,50},{3,51},{4,52},{5,53},{6,54},{7,55},{8,56},{9,... | collective-permute-start | bytes 835592 | tf_op jit(solution)/shard_map/ppermute | solution.py:52
  104.4 1.3 shard_map.80
  105.8 3.2 %collective-permute-start.22 = (bf16[2,17,16,256]{3,2,1,0:T(8,128)(2,1)S(1)}, bf16[2,17,16,256]{3,2,1,0:T(8,128)(2,1)S(1)}, u32[]{:S(2)}, u32[]{:S(2)}) collective-permute-start(bf16[2,17,16,256]{3,2,1,0:T(8,128)(2,1)S(1)} %get-tuple-element.42), channel_id=1, source_target_pairs={{0,48},{1,49},{2,50},{3,51},{4,52},{5,53},{6,54},{7,55},{8,56},{9,... | collective-permute-start | bytes 835592 | tf_op jit(solution)/shard_map/ppermute | solution.py:52
  109.1 0.7 shard_map.83
  109.9 3.2 %collective-permute-start.29 = (bf16[4,17,16,256]{3,2,1,0:T(8,128)(2,1)S(1)}, bf16[4,17,16,256]{3,2,1,0:T(8,128)(2,1)S(1)}, u32[]{:S(2)}, u32[]{:S(2)}) collective-permute-start(bf16[4,17,16,256]{3,2,1,0:T(8,128)(2,1)S(1)} %get-tuple-element.50), channel_id=1, source_target_pairs={{0,48},{1,49},{2,50},{3,51},{4,52},{5,53},{6,54},{7,55},{8,56},{9,... | collective-permute-start | bytes 1671176 | tf_op jit(solution)/shard_map/ppermute | solution.py:52
  113.6 0.7 shard_map.81
  114.4 3.3 %collective-permute-start.24 = (bf16[4,17,16,256]{3,2,1,0:T(8,128)(2,1)S(1)}, bf16[4,17,16,256]{3,2,1,0:T(8,128)(2,1)S(1)}, u32[]{:S(2)}, u32[]{:S(2)}) collective-permute-start(bf16[4,17,16,256]{3,2,1,0:T(8,128)(2,1)S(1)} %get-tuple-element.44), channel_id=1, source_target_pairs={{0,48},{1,49},{2,50},{3,51},{4,52},{5,53},{6,54},{7,55},{8,56},{9,... | collective-permute-start | bytes 1671176 | tf_op jit(solution)/shard_map/ppermute | solution.py:52
  117.7 2.9 %collective-permute-done.28.high_a = bf16[4,17,16,256]{3,2,1,0:T(8,128)(2,1)S(1)} collective-permute-done((bf16[4,17,16,256]{3,2,1,0:T(8,128)(2,1)S(1)}, bf16[4,17,16,256]{3,2,1,0:T(8,128)(2,1)S(1)}, u32[]{:S(2)}, u32[]{:S(2)}) %collective-permute-start.28) | collective-permute-done | bytes 557088 | tf_op jit(solution)/shard_map/ppermute | solution.py:52
  120.6 6.0 %collective-permute-done.23.low_a = bf16[4,17,16,256]{3,2,1,0:T(8,128)(2,1)S(1)} collective-permute-done((bf16[4,17,16,256]{3,2,1,0:T(8,128)(2,1)S(1)}, bf16[4,17,16,256]{3,2,1,0:T(8,128)(2,1)S(1)}, u32[]{:S(2)}, u32[]{:S(2)}) %collective-permute-start.23) | collective-permute-done | bytes 557088 | tf_op jit(solution)/shard_map/ppermute | solution.py:52
  126.6 1.0 shard_map.84
  128.3 1.0 collective-permute-start.31
  129.4 2.2 %collective-permute-start.32 = (bf16[2,17,16,256]{3,2,1,0:T(8,128)(2,1)S(1)}, bf16[2,17,16,256]{3,2,1,0:T(8,128)(2,1)S(1)}, u32[]{:S(2)}, u32[]{:S(2)}) collective-permute-start(bf16[2,17,16,256]{3,2,1,0:T(8,128)(2,1)S(1)} %get-tuple-element.54), channel_id=1, source_target_pairs={{0,12},{1,13},{2,14},{3,15},{4,0},{5,1},{6,2},{7,3},{8,4},{9,5},{1... | collective-permute-start | bytes 835592 | tf_op jit(solution)/shard_map/ppermute | solution.py:52
  131.6 4.3 %collective-permute-done.30 = bf16[2,17,16,256]{3,2,1,0:T(8,128)(2,1)S(1)} collective-permute-done((bf16[2,17,16,256]{3,2,1,0:T(8,128)(2,1)S(1)}, bf16[2,17,16,256]{3,2,1,0:T(8,128)(2,1)S(1)}, u32[]{:S(2)}, u32[]{:S(2)}) %collective-permute-start.30) | collective-permute-done | bytes 278560 | tf_op jit(solution)/shard_map/ppermute | solution.py:52
  135.9 2.9 %collective-permute-done.31 = bf16[2,17,16,256]{3,2,1,0:T(8,128)(2,1)S(1)} collective-permute-done((bf16[2,17,16,256]{3,2,1,0:T(8,128)(2,1)S(1)}, bf16[2,17,16,256]{3,2,1,0:T(8,128)(2,1)S(1)}, u32[]{:S(2)}, u32[]{:S(2)}) %collective-permute-start.31) | collective-permute-done | bytes 278560 | tf_op jit(solution)/shard_map/ppermute | solution.py:52
  139.2 12.4 %all_to_all.11.parts = bf16[8,72,256]{2,1,0:T(8,128)(2,1)S(1)} all-to-all(bf16[8,72,256]{2,1,0:T(8,128)(2,1)S(1)} %pad_maximum_fusion.2), channel_id=1, replica_groups=mesh['zl'=2,'c'=2,'x'=4,'y'=4,'zh'=4] {'zl','zh'}, dimensions={0} | all-to-all | bytes 589824 | tf_op jit(solution)/shard_map/all_to_all | solution.py:480
  151.6 1.2 shard_map.85
  (81 shorter events, 6.8 us)
Async XLA Ops:
  21.8 59.7 %copy-start = (bf16[2,2,128,2048]{3,2,1,0:T(8,128)(2,1)S(1)}, bf16[2,2,128,2048]{3,2,1,0:T(8,128)(2,1)}, u32[]{:S(2)}) copy-start(bf16[2,2,128,2048]{3,2,1,0:T(8,128)(2,1)} %xs.5) | copy-start | bytes 6291460
  22.1 6.9 %collective-permute-start = (bf16[17,16,256]{2,1,0:T(8,128)(2,1)S(1)}, bf16[17,16,256]{2,1,0:T(8,128)(2,1)S(1)}, u32[]{:S(2)}, u32[]{:S(2)}) collective-permute-start(bf16[17,16,256]{2,1,0:T(8,128)(2,1)S(1)} %get-tuple-element.60), channel_id=1, source_target_pairs={{0,48},{1,49},{2,50},{3,51},{4,52},{5,53},{6,54},{7,55},{8,56},{9,... | collective-permute-start | bytes 417800 | tf_op jit(solution)/shard_map/ppermute | solution.py:52
  24.9 6.7 %collective-permute-start.1 = (bf16[17,16,256]{2,1,0:T(8,128)(2,1)S(1)}, bf16[17,16,256]{2,1,0:T(8,128)(2,1)S(1)}, u32[]{:S(2)}, u32[]{:S(2)}) collective-permute-start(bf16[17,16,256]{2,1,0:T(8,128)(2,1)S(1)} %get-tuple-element.60), channel_id=1, source_target_pairs={{0,32},{1,33},{2,34},{3,35},{4,36},{5,37},{6,38},{7,39},{8,40},{9,... | collective-permute-start | bytes 417800 | tf_op jit(solution)/shard_map/ppermute | solution.py:52
  25.7 7.3 %collective-permute-start.2 = (bf16[17,16,256]{2,1,0:T(8,128)(2,1)S(1)}, bf16[17,16,256]{2,1,0:T(8,128)(2,1)S(1)}, u32[]{:S(2)}, u32[]{:S(2)}) collective-permute-start(bf16[17,16,256]{2,1,0:T(8,128)(2,1)S(1)} %get-tuple-element.60), channel_id=1, source_target_pairs={{0,16},{1,17},{2,18},{3,19},{4,20},{5,21},{6,22},{7,23},{8,24},{9,... | collective-permute-start | bytes 417800 | tf_op jit(solution)/shard_map/ppermute | solution.py:52
  33.0 29.0 %collective-permute-start.3 = (bf16[4,17,16,256]{3,2,1,0:T(8,128)(2,1)S(1)}, bf16[4,17,16,256]{3,2,1,0:T(8,128)(2,1)S(1)}, u32[]{:S(2)}, u32[]{:S(2)}) collective-permute-start(bf16[4,17,16,256]{3,2,1,0:T(8,128)(2,1)S(1)} %pad_maximum_fusion.refs_0_), channel_id=1, source_target_pairs={{0,12},{1,13},{2,14},{3,15},{4,0},{5,1},{6,2},{7,3},{8,4},{9,5},{1... | collective-permute-start | bytes 1671176 | tf_op jit(solution)/shard_map/ppermute | solution.py:52
  36.1 26.6 %collective-permute-start.4 = (bf16[4,17,16,256]{3,2,1,0:T(8,128)(2,1)S(1)}, bf16[4,17,16,256]{3,2,1,0:T(8,128)(2,1)S(1)}, u32[]{:S(2)}, u32[]{:S(2)}) collective-permute-start(bf16[4,17,16,256]{3,2,1,0:T(8,128)(2,1)S(1)} %pad_maximum_fusion.refs_0_), channel_id=1, source_target_pairs={{0,8},{1,9},{2,10},{3,11},{4,12},{5,13},{6,14},{7,15},{8,0},{9,1},... | collective-permute-start | bytes 1671176 | tf_op jit(solution)/shard_map/ppermute | solution.py:52
  36.8 26.8 %collective-permute-start.5 = (bf16[4,17,16,256]{3,2,1,0:T(8,128)(2,1)S(1)}, bf16[4,17,16,256]{3,2,1,0:T(8,128)(2,1)}, u32[]{:S(2)}, u32[]{:S(2)}) collective-permute-start(bf16[4,17,16,256]{3,2,1,0:T(8,128)(2,1)S(1)} %pad_maximum_fusion.refs_0_), channel_id=1, source_target_pairs={{0,4},{1,5},{2,6},{3,7},{4,8},{5,9},{6,10},{7,11},{8,12},{9,13},{1... | collective-permute-start | bytes 1671176 | tf_op jit(solution)/shard_map/ppermute | solution.py:52
  37.7 26.7 %collective-permute-start.6 = (bf16[4,17,16,256]{3,2,1,0:T(8,128)(2,1)S(1)}, bf16[4,17,16,256]{3,2,1,0:T(8,128)(2,1)S(1)}, u32[]{:S(2)}, u32[]{:S(2)}) collective-permute-start(bf16[4,17,16,256]{3,2,1,0:T(8,128)(2,1)S(1)} %pad_maximum_fusion.refs_0_), channel_id=1, source_target_pairs={{0,64},{1,65},{2,66},{3,67},{4,68},{5,69},{6,70},{7,71},{8,72},{9,... | collective-permute-start | bytes 1671176 | tf_op jit(solution)/shard_map/ppermute | solution.py:52
  37.7 10.1 %collective-permute-start.10 = (bf16[17,16,256]{2,1,0:T(8,128)(2,1)S(1)}, bf16[17,16,256]{2,1,0:T(8,128)(2,1)S(1)}, u32[]{:S(2)}, u32[]{:S(2)}) collective-permute-start(bf16[17,16,256]{2,1,0:T(8,128)(2,1)S(1)} %get-tuple-element.61), channel_id=1, source_target_pairs={{0,48},{1,49},{2,50},{3,51},{4,52},{5,53},{6,54},{7,55},{8,56},{9,... | collective-permute-start | bytes 417800 | tf_op jit(solution)/shard_map/ppermute | solution.py:52
  47.8 6.6 %collective-permute-start.11 = (bf16[17,16,256]{2,1,0:T(8,128)(2,1)S(1)}, bf16[17,16,256]{2,1,0:T(8,128)(2,1)S(1)}, u32[]{:S(2)}, u32[]{:S(2)}) collective-permute-start(bf16[17,16,256]{2,1,0:T(8,128)(2,1)S(1)} %get-tuple-element.61), channel_id=1, source_target_pairs={{0,32},{1,33},{2,34},{3,35},{4,36},{5,37},{6,38},{7,39},{8,40},{9,... | collective-permute-start | bytes 417800 | tf_op jit(solution)/shard_map/ppermute | solution.py:52
  54.4 6.7 %collective-permute-start.12 = (bf16[17,16,256]{2,1,0:T(8,128)(2,1)S(1)}, bf16[17,16,256]{2,1,0:T(8,128)(2,1)S(1)}, u32[]{:S(2)}, u32[]{:S(2)}) collective-permute-start(bf16[17,16,256]{2,1,0:T(8,128)(2,1)S(1)} %get-tuple-element.61), channel_id=1, source_target_pairs={{0,16},{1,17},{2,18},{3,19},{4,20},{5,21},{6,22},{7,23},{8,24},{9,... | collective-permute-start | bytes 417800 | tf_op jit(solution)/shard_map/ppermute | solution.py:52
  61.1 9.7 %collective-permute-start.13 = (bf16[4,17,16,256]{3,2,1,0:T(8,128)(2,1)S(1)}, bf16[4,17,16,256]{3,2,1,0:T(8,128)(2,1)}, u32[]{:S(2)}, u32[]{:S(2)}) collective-permute-start(bf16[4,17,16,256]{3,2,1,0:T(8,128)(2,1)S(1)} %pad_maximum_fusion.1.refs_0_), channel_id=1, source_target_pairs={{0,12},{1,13},{2,14},{3,15},{4,0},{5,1},{6,2},{7,3},{8,4},{9,5},{1... | collective-permute-start | bytes 1671176 | tf_op jit(solution)/shard_map/ppermute | solution.py:52
  62.1 11.2 %collective-permute-start.14 = (bf16[4,17,16,256]{3,2,1,0:T(8,128)(2,1)S(1)}, bf16[4,17,16,256]{3,2,1,0:T(8,128)(2,1)}, u32[]{:S(2)}, u32[]{:S(2)}) collective-permute-start(bf16[4,17,16,256]{3,2,1,0:T(8,128)(2,1)S(1)} %pad_maximum_fusion.1.refs_0_), channel_id=1, source_target_pairs={{0,8},{1,9},{2,10},{3,11},{4,12},{5,13},{6,14},{7,15},{8,0},{9,1},... | collective-permute-start | bytes 1671176 | tf_op jit(solution)/shard_map/ppermute | solution.py:52
  62.7 16.5 %collective-permute-start.15 = (bf16[4,17,16,256]{3,2,1,0:T(8,128)(2,1)S(1)}, bf16[4,17,16,256]{3,2,1,0:T(8,128)(2,1)}, u32[]{:S(2)}, u32[]{:S(2)}) collective-permute-start(bf16[4,17,16,256]{3,2,1,0:T(8,128)(2,1)S(1)} %pad_maximum_fusion.1.refs_0_), channel_id=1, source_target_pairs={{0,4},{1,5},{2,6},{3,7},{4,8},{5,9},{6,10},{7,11},{8,12},{9,13},{1... | collective-permute-start | bytes 1671176 | tf_op jit(solution)/shard_map/ppermute | solution.py:52
  63.6 15.6 %collective-permute-start.7 = (bf16[4,17,16,256]{3,2,1,0:T(8,128)(2,1)S(1)}, bf16[4,17,16,256]{3,2,1,0:T(8,128)(2,1)S(1)}, u32[]{:S(2)}, u32[]{:S(2)}) collective-permute-start(bf16[4,17,16,256]{3,2,1,0:T(8,128)(2,1)S(1)} %collective-permute-done.3.refs_1_), channel_id=1, source_target_pairs={{0,64},{1,65},{2,66},{3,67},{4,68},{5,69},{6,70},{7,71},{8,72},{9,... | collective-permute-start | bytes 1671176 | tf_op jit(solution)/shard_map/ppermute | solution.py:52
  63.6 0.8 copy-start.2
  64.4 0.8 copy-start.6
  65.2 15.3 %collective-permute-start.8 = (bf16[4,17,16,256]{3,2,1,0:T(8,128)(2,1)S(1)}, bf16[4,17,16,256]{3,2,1,0:T(8,128)(2,1)S(1)}, u32[]{:S(2)}, u32[]{:S(2)}) collective-permute-start(bf16[4,17,16,256]{3,2,1,0:T(8,128)(2,1)S(1)} %collective-permute-done.4.refs_2_), channel_id=1, source_target_pairs={{0,64},{1,65},{2,66},{3,67},{4,68},{5,69},{6,70},{7,71},{8,72},{9,... | collective-permute-start | bytes 1671176 | tf_op jit(solution)/shard_map/ppermute | solution.py:52
  65.7 0.8 copy-start.4
  70.9 18.1 %collective-permute-start.16 = (bf16[4,17,16,256]{3,2,1,0:T(8,128)(2,1)S(1)}, bf16[4,17,16,256]{3,2,1,0:T(8,128)(2,1)}, u32[]{:S(2)}, u32[]{:S(2)}) collective-permute-start(bf16[4,17,16,256]{3,2,1,0:T(8,128)(2,1)S(1)} %pad_maximum_fusion.1.refs_0_), channel_id=1, source_target_pairs={{0,64},{1,65},{2,66},{3,67},{4,68},{5,69},{6,70},{7,71},{8,72},{9,... | collective-permute-start | bytes 1671176 | tf_op jit(solution)/shard_map/ppermute | solution.py:52
  73.3 9.0 %collective-permute-start.9 = (bf16[4,17,16,256]{3,2,1,0:T(8,128)(2,1)}, bf16[4,17,16,256]{3,2,1,0:T(8,128)(2,1)}, u32[]{:S(2)}, u32[]{:S(2)}) collective-permute-start(bf16[4,17,16,256]{3,2,1,0:T(8,128)(2,1)} %collective-permute-done.5.refs_3_), channel_id=1, source_target_pairs={{0,64},{1,65},{2,66},{3,67},{4,68},{5,69},{6,70},{7,71},{8,72},{9,... | collective-permute-start | bytes 1671176 | tf_op jit(solution)/shard_map/ppermute | solution.py:52
  79.2 9.7 %collective-permute-start.17 = (bf16[4,17,16,256]{3,2,1,0:T(8,128)(2,1)}, bf16[4,17,16,256]{3,2,1,0:T(8,128)(2,1)}, u32[]{:S(2)}, u32[]{:S(2)}) collective-permute-start(bf16[4,17,16,256]{3,2,1,0:T(8,128)(2,1)} %collective-permute-done.13.refs_1_), channel_id=1, source_target_pairs={{0,64},{1,65},{2,66},{3,67},{4,68},{5,69},{6,70},{7,71},{8,72},{9,... | collective-permute-start | bytes 1671176 | tf_op jit(solution)/shard_map/ppermute | solution.py:52
  79.2 0.8 copy-start.8
  80.0 8.9 %collective-permute-start.18 = (bf16[4,17,16,256]{3,2,1,0:T(8,128)(2,1)}, bf16[4,17,16,256]{3,2,1,0:T(8,128)(2,1)}, u32[]{:S(2)}, u32[]{:S(2)}) collective-permute-start(bf16[4,17,16,256]{3,2,1,0:T(8,128)(2,1)} %collective-permute-done.14.refs_2_), channel_id=1, source_target_pairs={{0,64},{1,65},{2,66},{3,67},{4,68},{5,69},{6,70},{7,71},{8,72},{9,... | collective-permute-start | bytes 1671176 | tf_op jit(solution)/shard_map/ppermute | solution.py:52
  80.5 0.8 copy-start.10
  81.4 7.6 %collective-permute-start.19 = (bf16[4,17,16,256]{3,2,1,0:T(8,128)(2,1)}, bf16[4,17,16,256]{3,2,1,0:T(8,128)(2,1)}, u32[]{:S(2)}, u32[]{:S(2)}) collective-permute-start(bf16[4,17,16,256]{3,2,1,0:T(8,128)(2,1)} %collective-permute-done.15.refs_3_), channel_id=1, source_target_pairs={{0,64},{1,65},{2,66},{3,67},{4,68},{5,69},{6,70},{7,71},{8,72},{9,... | collective-permute-start | bytes 1671176 | tf_op jit(solution)/shard_map/ppermute | solution.py:52
  81.4 1.1 copy-start.3
  81.4 1.2 copy-start.5
  81.4 1.4 copy-start.7
  82.7 1.1 copy-start.9
  83.8 1.1 copy-start.11
  84.9 4.1 %copy-start.1 = (bf16[2,2,128,2048]{3,2,1,0:T(8,128)(2,1)S(1)}, bf16[2,2,128,2048]{3,2,1,0:T(8,128)(2,1)}, u32[]{:S(2)}) copy-start(bf16[2,2,128,2048]{3,2,1,0:T(8,128)(2,1)} %cots.1) | copy-start | bytes 6291460
  95.5 4.2 %collective-permute-start.25 = (bf16[144,4608]{1,0:T(8,128)(2,1)S(1)}, bf16[144,4608]{1,0:T(8,128)(2,1)S(1)}, u32[]{:S(2)}, u32[]{:S(2)}) collective-permute-start(bf16[144,4608]{1,0:T(8,128)(2,1)S(1)} %slice_bitcast_fusion.1), channel_id=1, source_target_pairs={{0,64},{1,65},{2,66},{3,67},{4,68},{5,69},{6,70},{7,71},{8,72},{9,... | collective-permute-start | bytes 3981320 | tf_op jit(solution)/shard_map/ppermute | solution.py:52
  99.6 4.8 %collective-permute-start.20 = (bf16[144,4608]{1,0:T(8,128)(2,1)S(1)}, bf16[144,4608]{1,0:T(8,128)(2,1)S(1)}, u32[]{:S(2)}, u32[]{:S(2)}) collective-permute-start(bf16[144,4608]{1,0:T(8,128)(2,1)S(1)} %slice_bitcast_fusion), channel_id=1, source_target_pairs={{0,64},{1,65},{2,66},{3,67},{4,68},{5,69},{6,70},{7,71},{8,72},{9,... | collective-permute-start | bytes 3981320 | tf_op jit(solution)/shard_map/ppermute | solution.py:52
  101.1 8.0 %collective-permute-start.26 = (bf16[2,17,16,256]{3,2,1,0:T(8,128)(2,1)S(1)}, bf16[2,17,16,256]{3,2,1,0:T(8,128)(2,1)S(1)}, u32[]{:S(2)}, u32[]{:S(2)}) collective-permute-start(bf16[2,17,16,256]{3,2,1,0:T(8,128)(2,1)S(1)} %get-tuple-element.47), channel_id=1, source_target_pairs={{0,16},{1,17},{2,18},{3,19},{4,20},{5,21},{6,22},{7,23},{8,24},{9,... | collective-permute-start | bytes 835592 | tf_op jit(solution)/shard_map/ppermute | solution.py:52
  101.2 7.9 %collective-permute-start.27 = (bf16[2,17,16,256]{3,2,1,0:T(8,128)(2,1)S(1)}, bf16[2,17,16,256]{3,2,1,0:T(8,128)(2,1)S(1)}, u32[]{:S(2)}, u32[]{:S(2)}) collective-permute-start(bf16[2,17,16,256]{3,2,1,0:T(8,128)(2,1)S(1)} %get-tuple-element.48), channel_id=1, source_target_pairs={{0,48},{1,49},{2,50},{3,51},{4,52},{5,53},{6,54},{7,55},{8,56},{9,... | collective-permute-start | bytes 835592 | tf_op jit(solution)/shard_map/ppermute | solution.py:52
  105.7 7.8 %collective-permute-start.21 = (bf16[2,17,16,256]{3,2,1,0:T(8,128)(2,1)S(1)}, bf16[2,17,16,256]{3,2,1,0:T(8,128)(2,1)S(1)}, u32[]{:S(2)}, u32[]{:S(2)}) collective-permute-start(bf16[2,17,16,256]{3,2,1,0:T(8,128)(2,1)S(1)} %get-tuple-element.41), channel_id=1, source_target_pairs={{0,16},{1,17},{2,18},{3,19},{4,20},{5,21},{6,22},{7,23},{8,24},{9,... | collective-permute-start | bytes 835592 | tf_op jit(solution)/shard_map/ppermute | solution.py:52
  105.8 7.7 %collective-permute-start.22 = (bf16[2,17,16,256]{3,2,1,0:T(8,128)(2,1)S(1)}, bf16[2,17,16,256]{3,2,1,0:T(8,128)(2,1)S(1)}, u32[]{:S(2)}, u32[]{:S(2)}) collective-permute-start(bf16[2,17,16,256]{3,2,1,0:T(8,128)(2,1)S(1)} %get-tuple-element.42), channel_id=1, source_target_pairs={{0,48},{1,49},{2,50},{3,51},{4,52},{5,53},{6,54},{7,55},{8,56},{9,... | collective-permute-start | bytes 835592 | tf_op jit(solution)/shard_map/ppermute | solution.py:52
  109.8 10.8 %collective-permute-start.28 = (bf16[4,17,16,256]{3,2,1,0:T(8,128)(2,1)S(1)}, bf16[4,17,16,256]{3,2,1,0:T(8,128)(2,1)S(1)}, u32[]{:S(2)}, u32[]{:S(2)}) collective-permute-start(bf16[4,17,16,256]{3,2,1,0:T(8,128)(2,1)S(1)} %get-tuple-element.49), channel_id=1, source_target_pairs={{0,16},{1,17},{2,18},{3,19},{4,20},{5,21},{6,22},{7,23},{8,24},{9,... | collective-permute-start | bytes 1671176 | tf_op jit(solution)/shard_map/ppermute | solution.py:52
  109.9 10.7 %collective-permute-start.29 = (bf16[4,17,16,256]{3,2,1,0:T(8,128)(2,1)S(1)}, bf16[4,17,16,256]{3,2,1,0:T(8,128)(2,1)S(1)}, u32[]{:S(2)}, u32[]{:S(2)}) collective-permute-start(bf16[4,17,16,256]{3,2,1,0:T(8,128)(2,1)S(1)} %get-tuple-element.50), channel_id=1, source_target_pairs={{0,48},{1,49},{2,50},{3,51},{4,52},{5,53},{6,54},{7,55},{8,56},{9,... | collective-permute-start | bytes 1671176 | tf_op jit(solution)/shard_map/ppermute | solution.py:52
  114.3 12.3 %collective-permute-start.23 = (bf16[4,17,16,256]{3,2,1,0:T(8,128)(2,1)S(1)}, bf16[4,17,16,256]{3,2,1,0:T(8,128)(2,1)S(1)}, u32[]{:S(2)}, u32[]{:S(2)}) collective-permute-start(bf16[4,17,16,256]{3,2,1,0:T(8,128)(2,1)S(1)} %get-tuple-element.43), channel_id=1, source_target_pairs={{0,16},{1,17},{2,18},{3,19},{4,20},{5,21},{6,22},{7,23},{8,24},{9,... | collective-permute-start | bytes 1671176 | tf_op jit(solution)/shard_map/ppermute | solution.py:52
  114.4 12.2 %collective-permute-start.24 = (bf16[4,17,16,256]{3,2,1,0:T(8,128)(2,1)S(1)}, bf16[4,17,16,256]{3,2,1,0:T(8,128)(2,1)S(1)}, u32[]{:S(2)}, u32[]{:S(2)}) collective-permute-start(bf16[4,17,16,256]{3,2,1,0:T(8,128)(2,1)S(1)} %get-tuple-element.44), channel_id=1, source_target_pairs={{0,48},{1,49},{2,50},{3,51},{4,52},{5,53},{6,54},{7,55},{8,56},{9,... | collective-permute-start | bytes 1671176 | tf_op jit(solution)/shard_map/ppermute | solution.py:52
  127.6 8.2 %collective-permute-start.30 = (bf16[2,17,16,256]{3,2,1,0:T(8,128)(2,1)S(1)}, bf16[2,17,16,256]{3,2,1,0:T(8,128)(2,1)S(1)}, u32[]{:S(2)}, u32[]{:S(2)}) collective-permute-start(bf16[2,17,16,256]{3,2,1,0:T(8,128)(2,1)S(1)} %get-tuple-element.52), channel_id=1, source_target_pairs={{0,8},{1,9},{2,10},{3,11},{4,12},{5,13},{6,14},{7,15},{8,0},{9,1},... | collective-permute-start | bytes 835592 | tf_op jit(solution)/shard_map/ppermute | solution.py:52
  128.3 10.4 %collective-permute-start.31 = (bf16[2,17,16,256]{3,2,1,0:T(8,128)(2,1)S(1)}, bf16[2,17,16,256]{3,2,1,0:T(8,128)(2,1)S(1)}, u32[]{:S(2)}, u32[]{:S(2)}) collective-permute-start(bf16[2,17,16,256]{3,2,1,0:T(8,128)(2,1)S(1)} %get-tuple-element.53), channel_id=1, source_target_pairs={{0,4},{1,5},{2,6},{3,7},{4,8},{5,9},{6,10},{7,11},{8,12},{9,13},{1... | collective-permute-start | bytes 835592 | tf_op jit(solution)/shard_map/ppermute | solution.py:52
  129.4 9.4 %collective-permute-start.32 = (bf16[2,17,16,256]{3,2,1,0:T(8,128)(2,1)S(1)}, bf16[2,17,16,256]{3,2,1,0:T(8,128)(2,1)S(1)}, u32[]{:S(2)}, u32[]{:S(2)}) collective-permute-start(bf16[2,17,16,256]{3,2,1,0:T(8,128)(2,1)S(1)} %get-tuple-element.54), channel_id=1, source_target_pairs={{0,12},{1,13},{2,14},{3,15},{4,0},{5,1},{6,2},{7,3},{8,4},{9,5},{1... | collective-permute-start | bytes 835592 | tf_op jit(solution)/shard_map/ppermute | solution.py:52

commit v10 on v9

--- a/solution.py
+++ b/solution.py
@@ -53,8 +53,8 @@
 
 
 def around(value, send):
-    across = shift(value, send(-2))
-    return [shift(value, send(-1)), across, shift(value, send(-3))]
+    after, before = shift(value, send(-1)), shift(value, send(-3))
+    return [after, shift(value, send(-2)), before]
 
 
 def dot(left, right, left_dim=1, right_dim=0):
@@ -396,7 +396,8 @@
 def scatter_second(scalars, low, high):
     piece = array(2, 17, 16, 256)
     own, *pieces = call(kernel_sum, scalars, [*low, *high], [piece] * 4, [])
-    got = [shift(pieces[k - 1], send_second(k)) for k in (2, 1, 3)]
+    got = [shift(pieces[k - 1], send_second(k)) for k in (1, 3)]
+    got.append(shift(pieces[1], send_second(2)))
     return add_up(own, got)
 
 

time: 155 us -> 155 us (level)
  transfers between devices with their start and end apart: 33 -> 33, of which waited for: 14 -> 15; matrix products, arithmetic and copies ran while one was open for 0% -> 0% of each run, Pallas kernels for 8% -> 8%
where the time goes in v10:
time: 155 us; the launch traced here: 153 us
  waiting for transfers between devices  58.2 us (38%)
  blocking collectives  31.9 us (21%)
  starting transfers between devices  31.5 us (20%)
  Pallas kernels  21.2 us (14%)
  local copies, waits for them, and re-layouts  8.14 us (5%)
    ppermute x33, waiting for transfers between devices, shift(): return lax.ppermute(value, AXES, pairs)  58.2 us
    ppermute x33, starting transfers between devices, shift(): return lax.ppermute(value, AXES, pairs)  31.5 us
    pallas_call x10, Pallas kernels, call(): pl.pallas_call(body, in_specs=[pl.BlockSpec(memory_space=pltpu.SMEM)] + [...  21.2 us
    all_to_all x1, blocking collectives, device_body(): lax.all_to_all(jnp.broadcast_to(shard[None], (8, 72, 256)), ('zl', 'zh'),...  19.5 us
    all_to_all x1, blocking collectives, device_body(): lax.all_to_all(parts, ('zl', 'zh'), 0, 0)  12.4 us
    unnamed x26, local copies, waits for them, and re-layouts  7.41 us
  transfers between devices with their start and end apart: 33, of which 15 were waited for; matrix products, arithmetic and copies ran while one was open for 0% of the time, Pallas kernels for 8%

profile of v10, /device:TPU:32, one launch (start us, length us, event | category | flops | bytes accessed | tf_op | source)
XLA Modules:
  0.0 153.0 jit_solution(12376426002362896771)
XLA Ops:
  0.6 0.7 copy.39
  1.4 0.7 fusion.3
  2.1 19.5 %all_to_all.10 = bf16[8,72,256]{2,1,0:T(8,128)(2,1)S(1)} all-to-all(bf16[8,72,256]{2,1,0:T(8,128)(2,1)S(1)} %broadcast_in_dim.2), channel_id=1, replica_groups=mesh['zl'=2,'c'=2,'x'=4,'y'=4,'zh'=4] {'zl','zh'}, dimensions={0} | all-to-all | bytes 589824 | tf_op jit(solution)/shard_map/all_to_all | solution.py:415
  22.1 2.8 %collective-permute-start = (bf16[17,16,256]{2,1,0:T(8,128)(2,1)S(1)}, bf16[17,16,256]{2,1,0:T(8,128)(2,1)S(1)}, u32[]{:S(2)}, u32[]{:S(2)}) collective-permute-start(bf16[17,16,256]{2,1,0:T(8,128)(2,1)S(1)} %get-tuple-element.60), channel_id=1, source_target_pairs={{0,48},{1,49},{2,50},{3,51},{4,52},{5,53},{6,54},{7,55},{8,56},{9,... | collective-permute-start | bytes 417800 | tf_op jit(solution)/shard_map/ppermute | solution.py:52
  24.9 0.8 collective-permute-start.1
  25.7 0.9 collective-permute-start.2
  26.6 2.4 %collective-permute-done = bf16[17,16,256]{2,1,0:T(8,128)(2,1)S(1)} collective-permute-done((bf16[17,16,256]{2,1,0:T(8,128)(2,1)S(1)}, bf16[17,16,256]{2,1,0:T(8,128)(2,1)S(1)}, u32[]{:S(2)}, u32[]{:S(2)}) %collective-permute-start) | collective-permute-done | bytes 139296 | tf_op jit(solution)/shard_map/ppermute | solution.py:52
  29.0 2.6 %collective-permute-done.1 = bf16[17,16,256]{2,1,0:T(8,128)(2,1)S(1)} collective-permute-done((bf16[17,16,256]{2,1,0:T(8,128)(2,1)S(1)}, bf16[17,16,256]{2,1,0:T(8,128)(2,1)S(1)}, u32[]{:S(2)}, u32[]{:S(2)}) %collective-permute-start.1) | collective-permute-done | bytes 139296 | tf_op jit(solution)/shard_map/ppermute | solution.py:52
  31.6 1.4 collective-permute-done.2
  33.0 3.1 %collective-permute-start.3 = (bf16[4,17,16,256]{3,2,1,0:T(8,128)(2,1)S(1)}, bf16[4,17,16,256]{3,2,1,0:T(8,128)(2,1)S(1)}, u32[]{:S(2)}, u32[]{:S(2)}) collective-permute-start(bf16[4,17,16,256]{3,2,1,0:T(8,128)(2,1)S(1)} %pad_maximum_fusion.refs_0_), channel_id=1, source_target_pairs={{0,12},{1,13},{2,14},{3,15},{4,0},{5,1},{6,2},{7,3},{8,4},{9,5},{1... | collective-permute-start | bytes 1671176 | tf_op jit(solution)/shard_map/ppermute | solution.py:52
  36.8 1.0 collective-permute-start.5
  38.3 9.5 %collective-permute-done.10 = bf16[17,16,256]{2,1,0:T(8,128)(2,1)S(1)} collective-permute-done((bf16[17,16,256]{2,1,0:T(8,128)(2,1)S(1)}, bf16[17,16,256]{2,1,0:T(8,128)(2,1)S(1)}, u32[]{:S(2)}, u32[]{:S(2)}) %collective-permute-start.10) | collective-permute-done | bytes 139296 | tf_op jit(solution)/shard_map/ppermute | solution.py:52
  47.8 6.6 %collective-permute-done.11 = bf16[17,16,256]{2,1,0:T(8,128)(2,1)S(1)} collective-permute-done((bf16[17,16,256]{2,1,0:T(8,128)(2,1)S(1)}, bf16[17,16,256]{2,1,0:T(8,128)(2,1)S(1)}, u32[]{:S(2)}, u32[]{:S(2)}) %collective-permute-start.11) | collective-permute-done | bytes 139296 | tf_op jit(solution)/shard_map/ppermute | solution.py:52
  54.4 1.0 collective-permute-start.12
  55.4 5.7 %collective-permute-done.12 = bf16[17,16,256]{2,1,0:T(8,128)(2,1)S(1)} collective-permute-done((bf16[17,16,256]{2,1,0:T(8,128)(2,1)S(1)}, bf16[17,16,256]{2,1,0:T(8,128)(2,1)S(1)}, u32[]{:S(2)}, u32[]{:S(2)}) %collective-permute-start.12) | collective-permute-done | bytes 139296 | tf_op jit(solution)/shard_map/ppermute | solution.py:52
  61.1 0.9 collective-permute-start.13
  62.7 0.9 collective-permute-start.15
  63.6 0.8 copy-done.2
  64.4 0.8 copy-done.6
  65.7 0.8 copy-done.4
  66.5 4.3 %collective-permute-done.13.refs_1_ = bf16[4,17,16,256]{3,2,1,0:T(8,128)(2,1)} collective-permute-done((bf16[4,17,16,256]{3,2,1,0:T(8,128)(2,1)S(1)}, bf16[4,17,16,256]{3,2,1,0:T(8,128)(2,1)}, u32[]{:S(2)}, u32[]{:S(2)}) %collective-permute-start.13) | collective-permute-done | bytes 557088 | tf_op jit(solution)/shard_map/ppermute | solution.py:52
  70.9 2.5 %collective-permute-done.14.refs_2_ = bf16[4,17,16,256]{3,2,1,0:T(8,128)(2,1)} collective-permute-done((bf16[4,17,16,256]{3,2,1,0:T(8,128)(2,1)S(1)}, bf16[4,17,16,256]{3,2,1,0:T(8,128)(2,1)}, u32[]{:S(2)}, u32[]{:S(2)}) %collective-permute-start.14) | collective-permute-done | bytes 557088 | tf_op jit(solution)/shard_map/ppermute | solution.py:52
  73.3 5.9 %collective-permute-done.15.refs_3_ = bf16[4,17,16,256]{3,2,1,0:T(8,128)(2,1)} collective-permute-done((bf16[4,17,16,256]{3,2,1,0:T(8,128)(2,1)S(1)}, bf16[4,17,16,256]{3,2,1,0:T(8,128)(2,1)}, u32[]{:S(2)}, u32[]{:S(2)}) %collective-permute-start.15) | collective-permute-done | bytes 557088 | tf_op jit(solution)/shard_map/ppermute | solution.py:52
  79.2 0.8 copy-done.8
  80.5 0.8 copy-done.10
  81.4 0.9 shard_map.76
  82.8 1.1 copy-done.9
  83.8 1.1 copy-done.11
  84.9 4.0 %shard_map.77 = (bf16[128,2048]{1,0:T(8,128)(2,1)S(1)}, bf16[128,2048]{1,0:T(8,128)(2,1)S(1)}, bf16[2,128,16,256]{3,2,1,0:T(8,128)(2,1)S(1)}, bf16[2,9,16,16,256...) custom-call(s32[4]{0:T(128)S(1)} %pad_add_fusion.s_ref, ...), custom_call_target="tpu_custom_call" | custom-call | tf_op jit(solution)/shard_map/pallas_call | solution.py:368
  89.0 6.5 %shard_map.78 = (bf16[128,2048]{1,0:T(8,128)(2,1)S(1)}, bf16[2,144,4608]{2,1,0:T(8,128)(2,1)S(1)}) custom-call(s32[4]{0:T(128)S(1)} %pad_add_fusion.s_ref, bf16[128,2048]{1,0:T(8,128)(2,1)S(1)} %get-tuple-element.31.x2, f32[128,2048]{1,0:T(8,128)S(1)} %get-tuple-element.32.hat0, f32[128,128]{1,0:T(8,128)S(1)} %get-tuple-element.33.rstd0, ...), custom_call_target="tpu_custom_call" | custom-call | tf_op jit(solution)/shard_map/pallas_call | solution.py:368
  96.1 3.4 %shard_map.79.acts = bf16[2,144,4608]{2,1,0:T(8,128)(2,1)S(1)} custom-call(s32[4]{0:T(128)S(1)} %pad_add_fusion.s_ref, bf16[2,2,128,2048]{3,2,1,0:T(8,128)(2,1)S(1)} %copy-done, bf16[128,2048]{1,0:T(8,128)(2,1)S(1)} %get-tuple-element.30.x1, bf16[128,2048]{1,0:T(8,128)(2,1)S(1)} %get-tuple-element.34.up2, ...), custom_call_target="tpu_custom_call" | custom-call | tf_op jit(solution)/shard_map/pallas_call | solution.py:368
  99.7 1.3 shard_map.82
  101.2 3.2 %collective-permute-start.27 = (bf16[2,17,16,256]{3,2,1,0:T(8,128)(2,1)S(1)}, bf16[2,17,16,256]{3,2,1,0:T(8,128)(2,1)S(1)}, u32[]{:S(2)}, u32[]{:S(2)}) collective-permute-start(bf16[2,17,16,256]{3,2,1,0:T(8,128)(2,1)S(1)} %get-tuple-element.48), channel_id=1, source_target_pairs={{0,48},{1,49},{2,50},{3,51},{4,52},{5,53},{6,54},{7,55},{8,56},{9,... | collective-permute-start | bytes 835592 | tf_op jit(solution)/shard_map/ppermute | solution.py:52
  104.4 1.3 shard_map.80
  105.8 3.2 %collective-permute-start.22 = (bf16[2,17,16,256]{3,2,1,0:T(8,128)(2,1)S(1)}, bf16[2,17,16,256]{3,2,1,0:T(8,128)(2,1)S(1)}, u32[]{:S(2)}, u32[]{:S(2)}) collective-permute-start(bf16[2,17,16,256]{3,2,1,0:T(8,128)(2,1)S(1)} %get-tuple-element.42), channel_id=1, source_target_pairs={{0,48},{1,49},{2,50},{3,51},{4,52},{5,53},{6,54},{7,55},{8,56},{9,... | collective-permute-start | bytes 835592 | tf_op jit(solution)/shard_map/ppermute | solution.py:52
  109.1 0.7 shard_map.83
  109.9 3.2 %collective-permute-start.29 = (bf16[4,17,16,256]{3,2,1,0:T(8,128)(2,1)S(1)}, bf16[4,17,16,256]{3,2,1,0:T(8,128)(2,1)S(1)}, u32[]{:S(2)}, u32[]{:S(2)}) collective-permute-start(bf16[4,17,16,256]{3,2,1,0:T(8,128)(2,1)S(1)} %get-tuple-element.50), channel_id=1, source_target_pairs={{0,48},{1,49},{2,50},{3,51},{4,52},{5,53},{6,54},{7,55},{8,56},{9,... | collective-permute-start | bytes 1671176 | tf_op jit(solution)/shard_map/ppermute | solution.py:52
  113.6 0.7 shard_map.81
  114.4 3.3 %collective-permute-start.24 = (bf16[4,17,16,256]{3,2,1,0:T(8,128)(2,1)S(1)}, bf16[4,17,16,256]{3,2,1,0:T(8,128)(2,1)S(1)}, u32[]{:S(2)}, u32[]{:S(2)}) collective-permute-start(bf16[4,17,16,256]{3,2,1,0:T(8,128)(2,1)S(1)} %get-tuple-element.44), channel_id=1, source_target_pairs={{0,48},{1,49},{2,50},{3,51},{4,52},{5,53},{6,54},{7,55},{8,56},{9,... | collective-permute-start | bytes 1671176 | tf_op jit(solution)/shard_map/ppermute | solution.py:52
  117.7 2.9 %collective-permute-done.28.high_a = bf16[4,17,16,256]{3,2,1,0:T(8,128)(2,1)S(1)} collective-permute-done((bf16[4,17,16,256]{3,2,1,0:T(8,128)(2,1)S(1)}, bf16[4,17,16,256]{3,2,1,0:T(8,128)(2,1)S(1)}, u32[]{:S(2)}, u32[]{:S(2)}) %collective-permute-start.28) | collective-permute-done | bytes 557088 | tf_op jit(solution)/shard_map/ppermute | solution.py:52
  120.6 6.0 %collective-permute-done.23.low_a = bf16[4,17,16,256]{3,2,1,0:T(8,128)(2,1)S(1)} collective-permute-done((bf16[4,17,16,256]{3,2,1,0:T(8,128)(2,1)S(1)}, bf16[4,17,16,256]{3,2,1,0:T(8,128)(2,1)S(1)}, u32[]{:S(2)}, u32[]{:S(2)}) %collective-permute-start.23) | collective-permute-done | bytes 557088 | tf_op jit(solution)/shard_map/ppermute | solution.py:52
  126.6 1.0 shard_map.84
  127.7 3.2 %collective-permute-start.31 = (bf16[2,17,16,256]{3,2,1,0:T(8,128)(2,1)S(1)}, bf16[2,17,16,256]{3,2,1,0:T(8,128)(2,1)S(1)}, u32[]{:S(2)}, u32[]{:S(2)}) collective-permute-start(bf16[2,17,16,256]{3,2,1,0:T(8,128)(2,1)S(1)} %get-tuple-element.53), channel_id=1, source_target_pairs={{0,12},{1,13},{2,14},{3,15},{4,0},{5,1},{6,2},{7,3},{8,4},{9,5},{1... | collective-permute-start | bytes 835592 | tf_op jit(solution)/shard_map/ppermute | solution.py:52
  130.9 4.5 %collective-permute-done.30 = bf16[2,17,16,256]{3,2,1,0:T(8,128)(2,1)S(1)} collective-permute-done((bf16[2,17,16,256]{3,2,1,0:T(8,128)(2,1)S(1)}, bf16[2,17,16,256]{3,2,1,0:T(8,128)(2,1)S(1)}, u32[]{:S(2)}, u32[]{:S(2)}) %collective-permute-start.30) | collective-permute-done | bytes 278560 | tf_op jit(solution)/shard_map/ppermute | solution.py:52
  135.5 2.5 %collective-permute-done.31 = bf16[2,17,16,256]{3,2,1,0:T(8,128)(2,1)S(1)} collective-permute-done((bf16[2,17,16,256]{3,2,1,0:T(8,128)(2,1)S(1)}, bf16[2,17,16,256]{3,2,1,0:T(8,128)(2,1)S(1)}, u32[]{:S(2)}, u32[]{:S(2)}) %collective-permute-start.31) | collective-permute-done | bytes 278560 | tf_op jit(solution)/shard_map/ppermute | solution.py:52
  138.0 1.0 collective-permute-done.32
  139.4 12.4 %all_to_all.11.parts = bf16[8,72,256]{2,1,0:T(8,128)(2,1)S(1)} all-to-all(bf16[8,72,256]{2,1,0:T(8,128)(2,1)S(1)} %pad_maximum_fusion.2), channel_id=1, replica_groups=mesh['zl'=2,'c'=2,'x'=4,'y'=4,'zh'=4] {'zl','zh'}, dimensions={0} | all-to-all | bytes 589824 | tf_op jit(solution)/shard_map/all_to_all | solution.py:481
  151.8 1.2 shard_map.85
  (81 shorter events, 6.2 us)
Async XLA Ops:
  21.8 59.7 %copy-start = (bf16[2,2,128,2048]{3,2,1,0:T(8,128)(2,1)S(1)}, bf16[2,2,128,2048]{3,2,1,0:T(8,128)(2,1)}, u32[]{:S(2)}) copy-start(bf16[2,2,128,2048]{3,2,1,0:T(8,128)(2,1)} %xs.5) | copy-start | bytes 6291460
  22.1 6.9 %collective-permute-start = (bf16[17,16,256]{2,1,0:T(8,128)(2,1)S(1)}, bf16[17,16,256]{2,1,0:T(8,128)(2,1)S(1)}, u32[]{:S(2)}, u32[]{:S(2)}) collective-permute-start(bf16[17,16,256]{2,1,0:T(8,128)(2,1)S(1)} %get-tuple-element.60), channel_id=1, source_target_pairs={{0,48},{1,49},{2,50},{3,51},{4,52},{5,53},{6,54},{7,55},{8,56},{9,... | collective-permute-start | bytes 417800 | tf_op jit(solution)/shard_map/ppermute | solution.py:52
  24.9 6.7 %collective-permute-start.1 = (bf16[17,16,256]{2,1,0:T(8,128)(2,1)S(1)}, bf16[17,16,256]{2,1,0:T(8,128)(2,1)S(1)}, u32[]{:S(2)}, u32[]{:S(2)}) collective-permute-start(bf16[17,16,256]{2,1,0:T(8,128)(2,1)S(1)} %get-tuple-element.60), channel_id=1, source_target_pairs={{0,32},{1,33},{2,34},{3,35},{4,36},{5,37},{6,38},{7,39},{8,40},{9,... | collective-permute-start | bytes 417800 | tf_op jit(solution)/shard_map/ppermute | solution.py:52
  25.7 7.3 %collective-permute-start.2 = (bf16[17,16,256]{2,1,0:T(8,128)(2,1)S(1)}, bf16[17,16,256]{2,1,0:T(8,128)(2,1)S(1)}, u32[]{:S(2)}, u32[]{:S(2)}) collective-permute-start(bf16[17,16,256]{2,1,0:T(8,128)(2,1)S(1)} %get-tuple-element.60), channel_id=1, source_target_pairs={{0,16},{1,17},{2,18},{3,19},{4,20},{5,21},{6,22},{7,23},{8,24},{9,... | collective-permute-start | bytes 417800 | tf_op jit(solution)/shard_map/ppermute | solution.py:52
  33.0 29.0 %collective-permute-start.3 = (bf16[4,17,16,256]{3,2,1,0:T(8,128)(2,1)S(1)}, bf16[4,17,16,256]{3,2,1,0:T(8,128)(2,1)S(1)}, u32[]{:S(2)}, u32[]{:S(2)}) collective-permute-start(bf16[4,17,16,256]{3,2,1,0:T(8,128)(2,1)S(1)} %pad_maximum_fusion.refs_0_), channel_id=1, source_target_pairs={{0,12},{1,13},{2,14},{3,15},{4,0},{5,1},{6,2},{7,3},{8,4},{9,5},{1... | collective-permute-start | bytes 1671176 | tf_op jit(solution)/shard_map/ppermute | solution.py:52
  36.1 26.6 %collective-permute-start.4 = (bf16[4,17,16,256]{3,2,1,0:T(8,128)(2,1)S(1)}, bf16[4,17,16,256]{3,2,1,0:T(8,128)(2,1)S(1)}, u32[]{:S(2)}, u32[]{:S(2)}) collective-permute-start(bf16[4,17,16,256]{3,2,1,0:T(8,128)(2,1)S(1)} %pad_maximum_fusion.refs_0_), channel_id=1, source_target_pairs={{0,8},{1,9},{2,10},{3,11},{4,12},{5,13},{6,14},{7,15},{8,0},{9,1},... | collective-permute-start | bytes 1671176 | tf_op jit(solution)/shard_map/ppermute | solution.py:52
  36.8 26.8 %collective-permute-start.5 = (bf16[4,17,16,256]{3,2,1,0:T(8,128)(2,1)S(1)}, bf16[4,17,16,256]{3,2,1,0:T(8,128)(2,1)}, u32[]{:S(2)}, u32[]{:S(2)}) collective-permute-start(bf16[4,17,16,256]{3,2,1,0:T(8,128)(2,1)S(1)} %pad_maximum_fusion.refs_0_), channel_id=1, source_target_pairs={{0,4},{1,5},{2,6},{3,7},{4,8},{5,9},{6,10},{7,11},{8,12},{9,13},{1... | collective-permute-start | bytes 1671176 | tf_op jit(solution)/shard_map/ppermute | solution.py:52
  37.7 26.7 %collective-permute-start.6 = (bf16[4,17,16,256]{3,2,1,0:T(8,128)(2,1)S(1)}, bf16[4,17,16,256]{3,2,1,0:T(8,128)(2,1)S(1)}, u32[]{:S(2)}, u32[]{:S(2)}) collective-permute-start(bf16[4,17,16,256]{3,2,1,0:T(8,128)(2,1)S(1)} %pad_maximum_fusion.refs_0_), channel_id=1, source_target_pairs={{0,64},{1,65},{2,66},{3,67},{4,68},{5,69},{6,70},{7,71},{8,72},{9,... | collective-permute-start | bytes 1671176 | tf_op jit(solution)/shard_map/ppermute | solution.py:52
  37.7 10.1 %collective-permute-start.10 = (bf16[17,16,256]{2,1,0:T(8,128)(2,1)S(1)}, bf16[17,16,256]{2,1,0:T(8,128)(2,1)S(1)}, u32[]{:S(2)}, u32[]{:S(2)}) collective-permute-start(bf16[17,16,256]{2,1,0:T(8,128)(2,1)S(1)} %get-tuple-element.61), channel_id=1, source_target_pairs={{0,48},{1,49},{2,50},{3,51},{4,52},{5,53},{6,54},{7,55},{8,56},{9,... | collective-permute-start | bytes 417800 | tf_op jit(solution)/shard_map/ppermute | solution.py:52
  47.8 6.6 %collective-permute-start.11 = (bf16[17,16,256]{2,1,0:T(8,128)(2,1)S(1)}, bf16[17,16,256]{2,1,0:T(8,128)(2,1)S(1)}, u32[]{:S(2)}, u32[]{:S(2)}) collective-permute-start(bf16[17,16,256]{2,1,0:T(8,128)(2,1)S(1)} %get-tuple-element.61), channel_id=1, source_target_pairs={{0,32},{1,33},{2,34},{3,35},{4,36},{5,37},{6,38},{7,39},{8,40},{9,... | collective-permute-start | bytes 417800 | tf_op jit(solution)/shard_map/ppermute | solution.py:52
  54.4 6.7 %collective-permute-start.12 = (bf16[17,16,256]{2,1,0:T(8,128)(2,1)S(1)}, bf16[17,16,256]{2,1,0:T(8,128)(2,1)S(1)}, u32[]{:S(2)}, u32[]{:S(2)}) collective-permute-start(bf16[17,16,256]{2,1,0:T(8,128)(2,1)S(1)} %get-tuple-element.61), channel_id=1, source_target_pairs={{0,16},{1,17},{2,18},{3,19},{4,20},{5,21},{6,22},{7,23},{8,24},{9,... | collective-permute-start | bytes 417800 | tf_op jit(solution)/shard_map/ppermute | solution.py:52
  61.1 9.7 %collective-permute-start.13 = (bf16[4,17,16,256]{3,2,1,0:T(8,128)(2,1)S(1)}, bf16[4,17,16,256]{3,2,1,0:T(8,128)(2,1)}, u32[]{:S(2)}, u32[]{:S(2)}) collective-permute-start(bf16[4,17,16,256]{3,2,1,0:T(8,128)(2,1)S(1)} %pad_maximum_fusion.1.refs_0_), channel_id=1, source_target_pairs={{0,12},{1,13},{2,14},{3,15},{4,0},{5,1},{6,2},{7,3},{8,4},{9,5},{1... | collective-permute-start | bytes 1671176 | tf_op jit(solution)/shard_map/ppermute | solution.py:52
  62.1 11.2 %collective-permute-start.14 = (bf16[4,17,16,256]{3,2,1,0:T(8,128)(2,1)S(1)}, bf16[4,17,16,256]{3,2,1,0:T(8,128)(2,1)}, u32[]{:S(2)}, u32[]{:S(2)}) collective-permute-start(bf16[4,17,16,256]{3,2,1,0:T(8,128)(2,1)S(1)} %pad_maximum_fusion.1.refs_0_), channel_id=1, source_target_pairs={{0,8},{1,9},{2,10},{3,11},{4,12},{5,13},{6,14},{7,15},{8,0},{9,1},... | collective-permute-start | bytes 1671176 | tf_op jit(solution)/shard_map/ppermute | solution.py:52
  62.7 16.5 %collective-permute-start.15 = (bf16[4,17,16,256]{3,2,1,0:T(8,128)(2,1)S(1)}, bf16[4,17,16,256]{3,2,1,0:T(8,128)(2,1)}, u32[]{:S(2)}, u32[]{:S(2)}) collective-permute-start(bf16[4,17,16,256]{3,2,1,0:T(8,128)(2,1)S(1)} %pad_maximum_fusion.1.refs_0_), channel_id=1, source_target_pairs={{0,4},{1,5},{2,6},{3,7},{4,8},{5,9},{6,10},{7,11},{8,12},{9,13},{1... | collective-permute-start | bytes 1671176 | tf_op jit(solution)/shard_map/ppermute | solution.py:52
  63.6 15.6 %collective-permute-start.7 = (bf16[4,17,16,256]{3,2,1,0:T(8,128)(2,1)S(1)}, bf16[4,17,16,256]{3,2,1,0:T(8,128)(2,1)S(1)}, u32[]{:S(2)}, u32[]{:S(2)}) collective-permute-start(bf16[4,17,16,256]{3,2,1,0:T(8,128)(2,1)S(1)} %collective-permute-done.3.refs_1_), channel_id=1, source_target_pairs={{0,64},{1,65},{2,66},{3,67},{4,68},{5,69},{6,70},{7,71},{8,72},{9,... | collective-permute-start | bytes 1671176 | tf_op jit(solution)/shard_map/ppermute | solution.py:52
  63.6 0.8 copy-start.2
  64.4 0.8 copy-start.6
  65.2 15.3 %collective-permute-start.8 = (bf16[4,17,16,256]{3,2,1,0:T(8,128)(2,1)S(1)}, bf16[4,17,16,256]{3,2,1,0:T(8,128)(2,1)S(1)}, u32[]{:S(2)}, u32[]{:S(2)}) collective-permute-start(bf16[4,17,16,256]{3,2,1,0:T(8,128)(2,1)S(1)} %collective-permute-done.4.refs_2_), channel_id=1, source_target_pairs={{0,64},{1,65},{2,66},{3,67},{4,68},{5,69},{6,70},{7,71},{8,72},{9,... | collective-permute-start | bytes 1671176 | tf_op jit(solution)/shard_map/ppermute | solution.py:52
  65.7 0.8 copy-start.4
  70.9 18.1 %collective-permute-start.16 = (bf16[4,17,16,256]{3,2,1,0:T(8,128)(2,1)S(1)}, bf16[4,17,16,256]{3,2,1,0:T(8,128)(2,1)}, u32[]{:S(2)}, u32[]{:S(2)}) collective-permute-start(bf16[4,17,16,256]{3,2,1,0:T(8,128)(2,1)S(1)} %pad_maximum_fusion.1.refs_0_), channel_id=1, source_target_pairs={{0,64},{1,65},{2,66},{3,67},{4,68},{5,69},{6,70},{7,71},{8,72},{9,... | collective-permute-start | bytes 1671176 | tf_op jit(solution)/shard_map/ppermute | solution.py:52
  73.3 9.0 %collective-permute-start.9 = (bf16[4,17,16,256]{3,2,1,0:T(8,128)(2,1)}, bf16[4,17,16,256]{3,2,1,0:T(8,128)(2,1)}, u32[]{:S(2)}, u32[]{:S(2)}) collective-permute-start(bf16[4,17,16,256]{3,2,1,0:T(8,128)(2,1)} %collective-permute-done.5.refs_3_), channel_id=1, source_target_pairs={{0,64},{1,65},{2,66},{3,67},{4,68},{5,69},{6,70},{7,71},{8,72},{9,... | collective-permute-start | bytes 1671176 | tf_op jit(solution)/shard_map/ppermute | solution.py:52
  79.2 9.7 %collective-permute-start.17 = (bf16[4,17,16,256]{3,2,1,0:T(8,128)(2,1)}, bf16[4,17,16,256]{3,2,1,0:T(8,128)(2,1)}, u32[]{:S(2)}, u32[]{:S(2)}) collective-permute-start(bf16[4,17,16,256]{3,2,1,0:T(8,128)(2,1)} %collective-permute-done.13.refs_1_), channel_id=1, source_target_pairs={{0,64},{1,65},{2,66},{3,67},{4,68},{5,69},{6,70},{7,71},{8,72},{9,... | collective-permute-start | bytes 1671176 | tf_op jit(solution)/shard_map/ppermute | solution.py:52
  79.2 0.8 copy-start.8
  80.0 8.9 %collective-permute-start.18 = (bf16[4,17,16,256]{3,2,1,0:T(8,128)(2,1)}, bf16[4,17,16,256]{3,2,1,0:T(8,128)(2,1)}, u32[]{:S(2)}, u32[]{:S(2)}) collective-permute-start(bf16[4,17,16,256]{3,2,1,0:T(8,128)(2,1)} %collective-permute-done.14.refs_2_), channel_id=1, source_target_pairs={{0,64},{1,65},{2,66},{3,67},{4,68},{5,69},{6,70},{7,71},{8,72},{9,... | collective-permute-start | bytes 1671176 | tf_op jit(solution)/shard_map/ppermute | solution.py:52
  80.5 0.8 copy-start.10
  81.4 7.6 %collective-permute-start.19 = (bf16[4,17,16,256]{3,2,1,0:T(8,128)(2,1)}, bf16[4,17,16,256]{3,2,1,0:T(8,128)(2,1)}, u32[]{:S(2)}, u32[]{:S(2)}) collective-permute-start(bf16[4,17,16,256]{3,2,1,0:T(8,128)(2,1)} %collective-permute-done.15.refs_3_), channel_id=1, source_target_pairs={{0,64},{1,65},{2,66},{3,67},{4,68},{5,69},{6,70},{7,71},{8,72},{9,... | collective-permute-start | bytes 1671176 | tf_op jit(solution)/shard_map/ppermute | solution.py:52
  81.4 1.1 copy-start.3
  81.4 1.2 copy-start.5
  81.4 1.4 copy-start.7
  82.7 1.1 copy-start.9
  83.8 1.1 copy-start.11
  84.9 4.1 %copy-start.1 = (bf16[2,2,128,2048]{3,2,1,0:T(8,128)(2,1)S(1)}, bf16[2,2,128,2048]{3,2,1,0:T(8,128)(2,1)}, u32[]{:S(2)}) copy-start(bf16[2,2,128,2048]{3,2,1,0:T(8,128)(2,1)} %cots.1) | copy-start | bytes 6291460
  95.5 4.2 %collective-permute-start.25 = (bf16[144,4608]{1,0:T(8,128)(2,1)S(1)}, bf16[144,4608]{1,0:T(8,128)(2,1)S(1)}, u32[]{:S(2)}, u32[]{:S(2)}) collective-permute-start(bf16[144,4608]{1,0:T(8,128)(2,1)S(1)} %slice_bitcast_fusion.1), channel_id=1, source_target_pairs={{0,64},{1,65},{2,66},{3,67},{4,68},{5,69},{6,70},{7,71},{8,72},{9,... | collective-permute-start | bytes 3981320 | tf_op jit(solution)/shard_map/ppermute | solution.py:52
  99.6 4.8 %collective-permute-start.20 = (bf16[144,4608]{1,0:T(8,128)(2,1)S(1)}, bf16[144,4608]{1,0:T(8,128)(2,1)S(1)}, u32[]{:S(2)}, u32[]{:S(2)}) collective-permute-start(bf16[144,4608]{1,0:T(8,128)(2,1)S(1)} %slice_bitcast_fusion), channel_id=1, source_target_pairs={{0,64},{1,65},{2,66},{3,67},{4,68},{5,69},{6,70},{7,71},{8,72},{9,... | collective-permute-start | bytes 3981320 | tf_op jit(solution)/shard_map/ppermute | solution.py:52
  101.1 8.0 %collective-permute-start.26 = (bf16[2,17,16,256]{3,2,1,0:T(8,128)(2,1)S(1)}, bf16[2,17,16,256]{3,2,1,0:T(8,128)(2,1)S(1)}, u32[]{:S(2)}, u32[]{:S(2)}) collective-permute-start(bf16[2,17,16,256]{3,2,1,0:T(8,128)(2,1)S(1)} %get-tuple-element.47), channel_id=1, source_target_pairs={{0,16},{1,17},{2,18},{3,19},{4,20},{5,21},{6,22},{7,23},{8,24},{9,... | collective-permute-start | bytes 835592 | tf_op jit(solution)/shard_map/ppermute | solution.py:52
  101.2 7.9 %collective-permute-start.27 = (bf16[2,17,16,256]{3,2,1,0:T(8,128)(2,1)S(1)}, bf16[2,17,16,256]{3,2,1,0:T(8,128)(2,1)S(1)}, u32[]{:S(2)}, u32[]{:S(2)}) collective-permute-start(bf16[2,17,16,256]{3,2,1,0:T(8,128)(2,1)S(1)} %get-tuple-element.48), channel_id=1, source_target_pairs={{0,48},{1,49},{2,50},{3,51},{4,52},{5,53},{6,54},{7,55},{8,56},{9,... | collective-permute-start | bytes 835592 | tf_op jit(solution)/shard_map/ppermute | solution.py:52
  105.7 7.8 %collective-permute-start.21 = (bf16[2,17,16,256]{3,2,1,0:T(8,128)(2,1)S(1)}, bf16[2,17,16,256]{3,2,1,0:T(8,128)(2,1)S(1)}, u32[]{:S(2)}, u32[]{:S(2)}) collective-permute-start(bf16[2,17,16,256]{3,2,1,0:T(8,128)(2,1)S(1)} %get-tuple-element.41), channel_id=1, source_target_pairs={{0,16},{1,17},{2,18},{3,19},{4,20},{5,21},{6,22},{7,23},{8,24},{9,... | collective-permute-start | bytes 835592 | tf_op jit(solution)/shard_map/ppermute | solution.py:52
  105.8 7.7 %collective-permute-start.22 = (bf16[2,17,16,256]{3,2,1,0:T(8,128)(2,1)S(1)}, bf16[2,17,16,256]{3,2,1,0:T(8,128)(2,1)S(1)}, u32[]{:S(2)}, u32[]{:S(2)}) collective-permute-start(bf16[2,17,16,256]{3,2,1,0:T(8,128)(2,1)S(1)} %get-tuple-element.42), channel_id=1, source_target_pairs={{0,48},{1,49},{2,50},{3,51},{4,52},{5,53},{6,54},{7,55},{8,56},{9,... | collective-permute-start | bytes 835592 | tf_op jit(solution)/shard_map/ppermute | solution.py:52
  109.8 10.8 %collective-permute-start.28 = (bf16[4,17,16,256]{3,2,1,0:T(8,128)(2,1)S(1)}, bf16[4,17,16,256]{3,2,1,0:T(8,128)(2,1)S(1)}, u32[]{:S(2)}, u32[]{:S(2)}) collective-permute-start(bf16[4,17,16,256]{3,2,1,0:T(8,128)(2,1)S(1)} %get-tuple-element.49), channel_id=1, source_target_pairs={{0,16},{1,17},{2,18},{3,19},{4,20},{5,21},{6,22},{7,23},{8,24},{9,... | collective-permute-start | bytes 1671176 | tf_op jit(solution)/shard_map/ppermute | solution.py:52
  109.9 10.7 %collective-permute-start.29 = (bf16[4,17,16,256]{3,2,1,0:T(8,128)(2,1)S(1)}, bf16[4,17,16,256]{3,2,1,0:T(8,128)(2,1)S(1)}, u32[]{:S(2)}, u32[]{:S(2)}) collective-permute-start(bf16[4,17,16,256]{3,2,1,0:T(8,128)(2,1)S(1)} %get-tuple-element.50), channel_id=1, source_target_pairs={{0,48},{1,49},{2,50},{3,51},{4,52},{5,53},{6,54},{7,55},{8,56},{9,... | collective-permute-start | bytes 1671176 | tf_op jit(solution)/shard_map/ppermute | solution.py:52
  114.3 12.3 %collective-permute-start.23 = (bf16[4,17,16,256]{3,2,1,0:T(8,128)(2,1)S(1)}, bf16[4,17,16,256]{3,2,1,0:T(8,128)(2,1)S(1)}, u32[]{:S(2)}, u32[]{:S(2)}) collective-permute-start(bf16[4,17,16,256]{3,2,1,0:T(8,128)(2,1)S(1)} %get-tuple-element.43), channel_id=1, source_target_pairs={{0,16},{1,17},{2,18},{3,19},{4,20},{5,21},{6,22},{7,23},{8,24},{9,... | collective-permute-start | bytes 1671176 | tf_op jit(solution)/shard_map/ppermute | solution.py:52
  114.4 12.2 %collective-permute-start.24 = (bf16[4,17,16,256]{3,2,1,0:T(8,128)(2,1)S(1)}, bf16[4,17,16,256]{3,2,1,0:T(8,128)(2,1)S(1)}, u32[]{:S(2)}, u32[]{:S(2)}) collective-permute-start(bf16[4,17,16,256]{3,2,1,0:T(8,128)(2,1)S(1)} %get-tuple-element.44), channel_id=1, source_target_pairs={{0,48},{1,49},{2,50},{3,51},{4,52},{5,53},{6,54},{7,55},{8,56},{9,... | collective-permute-start | bytes 1671176 | tf_op jit(solution)/shard_map/ppermute | solution.py:52
  127.6 7.8 %collective-permute-start.30 = (bf16[2,17,16,256]{3,2,1,0:T(8,128)(2,1)S(1)}, bf16[2,17,16,256]{3,2,1,0:T(8,128)(2,1)S(1)}, u32[]{:S(2)}, u32[]{:S(2)}) collective-permute-start(bf16[2,17,16,256]{3,2,1,0:T(8,128)(2,1)S(1)} %get-tuple-element.52), channel_id=1, source_target_pairs={{0,4},{1,5},{2,6},{3,7},{4,8},{5,9},{6,10},{7,11},{8,12},{9,13},{1... | collective-permute-start | bytes 835592 | tf_op jit(solution)/shard_map/ppermute | solution.py:52
  127.7 10.3 %collective-permute-start.31 = (bf16[2,17,16,256]{3,2,1,0:T(8,128)(2,1)S(1)}, bf16[2,17,16,256]{3,2,1,0:T(8,128)(2,1)S(1)}, u32[]{:S(2)}, u32[]{:S(2)}) collective-permute-start(bf16[2,17,16,256]{3,2,1,0:T(8,128)(2,1)S(1)} %get-tuple-element.53), channel_id=1, source_target_pairs={{0,12},{1,13},{2,14},{3,15},{4,0},{5,1},{6,2},{7,3},{8,4},{9,5},{1... | collective-permute-start | bytes 835592 | tf_op jit(solution)/shard_map/ppermute | solution.py:52
  130.9 8.1 %collective-permute-start.32 = (bf16[2,17,16,256]{3,2,1,0:T(8,128)(2,1)S(1)}, bf16[2,17,16,256]{3,2,1,0:T(8,128)(2,1)S(1)}, u32[]{:S(2)}, u32[]{:S(2)}) collective-permute-start(bf16[2,17,16,256]{3,2,1,0:T(8,128)(2,1)S(1)} %get-tuple-element.54), channel_id=1, source_target_pairs={{0,8},{1,9},{2,10},{3,11},{4,12},{5,13},{6,14},{7,15},{8,0},{9,1},... | collective-permute-start | bytes 835592 | tf_op jit(solution)/shard_map/ppermute | solution.py:52
